TPU v7x, 32 devices: a whole 2x2x4 slice. The times are simulated.
32 devices in a mesh: dp: 8 (over z, x), fsdp: 4 (over y, core).
Axes of the slice: x: 2, y: 2, z: 4, core: 2. Of those that a mesh axis runs over, the one named last changes fastest.
Arguments:
- tokens: bfloat16 [4096, 2048], P(('dp', 'fsdp')), may hold values from -4 to 4
- cotangent: bfloat16 [4096, 2048], P(('dp', 'fsdp')), may hold values from -4 to 4
- context: bfloat16 [64, 128, 4096], P(('dp', 'fsdp')), may hold values from -6 to 6
- lengths: int32 [32, 2], P(('dp', 'fsdp')), may hold values from 0 to 128, as said below
- keep: int32 [4096], P(('dp', 'fsdp')), may hold values 0 or 1
- owners: int32 [18], replicated, may hold values from 0 to 3, as said below
- master: float32 [24, 2048, 2048], P('fsdp', 'dp'), may hold values from -0.125 to 0.125
- moment_one: float32 [24, 2048, 2048], P('fsdp', 'dp'), may hold values from -14 to 14
- moment_two: float32 [24, 2048, 2048], P('fsdp', 'dp'), may hold values from 20.48 to 86.016
- gains: float32 [3, 2048], replicated, may hold values from 0.5 to 1.5
- gain_one: float32 [3, 2048], replicated, may hold values from -20 to 20
- gain_two: float32 [3, 2048], replicated, may hold values from 53.248 to 204.8
Outputs:
- layer_out: bfloat16 [4096, 2048], P(('dp', 'fsdp'))
- grad_tokens: bfloat16 [4096, 2048], P(('dp', 'fsdp'))
- new_master: float32 [24, 2048, 2048], P('fsdp', 'dp')
- new_one: float32 [24, 2048, 2048], P('fsdp', 'dp')
- new_two: float32 [24, 2048, 2048], P('fsdp', 'dp')
- new_gains: float32 [3, 2048], replicated
- new_gain_one: float32 [3, 2048], replicated
- new_gain_two: float32 [3, 2048], replicated
Inputs may be any that keep to these rules, and one draw needn't show every extreme that they name: `lengths`: each device's row is either one item of 128 tokens followed by zeros, or 2 items of 64 tokens; both kinds occur in every draw. `owners`: every owner holds 1 to 6 tiles, and two hold exactly 6.
All inputs are finite; a program needn't handle non-finite values. No bound on the sum of `keep` on one device may be relied on, other than what follows from the above.
Results may differ from a plain program's by a relative error of at most 0.028.
Values may be sent and summed in bfloat16 or wider, within the bound.
No kernel may reach another device: no remote copies, remote signals or barrier semaphores. Data moves between devices by JAX's collectives and lax.ppermute only.
A program may use at most 576 MiB of HBM per device.

v0:
```python
import jax
import jax.numpy as jnp
from jax import lax
from jax.sharding import PartitionSpec as P

HEADS = 16
STEP = 10


norm_eps = 1e-06
beta_one = 0.9
beta_two = 0.95
adam_eps = 1e-08
decay_rate = 0.1
rate_matrix = 0.1
rate_gain = 0.8


def normalize(h, gain):
    scale = lax.rsqrt(jnp.mean(h * h, axis=-1, keepdims=True) + norm_eps)
    return h * scale * gain


def gelu_tanh(u):
    return 0.5 * u * (1.0 + jnp.tanh(0.7978845608028654 * (u + 0.044715 * u * u * u)))


def matmul(left, right):
    return jnp.dot(left, right, preferred_element_type=jnp.float32)


def matmul_left(left, right):
    return lax.dot_general(
        left, right, (((0,), (0,)), ((), ())), preferred_element_type=jnp.float32
    )


def matmul_right(left, right):
    return lax.dot_general(
        left, right, (((1,), (1,)), ((), ())), preferred_element_type=jnp.float32
    )


def slot_table(owners, cap):
    order = jnp.arange(owners.shape[0])
    same = (owners[:, None] == owners[None, :]) & (order[None, :] < order[:, None])
    return owners * cap + jnp.sum(same.astype(jnp.int32), axis=1)


def adam_update(weight, first, second, grad, rate, decay):
    first = beta_one * first + (1.0 - beta_one) * grad
    second = beta_two * second + (1.0 - beta_two) * grad * grad
    fix_one = 1.0 - beta_one**STEP
    fix_two = 1.0 - beta_two**STEP
    move = first / fix_one / (jnp.sqrt(second / fix_two) + adam_eps)
    return (weight - rate * (move + decay * weight), first, second)


def assemble(tiles):
    w_ck = jnp.concatenate([tiles[5], tiles[6]], axis=0)
    w_cv = jnp.concatenate([tiles[7], tiles[8]], axis=0)
    w_in = jnp.concatenate([tiles[10], tiles[11], tiles[12], tiles[13]], axis=1)
    w_out = jnp.concatenate([tiles[14], tiles[15], tiles[16], tiles[17]], axis=0)
    return (w_ck, w_cv, w_in, w_out)


def tile_term(left, right):
    return matmul_left(left, right)


def self_mask(seg_rows, rows, seg, live, places):
    return (seg_rows[:, None] == seg[None, :]) & (
        live[None, :] | (rows[:, None] == places[None, :])
    )


def attend_forward(query, keys, values, seg, live, block, scale):
    count = query.shape[0]
    places = jnp.arange(count)

    def one(start):
        allowed = self_mask(seg, start + jnp.arange(block), seg, live, places)
        scores = jnp.einsum("qhd,khd->hqk", query, keys, preferred_element_type=jnp.float32) * scale
        scores = jnp.where(allowed[None], scores, -1e30)
        top = jnp.max(scores, axis=-1, keepdims=True)
        total = jnp.sum(jnp.exp(scores - top), axis=-1, keepdims=True)
        log_total = top + jnp.log(total)
        probs = jnp.exp(scores - log_total).astype(jnp.bfloat16)
        attended = jnp.einsum("hqk,khd->qhd", probs, values, preferred_element_type=jnp.float32)
        return (attended.astype(jnp.bfloat16), log_total)

    starts = jnp.arange(count // block) * block
    attended, log_totals = lax.map(one, starts)
    return (attended.reshape(count, -1), log_totals)


def attend_backward(query, keys, values, d_attended, log_totals, seg, live, block, scale):
    count = query.shape[0]
    places = jnp.arange(count)
    heads = query.shape[1]
    d_heads = d_attended.reshape(count, heads, -1)

    def one(carry, start):
        dk_sum, dv_sum = carry
        log_blk = lax.dynamic_index_in_dim(log_totals, start // block, 0, keepdims=False)
        allowed = self_mask(seg, start + jnp.arange(block), seg, live, places)
        scores = jnp.einsum("qhd,khd->hqk", query, keys, preferred_element_type=jnp.float32) * scale
        scores = jnp.where(allowed[None], scores, -1e30)
        probs = jnp.exp(scores - log_blk)
        probs_low = probs.astype(jnp.bfloat16)
        d_probs = jnp.einsum("qhd,khd->hqk", d_heads, values, preferred_element_type=jnp.float32)
        d_scores = (probs * (d_probs - jnp.sum(probs * d_probs, axis=-1, keepdims=True))).astype(
            jnp.bfloat16
        )
        dq_blk = (
            jnp.einsum("hqk,khd->qhd", d_scores, keys, preferred_element_type=jnp.float32) * scale
        ).astype(jnp.bfloat16)
        dk_sum = (
            dk_sum
            + jnp.einsum("hqk,qhd->khd", d_scores, query, preferred_element_type=jnp.float32)
            * scale
        )
        dv_sum = dv_sum + jnp.einsum(
            "hqk,qhd->khd", probs_low, d_heads, preferred_element_type=jnp.float32
        )
        return ((dk_sum, dv_sum), dq_blk)

    empty = jnp.zeros(keys.shape, jnp.float32)
    starts = jnp.arange(count // block) * block
    (dk_sum, dv_sum), dq_blocks = lax.scan(one, (empty, empty), starts)
    width = keys.shape[1] * keys.shape[2]
    return (
        dq_blocks.reshape(count, width),
        dk_sum.reshape(count, width).astype(jnp.bfloat16),
        dv_sum.reshape(count, width).astype(jnp.bfloat16),
    )


def body(
    tokens,
    cotangent,
    context,
    lengths,
    keep,
    owners,
    master,
    moment_one,
    moment_two,
    gains,
    gain_one,
    gain_two,
):
    cap = master.shape[0]
    slot_of = slot_table(owners, cap)
    shard = master.astype(jnp.bfloat16)
    owner_rows = lax.all_gather(shard, "fsdp", axis=0, tiled=True)
    tiles = lax.all_gather(owner_rows[slot_of], "dp", axis=1, tiled=True)
    w_ck, w_cv, w_in, w_out = assemble(tiles)
    count, width = tokens.shape
    heads = HEADS
    head_dim = width // heads
    scale = head_dim ** (-0.5)
    block = min(count, 512)
    ends = jnp.cumsum(lengths[0])
    seg = jnp.sum((jnp.arange(count)[:, None] >= ends[None, :]).astype(jnp.int32), axis=1)
    live = keep == 1
    h0 = tokens.astype(jnp.float32)
    a_in = normalize(h0, gains[0]).astype(jnp.bfloat16)
    query = matmul(a_in, tiles[0]).astype(jnp.bfloat16).reshape(count, heads, head_dim)
    keys = matmul(a_in, tiles[1]).astype(jnp.bfloat16).reshape(count, heads, head_dim)
    values = matmul(a_in, tiles[2]).astype(jnp.bfloat16).reshape(count, heads, head_dim)
    attended, log_totals = attend_forward(query, keys, values, seg, live, block, scale)
    h1 = h0 + matmul(attended, tiles[3])
    b_in = normalize(h1, gains[1]).astype(jnp.bfloat16)
    slots, ctx_len, ctx_width = context.shape
    ctx_flat = context.reshape(slots * ctx_len, ctx_width)
    cross_q = matmul(b_in, tiles[4]).astype(jnp.bfloat16).reshape(count, heads, head_dim)
    cross_k = matmul(ctx_flat, w_ck).astype(jnp.bfloat16).reshape(slots * ctx_len, heads, head_dim)
    cross_v = matmul(ctx_flat, w_cv).astype(jnp.bfloat16).reshape(slots * ctx_len, heads, head_dim)
    owner_slot = jnp.arange(slots * ctx_len) // ctx_len
    mine = seg[:, None] == owner_slot[None, :]
    cross_s = (
        jnp.einsum("qhd,khd->hqk", cross_q, cross_k, preferred_element_type=jnp.float32) * scale
    )
    cross_s = jnp.where(mine[None], cross_s, -1e30)
    expo = jnp.exp(cross_s - jnp.max(cross_s, axis=-1, keepdims=True))
    cross_p = expo / jnp.sum(expo, axis=-1, keepdims=True)
    cross_low = cross_p.astype(jnp.bfloat16)
    cross_o = jnp.einsum("hqk,khd->qhd", cross_low, cross_v, preferred_element_type=jnp.float32)
    cross_o = cross_o.astype(jnp.bfloat16).reshape(count, width)
    h2 = h1 + matmul(cross_o, tiles[9])
    c_in = normalize(h2, gains[2]).astype(jnp.bfloat16)
    hidden = matmul(c_in, w_in)
    activated = gelu_tanh(hidden).astype(jnp.bfloat16)
    layer_out = (h2 + matmul(activated, w_out)).astype(jnp.bfloat16)
    owner_back = lax.all_gather(shard, "fsdp", axis=0, tiled=True)
    tiles = lax.all_gather(owner_back[slot_of], "dp", axis=1, tiled=True)
    w_ck, w_cv, w_in, w_out = assemble(tiles)
    grad_out = cotangent.astype(jnp.float32) * live.astype(jnp.float32)[:, None]
    d_ff = grad_out.astype(jnp.bfloat16)
    d_act = matmul_right(d_ff, w_out)
    gelu_back = jax.vjp(gelu_tanh, hidden)[1]
    d_hidden = gelu_back(d_act)[0].astype(jnp.bfloat16)
    d_c = matmul_right(d_hidden, w_in)
    norm_two = jax.vjp(normalize, h2, gains[2])[1]
    part_two, gain_grad_two = norm_two(d_c)
    dh2 = grad_out + part_two
    d_cross_out = dh2.astype(jnp.bfloat16)
    d_co = matmul_right(d_cross_out, tiles[9]).astype(jnp.bfloat16).reshape(count, heads, head_dim)
    d_cp = jnp.einsum("qhd,khd->hqk", d_co, cross_v, preferred_element_type=jnp.float32)
    d_cs = (cross_p * (d_cp - jnp.sum(cross_p * d_cp, axis=-1, keepdims=True))).astype(jnp.bfloat16)
    d_cq = jnp.einsum("hqk,khd->qhd", d_cs, cross_k, preferred_element_type=jnp.float32) * scale
    d_cq = d_cq.astype(jnp.bfloat16).reshape(count, width)
    d_ck = jnp.einsum("hqk,qhd->khd", d_cs, cross_q, preferred_element_type=jnp.float32) * scale
    d_ck = d_ck.astype(jnp.bfloat16).reshape(slots * ctx_len, width)
    d_cv = jnp.einsum("hqk,qhd->khd", cross_low, d_co, preferred_element_type=jnp.float32)
    d_cv = d_cv.astype(jnp.bfloat16).reshape(slots * ctx_len, width)
    d_b = matmul_right(d_cq, tiles[4])
    norm_one = jax.vjp(normalize, h1, gains[1])[1]
    part_one, gain_grad_one = norm_one(d_b)
    dh1 = dh2 + part_one
    d_self_out = dh1.astype(jnp.bfloat16)
    d_att = matmul_right(d_self_out, tiles[3]).astype(jnp.bfloat16)
    d_query, d_keys, d_values = attend_backward(
        query, keys, values, d_att, log_totals, seg, live, block, scale
    )
    d_a = (
        matmul_right(d_query, tiles[0])
        + matmul_right(d_keys, tiles[1])
        + matmul_right(d_values, tiles[2])
    )
    norm_zero = jax.vjp(normalize, h0, gains[0])[1]
    part_zero, gain_grad_zero = norm_zero(d_a)
    grad_tokens = (dh1 + part_zero).astype(jnp.bfloat16)
    padded_rows = max(count, slots * ctx_len)

    def padded(value):
        return jnp.pad(value, ((0, padded_rows - value.shape[0]), (0, 0)))

    ctx_low = ctx_flat[:, :width]
    ctx_high = ctx_flat[:, width:]
    left_list = [a_in, a_in, a_in, attended, b_in, ctx_low, ctx_high, ctx_low, ctx_high, cross_o]
    right_list = [d_query, d_keys, d_values, d_self_out, d_cq, d_ck, d_ck, d_cv, d_cv, d_cross_out]
    for part in range(4):
        left_list.append(c_in)
        right_list.append(d_hidden[:, part * width : (part + 1) * width])
    for part in range(4):
        left_list.append(activated[:, part * width : (part + 1) * width])
        right_list.append(d_ff)
    lefts = jnp.stack([padded(value) for value in left_list])
    rights = jnp.stack([padded(value) for value in right_list])
    total_slots = lax.axis_size("fsdp") * cap
    my_slots = lax.axis_index("fsdp") * cap + jnp.arange(cap)
    matches = slot_of[None, :] == my_slots[:, None]
    used = jnp.any(matches, axis=1)

    def reduce_rows(pair):
        return lax.psum_scatter(
            tile_term(pair[0], pair[1]).astype(jnp.bfloat16), "dp", scatter_dimension=0, tiled=True
        ).astype(jnp.float32)

    row_part = lax.map(reduce_rows, (lefts, rights))
    placed = jnp.zeros((total_slots,) + row_part.shape[1:], jnp.float32).at[slot_of].set(row_part)
    owned = lax.psum_scatter(
        placed.astype(jnp.bfloat16), "fsdp", scatter_dimension=0, tiled=True
    ).astype(jnp.float32)
    new_w, new_m, new_v = adam_update(
        master, moment_one, moment_two, owned, rate_matrix, decay_rate
    )
    zero = jnp.zeros_like(master)
    new_w = jnp.where(used[:, None, None], new_w, zero)
    new_m = jnp.where(used[:, None, None], new_m, zero)
    new_v = jnp.where(used[:, None, None], new_v, zero)
    gain_grads = jnp.stack([gain_grad_zero, gain_grad_one, gain_grad_two])
    gain_total = lax.psum(gain_grads, ("dp", "fsdp"))
    new_g, new_gm, new_gv = adam_update(gains, gain_one, gain_two, gain_total, rate_gain, 0.0)
    return (layer_out, grad_tokens, new_w, new_m, new_v, new_g, new_gm, new_gv)


def solution(mesh):
    placed = (
        P(("dp", "fsdp"), None),
        P(("dp", "fsdp"), None),
        P(("dp", "fsdp"), None, None),
        P(("dp", "fsdp"), None),
        P(("dp", "fsdp")),
        P(),
        P("fsdp", "dp", None),
        P("fsdp", "dp", None),
        P("fsdp", "dp", None),
        P(),
        P(),
        P(),
    )
    return jax.shard_map(
        body,
        mesh=mesh,
        in_specs=placed,
        out_specs=(
            P(("dp", "fsdp"), None),
            P(("dp", "fsdp"), None),
            P("fsdp", "dp", None),
            P("fsdp", "dp", None),
            P("fsdp", "dp", None),
            P(),
            P(),
            P(),
        ),
        check_vma=False,
    )
```

profile of v0, /device:TPU:0, one launch (start us, length us, event | category | flops | bytes accessed | tf_op | source)
XLA Modules:
  0.0 6496.6 jit_solution(16509423679505192518)
XLA Ops:
  16.9 156.2 %all-gather.4.cloned.1.call-done = bf16[24,256,2048]{2,1,0:T(8,128)(2,1)} async-done(((bf16[6,256,2048]{2,1,0:T(8,128)(2,1)}), bf16[24,256,2048]{2,1,0:T(8,128)(2,1)}) %all-gather.4.cloned.1.call-update) | async-done | bytes 25165840 | tf_op jit(solution)/shard_map/all_gather | solution.py:156
  196.0 2833.6 %all-gather.6.cloned.1.call-done = bf16[18,2048,2048]{2,1,0:T(8,128)(2,1)} async-done(((bf16[18,256,2048]{2,1,0:T(8,128)(2,1)}), bf16[18,2048,2048]{2,1,0:T(8,128)(2,1)}) %all-gather.6.cloned.1.call-update) | async-done | bytes 150994960 | tf_op jit(solution)/shard_map/all_gather | solution.py:157
  3056.9 64.8 slice_bitcast_fusion.3
  3319.0 2847.6 %while.2 = (s32[]{:T(128)}, f32[18,256,2048]{2,1,0:T(8,128)}, bf16[18,256,2048]{2,1,0:T(8,128)(2,1)}, bf16[18,256,2048]{2,1,0:T(8,128)(2,1)}, s32[]{:T(128)}) while((s32[]{:T(128)}, f32[18,256,2048]{2,1,0:T(8,128)}, bf16[18,256,2048]{2,1,0:T(8,128)(2,1)}, bf16[18,256,2048]{2,1,0:T(8,128)(2,1)}, s32[]{:T(128)}) %tuple.67), condition=%wide.region_18.19_spmd, body=%wide.region_16.18_spmd.sunk | while | flops 2152202240 | bytes 41944176 | solution.py:262
  3326.2 149.1 %reduce-scatter.5.cloned.1.call-done = bf16[256,2048]{1,0:T(8,128)(2,1)} async-done(((bf16[2048,2048]{1,0:T(8,128)(2,1)}), bf16[256,2048]{1,0:T(8,128)(2,1)}) %reduce-scatter.5.cloned.1.call-update) | async-done | bytes 1048592 | tf_op jit(solution)/shard_map/while/body/eval_jaxpr/reduce_scatter | solution.py:258
  3485.3 148.1 %reduce-scatter.5.cloned.1.call-done = bf16[256,2048]{1,0:T(8,128)(2,1)} async-done(((bf16[2048,2048]{1,0:T(8,128)(2,1)}), bf16[256,2048]{1,0:T(8,128)(2,1)}) %reduce-scatter.5.cloned.1.call-update) | async-done | bytes 1048592 | tf_op jit(solution)/shard_map/while/body/eval_jaxpr/reduce_scatter | solution.py:258
  3643.4 148.2 %reduce-scatter.5.cloned.1.call-done = bf16[256,2048]{1,0:T(8,128)(2,1)} async-done(((bf16[2048,2048]{1,0:T(8,128)(2,1)}), bf16[256,2048]{1,0:T(8,128)(2,1)}) %reduce-scatter.5.cloned.1.call-update) | async-done | bytes 1048592 | tf_op jit(solution)/shard_map/while/body/eval_jaxpr/reduce_scatter | solution.py:258
  3801.5 148.2 %reduce-scatter.5.cloned.1.call-done = bf16[256,2048]{1,0:T(8,128)(2,1)} async-done(((bf16[2048,2048]{1,0:T(8,128)(2,1)}), bf16[256,2048]{1,0:T(8,128)(2,1)}) %reduce-scatter.5.cloned.1.call-update) | async-done | bytes 1048592 | tf_op jit(solution)/shard_map/while/body/eval_jaxpr/reduce_scatter | solution.py:258
  3959.6 148.2 %reduce-scatter.5.cloned.1.call-done = bf16[256,2048]{1,0:T(8,128)(2,1)} async-done(((bf16[2048,2048]{1,0:T(8,128)(2,1)}), bf16[256,2048]{1,0:T(8,128)(2,1)}) %reduce-scatter.5.cloned.1.call-update) | async-done | bytes 1048592 | tf_op jit(solution)/shard_map/while/body/eval_jaxpr/reduce_scatter | solution.py:258
  4117.8 148.2 %reduce-scatter.5.cloned.1.call-done = bf16[256,2048]{1,0:T(8,128)(2,1)} async-done(((bf16[2048,2048]{1,0:T(8,128)(2,1)}), bf16[256,2048]{1,0:T(8,128)(2,1)}) %reduce-scatter.5.cloned.1.call-update) | async-done | bytes 1048592 | tf_op jit(solution)/shard_map/while/body/eval_jaxpr/reduce_scatter | solution.py:258
  4275.9 148.2 %reduce-scatter.5.cloned.1.call-done = bf16[256,2048]{1,0:T(8,128)(2,1)} async-done(((bf16[2048,2048]{1,0:T(8,128)(2,1)}), bf16[256,2048]{1,0:T(8,128)(2,1)}) %reduce-scatter.5.cloned.1.call-update) | async-done | bytes 1048592 | tf_op jit(solution)/shard_map/while/body/eval_jaxpr/reduce_scatter | solution.py:258
  4434.1 148.2 %reduce-scatter.5.cloned.1.call-done = bf16[256,2048]{1,0:T(8,128)(2,1)} async-done(((bf16[2048,2048]{1,0:T(8,128)(2,1)}), bf16[256,2048]{1,0:T(8,128)(2,1)}) %reduce-scatter.5.cloned.1.call-update) | async-done | bytes 1048592 | tf_op jit(solution)/shard_map/while/body/eval_jaxpr/reduce_scatter | solution.py:258
  4592.3 148.2 %reduce-scatter.5.cloned.1.call-done = bf16[256,2048]{1,0:T(8,128)(2,1)} async-done(((bf16[2048,2048]{1,0:T(8,128)(2,1)}), bf16[256,2048]{1,0:T(8,128)(2,1)}) %reduce-scatter.5.cloned.1.call-update) | async-done | bytes 1048592 | tf_op jit(solution)/shard_map/while/body/eval_jaxpr/reduce_scatter | solution.py:258
  4750.5 148.2 %reduce-scatter.5.cloned.1.call-done = bf16[256,2048]{1,0:T(8,128)(2,1)} async-done(((bf16[2048,2048]{1,0:T(8,128)(2,1)}), bf16[256,2048]{1,0:T(8,128)(2,1)}) %reduce-scatter.5.cloned.1.call-update) | async-done | bytes 1048592 | tf_op jit(solution)/shard_map/while/body/eval_jaxpr/reduce_scatter | solution.py:258
  4908.6 148.2 %reduce-scatter.5.cloned.1.call-done = bf16[256,2048]{1,0:T(8,128)(2,1)} async-done(((bf16[2048,2048]{1,0:T(8,128)(2,1)}), bf16[256,2048]{1,0:T(8,128)(2,1)}) %reduce-scatter.5.cloned.1.call-update) | async-done | bytes 1048592 | tf_op jit(solution)/shard_map/while/body/eval_jaxpr/reduce_scatter | solution.py:258
  5066.8 148.2 %reduce-scatter.5.cloned.1.call-done = bf16[256,2048]{1,0:T(8,128)(2,1)} async-done(((bf16[2048,2048]{1,0:T(8,128)(2,1)}), bf16[256,2048]{1,0:T(8,128)(2,1)}) %reduce-scatter.5.cloned.1.call-update) | async-done | bytes 1048592 | tf_op jit(solution)/shard_map/while/body/eval_jaxpr/reduce_scatter | solution.py:258
  5224.9 148.2 %reduce-scatter.5.cloned.1.call-done = bf16[256,2048]{1,0:T(8,128)(2,1)} async-done(((bf16[2048,2048]{1,0:T(8,128)(2,1)}), bf16[256,2048]{1,0:T(8,128)(2,1)}) %reduce-scatter.5.cloned.1.call-update) | async-done | bytes 1048592 | tf_op jit(solution)/shard_map/while/body/eval_jaxpr/reduce_scatter | solution.py:258
  5383.1 148.2 %reduce-scatter.5.cloned.1.call-done = bf16[256,2048]{1,0:T(8,128)(2,1)} async-done(((bf16[2048,2048]{1,0:T(8,128)(2,1)}), bf16[256,2048]{1,0:T(8,128)(2,1)}) %reduce-scatter.5.cloned.1.call-update) | async-done | bytes 1048592 | tf_op jit(solution)/shard_map/while/body/eval_jaxpr/reduce_scatter | solution.py:258
  5541.2 148.2 %reduce-scatter.5.cloned.1.call-done = bf16[256,2048]{1,0:T(8,128)(2,1)} async-done(((bf16[2048,2048]{1,0:T(8,128)(2,1)}), bf16[256,2048]{1,0:T(8,128)(2,1)}) %reduce-scatter.5.cloned.1.call-update) | async-done | bytes 1048592 | tf_op jit(solution)/shard_map/while/body/eval_jaxpr/reduce_scatter | solution.py:258
  5699.4 148.2 %reduce-scatter.5.cloned.1.call-done = bf16[256,2048]{1,0:T(8,128)(2,1)} async-done(((bf16[2048,2048]{1,0:T(8,128)(2,1)}), bf16[256,2048]{1,0:T(8,128)(2,1)}) %reduce-scatter.5.cloned.1.call-update) | async-done | bytes 1048592 | tf_op jit(solution)/shard_map/while/body/eval_jaxpr/reduce_scatter | solution.py:258
  5857.5 148.2 %reduce-scatter.5.cloned.1.call-done = bf16[256,2048]{1,0:T(8,128)(2,1)} async-done(((bf16[2048,2048]{1,0:T(8,128)(2,1)}), bf16[256,2048]{1,0:T(8,128)(2,1)}) %reduce-scatter.5.cloned.1.call-update) | async-done | bytes 1048592 | tf_op jit(solution)/shard_map/while/body/eval_jaxpr/reduce_scatter | solution.py:258
  6015.7 148.2 %reduce-scatter.5.cloned.1.call-done = bf16[256,2048]{1,0:T(8,128)(2,1)} async-done(((bf16[2048,2048]{1,0:T(8,128)(2,1)}), bf16[256,2048]{1,0:T(8,128)(2,1)}) %reduce-scatter.5.cloned.1.call-update) | async-done | bytes 1048592 | tf_op jit(solution)/shard_map/while/body/eval_jaxpr/reduce_scatter | solution.py:258
  6182.9 66.8 %scatter_fusion = f32[24,256,2048]{2,1,0:T(8,128)} fusion(f32[24,256,2048]{2,1,0:T(8,128)} %broadcast_in_dim.153, s32[18]{0:T(128)S(1)} %copy-done.47, f32[18,256,2048]{2,1,0:T(8,128)} %get-tuple-element.85), kind=kCustom, calls=%fused_computation.1 | custom fusion | bytes 113246280 | tf_op jit(solution)/shard_map/scatter | solution.py:263
  6358.7 97.4 %reduce-scatter.3.cloned.1.call-done = bf16[6,256,2048]{2,1,0:T(8,128)(2,1)} async-done(((bf16[24,256,2048]{2,1,0:T(8,128)(2,1)}), bf16[6,256,2048]{2,1,0:T(8,128)(2,1)}) %reduce-scatter.3.cloned.1.call-update) | async-done | bytes 6291472 | tf_op jit(solution)/shard_map/reduce_scatter | solution.py:264
  (326 shorter events, 594.0 us)
Async XLA Ops:
  7.2 166.0 %all-gather.4.cloned.1.call-start = ((), (), s32[]{:S(2)}) async-start(), calls=%async_computation.2 | async-start | bytes 31457280 | tf_op jit(solution)/shard_map/all_gather | solution.py:156
  15.5 3014.0 %all-gather.6.cloned.1.call-start = ((), (), s32[]{:S(2)}) async-start(), calls=%async_computation.4 | async-start | bytes 169869312 | tf_op jit(solution)/shard_map/all_gather | solution.py:157
  190.7 2848.6 %copy-start.48 = (f32[128]{0:T(128)}, f32[128]{0:T(128)S(1)}, u32[]{:S(2)}) copy-start(f32[128]{0:T(128)S(1)} %fusion.102) | copy-start | bytes 1540
  191.2 2848.1 %copy-start.50 = (f32[128]{0:T(128)}, f32[128]{0:T(128)S(1)}, u32[]{:S(2)}) copy-start(f32[128]{0:T(128)S(1)} %get-tuple-element.143) | copy-start | bytes 1540
  191.5 2859.4 %copy-start.40 = (f32[1,2048]{1,0:T(1,128)}, f32[1,2048]{1,0:T(1,128)S(1)}, u32[]{:S(2)}) copy-start(f32[1,2048]{1,0:T(1,128)S(1)} %get-tuple-element.141) | copy-start | bytes 24580
  3319.0 156.3 %reduce-scatter.5.cloned.1.call-start = ((), (), s32[]{:S(2)}) async-start(), calls=%async_computation.5 | async-start | bytes 9437184 | tf_op jit(solution)/shard_map/while/body/eval_jaxpr/reduce_scatter | solution.py:258
  3478.1 155.3 %reduce-scatter.5.cloned.1.call-start = ((), (), s32[]{:S(2)}) async-start(), calls=%async_computation.5 | async-start | bytes 9437184 | tf_op jit(solution)/shard_map/while/body/eval_jaxpr/reduce_scatter | solution.py:258
  3636.2 155.3 %reduce-scatter.5.cloned.1.call-start = ((), (), s32[]{:S(2)}) async-start(), calls=%async_computation.5 | async-start | bytes 9437184 | tf_op jit(solution)/shard_map/while/body/eval_jaxpr/reduce_scatter | solution.py:258
  3794.3 155.3 %reduce-scatter.5.cloned.1.call-start = ((), (), s32[]{:S(2)}) async-start(), calls=%async_computation.5 | async-start | bytes 9437184 | tf_op jit(solution)/shard_map/while/body/eval_jaxpr/reduce_scatter | solution.py:258
  3952.5 155.3 %reduce-scatter.5.cloned.1.call-start = ((), (), s32[]{:S(2)}) async-start(), calls=%async_computation.5 | async-start | bytes 9437184 | tf_op jit(solution)/shard_map/while/body/eval_jaxpr/reduce_scatter | solution.py:258
  4110.6 155.3 %reduce-scatter.5.cloned.1.call-start = ((), (), s32[]{:S(2)}) async-start(), calls=%async_computation.5 | async-start | bytes 9437184 | tf_op jit(solution)/shard_map/while/body/eval_jaxpr/reduce_scatter | solution.py:258
  4268.8 155.3 %reduce-scatter.5.cloned.1.call-start = ((), (), s32[]{:S(2)}) async-start(), calls=%async_computation.5 | async-start | bytes 9437184 | tf_op jit(solution)/shard_map/while/body/eval_jaxpr/reduce_scatter | solution.py:258
  4427.0 155.3 %reduce-scatter.5.cloned.1.call-start = ((), (), s32[]{:S(2)}) async-start(), calls=%async_computation.5 | async-start | bytes 9437184 | tf_op jit(solution)/shard_map/while/body/eval_jaxpr/reduce_scatter | solution.py:258
  4585.1 155.3 %reduce-scatter.5.cloned.1.call-start = ((), (), s32[]{:S(2)}) async-start(), calls=%async_computation.5 | async-start | bytes 9437184 | tf_op jit(solution)/shard_map/while/body/eval_jaxpr/reduce_scatter | solution.py:258
  4743.3 155.3 %reduce-scatter.5.cloned.1.call-start = ((), (), s32[]{:S(2)}) async-start(), calls=%async_computation.5 | async-start | bytes 9437184 | tf_op jit(solution)/shard_map/while/body/eval_jaxpr/reduce_scatter | solution.py:258
  4901.4 155.3 %reduce-scatter.5.cloned.1.call-start = ((), (), s32[]{:S(2)}) async-start(), calls=%async_computation.5 | async-start | bytes 9437184 | tf_op jit(solution)/shard_map/while/body/eval_jaxpr/reduce_scatter | solution.py:258
  5059.6 155.3 %reduce-scatter.5.cloned.1.call-start = ((), (), s32[]{:S(2)}) async-start(), calls=%async_computation.5 | async-start | bytes 9437184 | tf_op jit(solution)/shard_map/while/body/eval_jaxpr/reduce_scatter | solution.py:258
  5217.8 155.3 %reduce-scatter.5.cloned.1.call-start = ((), (), s32[]{:S(2)}) async-start(), calls=%async_computation.5 | async-start | bytes 9437184 | tf_op jit(solution)/shard_map/while/body/eval_jaxpr/reduce_scatter | solution.py:258
  5375.9 155.3 %reduce-scatter.5.cloned.1.call-start = ((), (), s32[]{:S(2)}) async-start(), calls=%async_computation.5 | async-start | bytes 9437184 | tf_op jit(solution)/shard_map/while/body/eval_jaxpr/reduce_scatter | solution.py:258
  5534.0 155.3 %reduce-scatter.5.cloned.1.call-start = ((), (), s32[]{:S(2)}) async-start(), calls=%async_computation.5 | async-start | bytes 9437184 | tf_op jit(solution)/shard_map/while/body/eval_jaxpr/reduce_scatter | solution.py:258
  5692.2 155.3 %reduce-scatter.5.cloned.1.call-start = ((), (), s32[]{:S(2)}) async-start(), calls=%async_computation.5 | async-start | bytes 9437184 | tf_op jit(solution)/shard_map/while/body/eval_jaxpr/reduce_scatter | solution.py:258
  5850.4 155.4 %reduce-scatter.5.cloned.1.call-start = ((), (), s32[]{:S(2)}) async-start(), calls=%async_computation.5 | async-start | bytes 9437184 | tf_op jit(solution)/shard_map/while/body/eval_jaxpr/reduce_scatter | solution.py:258
  6008.5 155.3 %reduce-scatter.5.cloned.1.call-start = ((), (), s32[]{:S(2)}) async-start(), calls=%async_computation.5 | async-start | bytes 9437184 | tf_op jit(solution)/shard_map/while/body/eval_jaxpr/reduce_scatter | solution.py:258
  6166.6 289.4 %reduce-scatter.3.cloned.1.call-start = ((), (), s32[]{:S(2)}) async-start(), calls=%async_computation.3 | async-start | bytes 31457280 | tf_op jit(solution)/shard_map/reduce_scatter | solution.py:264
  (60 other events, 1227.7 us)
Sparse Core Ops, SparseCore 0:
  15.6 157.4 all-gather.3
  189.6 2839.8 all-gather.5
  3326.3 148.9 reduce-scatter.4
  3485.4 147.9 reduce-scatter.4
  3643.5 147.9 reduce-scatter.4
  3801.6 148.0 reduce-scatter.4
  3959.8 148.0 reduce-scatter.4
  4117.9 148.0 reduce-scatter.4
  4276.1 148.0 reduce-scatter.4
  4434.3 148.0 reduce-scatter.4
  4592.4 148.0 reduce-scatter.4
  4750.6 148.0 reduce-scatter.4
  4908.7 148.0 reduce-scatter.4
  5066.9 148.0 reduce-scatter.4
  5225.1 148.0 reduce-scatter.4
  5383.2 147.9 reduce-scatter.4
  5541.3 148.0 reduce-scatter.4
  5699.5 148.0 reduce-scatter.4
  5857.7 148.0 reduce-scatter.4
  6015.8 148.0 reduce-scatter.4
  6275.8 180.1 reduce-scatter.2
where the time goes:
time: 6510 us; the launch traced here: 6500 us
  waiting for transfers between devices  5760 us (88%)
  matrix products  315 us (5%)
  local copies, waits for them, and re-layouts  238 us (4%)
  other arithmetic  132 us (2%)
    all_gather x1, waiting for transfers between devices, body(): tiles = lax.all_gather(owner_rows[slot_of], 'dp', axis=1, tiled=True)  2830 us
    reduce_scatter x18, waiting for transfers between devices, reduce_rows(): lax.psum_scatter(tile_term(pair[0], pair[1]).astype(jnp.bfloat16), 'dp',...  2670 us
    all_gather x1, waiting for transfers between devices, body(): owner_rows = lax.all_gather(shard, 'fsdp', axis=0, tiled=True)  156 us
  transfers between devices with their start and end apart: 21, of which 21 were waited for; matrix products, arithmetic and copies ran while one was open for 1% of the time, Pallas kernels for 0%

commit v1 on v0

v1 whole, which is shorter than its diff:
```python
import jax
import jax.numpy as jnp
import numpy as np
from jax import lax
from jax.experimental import pallas as pl
from jax.experimental.pallas import tpu as pltpu
from jax.sharding import Mesh
from jax.sharding import PartitionSpec as P

HEADS = 16
STEP = 10

norm_eps = 1e-06
beta_one = 0.9
beta_two = 0.95
adam_eps = 1e-08
decay_rate = 0.1
rate_matrix = 0.1
rate_gain = 0.8

f32 = jnp.float32
bf16 = jnp.bfloat16

SHIFT = (0, 0, 0, 0, 2, 2, 2, 2, 2, 2, 0, 1, 2, 3, 0, 1, 2, 3)
ROW_TILES = (3, 9, 14, 15, 16, 17)
VMEM_LIMIT = 48 << 20


def normalize(h, gain):
    scale = lax.rsqrt(jnp.mean(h * h, axis=-1, keepdims=True) + norm_eps)
    return h * scale * gain


def gelu_tanh(u):
    return 0.5 * u * (1.0 + jnp.tanh(0.7978845608028654 * (u + 0.044715 * u * u * u)))


def matmul(left, right):
    return jnp.dot(left, right, preferred_element_type=f32)


def matmul_left(left, right):
    return lax.dot_general(left, right, (((0,), (0,)), ((), ())), preferred_element_type=f32)


def matmul_right(left, right):
    return lax.dot_general(left, right, (((1,), (1,)), ((), ())), preferred_element_type=f32)


def ranks_of(owners):
    order = jnp.arange(owners.shape[0])
    same = (owners[:, None] == owners[None, :]) & (order[None, :] < order[:, None])
    return jnp.sum(same.astype(jnp.int32), axis=1)


def segments(lengths, count):
    places = jnp.arange(count)
    end = jnp.zeros((), jnp.int32)
    seg = jnp.zeros((count,), jnp.int32)
    for item in range(lengths.shape[0]):
        end = end + lengths[item]
        seg = seg + (places >= end).astype(jnp.int32)
    return seg


def adam_update(weight, first, second, grad, rate, decay):
    first = beta_one * first + (1.0 - beta_one) * grad
    second = beta_two * second + (1.0 - beta_two) * grad * grad
    fix_one = 1.0 - beta_one**STEP
    fix_two = 1.0 - beta_two**STEP
    move = first / fix_one / (jnp.sqrt(second / fix_two) + adam_eps)
    return (weight - rate * (move + decay * weight), first, second)


def pack_columns(master, table, first_slot, slots):
    _, rows, columns = master.shape
    width = columns // 8

    def kernel(table_ref, in_ref, out_ref):
        slot = pl.program_id(0)
        for rank in range(8):
            start = pl.multiple_of(table_ref[slot * 8 + rank] * width, width)
            out_ref[rank, 0] = in_ref[0, :, pl.ds(start, width)].astype(bf16)

    return pl.pallas_call(
        kernel,
        out_shape=jax.ShapeDtypeStruct((8, slots, rows, width), bf16),
        grid_spec=pltpu.PrefetchScalarGridSpec(
            num_scalar_prefetch=1,
            grid=(slots,),
            in_specs=[pl.BlockSpec((1, rows, columns), lambda k, t: (first_slot + k, 0, 0))],
            out_specs=pl.BlockSpec((8, 1, rows, width), lambda k, t: (0, k, 0, 0)),
        ),
        compiler_params=pltpu.CompilerParams(vmem_limit_bytes=VMEM_LIMIT),
        name="pack_columns",
    )(table, master)


def pick_blocks(sources, which, index, count):
    _, rows, width = sources[0].shape
    n_src = len(sources)

    def kernel(which_ref, index_ref, *refs):
        place = pl.program_id(0) * 2 + pl.program_id(1)
        out_ref = refs[n_src]
        for number in range(n_src):

            @pl.when(which_ref[place] == number)
            def _():
                out_ref[...] = refs[number][0]

    def spec(number):
        def at(n, half, which, index):
            place = n * 2 + half
            return (jnp.where(which[place] == number, index[place], 0), 0, 0)

        return pl.BlockSpec((1, rows, width), at)

    return pl.pallas_call(
        kernel,
        out_shape=jax.ShapeDtypeStruct((2 * rows, count * width), bf16),
        grid_spec=pltpu.PrefetchScalarGridSpec(
            num_scalar_prefetch=2,
            grid=(count, 2),
            in_specs=[spec(number) for number in range(n_src)],
            out_specs=pl.BlockSpec((rows, width), lambda n, half, which, index: (half, n)),
        ),
        compiler_params=pltpu.CompilerParams(vmem_limit_bytes=VMEM_LIMIT),
        name="pick_blocks",
    )(which, index, *sources)


def pack_gradients(groups, which, column, rows, width, slots):
    n_src = len(groups)

    def kernel(which_ref, column_ref, *refs):
        place = pl.program_id(0) * slots + pl.program_id(1)
        out_ref = refs[n_src]
        for number in range(n_src):

            @pl.when(which_ref[place] == number)
            def _():
                out_ref[0, 0] = refs[number][...]

    def spec(number):
        def at(rank, k, which, column):
            place = rank * slots + k
            return (rank // 4, jnp.where(which[place] == number, column[place], 0))

        return pl.BlockSpec((rows, width), at)

    return pl.pallas_call(
        kernel,
        out_shape=jax.ShapeDtypeStruct((8, slots, rows, width), bf16),
        grid_spec=pltpu.PrefetchScalarGridSpec(
            num_scalar_prefetch=2,
            grid=(8, slots),
            in_specs=[spec(number) for number in range(n_src)],
            out_specs=pl.BlockSpec((1, 1, rows, width), lambda rank, k, which, column: (rank, k, 0, 0)),
        ),
        compiler_params=pltpu.CompilerParams(vmem_limit_bytes=VMEM_LIMIT),
        name="pack_gradients",
    )(which, column, *groups)


def adam_tiles(master, one, two, col_grads, row_grads, used, is_row, col_source, row_source):
    cap, rows, columns = master.shape
    width = columns // 8

    def kernel(used_ref, is_row_ref, cs_ref, rs_ref, w_ref, m_ref, v_ref, cg_ref, rg_ref, nw_ref, nm_ref, nv_ref):
        slot = pl.program_id(0)

        @pl.when(used_ref[slot] == 0)
        def _():
            for ref in (nw_ref, nm_ref, nv_ref):
                ref[...] = jnp.zeros_like(ref)

        def update(grad):
            w, m, v = adam_update(w_ref[0], m_ref[0], v_ref[0], grad.astype(f32), rate_matrix, decay_rate)
            nw_ref[0] = w
            nm_ref[0] = m
            nv_ref[0] = v

        @pl.when((used_ref[slot] == 1) & (is_row_ref[slot] == 0))
        def _():
            update(cg_ref[0])

        @pl.when((used_ref[slot] == 1) & (is_row_ref[slot] == 1))
        def _():
            update(rg_ref[0])

    state = pl.BlockSpec((1, rows, width), lambda k, b, u, i, cs, rs: (k, 0, b))
    shape = jax.ShapeDtypeStruct(master.shape, f32)
    return pl.pallas_call(
        kernel,
        out_shape=(shape, shape, shape),
        grid_spec=pltpu.PrefetchScalarGridSpec(
            num_scalar_prefetch=4,
            grid=(cap, 8),
            in_specs=[
                state,
                state,
                state,
                pl.BlockSpec((1, rows, width), lambda k, b, u, i, cs, rs: (cs[k * 8 + b] * cap + k, 0, 0)),
                pl.BlockSpec((1, rows, width), lambda k, b, u, i, cs, rs: (rs[k], 0, b)),
            ],
            out_specs=(state, state, state),
        ),
        compiler_params=pltpu.CompilerParams(vmem_limit_bytes=VMEM_LIMIT),
        name="adam_tiles",
    )(used, is_row, col_source, row_source, master, one, two, col_grads, row_grads)


def swap(value, axis):
    return lax.ppermute(value, axis, [(0, 1), (1, 0)])


def gather_rows(value):
    half = value.shape[0] // 2
    over_x = swap(value, "x")
    over_y = swap(value, "y")
    far_low = swap(over_y[:half], "x")
    far_high = swap(over_x[half:], "y")
    four = jnp.concatenate([value, over_y, over_x, far_low, far_high], axis=0)
    return jnp.concatenate([four, swap(four, "c")], axis=0)


def scatter_rows(part):
    rows, width = part.shape[0] // 8, part.shape[1]
    half = width // 2
    part = part.reshape(2, 2, 2, rows, width)
    chip = part[0] + swap(part[1], "c")
    low, high = chip[..., :half], chip[..., half:]
    low_two = low[:, 0] + swap(low[:, 1].astype(bf16), "y").astype(f32)
    high_two = high[0] + swap(high[1].astype(bf16), "x").astype(f32)
    low_one = low_two[0] + swap(low_two[1].astype(bf16), "x").astype(f32)
    high_one = high_two[0] + swap(high_two[1].astype(bf16), "y").astype(f32)
    return jnp.concatenate([low_one, high_one], axis=1)


def flip_pairs(mask, keep=None):
    pairs = []
    for z in range(4):
        for place in range(8):
            target = place ^ mask
            if keep is None or keep(z, place, target):
                pairs.append((z * 8 + place, z * 8 + target))
    return pairs


ALL_AXES = ("z", "x", "y", "c")
PLANE = ("x", "y", "c")


def plane_body(
    tokens, cotangent, context, lengths, keep, owners, master, moment_one, moment_two, gains, gain_one, gain_two
):
    cap, rows, _ = master.shape
    count, width = tokens.shape
    heads_here = HEADS // 8
    head_dim = width // HEADS
    scale = head_dim ** (-0.5)
    block = width // 8
    z = lax.axis_index("z")
    x = lax.axis_index("x")
    f = lax.axis_index("y") * 2 + lax.axis_index("c")

    n_tiles = owners.shape[0]
    rank = ranks_of(owners)
    shift_of = np.array(SHIFT, np.int32)
    row_of = np.array([t in ROW_TILES for t in range(n_tiles)])
    all_slots = jnp.arange(4 * cap).reshape(4, cap)
    holds = (owners * cap + rank)[None, None, :] == all_slots[:, :, None]
    used_at = jnp.any(holds, axis=2)
    tile_at = jnp.sum(jnp.where(holds, np.arange(n_tiles, dtype=np.int32), 0), axis=2)
    shift_at = jnp.sum(jnp.where(holds, shift_of, 0), axis=2)
    row_at = jnp.any(holds & row_of, axis=2)
    mine = (jnp.arange(4) == f)[:, None]

    def my(value):
        return jnp.sum(jnp.where(mine, value.astype(jnp.int32), 0), axis=0)

    my_used, my_tile, my_shift, my_row = my(used_at), my(tile_at), my(shift_at), my(row_at)

    to_x = np.arange(8) // 4
    to_f = np.arange(8) % 4
    column_table = 2 * ((to_f[None, :] + my_shift[:, None]) % 4) + to_x[None, :]
    half_cap = cap // 2
    received = []
    for first in (0, half_cap):
        sent = pack_columns(master, column_table[first : first + half_cap].reshape(-1), first, half_cap)
        got = lax.all_to_all(sent, PLANE, 0, 0, tiled=True)
        received.append(got.reshape(8 * half_cap, rows, block))

    def source_of(tile):
        if isinstance(tile, int):
            owner, slot = owners[tile], rank[tile]
        else:
            chosen = jnp.arange(n_tiles) == tile
            owner = jnp.sum(jnp.where(chosen, owners, 0))
            slot = jnp.sum(jnp.where(chosen, rank, 0))
        part = slot // half_cap
        return part, owner * half_cap + slot % half_cap

    def gather_columns(tiles, parts):
        which, index = [], []
        for tile in tiles:
            part, place = source_of(tile)
            for side in range(2):
                which.append(part)
                index.append(side * 4 * half_cap + place)
        local = pick_blocks(received[:parts], jnp.stack(which), jnp.stack(index), len(tiles))
        return lax.all_gather(local, "z", axis=0, tiled=True)

    w_qkv = gather_columns([0, 1, 2], 1)

    def my_block(tile):
        chosen = jnp.arange(n_tiles) == tile
        slot = jnp.sum(jnp.where(chosen, rank, 0))
        return lax.dynamic_index_in_dim(master, slot, 0, keepdims=False).astype(bf16)

    def owner_of(tile):
        return jnp.sum(jnp.where(jnp.arange(n_tiles) == tile, owners, 0))

    def take_rows(tile_for, keep_pair):
        found = None
        source = owner_of(tile_for(f)) ^ f
        for mask in range(4):
            got = my_block(tile_for(f ^ mask))
            if mask:
                got = lax.ppermute(got, ALL_AXES, flip_pairs(mask, keep_pair))
            found = got if found is None else jnp.where(source == mask, got, found)
        return found

    def self_or_cross(place):
        return jnp.where(place == z, 3, 9)

    def needs_outer(zz, place, target):
        return target % 4 in (zz, (zz + 2) % 4)

    outer = take_rows(self_or_cross, needs_outer)
    half_rows = rows // 2
    odd = z % 2
    to_pair = lax.dynamic_slice_in_dim(outer, (1 - odd) * half_rows, half_rows, 0)
    own_half = lax.dynamic_slice_in_dim(outer, odd * half_rows, half_rows, 0)
    pair_swap = [
        (zz * 8 + place, (zz ^ 1) * 8 + place)
        for zz in range(4)
        for place in range(8)
        if place % 4 in (zz, (zz + 2) % 4)
    ]
    from_pair = lax.ppermute(to_pair, ALL_AXES, pair_swap)
    has_outer = (f == z) | (f == (z + 2) % 4)
    outer_all = lax.all_gather(jnp.where(has_outer, own_half, from_pair), "z", axis=0, tiled=True)
    low_y = lax.axis_index("y") == 0
    w_self_out = jnp.where(low_y, outer_all[:rows], outer_all[rows:])
    w_cross_out = jnp.where(low_y, outer_all[rows:], outer_all[:rows])

    w_cross = gather_columns([4, 5, 7, 6, 8], 2)
    w_in = gather_columns([10 + (place - f) % 4 for place in range(4)], 2)
    w_out = lax.all_gather(take_rows(lambda place: 14 + (z - place) % 4, None), "z", axis=0, tiled=True)

    seg = segments(lengths[0], count)
    live = keep == 1
    code = seg * 2 + live.astype(jnp.int32)
    for axis in ("y", "x", "c"):
        code = jnp.concatenate([code, swap(code, axis)])
    seg_all = (code // 2).reshape(8, count)
    live_all = (code % 2 == 1).reshape(8, count)

    h0 = tokens.astype(f32)
    a_all = gather_rows(normalize(h0, gains[0]).astype(bf16))
    slots, ctx_len, ctx_width = context.shape
    ctx_all = gather_rows(context.reshape(slots * ctx_len, ctx_width))
    grad_out = cotangent.astype(f32) * live.astype(f32)[:, None]
    d_ff = gather_rows(grad_out.astype(bf16))

    def split(value):
        return value.reshape(8, -1, heads_here, head_dim)

    qkv = matmul(a_all, w_qkv).astype(bf16)
    query, keys, values = (split(qkv[:, n * block : (n + 1) * block]) for n in range(3))
    places = jnp.arange(count)
    allowed = (seg_all[:, :, None] == seg_all[:, None, :]) & (
        live_all[:, None, :] | (places[:, None] == places[None, :])
    )

    def probabilities(left, right, mask):
        scores = jnp.einsum("bqhd,bkhd->bhqk", left, right, preferred_element_type=f32) * scale
        scores = jnp.where(mask[:, None], scores, -1e30)
        expo = jnp.exp(scores - jnp.max(scores, axis=-1, keepdims=True))
        return expo / jnp.sum(expo, axis=-1, keepdims=True)

    def weighted(probs, right):
        return jnp.einsum("bhqk,bkhd->bqhd", probs, right, preferred_element_type=f32)

    def joined(value):
        return value.astype(bf16).reshape(-1, block)

    probs = probabilities(query, keys, allowed)
    probs_low = probs.astype(bf16)
    attended = joined(weighted(probs_low, values))
    h1 = h0 + scatter_rows(matmul(attended, w_self_out))
    b_all = gather_rows(normalize(h1, gains[1]).astype(bf16))

    w_cross_q = w_cross[:, :block]
    w_low = w_cross[:, block : 3 * block]
    w_high = w_cross[:, 3 * block :]
    ctx_low, ctx_high = ctx_all[:, :width], ctx_all[:, width:]
    ctx_kv = (matmul(ctx_low, w_low) + matmul(ctx_high, w_high)).astype(bf16)
    cross_q = split(matmul(b_all, w_cross_q).astype(bf16))
    cross_k, cross_v = split(ctx_kv[:, :block]), split(ctx_kv[:, block:])
    item = jnp.arange(slots * ctx_len) // ctx_len
    own_item = seg_all[:, :, None] == item[None, None, :]
    cross_p = probabilities(cross_q, cross_k, own_item)
    cross_low = cross_p.astype(bf16)
    cross_o = joined(weighted(cross_low, cross_v))
    h2 = h1 + scatter_rows(matmul(cross_o, w_cross_out))
    c_all = gather_rows(normalize(h2, gains[2]).astype(bf16))

    hidden = matmul(c_all, w_in)
    activated = gelu_tanh(hidden).astype(bf16)
    layer_out = (h2 + scatter_rows(matmul(activated, w_out))).astype(bf16)

    def sum_rows(value):
        return lax.psum_scatter(value.astype(bf16), "z", scatter_dimension=0, tiled=True)

    g_out = sum_rows(matmul_left(activated, d_ff))
    d_act = matmul_right(d_ff, w_out)
    d_hidden = jax.vjp(gelu_tanh, hidden)[1](d_act)[0].astype(bf16)
    g_in = sum_rows(matmul_left(c_all, d_hidden))
    part_two, gain_grad_two = jax.vjp(normalize, h2, gains[2])[1](scatter_rows(matmul_right(d_hidden, w_in)))
    dh2 = grad_out + part_two
    d_cross_out = gather_rows(dh2.astype(bf16))
    g_cross_out = matmul_left(cross_o, d_cross_out)

    def through(weights, d_out, left, right, probs, probs_low, values):
        d_mixed = split(matmul_right(d_out, weights).astype(bf16))
        d_probs = jnp.einsum("bqhd,bkhd->bhqk", d_mixed, values, preferred_element_type=f32)
        d_scores = (probs * (d_probs - jnp.sum(probs * d_probs, axis=-1, keepdims=True))).astype(bf16)
        d_left = joined(weighted(d_scores, right) * scale)
        d_right = joined(jnp.einsum("bhqk,bqhd->bkhd", d_scores, left, preferred_element_type=f32) * scale)
        d_values = joined(jnp.einsum("bhqk,bqhd->bkhd", probs_low, d_mixed, preferred_element_type=f32))
        return d_left, d_right, d_values

    d_cq, d_ck, d_cv = through(w_cross_out, d_cross_out, cross_q, cross_k, cross_p, cross_low, cross_v)
    d_ckv = jnp.concatenate([d_ck, d_cv], axis=1)
    g_cross = sum_rows(
        jnp.concatenate(
            [
                value.astype(bf16)
                for value in (matmul_left(b_all, d_cq), matmul_left(ctx_low, d_ckv), matmul_left(ctx_high, d_ckv))
            ],
            axis=1,
        )
    )
    part_one, gain_grad_one = jax.vjp(normalize, h1, gains[1])[1](scatter_rows(matmul_right(d_cq, w_cross_q)))
    dh1 = dh2 + part_one
    d_self_out = gather_rows(dh1.astype(bf16))
    g_self_out = matmul_left(attended, d_self_out)
    d_q, d_k, d_v = through(w_self_out, d_self_out, query, keys, probs, probs_low, values)
    d_qkv = jnp.concatenate([d_q, d_k, d_v], axis=1)
    g_qkv = sum_rows(matmul_left(a_all, d_qkv))
    g_outer = sum_rows(
        jnp.concatenate(
            [
                jnp.where(low_y, g_self_out, g_cross_out).astype(bf16),
                jnp.where(low_y, g_cross_out, g_self_out).astype(bf16),
            ],
            axis=0,
        )
    )
    part_zero, gain_grad_zero = jax.vjp(normalize, h0, gains[0])[1](scatter_rows(matmul_right(d_qkv, w_qkv)))
    grad_tokens = (dh1 + part_zero).astype(bf16)

    back_swap = [(target, source) for source, target in pair_swap]
    other_half = lax.ppermute(g_outer, ALL_AXES, back_swap)
    outer_grad = jnp.where(
        odd == 0,
        jnp.concatenate([g_outer, other_half], axis=0),
        jnp.concatenate([other_half, g_outer], axis=0),
    )

    def from_outer(zz, place, target):
        return place % 4 in (zz, (zz + 2) % 4)

    row_grads = []
    for value, keep_pair in ((g_out, None), (outer_grad, from_outer)):
        for mask in range(4):
            row_grads.append(lax.ppermute(value, ALL_AXES, flip_pairs(mask, keep_pair)) if mask else value)
    row_grads = jnp.stack(row_grads)

    group_of = np.array([0, 0, 0, 0, 1, 1, 1, 1, 1, 1, 2, 2, 2, 2, 0, 0, 0, 0], np.int32)
    column_of = np.array([0, 1, 2, 0, 0, 1, 3, 2, 4, 0, 0, 1, 2, 3, 0, 0, 0, 0], np.int32)
    group_at = jnp.sum(jnp.where(holds, group_of, 0), axis=2)
    column_at = jnp.sum(jnp.where(holds, column_of, 0), axis=2)
    column_at = jnp.where(group_at == 2, (column_at + f) % 4, column_at)
    sent = pack_gradients(
        [g_qkv, g_cross, g_in],
        jnp.tile(group_at.reshape(-1), 2),
        jnp.tile(column_at.reshape(-1), 2),
        rows,
        block,
        cap,
    )
    col_grads = lax.all_to_all(sent, PLANE, 0, 0, tiled=True).reshape(8 * cap, rows, block)
    place = np.arange(8)
    col_source = (place % 2)[None, :] * 4 + ((place // 2)[None, :] - my_shift[:, None]) % 4
    from_f = (z - my_shift) % 4
    row_source = (from_f ^ f) + jnp.where(my_tile < 10, 4, 0)
    new_w, new_m, new_v = adam_tiles(
        master,
        moment_one,
        moment_two,
        col_grads,
        row_grads,
        my_used,
        my_row,
        col_source.reshape(-1),
        row_source,
    )
    gain_grads = jnp.stack([gain_grad_zero, gain_grad_one, gain_grad_two])
    gain_total = lax.psum(gain_grads, ALL_AXES)
    new_g, new_gm, new_gv = adam_update(gains, gain_one, gain_two, gain_total, rate_gain, 0.0)
    return (layer_out, grad_tokens, new_w, new_m, new_v, new_g, new_gm, new_gv)


def whole_body(
    tokens, cotangent, context, lengths, keep, owners, master, moment_one, moment_two, gains, gain_one, gain_two
):
    cap = master.shape[0]
    n_tiles = owners.shape[0]
    slot_of = owners * cap + ranks_of(owners)
    owner_rows = lax.all_gather(master.astype(bf16), "fsdp", axis=0, tiled=True)
    tiles = [
        lax.all_gather(
            lax.dynamic_index_in_dim(owner_rows, slot_of[tile], 0, keepdims=False), "dp", axis=0, tiled=True
        )
        for tile in range(n_tiles)
    ]
    w_in = jnp.concatenate(tiles[10:14], axis=1)
    w_out = jnp.concatenate(tiles[14:18], axis=0)
    count, width = tokens.shape
    head_dim = width // HEADS
    scale = head_dim ** (-0.5)
    seg = segments(lengths[0], count)
    live = keep == 1
    places = jnp.arange(count)

    def split(value):
        return value.astype(bf16).reshape(-1, HEADS, head_dim)

    def joined(value):
        return value.astype(bf16).reshape(-1, width)

    def probabilities(left, right, mask):
        scores = jnp.einsum("qhd,khd->hqk", left, right, preferred_element_type=f32) * scale
        scores = jnp.where(mask[None], scores, -1e30)
        expo = jnp.exp(scores - jnp.max(scores, axis=-1, keepdims=True))
        return expo / jnp.sum(expo, axis=-1, keepdims=True)

    def weighted(probs, right):
        return jnp.einsum("hqk,khd->qhd", probs, right, preferred_element_type=f32)

    def through(weights, d_out, left, right, probs, values):
        d_mixed = split(matmul_right(d_out, weights))
        d_probs = jnp.einsum("qhd,khd->hqk", d_mixed, values, preferred_element_type=f32)
        d_scores = (probs * (d_probs - jnp.sum(probs * d_probs, axis=-1, keepdims=True))).astype(bf16)
        d_left = joined(weighted(d_scores, right) * scale)
        d_right = joined(jnp.einsum("hqk,qhd->khd", d_scores, left, preferred_element_type=f32) * scale)
        d_values = joined(jnp.einsum("hqk,qhd->khd", probs.astype(bf16), d_mixed, preferred_element_type=f32))
        return d_left, d_right, d_values

    h0 = tokens.astype(f32)
    a_in = normalize(h0, gains[0]).astype(bf16)
    query, keys, values = (split(matmul(a_in, tiles[n])) for n in range(3))
    allowed = (seg[:, None] == seg[None, :]) & (live[None, :] | (places[:, None] == places[None, :]))
    probs = probabilities(query, keys, allowed)
    attended = joined(weighted(probs.astype(bf16), values))
    h1 = h0 + matmul(attended, tiles[3])
    b_in = normalize(h1, gains[1]).astype(bf16)
    slots, ctx_len, ctx_width = context.shape
    ctx = context.reshape(slots * ctx_len, ctx_width)
    ctx_low, ctx_high = ctx[:, :width], ctx[:, width:]
    cross_q = split(matmul(b_in, tiles[4]))
    cross_k = split(matmul(ctx_low, tiles[5]) + matmul(ctx_high, tiles[6]))
    cross_v = split(matmul(ctx_low, tiles[7]) + matmul(ctx_high, tiles[8]))
    item = jnp.arange(slots * ctx_len) // ctx_len
    cross_p = probabilities(cross_q, cross_k, seg[:, None] == item[None, :])
    cross_o = joined(weighted(cross_p.astype(bf16), cross_v))
    h2 = h1 + matmul(cross_o, tiles[9])
    c_in = normalize(h2, gains[2]).astype(bf16)
    hidden = matmul(c_in, w_in)
    activated = gelu_tanh(hidden).astype(bf16)
    layer_out = (h2 + matmul(activated, w_out)).astype(bf16)
    grad_out = cotangent.astype(f32) * live.astype(f32)[:, None]
    d_ff = grad_out.astype(bf16)
    d_hidden = jax.vjp(gelu_tanh, hidden)[1](matmul_right(d_ff, w_out))[0].astype(bf16)
    part_two, gain_grad_two = jax.vjp(normalize, h2, gains[2])[1](matmul_right(d_hidden, w_in))
    dh2 = grad_out + part_two
    d_cross_out = dh2.astype(bf16)
    d_cq, d_ck, d_cv = through(tiles[9], d_cross_out, cross_q, cross_k, cross_p, cross_v)
    part_one, gain_grad_one = jax.vjp(normalize, h1, gains[1])[1](matmul_right(d_cq, tiles[4]))
    dh1 = dh2 + part_one
    d_self_out = dh1.astype(bf16)
    d_q, d_k, d_v = through(tiles[3], d_self_out, query, keys, probs, values)
    d_a = matmul_right(d_q, tiles[0]) + matmul_right(d_k, tiles[1]) + matmul_right(d_v, tiles[2])
    part_zero, gain_grad_zero = jax.vjp(normalize, h0, gains[0])[1](d_a)
    grad_tokens = (dh1 + part_zero).astype(bf16)
    pairs = [
        (a_in, d_q),
        (a_in, d_k),
        (a_in, d_v),
        (attended, d_self_out),
        (b_in, d_cq),
        (ctx_low, d_ck),
        (ctx_high, d_ck),
        (ctx_low, d_cv),
        (ctx_high, d_cv),
        (cross_o, d_cross_out),
    ]
    for part in range(4):
        pairs.append((c_in, d_hidden[:, part * width : (part + 1) * width]))
    for part in range(4):
        pairs.append((activated[:, part * width : (part + 1) * width], d_ff))
    total_slots = lax.axis_size("fsdp") * cap
    placed = jnp.zeros((total_slots,) + master.shape[1:], bf16)
    for tile, (left, right) in enumerate(pairs):
        term = lax.psum_scatter(
            matmul_left(left, right).astype(bf16), "dp", scatter_dimension=0, tiled=True
        )
        placed = lax.dynamic_update_index_in_dim(placed, term, slot_of[tile], 0)
    owned = lax.psum_scatter(placed, "fsdp", scatter_dimension=0, tiled=True).astype(f32)
    my_slots = lax.axis_index("fsdp") * cap + jnp.arange(cap)
    used = jnp.any(slot_of[None, :] == my_slots[:, None], axis=1)[:, None, None]
    updated = adam_update(master, moment_one, moment_two, owned, rate_matrix, decay_rate)
    new_w, new_m, new_v = (jnp.where(used, value, 0.0) for value in updated)
    gain_grads = jnp.stack([gain_grad_zero, gain_grad_one, gain_grad_two])
    gain_total = lax.psum(gain_grads, ("dp", "fsdp"))
    new_g, new_gm, new_gv = adam_update(gains, gain_one, gain_two, gain_total, rate_gain, 0.0)
    return (layer_out, grad_tokens, new_w, new_m, new_v, new_g, new_gm, new_gv)


def solution(mesh):
    planes = mesh.shape["dp"] == 8 and mesh.shape["fsdp"] == 4
    if planes:
        used = Mesh(mesh.devices.reshape(4, 2, 2, 2), ALL_AXES)
        dp, fsdp, body = ("z", "x"), ("y", "c"), plane_body
    else:
        used, dp, fsdp, body = mesh, ("dp",), ("fsdp",), whole_body
    rows = P(dp + fsdp, None)
    tiles = P(fsdp, dp, None)
    return jax.shard_map(
        body,
        mesh=used,
        in_specs=(rows, rows, P(dp + fsdp, None, None), rows, P(dp + fsdp), P(), tiles, tiles, tiles, P(), P(), P()),
        out_specs=(rows, rows, tiles, tiles, tiles, P(), P(), P()),
        check_vma=False,
    )
```

time: 6510 us -> 1400 us (0.22)
  waiting for transfers between devices: 5760 us -> 715 us
  matrix products: 315 us -> 139 us
  starting transfers between devices: 0.12 us -> 98.6 us
  Pallas kernels: 0 us -> 81.7 us
  other arithmetic: 132 us -> 60.8 us
    all_gather x2 -> x5, waiting for transfers between devices: 2990 us -> 128 us  [the longest x1 70.8 us: plane_body(): lax.all_gather(take_rows(lambda place: 14 + (z - place) % 4, None), 'z',...]
    reduce_scatter x19 -> x5, waiting for transfers between devices: 2770 us -> 208 us  [sum_rows(): lax.psum_scatter(value.astype(bf16), 'z', scatter_dimension=0, tiled=True)]
    ppermute x0 -> x82, waiting for transfers between devices: none -> 353 us  [the longest x68 310 us: swap(): return lax.ppermute(value, axis, [(0, 1), (1, 0)])]
    dot_general x18 -> x8, matrix products: 128 us -> 39 us  [matmul_left(): lax.dot_general(left, right, (((0,), (0,)), ((), ())), preferred_element_...]
    ppermute x0 -> x82, starting transfers between devices: none -> 82.6 us  [the longest x68 63.5 us: swap(): return lax.ppermute(value, axis, [(0, 1), (1, 0)])]
    pallas_call x0 -> x7, Pallas kernels: none -> 81.7 us  [the longest x1 47.6 us: adam_tiles(): pl.pallas_call(kernel, out_shape=(shape, shape, shape), grid_spec=pltpu.P...]
    scatter x1 -> x0, local copies, waits for them, and re-layouts: 66.8 us -> none  [body(): jnp.zeros((total_slots,) + row_part.shape[1:], jnp.float32).at[slot_of]]
  transfers between devices with their start and end apart: 21 -> 95, of which waited for: 21 -> 57; matrix products, arithmetic and copies ran while one was open for 1% -> 20% of each run, Pallas kernels for 0% -> 2%
where the time goes in v1:
time: 1400 us; the launch traced here: 1380 us
  waiting for transfers between devices  715 us (51%)
  local copies, waits for them, and re-layouts  184 us (13%)
  matrix products  139 us (10%)
  starting transfers between devices  98.6 us (7%)
  Pallas kernels  81.7 us (6%)
  between operations  64.9 us (5%)
  other arithmetic  60.8 us (4%)
  blocking collectives  39.5 us (3%)
    ppermute x68, waiting for transfers between devices, swap(): return lax.ppermute(value, axis, [(0, 1), (1, 0)])  310 us
    reduce_scatter x5, waiting for transfers between devices, sum_rows(): lax.psum_scatter(value.astype(bf16), 'z', scatter_dimension=0, tiled=True)  208 us
    unnamed x219, local copies, waits for them, and re-layouts  75.2 us
    all_gather x1, waiting for transfers between devices, plane_body(): lax.all_gather(take_rows(lambda place: 14 + (z - place) % 4, None), 'z',...  70.8 us
    ppermute x68, starting transfers between devices, swap(): return lax.ppermute(value, axis, [(0, 1), (1, 0)])  63.5 us
    all_gather x3, waiting for transfers between devices, gather_columns(): return lax.all_gather(local, 'z', axis=0, tiled=True)  57.3 us
    dot_general x8, matrix products, matmul(): return jnp.dot(left, right, preferred_element_type=f32)  48.8 us
    pallas_call x1, Pallas kernels, adam_tiles(): pl.pallas_call(kernel, out_shape=(shape, shape, shape), grid_spec=pltpu.P...  47.6 us
  transfers between devices with their start and end apart: 95, of which 57 were waited for; matrix products, arithmetic and copies ran while one was open for 20% of the time, Pallas kernels for 2%

profile of v1, /device:TPU:0, one launch (start us, length us, event | category | flops | bytes accessed | tf_op | source)
XLA Modules:
  0.0 1383.5 jit_solution(14581915904533511766)
XLA Ops:
  37.3 25.7 %all-to-all-done = bf16[8,3,256,256]{3,2,1,0:T(8,128)(2,1)S(1)} async-done(((bf16[8,3,256,256]{3,2,1,0:T(8,128)(2,1)}), bf16[8,3,256,256]{3,2,1,0:T(8,128)(2,1)S(1)}, u32[]{:S(2)}, u32[]{:S(2)}) %all-to-all-start) | async-done | bytes 3145760 | tf_op jit(solution)/shard_map/all_to_all | solution.py:292
  118.0 11.0 collective-permute-done.5
  130.3 15.6 %collective-permute-done.6 = s32[256]{0:T(256)S(1)} collective-permute-done((s32[256]{0:T(256)S(1)}, s32[256]{0:T(256)S(1)}, u32[]{:S(2)}, u32[]{:S(2)}) %collective-permute-start.6) | collective-permute-done | bytes 1056 | tf_op jit(solution)/shard_map/ppermute | solution.py:215
  148.3 27.2 %collective-permute-done.3 = bf16[64,2048]{1,0:T(8,128)(2,1)S(1)} collective-permute-done((bf16[64,2048]{1,0:T(8,128)(2,1)}, bf16[64,2048]{1,0:T(8,128)(2,1)S(1)}, u32[]{:S(2)}, u32[]{:S(2)}) %collective-permute-start.3) | collective-permute-done | bytes 262176 | tf_op jit(solution)/shard_map/ppermute | solution.py:215
  192.3 11.5 collective-permute-done.9
  221.5 21.6 %collective-permute-done.17 = bf16[256,4096]{1,0:T(8,128)(2,1)} collective-permute-done((bf16[256,4096]{1,0:T(8,128)(2,1)}, bf16[256,4096]{1,0:T(8,128)(2,1)}, u32[]{:S(2)}, u32[]{:S(2)}) %collective-permute-start.17) | collective-permute-done | bytes 2097184 | tf_op jit(solution)/shard_map/ppermute | solution.py:215
  327.7 11.8 collective-permute-done.13
  374.0 47.3 %all-gather.10.cloned.1.call-done = bf16[2048,1280]{1,0:T(8,128)(2,1)} async-done(((bf16[512,1280]{1,0:T(8,128)(2,1)}), bf16[2048,1280]{1,0:T(8,128)(2,1)}) %all-gather.10.cloned.1.call-update) | async-done | bytes 5242896 | tf_op jit(solution)/shard_map/all_gather | solution.py:313
  556.7 10.1 all-gather.12.cloned.1.call-done
  566.8 9.9 fusion.203
  576.7 70.8 %all-gather.14.cloned.1.call-done = bf16[1024,2048]{1,0:T(8,128)(2,1)} async-done(((bf16[256,2048]{1,0:T(8,128)(2,1)}), bf16[1024,2048]{1,0:T(8,128)(2,1)}) %all-gather.14.cloned.1.call-update) | async-done | bytes 4194320 | tf_op jit(solution)/shard_map/all_gather | solution.py:361
  647.5 11.4 fusion.13
  725.1 11.2 collective-permute-done.55
  785.2 12.3 collective-permute-done.61
  810.4 9.8 collective-permute-done.65
  906.9 18.3 %collective-permute-done.76 = bf16[256,2048]{1,0:T(8,128)(2,1)} collective-permute-done((bf16[256,2048]{1,0:T(8,128)(2,1)}, bf16[256,2048]{1,0:T(8,128)(2,1)}, u32[]{:S(2)}, u32[]{:S(2)}) %collective-permute-start.76) | collective-permute-done | bytes 1048608 | tf_op jit(solution)/shard_map/ppermute | solution.py:490
  936.1 47.9 %reduce-scatter.10.cloned.1.call-done.refs_2_ = bf16[512,1024]{1,0:T(8,128)(2,1)} async-done(((bf16[2048,1024]{1,0:T(8,128)(2,1)}), bf16[512,1024]{1,0:T(8,128)(2,1)}) %reduce-scatter.10.cloned.1.call-update) | async-done | bytes 1048592 | tf_op jit(solution)/shard_map/reduce_scatter | solution.py:426
  984.0 97.1 %reduce-scatter.8.cloned.1.call-done.refs_1_ = bf16[512,1280]{1,0:T(8,128)(2,1)} async-done(((bf16[2048,1280]{1,0:T(8,128)(2,1)}), bf16[512,1280]{1,0:T(8,128)(2,1)}) %reduce-scatter.8.cloned.1.call-update) | async-done | bytes 1310736 | tf_op jit(solution)/shard_map/reduce_scatter | solution.py:426
  1081.1 63.1 %reduce-scatter.6.cloned.1.call-done.refs_0_ = bf16[512,768]{1,0:T(8,128)(2,1)} async-done(((bf16[2048,768]{1,0:T(8,128)(2,1)}), bf16[512,768]{1,0:T(8,128)(2,1)}) %reduce-scatter.6.cloned.1.call-update) | async-done | bytes 786448 | tf_op jit(solution)/shard_map/reduce_scatter | solution.py:426
  1147.8 17.3 %pack_gradients.1 = bf16[8,6,256,256]{3,2,1,0:T(8,128)(2,1)} custom-call(s32[48]{0:T(128)S(1)} %tile.20.which_ref, s32[48]{0:T(128)S(1)} %tile.22.column_ref, bf16[512,768]{1,0:T(8,128)(2,1)S(1)} %copy-done.7, bf16[512,1280]{1,0:T(8,128)(2,1)S(1)} %copy-done.5, bf16[512,1024]{1,0:T(8,128)(2,1)S(1)} %copy-done.6), custom_call_target="tpu_custom_call" | custom-call | tf_op jit(solution)/shard_map/pack_gradients/pallas_call | solution.py:152
  1184.5 67.3 %collective-permute-done.71 = bf16[2,128,1024]{2,1,0:T(8,128)(2,1)S(1)} collective-permute-done((bf16[2,128,1024]{2,1,0:T(8,128)(2,1)}, bf16[2,128,1024]{2,1,0:T(8,128)(2,1)S(1)}, u32[]{:S(2)}, u32[]{:S(2)}) %collective-permute-start.71) | collective-permute-done | bytes 524320 | tf_op jit(solution)/shard_map/ppermute | solution.py:215
  1255.8 24.0 %collective-permute-done.74 = bf16[128,1024]{1,0:T(8,128)(2,1)S(1)} collective-permute-done((bf16[128,1024]{1,0:T(8,128)(2,1)S(1)}, bf16[128,1024]{1,0:T(8,128)(2,1)S(1)}, u32[]{:S(2)}, u32[]{:S(2)}) %collective-permute-start.74) | collective-permute-done | bytes 262176 | tf_op jit(solution)/shard_map/ppermute | solution.py:215
  1281.6 39.5 %psum.7 = f32[3,2048]{1,0:T(4,128)S(1)} all-reduce(f32[3,2048]{1,0:T(4,128)S(1)} %pad_maximum_fusion.5), channel_id=1, replica_groups=mesh['z'=4,'x'=2,'y'=2,'c'=2] {'z','x','y','c'}, use_global_device_ids=true, to_apply=%region_49.50 | all-reduce | flops 6144 | bytes 49152 | tf_op jit(solution)/shard_map/psum | solution.py:523
  1328.9 47.6 %adam_tiles.1 = (f32[6,256,2048]{2,1,0:T(8,128)}, f32[6,256,2048]{2,1,0:T(8,128)}, f32[6,256,2048]{2,1,0:T(8,128)}) custom-call(s32[6]{0:T(128)S(1)} %get-tuple-element.27.used_ref, s32[6]{0:T(128)S(1)} %get-tuple-element.28.is_row_ref, s32[48]{0:T(128)S(1)} %fusion.150.cs_ref, s32[6]{0:T(128)S(1)} %fusion.173.rs_ref, f32[6,256,2048]{2,1,0:T(8,128)} %w_ref.1, ...), custom_call_target="tpu_custom_call" | custom-call | tf_op jit(solution)/shard_map/adam_tiles/pallas_call | solution.py:194
  (630 shorter events, 589.4 us)
Async XLA Ops:
  26.1 239.4 %all-gather.6.cloned.1.call-start = ((), (), s32[]{:S(2)}) async-start(), calls=%async_computation.8 | async-start | bytes 3932160 | tf_op jit(solution)/shard_map/all_gather | solution.py:313
  88.0 89.5 %collective-permute-start.37 = (bf16[256,2048]{1,0:T(8,128)(2,1)}, bf16[256,2048]{1,0:T(8,128)(2,1)}, u32[]{:S(2)}, u32[]{:S(2)}) collective-permute-start(bf16[256,2048]{1,0:T(8,128)(2,1)} %get-tuple-element.73), channel_id=1, source_target_pairs={{0,3},{1,2},{2,1},{3,0},{4,7},{5,6},{6,5},{7,4},{8,11},{9,10},{10,... | collective-permute-start | bytes 3145736 | tf_op jit(solution)/shard_map/ppermute | solution.py:331
  92.2 92.2 %collective-permute-start.38 = (bf16[256,2048]{1,0:T(8,128)(2,1)}, bf16[256,2048]{1,0:T(8,128)(2,1)}, u32[]{:S(2)}, u32[]{:S(2)}) collective-permute-start(bf16[256,2048]{1,0:T(8,128)(2,1)} %get-tuple-element.72), channel_id=1, source_target_pairs={{0,2},{1,3},{2,0},{3,1},{4,6},{5,7},{6,4},{7,5},{8,10},{9,11},{10,... | collective-permute-start | bytes 3145736 | tf_op jit(solution)/shard_map/ppermute | solution.py:331
  98.9 217.4 %all-to-all-start.1 = ((bf16[8,3,256,256]{3,2,1,0:T(8,128)(2,1)}), bf16[8,3,256,256]{3,2,1,0:T(8,128)(2,1)}, u32[]{:S(2)}, u32[]{:S(2)}) async-start(bf16[8,3,256,256]{3,2,1,0:T(8,128)(2,1)} %copy-done), calls=%async_computation.1 | async-start | bytes 6291456 | tf_op jit(solution)/shard_map/all_to_all | solution.py:292
  103.3 188.7 %all-gather.8.cloned.1.call-start = ((), (), s32[]{:S(2)}) async-start(), calls=%async_computation.9 | async-start | bytes 2621440 | tf_op jit(solution)/shard_map/all_gather | solution.py:354
  116.5 59.1 %collective-permute-start.3 = (bf16[64,2048]{1,0:T(8,128)(2,1)}, bf16[64,2048]{1,0:T(8,128)(2,1)S(1)}, u32[]{:S(2)}, u32[]{:S(2)}) collective-permute-start(bf16[64,2048]{1,0:T(8,128)(2,1)} %slice.516), channel_id=1, source_target_pairs={{0,2},{2,0},{1,3},{3,1},{4,6},{6,4},{5,7},{7,5},{8,10},{10,8},{9,1... | collective-permute-start | bytes 786440 | tf_op jit(solution)/shard_map/ppermute | solution.py:215
  186.3 58.8 %collective-permute-start.18 = (bf16[256,4096]{1,0:T(8,128)(2,1)}, bf16[256,4096]{1,0:T(8,128)(2,1)}, u32[]{:S(2)}, u32[]{:S(2)}) collective-permute-start(bf16[256,4096]{1,0:T(8,128)(2,1)} %bitcast.41), channel_id=1, source_target_pairs={{0,4},{4,0},{1,5},{5,1},{2,6},{6,2},{3,7},{7,3},{8,12},{12,8},{9,1... | collective-permute-start | bytes 6291464 | tf_op jit(solution)/shard_map/ppermute | solution.py:215
  221.3 200.0 %all-gather.10.cloned.1.call-start = ((), (), s32[]{:S(2)}) async-start(), calls=%async_computation.10 | async-start | bytes 6553600 | tf_op jit(solution)/shard_map/all_gather | solution.py:313
  321.2 245.6 %all-gather.12.cloned.1.call-start = ((), (), s32[]{:S(2)}) async-start(), calls=%async_computation.11 | async-start | bytes 5242880 | tf_op jit(solution)/shard_map/all_gather | solution.py:313
  374.0 73.0 %collective-permute-start.26 = (bf16[512,2048]{1,0:T(8,128)(2,1)}, bf16[512,2048]{1,0:T(8,128)(2,1)}, u32[]{:S(2)}, u32[]{:S(2)}) collective-permute-start(bf16[512,2048]{1,0:T(8,128)(2,1)} %get-tuple-element.159), channel_id=1, source_target_pairs={{0,1},{1,0},{2,3},{3,2},{4,5},{5,4},{6,7},{7,6},{8,9},{9,8},{10,11... | collective-permute-start | bytes 6291464 | tf_op jit(solution)/shard_map/ppermute | solution.py:215
  487.3 160.2 %all-gather.14.cloned.1.call-start = ((), (), s32[]{:S(2)}) async-start(), calls=%async_computation.12 | async-start | bytes 5242880 | tf_op jit(solution)/shard_map/all_gather | solution.py:361
  523.9 373.9 %reduce-scatter.12.cloned.1.call-start = ((), (), s32[]{:S(2)}) async-start(), calls=%async_computation.16 | async-start | bytes 5242880 | tf_op jit(solution)/shard_map/reduce_scatter | solution.py:426
  779.0 148.4 %reduce-scatter.14.cloned.1.call-start = ((), (), s32[]{:S(2)}) async-start(), calls=%async_computation.17 | async-start | bytes 2621440 | tf_op jit(solution)/shard_map/reduce_scatter | solution.py:426
  836.1 147.9 %reduce-scatter.10.cloned.1.call-start = ((), (), s32[]{:S(2)}) async-start(), calls=%async_computation.15 | async-start | bytes 5242880 | tf_op jit(solution)/shard_map/reduce_scatter | solution.py:426
  845.6 235.5 %reduce-scatter.8.cloned.1.call-start = ((), (), s32[]{:S(2)}) async-start(), calls=%async_computation.14 | async-start | bytes 6553600 | tf_op jit(solution)/shard_map/reduce_scatter | solution.py:426
  868.9 275.3 %reduce-scatter.6.cloned.1.call-start = ((), (), s32[]{:S(2)}) async-start(), calls=%async_computation.13 | async-start | bytes 3932160 | tf_op jit(solution)/shard_map/reduce_scatter | solution.py:426
  900.5 274.4 %collective-permute-start.77 = (bf16[256,2048]{1,0:T(8,128)(2,1)}, bf16[256,2048]{1,0:T(8,128)(2,1)S(1)}, u32[]{:S(2)}, u32[]{:S(2)}) collective-permute-start(bf16[256,2048]{1,0:T(8,128)(2,1)} %reduce-scatter.12.cloned.1.call-done), channel_id=1, source_target_pairs={{0,3},{1,2},{2,1},{3,0},{4,7},{5,6},{6,5},{7,4},{8,11},{9,10},{10,... | collective-permute-start | bytes 3145736 | tf_op jit(solution)/shard_map/ppermute | solution.py:490
  927.5 248.5 %collective-permute-start.78 = (bf16[128,2048]{1,0:T(8,128)(2,1)}, bf16[128,2048]{1,0:T(8,128)(2,1)S(1)}, u32[]{:S(2)}, u32[]{:S(2)}) collective-permute-start(bf16[128,2048]{1,0:T(8,128)(2,1)} %reduce-scatter.14.cloned.1.call-done), channel_id=1, source_target_pairs={{8,0},{10,2},{12,4},{14,6},{1,9},{3,11},{5,13},{7,15},{24,16},{26,... | collective-permute-start | bytes 1572872 | tf_op jit(solution)/shard_map/ppermute | solution.py:477
  1165.1 163.7 %all-to-all-start.2 = ((bf16[8,6,256,256]{3,2,1,0:T(8,128)(2,1)}), bf16[8,6,256,256]{3,2,1,0:T(8,128)(2,1)}, u32[]{:S(2)}, u32[]{:S(2)}) async-start(bf16[8,6,256,256]{3,2,1,0:T(8,128)(2,1)} %pack_gradients.1), calls=%async_computation.5 | async-start | bytes 12582912 | tf_op jit(solution)/shard_map/all_to_all | solution.py:506
  1171.5 80.3 %collective-permute-start.71 = (bf16[2,128,1024]{2,1,0:T(8,128)(2,1)}, bf16[2,128,1024]{2,1,0:T(8,128)(2,1)S(1)}, u32[]{:S(2)}, u32[]{:S(2)}) collective-permute-start(bf16[2,128,1024]{2,1,0:T(8,128)(2,1)} %slice_bitcast_fusion.15), channel_id=1, source_target_pairs={{0,2},{2,0},{1,3},{3,1},{4,6},{6,4},{5,7},{7,5},{8,10},{10,8},{9,1... | collective-permute-start | bytes 1572872 | tf_op jit(solution)/shard_map/ppermute | solution.py:215
  1173.4 78.3 %collective-permute-start.73 = (bf16[2,128,1024]{2,1,0:T(8,128)(2,1)S(1)}, bf16[2,128,1024]{2,1,0:T(8,128)(2,1)S(1)}, u32[]{:S(2)}, u32[]{:S(2)}) collective-permute-start(bf16[2,128,1024]{2,1,0:T(8,128)(2,1)S(1)} %slice_bitcast_fusion.13), channel_id=1, source_target_pairs={{0,4},{4,0},{1,5},{5,1},{2,6},{6,2},{3,7},{7,3},{8,12},{12,8},{9,1... | collective-permute-start | bytes 1572872 | tf_op jit(solution)/shard_map/ppermute | solution.py:215
  1177.3 144.6 %collective-permute-start.79 = (bf16[256,2048]{1,0:T(8,128)(2,1)}, bf16[256,2048]{1,0:T(8,128)(2,1)}, u32[]{:S(2)}, u32[]{:S(2)}) collective-permute-start(bf16[256,2048]{1,0:T(8,128)(2,1)} %maximum_select_fusion.1), channel_id=1, source_target_pairs={{0,1},{2,3},{4,5},{6,7},{9,8},{11,10},{13,12},{15,14},{16,17},{18,... | collective-permute-start | bytes 3145736 | tf_op jit(solution)/shard_map/ppermute | solution.py:490
  1179.7 144.4 %collective-permute-start.80 = (bf16[256,2048]{1,0:T(8,128)(2,1)}, bf16[256,2048]{1,0:T(8,128)(2,1)}, u32[]{:S(2)}, u32[]{:S(2)}) collective-permute-start(bf16[256,2048]{1,0:T(8,128)(2,1)} %maximum_select_fusion.1), channel_id=1, source_target_pairs={{0,2},{2,0},{4,6},{6,4},{9,11},{11,9},{13,15},{15,13},{16,18},{18,... | collective-permute-start | bytes 3145736 | tf_op jit(solution)/shard_map/ppermute | solution.py:490
  1182.2 144.4 %collective-permute-start.81 = (bf16[256,2048]{1,0:T(8,128)(2,1)}, bf16[256,2048]{1,0:T(8,128)(2,1)}, u32[]{:S(2)}, u32[]{:S(2)}) collective-permute-start(bf16[256,2048]{1,0:T(8,128)(2,1)} %maximum_select_fusion.1), channel_id=1, source_target_pairs={{0,3},{2,1},{4,7},{6,5},{9,10},{11,8},{13,14},{15,12},{16,19},{18,... | collective-permute-start | bytes 3145736 | tf_op jit(solution)/shard_map/ppermute | solution.py:490
  (161 other events, 2642.7 us)
Sparse Core Ops, SparseCore 0:
  64.9 63.7 all-gather.5
  221.4 47.5 all-gather.7
  321.3 99.9 all-gather.9
  487.5 79.2 all-gather.11
  568.2 79.2 all-gather.13
  779.2 73.9 reduce-scatter.11
  855.6 44.3 reduce-scatter.13
  902.3 81.6 reduce-scatter.9
  987.0 94.0 reduce-scatter.7
  1083.3 60.7 reduce-scatter.5

commit v2 on v1

--- a/solution.py
+++ b/solution.py
@@ -66,9 +66,9 @@
 def adam_update(weight, first, second, grad, rate, decay):
     first = beta_one * first + (1.0 - beta_one) * grad
     second = beta_two * second + (1.0 - beta_two) * grad * grad
-    fix_one = 1.0 - beta_one**STEP
-    fix_two = 1.0 - beta_two**STEP
-    move = first / fix_one / (jnp.sqrt(second / fix_two) + adam_eps)
+    fix_one = 1.0 / (1.0 - beta_one**STEP)
+    fix_two = 1.0 / (1.0 - beta_two**STEP)
+    move = first * fix_one / (jnp.sqrt(second * fix_two) + adam_eps)
     return (weight - rate * (move + decay * weight), first, second)
 
 
@@ -163,52 +163,77 @@
     )(which, column, *groups)
 
 
-def adam_tiles(master, one, two, col_grads, row_grads, used, is_row, col_source, row_source):
-    cap, rows, columns = master.shape
+def adam_tiles(master, one, two, columns_from, rows_from, visit, mode, column_place, row_place, hold, previous=None):
+    _, rows, columns = master.shape
     width = columns // 8
-
-    def kernel(used_ref, is_row_ref, cs_ref, rs_ref, w_ref, m_ref, v_ref, cg_ref, rg_ref, nw_ref, nm_ref, nv_ref):
-        slot = pl.program_id(0)
-
-        @pl.when(used_ref[slot] == 0)
+    n_visit = visit.shape[0]
+    n_col, n_row = len(columns_from), len(rows_from)
+    kept = () if previous is None else tuple(previous)
+
+    def kernel(visit_ref, mode_ref, cp_ref, rp_ref, hold_ref, *refs):
+        w_ref, m_ref, v_ref = refs[:3]
+        grads = refs[3 : 3 + n_col + n_row]
+        outs = refs[3 + n_col + n_row + len(kept) :]
+        how = mode_ref[pl.program_id(0)]
+
+        @pl.when(how == 1)
         def _():
-            for ref in (nw_ref, nm_ref, nv_ref):
+            for ref in outs:
                 ref[...] = jnp.zeros_like(ref)
 
-        def update(grad):
-            w, m, v = adam_update(w_ref[0], m_ref[0], v_ref[0], grad.astype(f32), rate_matrix, decay_rate)
-            nw_ref[0] = w
-            nm_ref[0] = m
-            nv_ref[0] = v
-
-        @pl.when((used_ref[slot] == 1) & (is_row_ref[slot] == 0))
-        def _():
-            update(cg_ref[0])
-
-        @pl.when((used_ref[slot] == 1) & (is_row_ref[slot] == 1))
-        def _():
-            update(rg_ref[0])
-
-    state = pl.BlockSpec((1, rows, width), lambda k, b, u, i, cs, rs: (k, 0, b))
+        for number, grad_ref in enumerate(grads):
+
+            @pl.when(how == number + 2)
+            def _():
+                grad = grad_ref[0].astype(f32)
+                results = adam_update(w_ref[0], m_ref[0], v_ref[0], grad, rate_matrix, decay_rate)
+                for ref, value in zip(outs, results, strict=True):
+                    ref[0] = value
+
+    def block_of(n, b, hold):
+        return jnp.where(hold[n] == 1, 7, b)
+
+    state = pl.BlockSpec((1, rows, width), lambda n, b, vi, mo, cp, rp, ho: (vi[n], 0, block_of(n, b, ho)))
+
+    def column_spec(number):
+        def at(n, b, vi, mo, cp, rp, ho):
+            return (jnp.where(mo[n] == number + 2, cp[n * 8 + block_of(n, b, ho)], 0), 0, 0)
+
+        return pl.BlockSpec((1, rows, width), at)
+
+    def row_spec(number):
+        def at(n, b, vi, mo, cp, rp, ho):
+            taken = mo[n] == number + 2
+            return (jnp.where(taken, rp[n], 0), 0, jnp.where(taken, block_of(n, b, ho), 0))
+
+        return pl.BlockSpec((1, rows, width), at)
+
     shape = jax.ShapeDtypeStruct(master.shape, f32)
+    n_before = 5 + 3 + n_col + n_row
     return pl.pallas_call(
         kernel,
         out_shape=(shape, shape, shape),
         grid_spec=pltpu.PrefetchScalarGridSpec(
-            num_scalar_prefetch=4,
-            grid=(cap, 8),
+            num_scalar_prefetch=5,
+            grid=(n_visit, 8),
             in_specs=[
                 state,
                 state,
                 state,
-                pl.BlockSpec((1, rows, width), lambda k, b, u, i, cs, rs: (cs[k * 8 + b] * cap + k, 0, 0)),
-                pl.BlockSpec((1, rows, width), lambda k, b, u, i, cs, rs: (rs[k], 0, b)),
+                *(column_spec(number) for number in range(n_col)),
+                *(row_spec(n_col + number) for number in range(n_row)),
+                *(pl.BlockSpec(memory_space=pl.ANY) for _ in kept),
             ],
             out_specs=(state, state, state),
         ),
+        input_output_aliases={n_before + n: n for n in range(len(kept))},
         compiler_params=pltpu.CompilerParams(vmem_limit_bytes=VMEM_LIMIT),
         name="adam_tiles",
-    )(used, is_row, col_source, row_source, master, one, two, col_grads, row_grads)
+    )(visit, mode, column_place, row_place, hold, master, one, two, *columns_from, *rows_from, *kept)
+
+
+def after(value, *others):
+    return lax.optimization_barrier((value, *others))[0]
 
 
 def swap(value, axis):
@@ -286,11 +311,13 @@
     to_f = np.arange(8) % 4
     column_table = 2 * ((to_f[None, :] + my_shift[:, None]) % 4) + to_x[None, :]
     half_cap = cap // 2
-    received = []
-    for first in (0, half_cap):
-        sent = pack_columns(master, column_table[first : first + half_cap].reshape(-1), first, half_cap)
-        got = lax.all_to_all(sent, PLANE, 0, 0, tiled=True)
-        received.append(got.reshape(8 * half_cap, rows, block))
+
+    def exchange_columns(first, weights):
+        table = column_table[first : first + half_cap].reshape(-1)
+        got = lax.all_to_all(pack_columns(weights, table, first, half_cap), PLANE, 0, 0, tiled=True)
+        return got.reshape(8 * half_cap, rows, block)
+
+    received = [exchange_columns(0, master)]
 
     def source_of(tile):
         if isinstance(tile, int):
@@ -319,14 +346,17 @@
         slot = jnp.sum(jnp.where(chosen, rank, 0))
         return lax.dynamic_index_in_dim(master, slot, 0, keepdims=False).astype(bf16)
 
+    h0 = tokens.astype(f32)
+    a_all = gather_rows(after(normalize(h0, gains[0]).astype(bf16), received[0]))
+
     def owner_of(tile):
         return jnp.sum(jnp.where(jnp.arange(n_tiles) == tile, owners, 0))
 
-    def take_rows(tile_for, keep_pair):
+    def take_rows(tile_for, keep_pair, *earlier):
         found = None
         source = owner_of(tile_for(f)) ^ f
         for mask in range(4):
-            got = my_block(tile_for(f ^ mask))
+            got = after(my_block(tile_for(f ^ mask)), *earlier)
             if mask:
                 got = lax.ppermute(got, ALL_AXES, flip_pairs(mask, keep_pair))
             found = got if found is None else jnp.where(source == mask, got, found)
@@ -338,7 +368,7 @@
     def needs_outer(zz, place, target):
         return target % 4 in (zz, (zz + 2) % 4)
 
-    outer = take_rows(self_or_cross, needs_outer)
+    outer = take_rows(self_or_cross, needs_outer, received[0])
     half_rows = rows // 2
     odd = z % 2
     to_pair = lax.dynamic_slice_in_dim(outer, (1 - odd) * half_rows, half_rows, 0)
@@ -356,9 +386,13 @@
     w_self_out = jnp.where(low_y, outer_all[:rows], outer_all[rows:])
     w_cross_out = jnp.where(low_y, outer_all[rows:], outer_all[:rows])
 
+    received.append(exchange_columns(half_cap, after(master, a_all, from_pair)))
     w_cross = gather_columns([4, 5, 7, 6, 8], 2)
     w_in = gather_columns([10 + (place - f) % 4 for place in range(4)], 2)
-    w_out = lax.all_gather(take_rows(lambda place: 14 + (z - place) % 4, None), "z", axis=0, tiled=True)
+    slots, ctx_len, ctx_width = context.shape
+    ctx_all = gather_rows(after(context.reshape(slots * ctx_len, ctx_width), received[1]))
+    out_rows = take_rows(lambda place: 14 + (z - place) % 4, None, ctx_all)
+    w_out = lax.all_gather(out_rows, "z", axis=0, tiled=True)
 
     seg = segments(lengths[0], count)
     live = keep == 1
@@ -368,12 +402,8 @@
     seg_all = (code // 2).reshape(8, count)
     live_all = (code % 2 == 1).reshape(8, count)
 
-    h0 = tokens.astype(f32)
-    a_all = gather_rows(normalize(h0, gains[0]).astype(bf16))
-    slots, ctx_len, ctx_width = context.shape
-    ctx_all = gather_rows(context.reshape(slots * ctx_len, ctx_width))
     grad_out = cotangent.astype(f32) * live.astype(f32)[:, None]
-    d_ff = gather_rows(grad_out.astype(bf16))
+    d_ff = gather_rows(after(grad_out.astype(bf16), out_rows))
 
     def split(value):
         return value.reshape(8, -1, heads_here, head_dim)
@@ -420,18 +450,20 @@
 
     hidden = matmul(c_all, w_in)
     activated = gelu_tanh(hidden).astype(bf16)
+
+    def sum_rows(value):
+        return lax.psum_scatter(value, "z", scatter_dimension=0, tiled=True)
+
+    t_out = matmul_left(activated, d_ff).astype(bf16)
+    g_out = sum_rows(t_out)
+    d_act = matmul_right(d_ff, after(w_out, t_out))
     layer_out = (h2 + scatter_rows(matmul(activated, w_out))).astype(bf16)
-
-    def sum_rows(value):
-        return lax.psum_scatter(value.astype(bf16), "z", scatter_dimension=0, tiled=True)
-
-    g_out = sum_rows(matmul_left(activated, d_ff))
-    d_act = matmul_right(d_ff, w_out)
     d_hidden = jax.vjp(gelu_tanh, hidden)[1](d_act)[0].astype(bf16)
-    g_in = sum_rows(matmul_left(c_all, d_hidden))
+    t_in = matmul_left(c_all, d_hidden).astype(bf16)
+    g_in = sum_rows(t_in)
     part_two, gain_grad_two = jax.vjp(normalize, h2, gains[2])[1](scatter_rows(matmul_right(d_hidden, w_in)))
     dh2 = grad_out + part_two
-    d_cross_out = gather_rows(dh2.astype(bf16))
+    d_cross_out = gather_rows(after(dh2.astype(bf16), t_in))
     g_cross_out = matmul_left(cross_o, d_cross_out)
 
     def through(weights, d_out, left, right, probs, probs_low, values):
@@ -445,22 +477,18 @@
 
     d_cq, d_ck, d_cv = through(w_cross_out, d_cross_out, cross_q, cross_k, cross_p, cross_low, cross_v)
     d_ckv = jnp.concatenate([d_ck, d_cv], axis=1)
-    g_cross = sum_rows(
-        jnp.concatenate(
-            [
-                value.astype(bf16)
-                for value in (matmul_left(b_all, d_cq), matmul_left(ctx_low, d_ckv), matmul_left(ctx_high, d_ckv))
-            ],
-            axis=1,
-        )
+    t_cross = jnp.concatenate(
+        [
+            value.astype(bf16)
+            for value in (matmul_left(b_all, d_cq), matmul_left(ctx_low, d_ckv), matmul_left(ctx_high, d_ckv))
+        ],
+        axis=1,
     )
+    g_cross = sum_rows(t_cross)
     part_one, gain_grad_one = jax.vjp(normalize, h1, gains[1])[1](scatter_rows(matmul_right(d_cq, w_cross_q)))
     dh1 = dh2 + part_one
-    d_self_out = gather_rows(dh1.astype(bf16))
+    d_self_out = gather_rows(after(dh1.astype(bf16), t_cross))
     g_self_out = matmul_left(attended, d_self_out)
-    d_q, d_k, d_v = through(w_self_out, d_self_out, query, keys, probs, probs_low, values)
-    d_qkv = jnp.concatenate([d_q, d_k, d_v], axis=1)
-    g_qkv = sum_rows(matmul_left(a_all, d_qkv))
     g_outer = sum_rows(
         jnp.concatenate(
             [
@@ -470,8 +498,48 @@
             axis=0,
         )
     )
+    d_q, d_k, d_v = through(w_self_out, d_self_out, query, keys, probs, probs_low, values)
+    d_qkv = jnp.concatenate([d_q, d_k, d_v], axis=1)
+    g_qkv = sum_rows(matmul_left(a_all, d_qkv).astype(bf16))
     part_zero, gain_grad_zero = jax.vjp(normalize, h0, gains[0])[1](scatter_rows(matmul_right(d_qkv, w_qkv)))
     grad_tokens = (dh1 + part_zero).astype(bf16)
+
+    def to_owners(value, keep_pair):
+        moved = [lax.ppermute(value, ALL_AXES, flip_pairs(mask, keep_pair)) for mask in range(1, 4)]
+        return jnp.stack([value, *moved])
+
+    out_grads = to_owners(g_out, None)
+    group_of = np.array([0, 0, 0, 0, 0, 0, 0, 0, 0, 0, 1, 1, 1, 1, 0, 0, 0, 0], np.int32)
+    column_of = np.array([0, 0, 0, 0, 0, 1, 3, 2, 4, 0, 0, 1, 2, 3, 0, 0, 0, 0], np.int32)
+    group_at = jnp.sum(jnp.where(holds, group_of, 0), axis=2)
+    column_at = jnp.sum(jnp.where(holds, column_of, 0), axis=2)
+    column_at = jnp.where(group_at == 1, (column_at + f) % 4, column_at)
+    sent = pack_gradients(
+        [g_cross, g_in],
+        jnp.tile(group_at.reshape(-1), 2),
+        jnp.tile(column_at.reshape(-1), 2),
+        rows,
+        block,
+        cap,
+    )
+    early_grads = lax.all_to_all(sent, PLANE, 0, 0, tiled=True).reshape(8 * cap, rows, block)
+    place = np.arange(8)
+    source = (place % 2)[None, :] * 4 + ((place // 2)[None, :] - my_shift[:, None]) % 4
+    row_source = ((z - my_shift) % 4) ^ f
+    late = (my_used == 1) & ((my_tile < 4) | (my_tile == 9))
+    early_mode = jnp.where(my_used == 0, 1, jnp.where(late, 0, jnp.where(my_row == 1, 3, 2)))
+    states = (master, moment_one, moment_two)
+    slot = np.arange(cap, dtype=np.int32)
+    early = adam_tiles(
+        *states,
+        [early_grads],
+        [out_grads],
+        slot,
+        early_mode,
+        (source * cap + slot[:, None]).reshape(-1),
+        row_source,
+        np.zeros(cap, np.int32),
+    )
 
     back_swap = [(target, source) for source, target in pair_swap]
     other_half = lax.ppermute(g_outer, ALL_AXES, back_swap)
@@ -480,44 +548,40 @@
         jnp.concatenate([g_outer, other_half], axis=0),
         jnp.concatenate([other_half, g_outer], axis=0),
     )
-
-    def from_outer(zz, place, target):
-        return place % 4 in (zz, (zz + 2) % 4)
-
-    row_grads = []
-    for value, keep_pair in ((g_out, None), (outer_grad, from_outer)):
-        for mask in range(4):
-            row_grads.append(lax.ppermute(value, ALL_AXES, flip_pairs(mask, keep_pair)) if mask else value)
-    row_grads = jnp.stack(row_grads)
-
-    group_of = np.array([0, 0, 0, 0, 1, 1, 1, 1, 1, 1, 2, 2, 2, 2, 0, 0, 0, 0], np.int32)
-    column_of = np.array([0, 1, 2, 0, 0, 1, 3, 2, 4, 0, 0, 1, 2, 3, 0, 0, 0, 0], np.int32)
-    group_at = jnp.sum(jnp.where(holds, group_of, 0), axis=2)
-    column_at = jnp.sum(jnp.where(holds, column_of, 0), axis=2)
-    column_at = jnp.where(group_at == 2, (column_at + f) % 4, column_at)
-    sent = pack_gradients(
-        [g_qkv, g_cross, g_in],
-        jnp.tile(group_at.reshape(-1), 2),
-        jnp.tile(column_at.reshape(-1), 2),
-        rows,
-        block,
-        cap,
-    )
-    col_grads = lax.all_to_all(sent, PLANE, 0, 0, tiled=True).reshape(8 * cap, rows, block)
-    place = np.arange(8)
-    col_source = (place % 2)[None, :] * 4 + ((place // 2)[None, :] - my_shift[:, None]) % 4
-    from_f = (z - my_shift) % 4
-    row_source = (from_f ^ f) + jnp.where(my_tile < 10, 4, 0)
+    outer_grads = to_owners(outer_grad, lambda zz, place, target: place % 4 in (zz, (zz + 2) % 4))
+    by_tile = jnp.swapaxes(g_qkv.reshape(2, rows, 3, block), 1, 2)
+    sent = jnp.broadcast_to(by_tile[:, None], (2, 4, 3, rows, block)).reshape(8, 3, rows, block)
+    late_grads = lax.all_to_all(sent, PLANE, 0, 0, tiled=True).reshape(8 * 3, rows, block)
+
+    n_late = 5
+    order = jnp.sum(jnp.where(slot[None, :] < slot[:, None], late.astype(jnp.int32)[None, :], 0), axis=1)
+    count_late = jnp.sum(late.astype(jnp.int32))
+    step = np.arange(n_late)
+    wanted = jnp.minimum(step, jnp.maximum(count_late - 1, 0))
+    here = late[None, :] & (order[None, :] == wanted[:, None])
+
+    def at_step(value):
+        return jnp.sum(jnp.where(here, value.astype(jnp.int32)[None, :], 0), axis=1)
+
+    hold = (step >= jnp.maximum(count_late, 1)).astype(jnp.int32)
+    tile = at_step(my_tile)
+    some = count_late > 0
+    visit = jnp.where(some, at_step(slot), 0)
+    first_mode = jnp.where(early_mode[0] == 3, 4, early_mode[0])
+    late_mode = jnp.where(at_step(my_row) == 1, 5, 3)
+    mode = jnp.where(hold == 1, 0, jnp.where(some, late_mode, first_mode))
+    late_place = (place % 2)[None, :] * 4 + (place // 2)[None, :]
+    column_place = jnp.where(some, late_place * 3 + tile[:, None], (source * cap + slot[:, None])[0][None, :])
     new_w, new_m, new_v = adam_tiles(
-        master,
-        moment_one,
-        moment_two,
-        col_grads,
-        row_grads,
-        my_used,
-        my_row,
-        col_source.reshape(-1),
-        row_source,
+        *states,
+        [early_grads, late_grads],
+        [out_grads, outer_grads],
+        visit,
+        mode,
+        column_place.reshape(-1),
+        jnp.where(some, at_step(row_source), row_source[0]),
+        hold,
+        early,
     )
     gain_grads = jnp.stack([gain_grad_zero, gain_grad_one, gain_grad_two])
     gain_total = lax.psum(gain_grads, ALL_AXES)

time: 1400 us -> 1190 us (0.85)
  waiting for transfers between devices: 715 us -> 472 us
  Pallas kernels: 81.7 us -> 104 us
  other arithmetic: 60.8 us -> 76.1 us
    ppermute x68, waiting for transfers between devices: 310 us -> 235 us  [swap(): return lax.ppermute(value, axis, [(0, 1), (1, 0)])]
    reduce_scatter x5, waiting for transfers between devices: 208 us -> 147 us  [sum_rows(): return lax.psum_scatter(value, 'z', scatter_dimension=0, tiled=True)]
    all_gather x1, waiting for transfers between devices: 70.8 us -> 13.2 us  [plane_body(): w_out = lax.all_gather(out_rows, 'z', axis=0, tiled=True)]
    all_gather x3, waiting for transfers between devices: 57.3 us -> 0.02 us  [gather_columns(): return lax.all_gather(local, 'z', axis=0, tiled=True)]
    ppermute x6, waiting for transfers between devices: 16.6 us -> 45.4 us  [take_rows(): got = lax.ppermute(got, ALL_AXES, flip_pairs(mask, keep_pair))]
    pallas_call x1 -> x2, Pallas kernels: 47.6 us -> 71.5 us  [adam_tiles(): pl.pallas_call(kernel, out_shape=(shape, shape, shape), grid_spec=pltpu.P...]
    unnamed x219 -> x237, local copies, waits for them, and re-layouts: 75.2 us -> 68.7 us
  transfers between devices with their start and end apart: 95 -> 96, of which waited for: 57 -> 59; matrix products, arithmetic and copies ran while one was open for 20% -> 27% of each run, Pallas kernels for 2% -> 6%
where the time goes in v2:
time: 1190 us; the launch traced here: 1180 us
  waiting for transfers between devices  472 us (40%)
  local copies, waits for them, and re-layouts  181 us (15%)
  matrix products  132 us (11%)
  starting transfers between devices  107 us (9%)
  Pallas kernels  104 us (9%)
  other arithmetic  76.1 us (6%)
  between operations  67.1 us (6%)
  blocking collectives  39.3 us (3%)
    ppermute x68, waiting for transfers between devices, swap(): return lax.ppermute(value, axis, [(0, 1), (1, 0)])  235 us
    reduce_scatter x5, waiting for transfers between devices, sum_rows(): return lax.psum_scatter(value, 'z', scatter_dimension=0, tiled=True)  147 us
    pallas_call x2, Pallas kernels, adam_tiles(): pl.pallas_call(kernel, out_shape=(shape, shape, shape), grid_spec=pltpu.P...  71.5 us
    unnamed x237, local copies, waits for them, and re-layouts  68.7 us
    ppermute x68, starting transfers between devices, swap(): return lax.ppermute(value, axis, [(0, 1), (1, 0)])  63.9 us
    dot_general x8, matrix products, matmul(): return jnp.dot(left, right, preferred_element_type=f32)  46.4 us
    ppermute x6, waiting for transfers between devices, take_rows(): got = lax.ppermute(got, ALL_AXES, flip_pairs(mask, keep_pair))  45.4 us
    dot_general x8, matrix products, matmul_left(): lax.dot_general(left, right, (((0,), (0,)), ((), ())), preferred_element_...  39.8 us
  transfers between devices with their start and end apart: 96, of which 59 were waited for; matrix products, arithmetic and copies ran while one was open for 27% of the time, Pallas kernels for 6%

profile of v2, /device:TPU:0, one launch (start us, length us, event | category | flops | bytes accessed | tf_op | source)
XLA Modules:
  0.0 1178.7 jit_solution(6281409443817421152)
XLA Ops:
  51.3 12.0 %all-to-all-done = bf16[8,3,256,256]{3,2,1,0:T(8,128)(2,1)S(1)} async-done(((bf16[8,3,256,256]{3,2,1,0:T(8,128)(2,1)}), bf16[8,3,256,256]{3,2,1,0:T(8,128)(2,1)S(1)}, u32[]{:S(2)}, u32[]{:S(2)}) %all-to-all-start) | async-done | bytes 3145760 | tf_op jit(solution)/shard_map/all_to_all | solution.py:317
  71.0 10.1 fusion.58
  100.0 14.4 %collective-permute-done.3 = bf16[64,2048]{1,0:T(8,128)(2,1)S(1)} collective-permute-done((bf16[64,2048]{1,0:T(8,128)(2,1)S(1)}, bf16[64,2048]{1,0:T(8,128)(2,1)S(1)}, u32[]{:S(2)}, u32[]{:S(2)}) %collective-permute-start.3) | collective-permute-done | bytes 262176 | tf_op jit(solution)/shard_map/ppermute | solution.py:240
  223.4 16.5 %collective-permute-done.17 = bf16[256,4096]{1,0:T(8,128)(2,1)} collective-permute-done((bf16[256,4096]{1,0:T(8,128)(2,1)}, bf16[256,4096]{1,0:T(8,128)(2,1)}, u32[]{:S(2)}, u32[]{:S(2)}) %collective-permute-start.17) | collective-permute-done | bytes 2097184 | tf_op jit(solution)/shard_map/ppermute | solution.py:240
  251.1 13.9 %collective-permute-done.19 = bf16[128,4096]{1,0:T(8,128)(2,1)S(1)} collective-permute-done((bf16[128,4096]{1,0:T(8,128)(2,1)S(1)}, bf16[128,4096]{1,0:T(8,128)(2,1)S(1)}, u32[]{:S(2)}, u32[]{:S(2)}) %collective-permute-start.19) | collective-permute-done | bytes 1048608 | tf_op jit(solution)/shard_map/ppermute | solution.py:240
  353.1 9.7 fusion.4
  386.9 22.6 %collective-permute-done.37 = bf16[256,2048]{1,0:T(8,128)(2,1)} collective-permute-done((bf16[256,2048]{1,0:T(8,128)(2,1)}, bf16[256,2048]{1,0:T(8,128)(2,1)}, u32[]{:S(2)}, u32[]{:S(2)}) %collective-permute-start.37) | collective-permute-done | bytes 1048608 | tf_op jit(solution)/shard_map/ppermute | solution.py:361
  409.6 22.8 %collective-permute-done.38 = bf16[256,2048]{1,0:T(8,128)(2,1)} collective-permute-done((bf16[256,2048]{1,0:T(8,128)(2,1)}, bf16[256,2048]{1,0:T(8,128)(2,1)}, u32[]{:S(2)}, u32[]{:S(2)}) %collective-permute-start.38) | collective-permute-done | bytes 1048608 | tf_op jit(solution)/shard_map/ppermute | solution.py:361
  475.8 10.2 collective-permute-done.32
  515.8 13.2 %all-gather.14.cloned.1.call-done = bf16[1024,2048]{1,0:T(8,128)(2,1)} async-done(((bf16[256,2048]{1,0:T(8,128)(2,1)}), bf16[1024,2048]{1,0:T(8,128)(2,1)}) %all-gather.14.cloned.1.call-update) | async-done | bytes 4194320 | tf_op jit(solution)/shard_map/all_gather | solution.py:395
  529.0 11.4 fusion.13
  618.3 10.3 collective-permute-done.55
  703.9 11.8 collective-permute-done.61
  729.1 9.4 collective-permute-done.65
  782.3 28.6 %reduce-scatter.6.cloned.1.call-done.refs_0_ = bf16[512,1280]{1,0:T(8,128)(2,1)} async-done(((bf16[2048,1280]{1,0:T(8,128)(2,1)}), bf16[512,1280]{1,0:T(8,128)(2,1)}) %reduce-scatter.6.cloned.1.call-update) | async-done | bytes 1310736 | tf_op jit(solution)/shard_map/reduce_scatter | solution.py:455
  813.4 17.0 %pack_gradients.1 = bf16[8,6,256,256]{3,2,1,0:T(8,128)(2,1)} custom-call(s32[48]{0:T(128)S(1)} %tile.20.which_ref, s32[48]{0:T(128)S(1)} %tile.22.column_ref, bf16[512,1280]{1,0:T(8,128)(2,1)S(1)} %copy-done.6, bf16[512,1024]{1,0:T(8,128)(2,1)S(1)} %copy-done.7), custom_call_target="tpu_custom_call" | custom-call | tf_op jit(solution)/shard_map/pack_gradients/pallas_call | solution.py:152
  839.5 51.1 %reduce-scatter.12.cloned.1.call-done = bf16[256,2048]{1,0:T(8,128)(2,1)} async-done(((bf16[1024,2048]{1,0:T(8,128)(2,1)}), bf16[256,2048]{1,0:T(8,128)(2,1)}) %reduce-scatter.12.cloned.1.call-update) | async-done | bytes 1048592 | tf_op jit(solution)/shard_map/reduce_scatter | solution.py:455
  901.1 36.2 %reduce-scatter.14.cloned.1.call-done = bf16[128,2048]{1,0:T(8,128)(2,1)} async-done(((bf16[512,2048]{1,0:T(8,128)(2,1)}), bf16[128,2048]{1,0:T(8,128)(2,1)}) %reduce-scatter.14.cloned.1.call-update) | async-done | bytes 524304 | tf_op jit(solution)/shard_map/reduce_scatter | solution.py:455
  941.4 9.7 collective-permute-done.76
  968.8 31.6 %reduce-scatter.10.cloned.1.call-done = bf16[512,768]{1,0:T(8,128)(2,1)} async-done(((bf16[2048,768]{1,0:T(8,128)(2,1)}), bf16[512,768]{1,0:T(8,128)(2,1)}) %reduce-scatter.10.cloned.1.call-update) | async-done | bytes 786448 | tf_op jit(solution)/shard_map/reduce_scatter | solution.py:455
  1015.6 35.1 %collective-permute-done.72 = bf16[128,1024]{1,0:T(8,128)(2,1)S(1)} collective-permute-done((bf16[128,1024]{1,0:T(8,128)(2,1)S(1)}, bf16[128,1024]{1,0:T(8,128)(2,1)S(1)}, u32[]{:S(2)}, u32[]{:S(2)}) %collective-permute-start.72) | collective-permute-done | bytes 262176 | tf_op jit(solution)/shard_map/ppermute | solution.py:240
  1051.7 39.3 %psum.7 = f32[3,2048]{1,0:T(4,128)S(1)} all-reduce(f32[3,2048]{1,0:T(4,128)S(1)} %pad_maximum_fusion.7), channel_id=1, replica_groups=mesh['z'=4,'x'=2,'y'=2,'c'=2] {'z','x','y','c'}, use_global_device_ids=true, to_apply=%region_55.56 | all-reduce | flops 6144 | bytes 49152 | tf_op jit(solution)/shard_map/psum | solution.py:587
  1100.1 45.0 %adam_tiles.2 = (f32[6,256,2048]{2,1,0:T(8,128)}, f32[6,256,2048]{2,1,0:T(8,128)}, f32[6,256,2048]{2,1,0:T(8,128)}) custom-call(s32[6]{0:T(128)S(1)} %call_exported.1.visit_ref, s32[6]{0:T(128)S(1)} %get-tuple-element.91.mode_ref, s32[48]{0:T(128)S(1)} %multiply_add_fusion.4.cp_ref, s32[6]{0:T(128)S(1)} %fusion.171.rp_ref, s32[6]{0:T(128)S(1)} %broadcast.444.hold_ref, ...), custom_call_target="tpu_custom_call" | custom-call | tf_op jit(solution)/shard_map/adam_tiles/pallas_call | solution.py:213
  1145.1 26.5 %adam_tiles.3 = (f32[6,256,2048]{2,1,0:T(8,128)}, f32[6,256,2048]{2,1,0:T(8,128)}, f32[6,256,2048]{2,1,0:T(8,128)}) custom-call(s32[5]{0:T(128)S(1)} %get-tuple-element.259.visit_ref, s32[5]{0:T(128)S(1)} %get-tuple-element.258.mode_ref, s32[40]{0:T(128)S(1)} %select_n.604.cp_ref, ...), custom_call_target="tpu_custom_call", output_to_operand_aliasing={{0}: (12, {}), {1}: (13, {}), {2}: (14, {})} | custom-call | tf_op jit(solution)/shard_map/adam_tiles/pallas_call | solution.py:213
  (674 shorter events, 603.3 us)
Async XLA Ops:
  26.3 130.1 %all-gather.6.cloned.1.call-start = ((), (), s32[]{:S(2)}) async-start(), calls=%async_computation.9 | async-start | bytes 3932160 | tf_op jit(solution)/shard_map/all_gather | solution.py:340
  65.0 118.0 %all-gather.8.cloned.1.call-start = ((), (), s32[]{:S(2)}) async-start(), calls=%async_computation.10 | async-start | bytes 2621440 | tf_op jit(solution)/shard_map/all_gather | solution.py:384
  155.5 184.3 %all-gather.10.cloned.1.call-start = ((), (), s32[]{:S(2)}) async-start(), calls=%async_computation.11 | async-start | bytes 6553600 | tf_op jit(solution)/shard_map/all_gather | solution.py:340
  193.9 48.0 %collective-permute-start.18 = (bf16[256,4096]{1,0:T(8,128)(2,1)}, bf16[256,4096]{1,0:T(8,128)(2,1)}, u32[]{:S(2)}, u32[]{:S(2)}) collective-permute-start(bf16[256,4096]{1,0:T(8,128)(2,1)} %bitcast.426), channel_id=1, source_target_pairs={{0,4},{4,0},{1,5},{5,1},{2,6},{6,2},{3,7},{7,3},{8,12},{12,8},{9,1... | collective-permute-start | bytes 6291464 | tf_op jit(solution)/shard_map/ppermute | solution.py:240
  203.0 64.6 %collective-permute-start.12 = (f32[2,2,128,2048]{3,2,0,1:T(8,128)}, f32[2,2,128,2048]{3,2,0,1:T(8,128)}, u32[]{:S(2)}, u32[]{:S(2)}) collective-permute-start(f32[2,2,128,2048]{3,2,0,1:T(8,128)} %copy.145), channel_id=1, source_target_pairs={{0,1},{1,0},{2,3},{3,2},{4,5},{5,4},{6,7},{7,6},{8,9},{9,8},{10,11... | collective-permute-start | bytes 12582920 | tf_op jit(solution)/shard_map/ppermute | solution.py:240
  220.0 279.5 %all-gather.12.cloned.1.call-start = ((), (), s32[]{:S(2)}) async-start(), calls=%async_computation.12 | async-start | bytes 5242880 | tf_op jit(solution)/shard_map/all_gather | solution.py:340
  267.6 76.8 %collective-permute-start.21 = (bf16[1024,4096]{1,0:T(8,128)(2,1)}, bf16[1024,4096]{1,0:T(8,128)(2,1)}, u32[]{:S(2)}, u32[]{:S(2)}) collective-permute-start(bf16[1024,4096]{1,0:T(8,128)(2,1)} %get-tuple-element.151), channel_id=1, source_target_pairs={{0,1},{1,0},{2,3},{3,2},{4,5},{5,4},{6,7},{7,6},{8,9},{9,8},{10,11... | collective-permute-start | bytes 25165832 | tf_op jit(solution)/shard_map/ppermute | solution.py:240
  336.6 192.5 %all-gather.14.cloned.1.call-start = ((), (), s32[]{:S(2)}) async-start(), calls=%async_computation.13 | async-start | bytes 5242880 | tf_op jit(solution)/shard_map/all_gather | solution.py:395
  383.6 54.0 %collective-permute-start.27 = (f32[2,2,128,2048]{3,2,0,1:T(8,128)}, f32[2,2,128,2048]{3,2,0,1:T(8,128)}, u32[]{:S(2)}, u32[]{:S(2)}) collective-permute-start(f32[2,2,128,2048]{3,2,0,1:T(8,128)} %copy.152), channel_id=1, source_target_pairs={{0,1},{1,0},{2,3},{3,2},{4,5},{5,4},{6,7},{7,6},{8,9},{9,8},{10,11... | collective-permute-start | bytes 12582920 | tf_op jit(solution)/shard_map/ppermute | solution.py:240
  446.1 336.2 %reduce-scatter.8.cloned.1.call-start = ((), (), s32[]{:S(2)}) async-start(), calls=%async_computation.15 | async-start | bytes 5242880 | tf_op jit(solution)/shard_map/reduce_scatter | solution.py:455
  639.3 171.6 %reduce-scatter.6.cloned.1.call-start = ((), (), s32[]{:S(2)}) async-start(), calls=%async_computation.14 | async-start | bytes 6553600 | tf_op jit(solution)/shard_map/reduce_scatter | solution.py:455
  681.7 208.9 %reduce-scatter.12.cloned.1.call-start = ((), (), s32[]{:S(2)}) async-start(), calls=%async_computation.17 | async-start | bytes 5242880 | tf_op jit(solution)/shard_map/reduce_scatter | solution.py:455
  689.9 247.4 %reduce-scatter.14.cloned.1.call-start = ((), (), s32[]{:S(2)}) async-start(), calls=%async_computation.18 | async-start | bytes 2621440 | tf_op jit(solution)/shard_map/reduce_scatter | solution.py:455
  759.9 240.4 %reduce-scatter.10.cloned.1.call-start = ((), (), s32[]{:S(2)}) async-start(), calls=%async_computation.16 | async-start | bytes 3932160 | tf_op jit(solution)/shard_map/reduce_scatter | solution.py:455
  775.4 117.0 %collective-permute-start.70 = (f32[2,2,128,2048]{3,2,0,1:T(8,128)}, f32[2,2,128,2048]{3,2,0,1:T(8,128)}, u32[]{:S(2)}, u32[]{:S(2)}) collective-permute-start(f32[2,2,128,2048]{3,2,0,1:T(8,128)} %copy.189), channel_id=1, source_target_pairs={{0,1},{1,0},{2,3},{3,2},{4,5},{5,4},{6,7},{7,6},{8,9},{9,8},{10,11... | collective-permute-start | bytes 12582920 | tf_op jit(solution)/shard_map/ppermute | solution.py:240
  830.4 172.1 %all-to-all-start.2 = ((bf16[8,6,256,256]{3,2,1,0:T(8,128)(2,1)}), bf16[8,6,256,256]{3,2,1,0:T(8,128)(2,1)}, u32[]{:S(2)}, u32[]{:S(2)}) async-start(bf16[8,6,256,256]{3,2,1,0:T(8,128)(2,1)} %pack_gradients.1), calls=%async_computation.4 | async-start | bytes 12582912 | tf_op jit(solution)/shard_map/all_to_all | solution.py:525
  890.6 49.3 %collective-permute-start.77 = (bf16[256,2048]{1,0:T(8,128)(2,1)}, bf16[256,2048]{1,0:T(8,128)(2,1)S(1)}, u32[]{:S(2)}, u32[]{:S(2)}) collective-permute-start(bf16[256,2048]{1,0:T(8,128)(2,1)} %reduce-scatter.12.cloned.1.call-done), channel_id=1, source_target_pairs={{0,3},{1,2},{2,1},{3,0},{4,7},{5,6},{6,5},{7,4},{8,11},{9,10},{10,... | collective-permute-start | bytes 3145736 | tf_op jit(solution)/shard_map/ppermute | solution.py:508
  891.5 59.6 %collective-permute-start.76 = (bf16[256,2048]{1,0:T(8,128)(2,1)}, bf16[256,2048]{1,0:T(8,128)(2,1)S(1)}, u32[]{:S(2)}, u32[]{:S(2)}) collective-permute-start(bf16[256,2048]{1,0:T(8,128)(2,1)} %reduce-scatter.12.cloned.1.call-done), channel_id=1, source_target_pairs={{0,2},{1,3},{2,0},{3,1},{4,6},{5,7},{6,4},{7,5},{8,10},{9,11},{10,... | collective-permute-start | bytes 3145736 | tf_op jit(solution)/shard_map/ppermute | solution.py:508
  892.1 59.1 %collective-permute-start.75 = (bf16[256,2048]{1,0:T(8,128)(2,1)}, bf16[256,2048]{1,0:T(8,128)(2,1)}, u32[]{:S(2)}, u32[]{:S(2)}) collective-permute-start(bf16[256,2048]{1,0:T(8,128)(2,1)} %reduce-scatter.12.cloned.1.call-done), channel_id=1, source_target_pairs={{0,1},{1,0},{2,3},{3,2},{4,5},{5,4},{6,7},{7,6},{8,9},{9,8},{10,11... | collective-permute-start | bytes 3145736 | tf_op jit(solution)/shard_map/ppermute | solution.py:508
  899.6 64.5 %collective-permute-start.71 = (bf16[2,128,1024]{2,1,0:T(8,128)(2,1)}, bf16[2,128,1024]{2,1,0:T(8,128)(2,1)}, u32[]{:S(2)}, u32[]{:S(2)}) collective-permute-start(bf16[2,128,1024]{2,1,0:T(8,128)(2,1)} %slice_bitcast_fusion.15), channel_id=1, source_target_pairs={{0,2},{2,0},{1,3},{3,1},{4,6},{6,4},{5,7},{7,5},{8,10},{10,8},{9,1... | collective-permute-start | bytes 1572872 | tf_op jit(solution)/shard_map/ppermute | solution.py:240
  955.9 139.3 %collective-permute-start.81 = (bf16[256,2048]{1,0:T(8,128)(2,1)}, bf16[256,2048]{1,0:T(8,128)(2,1)}, u32[]{:S(2)}, u32[]{:S(2)}) collective-permute-start(bf16[256,2048]{1,0:T(8,128)(2,1)} %maximum_select_fusion.1), channel_id=1, source_target_pairs={{0,3},{2,1},{4,7},{6,5},{9,10},{11,8},{13,14},{15,12},{16,19},{18,... | collective-permute-start | bytes 3145736 | tf_op jit(solution)/shard_map/ppermute | solution.py:508
  958.5 136.7 %collective-permute-start.80 = (bf16[256,2048]{1,0:T(8,128)(2,1)}, bf16[256,2048]{1,0:T(8,128)(2,1)}, u32[]{:S(2)}, u32[]{:S(2)}) collective-permute-start(bf16[256,2048]{1,0:T(8,128)(2,1)} %maximum_select_fusion.1), channel_id=1, source_target_pairs={{0,2},{2,0},{4,6},{6,4},{9,11},{11,9},{13,15},{15,13},{16,18},{18,... | collective-permute-start | bytes 3145736 | tf_op jit(solution)/shard_map/ppermute | solution.py:508
  961.9 133.4 %collective-permute-start.79 = (bf16[256,2048]{1,0:T(8,128)(2,1)}, bf16[256,2048]{1,0:T(8,128)(2,1)}, u32[]{:S(2)}, u32[]{:S(2)}) collective-permute-start(bf16[256,2048]{1,0:T(8,128)(2,1)} %maximum_select_fusion.1), channel_id=1, source_target_pairs={{0,1},{2,3},{4,5},{6,7},{9,8},{11,10},{13,12},{15,14},{16,17},{18,... | collective-permute-start | bytes 3145736 | tf_op jit(solution)/shard_map/ppermute | solution.py:508
  1004.6 140.5 %all-to-all-start.3 = ((bf16[8,3,256,256]{3,2,1,0:T(8,128)(2,1)}), bf16[8,3,256,256]{3,2,1,0:T(8,128)(2,1)S(1)}, u32[]{:S(2)}, u32[]{:S(2)}) async-start(bf16[8,3,256,256]{3,2,1,0:T(8,128)(2,1)} %bitcast.417), calls=%async_computation.6 | async-start | bytes 6291456 | tf_op jit(solution)/shard_map/all_to_all | solution.py:554
  (174 other events, 2753.0 us)
Sparse Core Ops, SparseCore 0:
  65.1 63.7 all-gather.5
  132.9 47.7 all-gather.7
  220.1 99.4 all-gather.9
  336.7 82.8 all-gather.11
  446.2 82.7 all-gather.13
  639.4 74.0 reduce-scatter.7
  716.6 94.2 reduce-scatter.5
  813.3 77.2 reduce-scatter.11
  892.9 44.3 reduce-scatter.13
  939.6 60.7 reduce-scatter.9

commit v3 on v2

--- a/solution.py
+++ b/solution.py
@@ -318,6 +318,7 @@
         return got.reshape(8 * half_cap, rows, block)
 
     received = [exchange_columns(0, master)]
+    received.append(exchange_columns(half_cap, after(master, received[0])))
 
     def source_of(tile):
         if isinstance(tile, int):
@@ -347,7 +348,7 @@
         return lax.dynamic_index_in_dim(master, slot, 0, keepdims=False).astype(bf16)
 
     h0 = tokens.astype(f32)
-    a_all = gather_rows(after(normalize(h0, gains[0]).astype(bf16), received[0]))
+    a_all = gather_rows(after(normalize(h0, gains[0]).astype(bf16), received[1]))
 
     def owner_of(tile):
         return jnp.sum(jnp.where(jnp.arange(n_tiles) == tile, owners, 0))
@@ -386,11 +387,10 @@
     w_self_out = jnp.where(low_y, outer_all[:rows], outer_all[rows:])
     w_cross_out = jnp.where(low_y, outer_all[rows:], outer_all[:rows])
 
-    received.append(exchange_columns(half_cap, after(master, a_all, from_pair)))
     w_cross = gather_columns([4, 5, 7, 6, 8], 2)
     w_in = gather_columns([10 + (place - f) % 4 for place in range(4)], 2)
     slots, ctx_len, ctx_width = context.shape
-    ctx_all = gather_rows(after(context.reshape(slots * ctx_len, ctx_width), received[1]))
+    ctx_all = gather_rows(after(context.reshape(slots * ctx_len, ctx_width), a_all))
     out_rows = take_rows(lambda place: 14 + (z - place) % 4, None, ctx_all)
     w_out = lax.all_gather(out_rows, "z", axis=0, tiled=True)
 
@@ -431,7 +431,7 @@
     probs_low = probs.astype(bf16)
     attended = joined(weighted(probs_low, values))
     h1 = h0 + scatter_rows(matmul(attended, w_self_out))
-    b_all = gather_rows(normalize(h1, gains[1]).astype(bf16))
+    b_all = gather_rows(after(normalize(h1, gains[1]).astype(bf16), w_cross))
 
     w_cross_q = w_cross[:, :block]
     w_low = w_cross[:, block : 3 * block]
@@ -445,25 +445,30 @@
     cross_p = probabilities(cross_q, cross_k, own_item)
     cross_low = cross_p.astype(bf16)
     cross_o = joined(weighted(cross_low, cross_v))
-    h2 = h1 + scatter_rows(matmul(cross_o, w_cross_out))
+    h2 = h1 + scatter_rows(matmul(after(cross_o, w_in), w_cross_out))
     c_all = gather_rows(normalize(h2, gains[2]).astype(bf16))
 
-    hidden = matmul(c_all, w_in)
+    hidden = matmul(after(c_all, w_out), w_in)
     activated = gelu_tanh(hidden).astype(bf16)
 
     def sum_rows(value):
         return lax.psum_scatter(value, "z", scatter_dimension=0, tiled=True)
 
+    def to_owners(value, keep_pair):
+        moved = [lax.ppermute(value, ALL_AXES, flip_pairs(mask, keep_pair)) for mask in range(1, 4)]
+        return jnp.stack([value, *moved])
+
     t_out = matmul_left(activated, d_ff).astype(bf16)
     g_out = sum_rows(t_out)
-    d_act = matmul_right(d_ff, after(w_out, t_out))
+    d_act = matmul_right(after(d_ff, t_out), w_out)
     layer_out = (h2 + scatter_rows(matmul(activated, w_out))).astype(bf16)
     d_hidden = jax.vjp(gelu_tanh, hidden)[1](d_act)[0].astype(bf16)
     t_in = matmul_left(c_all, d_hidden).astype(bf16)
     g_in = sum_rows(t_in)
     part_two, gain_grad_two = jax.vjp(normalize, h2, gains[2])[1](scatter_rows(matmul_right(d_hidden, w_in)))
     dh2 = grad_out + part_two
-    d_cross_out = gather_rows(after(dh2.astype(bf16), t_in))
+    d_cross_out = gather_rows(after(dh2.astype(bf16), t_in, g_out))
+    out_grads = to_owners(g_out, None)
     g_cross_out = matmul_left(cross_o, d_cross_out)
 
     def through(weights, d_out, left, right, probs, probs_low, values):
@@ -487,7 +492,7 @@
     g_cross = sum_rows(t_cross)
     part_one, gain_grad_one = jax.vjp(normalize, h1, gains[1])[1](scatter_rows(matmul_right(d_cq, w_cross_q)))
     dh1 = dh2 + part_one
-    d_self_out = gather_rows(after(dh1.astype(bf16), t_cross))
+    d_self_out = gather_rows(after(dh1.astype(bf16), t_cross, g_in, out_grads))
     g_self_out = matmul_left(attended, d_self_out)
     g_outer = sum_rows(
         jnp.concatenate(
@@ -504,11 +509,8 @@
     part_zero, gain_grad_zero = jax.vjp(normalize, h0, gains[0])[1](scatter_rows(matmul_right(d_qkv, w_qkv)))
     grad_tokens = (dh1 + part_zero).astype(bf16)
 
-    def to_owners(value, keep_pair):
-        moved = [lax.ppermute(value, ALL_AXES, flip_pairs(mask, keep_pair)) for mask in range(1, 4)]
-        return jnp.stack([value, *moved])
-
-    out_grads = to_owners(g_out, None)
+    gain_total = lax.psum(jnp.stack([gain_grad_zero, gain_grad_one, gain_grad_two]), ALL_AXES)
+
     group_of = np.array([0, 0, 0, 0, 0, 0, 0, 0, 0, 0, 1, 1, 1, 1, 0, 0, 0, 0], np.int32)
     column_of = np.array([0, 0, 0, 0, 0, 1, 3, 2, 4, 0, 0, 1, 2, 3, 0, 0, 0, 0], np.int32)
     group_at = jnp.sum(jnp.where(holds, group_of, 0), axis=2)
@@ -535,7 +537,7 @@
         [early_grads],
         [out_grads],
         slot,
-        early_mode,
+        after(early_mode, gain_total),
         (source * cap + slot[:, None]).reshape(-1),
         row_source,
         np.zeros(cap, np.int32),
@@ -548,7 +550,7 @@
         jnp.concatenate([g_outer, other_half], axis=0),
         jnp.concatenate([other_half, g_outer], axis=0),
     )
-    outer_grads = to_owners(outer_grad, lambda zz, place, target: place % 4 in (zz, (zz + 2) % 4))
+    outer_grads = to_owners(after(outer_grad, early_grads), lambda zz, place, target: place % 4 in (zz, (zz + 2) % 4))
     by_tile = jnp.swapaxes(g_qkv.reshape(2, rows, 3, block), 1, 2)
     sent = jnp.broadcast_to(by_tile[:, None], (2, 4, 3, rows, block)).reshape(8, 3, rows, block)
     late_grads = lax.all_to_all(sent, PLANE, 0, 0, tiled=True).reshape(8 * 3, rows, block)
@@ -583,8 +585,6 @@
         hold,
         early,
     )
-    gain_grads = jnp.stack([gain_grad_zero, gain_grad_one, gain_grad_two])
-    gain_total = lax.psum(gain_grads, ALL_AXES)
     new_g, new_gm, new_gv = adam_update(gains, gain_one, gain_two, gain_total, rate_gain, 0.0)
     return (layer_out, grad_tokens, new_w, new_m, new_v, new_g, new_gm, new_gv)
 

time: 1190 us -> 1260 us (1.059)
  waiting for transfers between devices: 472 us -> 541 us
  local copies, waits for them, and re-layouts: 181 us -> 168 us
    reduce_scatter x5, waiting for transfers between devices: 147 us -> 29.4 us  [sum_rows(): return lax.psum_scatter(value, 'z', scatter_dimension=0, tiled=True)]
    all_gather x3, waiting for transfers between devices: 0.02 us -> 67.8 us  [gather_columns(): return lax.all_gather(local, 'z', axis=0, tiled=True)]
    ppermute x6, waiting for transfers between devices: 9.73 us -> 42 us  [to_owners(): lax.ppermute(value, ALL_AXES, flip_pairs(mask, keep_pair))]
    ppermute x68, waiting for transfers between devices: 235 us -> 264 us  [swap(): return lax.ppermute(value, axis, [(0, 1), (1, 0)])]
    all_to_all x2, waiting for transfers between devices: 15 us -> 36.9 us  [exchange_columns(): lax.all_to_all(pack_columns(weights, table, first, half_cap), PLANE, 0, 0...]
    ppermute x6, waiting for transfers between devices: 45.4 us -> 63.7 us  [take_rows(): got = lax.ppermute(got, ALL_AXES, flip_pairs(mask, keep_pair))]
    all_gather x1, waiting for transfers between devices: 13.2 us -> 26.7 us  [plane_body(): w_out = lax.all_gather(out_rows, 'z', axis=0, tiled=True)]
    unnamed x237 -> x234, local copies, waits for them, and re-layouts: 68.7 us -> 65.2 us
  transfers between devices with their start and end apart: 96 -> 96, of which waited for: 59 -> 61; matrix products, arithmetic and copies ran while one was open for 27% -> 23% of each run, Pallas kernels for 6% -> 6%
where the time goes in v3:
time: 1260 us; the launch traced here: 1250 us
  waiting for transfers between devices  541 us (43%)
  local copies, waits for them, and re-layouts  168 us (13%)
  matrix products  133 us (11%)
  starting transfers between devices  115 us (9%)
  Pallas kernels  96 us (8%)
  other arithmetic  73.9 us (6%)
  between operations  66.6 us (5%)
  blocking collectives  51.6 us (4%)
    ppermute x68, waiting for transfers between devices, swap(): return lax.ppermute(value, axis, [(0, 1), (1, 0)])  264 us
    ppermute x68, starting transfers between devices, swap(): return lax.ppermute(value, axis, [(0, 1), (1, 0)])  69.1 us
    all_gather x3, waiting for transfers between devices, gather_columns(): return lax.all_gather(local, 'z', axis=0, tiled=True)  67.8 us
    unnamed x234, local copies, waits for them, and re-layouts  65.2 us
    ppermute x6, waiting for transfers between devices, take_rows(): got = lax.ppermute(got, ALL_AXES, flip_pairs(mask, keep_pair))  63.7 us
    pallas_call x2, Pallas kernels, adam_tiles(): pl.pallas_call(kernel, out_shape=(shape, shape, shape), grid_spec=pltpu.P...  63 us
    psum x1, blocking collectives, plane_body(): lax.psum(jnp.stack([gain_grad_zero, gain_grad_one, gain_grad_two]), ALL_A...  51.6 us
    dot_general x8, matrix products, matmul(): return jnp.dot(left, right, preferred_element_type=f32)  45.1 us
  transfers between devices with their start and end apart: 96, of which 61 were waited for; matrix products, arithmetic and copies ran while one was open for 23% of the time, Pallas kernels for 6%

profile of v3, /device:TPU:0, one launch (start us, length us, event | category | flops | bytes accessed | tf_op | source)
XLA Modules:
  0.0 1245.8 jit_solution(7403007784518872390)
XLA Ops:
  26.2 36.9 %all-to-all-done = bf16[8,3,256,256]{3,2,1,0:T(8,128)(2,1)S(1)} async-done(((bf16[8,3,256,256]{3,2,1,0:T(8,128)(2,1)}), bf16[8,3,256,256]{3,2,1,0:T(8,128)(2,1)S(1)}, u32[]{:S(2)}, u32[]{:S(2)}) %all-to-all-start) | async-done | bytes 3145760 | tf_op jit(solution)/shard_map/all_to_all | solution.py:317
  101.4 9.8 fusion.58
  122.2 14.6 %collective-permute-done.8 = bf16[256,2048]{1,0:T(8,128)(2,1)} collective-permute-done((bf16[256,2048]{1,0:T(8,128)(2,1)}, bf16[256,2048]{1,0:T(8,128)(2,1)}, u32[]{:S(2)}, u32[]{:S(2)}) %collective-permute-start.8) | collective-permute-done | bytes 1048608 | tf_op jit(solution)/shard_map/ppermute | solution.py:362
  264.5 14.5 %collective-permute-done.19 = bf16[128,4096]{1,0:T(8,128)(2,1)S(1)} collective-permute-done((bf16[128,4096]{1,0:T(8,128)(2,1)S(1)}, bf16[128,4096]{1,0:T(8,128)(2,1)S(1)}, u32[]{:S(2)}, u32[]{:S(2)}) %collective-permute-start.19) | collective-permute-done | bytes 1048608 | tf_op jit(solution)/shard_map/ppermute | solution.py:240
  293.8 11.3 collective-permute-done.13
  316.2 29.5 %all-gather.10.cloned.1.call-done = bf16[2048,1280]{1,0:T(8,128)(2,1)} async-done(((bf16[512,1280]{1,0:T(8,128)(2,1)}), bf16[2048,1280]{1,0:T(8,128)(2,1)}) %all-gather.10.cloned.1.call-update) | async-done | bytes 5242896 | tf_op jit(solution)/shard_map/all_gather | solution.py:341
  403.5 9.7 fusion.4
  426.7 38.3 %all-gather.12.cloned.1.call-done = bf16[2048,1024]{1,0:T(8,128)(2,1)} async-done(((bf16[512,1024]{1,0:T(8,128)(2,1)}), bf16[2048,1024]{1,0:T(8,128)(2,1)}) %all-gather.12.cloned.1.call-update) | async-done | bytes 4194320 | tf_op jit(solution)/shard_map/all_gather | solution.py:341
  476.0 22.4 %collective-permute-done.37 = bf16[256,2048]{1,0:T(8,128)(2,1)} collective-permute-done((bf16[256,2048]{1,0:T(8,128)(2,1)}, bf16[256,2048]{1,0:T(8,128)(2,1)}, u32[]{:S(2)}, u32[]{:S(2)}) %collective-permute-start.37) | collective-permute-done | bytes 1048608 | tf_op jit(solution)/shard_map/ppermute | solution.py:362
  498.5 22.8 %collective-permute-done.38 = bf16[256,2048]{1,0:T(8,128)(2,1)} collective-permute-done((bf16[256,2048]{1,0:T(8,128)(2,1)}, bf16[256,2048]{1,0:T(8,128)(2,1)}, u32[]{:S(2)}, u32[]{:S(2)}) %collective-permute-start.38) | collective-permute-done | bytes 1048608 | tf_op jit(solution)/shard_map/ppermute | solution.py:362
  587.8 26.7 %all-gather.14.cloned.1.call-done = bf16[1024,2048]{1,0:T(8,128)(2,1)} async-done(((bf16[256,2048]{1,0:T(8,128)(2,1)}), bf16[1024,2048]{1,0:T(8,128)(2,1)}) %all-gather.14.cloned.1.call-update) | async-done | bytes 4194320 | tf_op jit(solution)/shard_map/all_gather | solution.py:395
  630.9 11.4 fusion.13
  664.8 9.5 convolution_convert_fusion
  718.6 21.6 %reduce-scatter.6.cloned.1.call-done = bf16[256,2048]{1,0:T(8,128)(2,1)} async-done(((bf16[1024,2048]{1,0:T(8,128)(2,1)}), bf16[256,2048]{1,0:T(8,128)(2,1)}) %reduce-scatter.6.cloned.1.call-update) | async-done | bytes 1048592 | tf_op jit(solution)/shard_map/reduce_scatter | solution.py:455
  824.2 10.5 collective-permute-done.61
  837.6 18.4 %collective-permute-done.67 = bf16[256,2048]{1,0:T(8,128)(2,1)S(1)} collective-permute-done((bf16[256,2048]{1,0:T(8,128)(2,1)S(1)}, bf16[256,2048]{1,0:T(8,128)(2,1)S(1)}, u32[]{:S(2)}, u32[]{:S(2)}) %collective-permute-start.67) | collective-permute-done | bytes 1048608 | tf_op jit(solution)/shard_map/ppermute | solution.py:458
  856.0 23.6 %collective-permute-done.66 = bf16[256,2048]{1,0:T(8,128)(2,1)S(1)} collective-permute-done((bf16[256,2048]{1,0:T(8,128)(2,1)S(1)}, bf16[256,2048]{1,0:T(8,128)(2,1)S(1)}, u32[]{:S(2)}, u32[]{:S(2)}) %collective-permute-start.66) | collective-permute-done | bytes 1048608 | tf_op jit(solution)/shard_map/ppermute | solution.py:458
  888.7 10.7 collective-permute-done.68
  944.5 17.0 %pack_gradients.1 = bf16[8,6,256,256]{3,2,1,0:T(8,128)(2,1)} custom-call(s32[48]{0:T(128)S(1)} %tile.20.which_ref, s32[48]{0:T(128)S(1)} %tile.22.column_ref, bf16[512,1280]{1,0:T(8,128)(2,1)S(1)} %copy-done.6, bf16[512,1024]{1,0:T(8,128)(2,1)S(1)} %copy-done.7), custom_call_target="tpu_custom_call" | custom-call | tf_op jit(solution)/shard_map/pack_gradients/pallas_call | solution.py:152
  987.9 60.2 %collective-permute-done.74 = bf16[2,128,1024]{2,1,0:T(8,128)(2,1)S(1)} collective-permute-done((bf16[2,128,1024]{2,1,0:T(8,128)(2,1)S(1)}, bf16[2,128,1024]{2,1,0:T(8,128)(2,1)S(1)}, u32[]{:S(2)}, u32[]{:S(2)}) %collective-permute-start.74) | collective-permute-done | bytes 524320 | tf_op jit(solution)/shard_map/ppermute | solution.py:240
  1069.4 35.2 %collective-permute-done.75 = bf16[128,1024]{1,0:T(8,128)(2,1)S(1)} collective-permute-done((bf16[128,1024]{1,0:T(8,128)(2,1)S(1)}, bf16[128,1024]{1,0:T(8,128)(2,1)S(1)}, u32[]{:S(2)}, u32[]{:S(2)}) %collective-permute-start.75) | collective-permute-done | bytes 262176 | tf_op jit(solution)/shard_map/ppermute | solution.py:240
  1113.8 51.6 %psum.7 = f32[3,2048]{1,0:T(4,128)S(1)} all-reduce(f32[3,2048]{1,0:T(4,128)S(1)} %pad_maximum_fusion.7), channel_id=1, replica_groups=mesh['z'=4,'x'=2,'y'=2,'c'=2] {'z','x','y','c'}, use_global_device_ids=true, to_apply=%region_55.56 | all-reduce | flops 6144 | bytes 49152 | tf_op jit(solution)/shard_map/psum | solution.py:512
  1171.9 45.6 %adam_tiles.2 = (f32[6,256,2048]{2,1,0:T(8,128)}, f32[6,256,2048]{2,1,0:T(8,128)}, f32[6,256,2048]{2,1,0:T(8,128)}) custom-call(s32[6]{0:T(128)S(1)} %call_exported.1.visit_ref, s32[6]{0:T(128)S(1)} %get-tuple-element.53.mode_ref, s32[48]{0:T(128)S(1)} %multiply_add_fusion.4.cp_ref, s32[6]{0:T(128)S(1)} %fusion.166.rp_ref, s32[6]{0:T(128)S(1)} %broadcast.437.hold_ref, ...), custom_call_target="tpu_custom_call" | custom-call | tf_op jit(solution)/shard_map/adam_tiles/pallas_call | solution.py:213
  1221.3 17.4 %adam_tiles.3 = (f32[6,256,2048]{2,1,0:T(8,128)}, f32[6,256,2048]{2,1,0:T(8,128)}, f32[6,256,2048]{2,1,0:T(8,128)}) custom-call(s32[5]{0:T(128)S(1)} %get-tuple-element.269.visit_ref, s32[5]{0:T(128)S(1)} %get-tuple-element.268.mode_ref, s32[40]{0:T(128)S(1)} %select_n.593.cp_ref, ...), custom_call_target="tpu_custom_call", output_to_operand_aliasing={{0}: (12, {}), {1}: (13, {}), {2}: (14, {})} | custom-call | tf_op jit(solution)/shard_map/adam_tiles/pallas_call | solution.py:213
  (670 shorter events, 610.0 us)
Async XLA Ops:
  73.6 118.2 %all-gather.6.cloned.1.call-start = ((), (), s32[]{:S(2)}) async-start(), calls=%async_computation.9 | async-start | bytes 3932160 | tf_op jit(solution)/shard_map/all_gather | solution.py:341
  100.1 124.5 %all-gather.8.cloned.1.call-start = ((), (), s32[]{:S(2)}) async-start(), calls=%async_computation.10 | async-start | bytes 2621440 | tf_op jit(solution)/shard_map/all_gather | solution.py:385
  176.2 169.6 %all-gather.10.cloned.1.call-start = ((), (), s32[]{:S(2)}) async-start(), calls=%async_computation.11 | async-start | bytes 6553600 | tf_op jit(solution)/shard_map/all_gather | solution.py:341
  189.4 62.6 %collective-permute-start.17 = (bf16[256,4096]{1,0:T(8,128)(2,1)}, bf16[256,4096]{1,0:T(8,128)(2,1)}, u32[]{:S(2)}, u32[]{:S(2)}) collective-permute-start(bf16[256,4096]{1,0:T(8,128)(2,1)} %bitcast.42), channel_id=1, source_target_pairs={{0,2},{2,0},{1,3},{3,1},{4,6},{6,4},{5,7},{7,5},{8,10},{10,8},{9,1... | collective-permute-start | bytes 6291464 | tf_op jit(solution)/shard_map/ppermute | solution.py:240
  190.8 64.0 %collective-permute-start.18 = (bf16[256,4096]{1,0:T(8,128)(2,1)}, bf16[256,4096]{1,0:T(8,128)(2,1)}, u32[]{:S(2)}, u32[]{:S(2)}) collective-permute-start(bf16[256,4096]{1,0:T(8,128)(2,1)} %bitcast.42), channel_id=1, source_target_pairs={{0,4},{4,0},{1,5},{5,1},{2,6},{6,2},{3,7},{7,3},{8,12},{12,8},{9,1... | collective-permute-start | bytes 6291464 | tf_op jit(solution)/shard_map/ppermute | solution.py:240
  248.6 216.4 %all-gather.12.cloned.1.call-start = ((), (), s32[]{:S(2)}) async-start(), calls=%async_computation.12 | async-start | bytes 5242880 | tf_op jit(solution)/shard_map/all_gather | solution.py:341
  282.8 112.6 %collective-permute-start.21 = (bf16[1024,4096]{1,0:T(8,128)(2,1)}, bf16[1024,4096]{1,0:T(8,128)(2,1)}, u32[]{:S(2)}, u32[]{:S(2)}) collective-permute-start(bf16[1024,4096]{1,0:T(8,128)(2,1)} %get-tuple-element.159), channel_id=1, source_target_pairs={{0,1},{1,0},{2,3},{3,2},{4,5},{5,4},{6,7},{7,6},{8,9},{9,8},{10,11... | collective-permute-start | bytes 25165832 | tf_op jit(solution)/shard_map/ppermute | solution.py:240
  386.9 227.6 %all-gather.14.cloned.1.call-start = ((), (), s32[]{:S(2)}) async-start(), calls=%async_computation.13 | async-start | bytes 5242880 | tf_op jit(solution)/shard_map/all_gather | solution.py:395
  473.0 53.7 %collective-permute-start.27 = (f32[2,2,128,2048]{3,2,0,1:T(8,128)}, f32[2,2,128,2048]{3,2,0,1:T(8,128)}, u32[]{:S(2)}, u32[]{:S(2)}) collective-permute-start(f32[2,2,128,2048]{3,2,0,1:T(8,128)} %copy.152), channel_id=1, source_target_pairs={{0,1},{1,0},{2,3},{3,2},{4,5},{5,4},{6,7},{7,6},{8,9},{9,8},{10,11... | collective-permute-start | bytes 12582920 | tf_op jit(solution)/shard_map/ppermute | solution.py:240
  534.6 205.6 %reduce-scatter.6.cloned.1.call-start = ((), (), s32[]{:S(2)}) async-start(), calls=%async_computation.14 | async-start | bytes 5242880 | tf_op jit(solution)/shard_map/reduce_scatter | solution.py:455
  664.6 221.7 %reduce-scatter.8.cloned.1.call-start = ((), (), s32[]{:S(2)}) async-start(), calls=%async_computation.15 | async-start | bytes 5242880 | tf_op jit(solution)/shard_map/reduce_scatter | solution.py:455
  765.4 177.8 %reduce-scatter.10.cloned.1.call-start = ((), (), s32[]{:S(2)}) async-start(), calls=%async_computation.16 | async-start | bytes 6553600 | tf_op jit(solution)/shard_map/reduce_scatter | solution.py:455
  815.2 171.2 %reduce-scatter.14.cloned.1.call-start = ((), (), s32[]{:S(2)}) async-start(), calls=%async_computation.18 | async-start | bytes 2621440 | tf_op jit(solution)/shard_map/reduce_scatter | solution.py:455
  822.3 57.3 %collective-permute-start.66 = (bf16[256,2048]{1,0:T(8,128)(2,1)S(1)}, bf16[256,2048]{1,0:T(8,128)(2,1)S(1)}, u32[]{:S(2)}, u32[]{:S(2)}) collective-permute-start(bf16[256,2048]{1,0:T(8,128)(2,1)S(1)} %copy-done.43), channel_id=1, source_target_pairs={{0,2},{1,3},{2,0},{3,1},{4,6},{5,7},{6,4},{7,5},{8,10},{9,11},{10,... | collective-permute-start | bytes 3145736 | tf_op jit(solution)/shard_map/ppermute | solution.py:458
  823.5 56.1 %collective-permute-start.65 = (bf16[256,2048]{1,0:T(8,128)(2,1)S(1)}, bf16[256,2048]{1,0:T(8,128)(2,1)S(1)}, u32[]{:S(2)}, u32[]{:S(2)}) collective-permute-start(bf16[256,2048]{1,0:T(8,128)(2,1)S(1)} %copy-done.43), channel_id=1, source_target_pairs={{0,1},{1,0},{2,3},{3,2},{4,5},{5,4},{6,7},{7,6},{8,9},{9,8},{10,11... | collective-permute-start | bytes 3145736 | tf_op jit(solution)/shard_map/ppermute | solution.py:458
  920.9 133.3 %reduce-scatter.12.cloned.1.call-start = ((), (), s32[]{:S(2)}) async-start(), calls=%async_computation.17 | async-start | bytes 3932160 | tf_op jit(solution)/shard_map/reduce_scatter | solution.py:455
  961.6 94.8 %all-to-all-start.2 = ((bf16[8,6,256,256]{3,2,1,0:T(8,128)(2,1)}), bf16[8,6,256,256]{3,2,1,0:T(8,128)(2,1)}, u32[]{:S(2)}, u32[]{:S(2)}) async-start(bf16[8,6,256,256]{3,2,1,0:T(8,128)(2,1)} %pack_gradients.1), calls=%async_computation.5 | async-start | bytes 12582912 | tf_op jit(solution)/shard_map/all_to_all | solution.py:527
  975.0 73.1 %collective-permute-start.74 = (bf16[2,128,1024]{2,1,0:T(8,128)(2,1)S(1)}, bf16[2,128,1024]{2,1,0:T(8,128)(2,1)S(1)}, u32[]{:S(2)}, u32[]{:S(2)}) collective-permute-start(bf16[2,128,1024]{2,1,0:T(8,128)(2,1)S(1)} %slice_bitcast_fusion.15), channel_id=1, source_target_pairs={{0,2},{2,0},{1,3},{3,1},{4,6},{6,4},{5,7},{7,5},{8,10},{10,8},{9,1... | collective-permute-start | bytes 1572872 | tf_op jit(solution)/shard_map/ppermute | solution.py:240
  977.0 71.1 %collective-permute-start.76 = (bf16[2,128,1024]{2,1,0:T(8,128)(2,1)S(1)}, bf16[2,128,1024]{2,1,0:T(8,128)(2,1)S(1)}, u32[]{:S(2)}, u32[]{:S(2)}) collective-permute-start(bf16[2,128,1024]{2,1,0:T(8,128)(2,1)S(1)} %slice_bitcast_fusion.13), channel_id=1, source_target_pairs={{0,4},{4,0},{1,5},{5,1},{2,6},{6,2},{3,7},{7,3},{8,12},{12,8},{9,1... | collective-permute-start | bytes 1572872 | tf_op jit(solution)/shard_map/ppermute | solution.py:240
  986.4 78.9 %collective-permute-start.78 = (bf16[128,2048]{1,0:T(8,128)(2,1)}, bf16[128,2048]{1,0:T(8,128)(2,1)}, u32[]{:S(2)}, u32[]{:S(2)}) collective-permute-start(bf16[128,2048]{1,0:T(8,128)(2,1)} %reduce-scatter.14.cloned.1.call-done), channel_id=1, source_target_pairs={{8,0},{10,2},{12,4},{14,6},{1,9},{3,11},{5,13},{7,15},{24,16},{26,... | collective-permute-start | bytes 1572872 | tf_op jit(solution)/shard_map/ppermute | solution.py:547
  1058.4 162.9 %all-to-all-start.3 = ((bf16[8,3,256,256]{3,2,1,0:T(8,128)(2,1)}), bf16[8,3,256,256]{3,2,1,0:T(8,128)(2,1)S(1)}, u32[]{:S(2)}, u32[]{:S(2)}) async-start(bf16[8,3,256,256]{3,2,1,0:T(8,128)(2,1)} %bitcast.416), calls=%async_computation.7 | async-start | bytes 6291456 | tf_op jit(solution)/shard_map/all_to_all | solution.py:556
  1105.4 112.1 %collective-permute-start.81 = (bf16[256,2048]{1,0:T(8,128)(2,1)}, bf16[256,2048]{1,0:T(8,128)(2,1)}, u32[]{:S(2)}, u32[]{:S(2)}) collective-permute-start(bf16[256,2048]{1,0:T(8,128)(2,1)} %maximum_select_fusion), channel_id=1, source_target_pairs={{0,3},{2,1},{4,7},{6,5},{9,10},{11,8},{13,14},{15,12},{16,19},{18,... | collective-permute-start | bytes 3145736 | tf_op jit(solution)/shard_map/ppermute | solution.py:458
  1109.1 108.5 %collective-permute-start.80 = (bf16[256,2048]{1,0:T(8,128)(2,1)}, bf16[256,2048]{1,0:T(8,128)(2,1)}, u32[]{:S(2)}, u32[]{:S(2)}) collective-permute-start(bf16[256,2048]{1,0:T(8,128)(2,1)} %maximum_select_fusion), channel_id=1, source_target_pairs={{0,2},{2,0},{4,6},{6,4},{9,11},{11,9},{13,15},{15,13},{16,18},{18,... | collective-permute-start | bytes 3145736 | tf_op jit(solution)/shard_map/ppermute | solution.py:458
  1111.5 106.0 %collective-permute-start.79 = (bf16[256,2048]{1,0:T(8,128)(2,1)}, bf16[256,2048]{1,0:T(8,128)(2,1)}, u32[]{:S(2)}, u32[]{:S(2)}) collective-permute-start(bf16[256,2048]{1,0:T(8,128)(2,1)} %maximum_select_fusion), channel_id=1, source_target_pairs={{0,1},{2,3},{4,5},{6,7},{9,8},{11,10},{13,12},{15,14},{16,17},{18,... | collective-permute-start | bytes 3145736 | tf_op jit(solution)/shard_map/ppermute | solution.py:458
  (172 other events, 2863.8 us)
Sparse Core Ops, SparseCore 0:
  100.2 65.0 all-gather.5
  176.3 48.2 all-gather.7
  248.8 96.9 all-gather.9
  387.0 77.9 all-gather.11
  534.7 79.7 all-gather.13
  664.7 75.4 reduce-scatter.5
  765.5 76.9 reduce-scatter.7
  845.4 94.2 reduce-scatter.9
  942.0 44.3 reduce-scatter.13
  988.6 60.7 reduce-scatter.11

commit v4 on v3

--- a/solution.py
+++ b/solution.py
@@ -263,6 +263,14 @@
     return jnp.concatenate([low_one, high_one], axis=1)
 
 
+def sum_everywhere(value):
+    for axis in ("c", "y", "x"):
+        value = value + swap(value, axis)
+    for step in (1, 2):
+        value = value + lax.ppermute(value, "z", [(z, z ^ step) for z in range(4)])
+    return value
+
+
 def flip_pairs(mask, keep=None):
     pairs = []
     for z in range(4):
@@ -311,65 +319,59 @@
     to_f = np.arange(8) % 4
     column_table = 2 * ((to_f[None, :] + my_shift[:, None]) % 4) + to_x[None, :]
     half_cap = cap // 2
+    place = np.arange(4)
+
+    def of_tiles(tiles, values):
+        chosen = tiles[:, None] == np.arange(n_tiles)[None, :]
+        return jnp.sum(jnp.where(chosen, values[None, :], 0), axis=1)
+
+    column_tiles = jnp.concatenate([np.array([0, 1, 2, 4, 5, 7, 6, 8], np.int32), 10 + (place - f) % 4])
+    column_part = jnp.repeat(of_tiles(column_tiles, rank // half_cap), 2)
+    column_place = of_tiles(column_tiles, owners * half_cap + rank % half_cap)
+    column_place = (column_place[:, None] + np.array([0, 4 * half_cap])[None, :]).reshape(-1)
+    other_f = f ^ place
+    outer_tiles = jnp.where(other_f == z, 3, 9)
+    out_tiles = 14 + (z - other_f) % 4
+    row_slots = of_tiles(jnp.concatenate([outer_tiles, out_tiles]), rank)
+    row_owners = of_tiles(jnp.stack([outer_tiles[0], out_tiles[0]]), owners)
 
     def exchange_columns(first, weights):
         table = column_table[first : first + half_cap].reshape(-1)
         got = lax.all_to_all(pack_columns(weights, table, first, half_cap), PLANE, 0, 0, tiled=True)
         return got.reshape(8 * half_cap, rows, block)
 
-    received = [exchange_columns(0, master)]
+    received = [exchange_columns(0, after(master, column_part, column_place, row_slots, row_owners))]
     received.append(exchange_columns(half_cap, after(master, received[0])))
 
-    def source_of(tile):
-        if isinstance(tile, int):
-            owner, slot = owners[tile], rank[tile]
-        else:
-            chosen = jnp.arange(n_tiles) == tile
-            owner = jnp.sum(jnp.where(chosen, owners, 0))
-            slot = jnp.sum(jnp.where(chosen, rank, 0))
-        part = slot // half_cap
-        return part, owner * half_cap + slot % half_cap
-
-    def gather_columns(tiles, parts):
-        which, index = [], []
-        for tile in tiles:
-            part, place = source_of(tile)
-            for side in range(2):
-                which.append(part)
-                index.append(side * 4 * half_cap + place)
-        local = pick_blocks(received[:parts], jnp.stack(which), jnp.stack(index), len(tiles))
-        return lax.all_gather(local, "z", axis=0, tiled=True)
-
-    w_qkv = gather_columns([0, 1, 2], 1)
-
-    def my_block(tile):
-        chosen = jnp.arange(n_tiles) == tile
-        slot = jnp.sum(jnp.where(chosen, rank, 0))
+    def columns_here(first, count, parts):
+        chosen = slice(2 * first, 2 * (first + count))
+        return pick_blocks(received[:parts], column_part[chosen], column_place[chosen], count)
+
+    def gather_z(value):
+        return lax.all_gather(value, "z", axis=0, tiled=True)
+
+    w_qkv = gather_z(columns_here(0, 3, 1))
+
+    def my_block(slot):
         return lax.dynamic_index_in_dim(master, slot, 0, keepdims=False).astype(bf16)
 
     h0 = tokens.astype(f32)
     a_all = gather_rows(after(normalize(h0, gains[0]).astype(bf16), received[1]))
 
-    def owner_of(tile):
-        return jnp.sum(jnp.where(jnp.arange(n_tiles) == tile, owners, 0))
-
-    def take_rows(tile_for, keep_pair, *earlier):
+    def take_rows(kind, keep_pair, *earlier):
         found = None
-        source = owner_of(tile_for(f)) ^ f
+        source = row_owners[kind] ^ f
         for mask in range(4):
-            got = after(my_block(tile_for(f ^ mask)), *earlier)
+            got = after(my_block(row_slots[4 * kind + mask]), *earlier)
             if mask:
                 got = lax.ppermute(got, ALL_AXES, flip_pairs(mask, keep_pair))
             found = got if found is None else jnp.where(source == mask, got, found)
         return found
 
-    def self_or_cross(place):
-        return jnp.where(place == z, 3, 9)
-
     def needs_outer(zz, place, target):
         return target % 4 in (zz, (zz + 2) % 4)
 
-    outer = take_rows(self_or_cross, needs_outer, received[0])
+    outer = take_rows(0, needs_outer, received[0])
     half_rows = rows // 2
     odd = z % 2
     to_pair = lax.dynamic_slice_in_dim(outer, (1 - odd) * half_rows, half_rows, 0)
@@ -387,12 +389,12 @@
     w_self_out = jnp.where(low_y, outer_all[:rows], outer_all[rows:])
     w_cross_out = jnp.where(low_y, outer_all[rows:], outer_all[:rows])
 
-    w_cross = gather_columns([4, 5, 7, 6, 8], 2)
-    w_in = gather_columns([10 + (place - f) % 4 for place in range(4)], 2)
+    w_cross = gather_z(columns_here(3, 5, 2))
+    w_in = gather_z(columns_here(8, 4, 2))
     slots, ctx_len, ctx_width = context.shape
     ctx_all = gather_rows(after(context.reshape(slots * ctx_len, ctx_width), a_all))
-    out_rows = take_rows(lambda place: 14 + (z - place) % 4, None, ctx_all)
-    w_out = lax.all_gather(out_rows, "z", axis=0, tiled=True)
+    out_rows = take_rows(1, None, ctx_all)
+    w_out = gather_z(out_rows)
 
     seg = segments(lengths[0], count)
     live = keep == 1
@@ -405,10 +407,21 @@
     grad_out = cotangent.astype(f32) * live.astype(f32)[:, None]
     d_ff = gather_rows(after(grad_out.astype(bf16), out_rows))
 
+    present = owners[0] >= 0
+
+    def gather_step(value):
+        shape = jax.ShapeDtypeStruct((8 * value.shape[0], value.shape[1]), value.dtype)
+        return lax.cond(present, gather_rows, lambda _: jnp.zeros(shape.shape, shape.dtype), value)
+
+    def scatter_step(part):
+        shape = (part.shape[0] // 8, part.shape[1])
+        return lax.cond(present, scatter_rows, lambda _: jnp.zeros(shape, f32), part)
+
     def split(value):
         return value.reshape(8, -1, heads_here, head_dim)
 
-    qkv = matmul(a_all, w_qkv).astype(bf16)
+    qkv = matmul(a_all, w_qkv)
+    qkv = qkv.astype(bf16)
     query, keys, values = (split(qkv[:, n * block : (n + 1) * block]) for n in range(3))
     places = jnp.arange(count)
     allowed = (seg_all[:, :, None] == seg_all[:, None, :]) & (
@@ -430,25 +443,27 @@
     probs = probabilities(query, keys, allowed)
     probs_low = probs.astype(bf16)
     attended = joined(weighted(probs_low, values))
-    h1 = h0 + scatter_rows(matmul(attended, w_self_out))
-    b_all = gather_rows(after(normalize(h1, gains[1]).astype(bf16), w_cross))
+    part = matmul(attended, w_self_out)
+    h1 = h0 + scatter_step(part)
+    b_all = gather_step(normalize(h1, gains[1]).astype(bf16))
 
     w_cross_q = w_cross[:, :block]
     w_low = w_cross[:, block : 3 * block]
     w_high = w_cross[:, 3 * block :]
     ctx_low, ctx_high = ctx_all[:, :width], ctx_all[:, width:]
     ctx_kv = (matmul(ctx_low, w_low) + matmul(ctx_high, w_high)).astype(bf16)
-    cross_q = split(matmul(b_all, w_cross_q).astype(bf16))
+    cross_q = matmul(b_all, w_cross_q)
+    cross_q = split(cross_q.astype(bf16))
     cross_k, cross_v = split(ctx_kv[:, :block]), split(ctx_kv[:, block:])
     item = jnp.arange(slots * ctx_len) // ctx_len
     own_item = seg_all[:, :, None] == item[None, None, :]
     cross_p = probabilities(cross_q, cross_k, own_item)
     cross_low = cross_p.astype(bf16)
     cross_o = joined(weighted(cross_low, cross_v))
-    h2 = h1 + scatter_rows(matmul(after(cross_o, w_in), w_cross_out))
-    c_all = gather_rows(normalize(h2, gains[2]).astype(bf16))
-
-    hidden = matmul(after(c_all, w_out), w_in)
+    h2 = h1 + scatter_step(matmul(cross_o, w_cross_out))
+    c_all = gather_step(normalize(h2, gains[2]).astype(bf16))
+
+    hidden = matmul(c_all, w_in)
     activated = gelu_tanh(hidden).astype(bf16)
 
     def sum_rows(value):
@@ -461,18 +476,19 @@
     t_out = matmul_left(activated, d_ff).astype(bf16)
     g_out = sum_rows(t_out)
     d_act = matmul_right(after(d_ff, t_out), w_out)
-    layer_out = (h2 + scatter_rows(matmul(activated, w_out))).astype(bf16)
+    layer_out = (h2 + scatter_step(matmul(activated, w_out))).astype(bf16)
     d_hidden = jax.vjp(gelu_tanh, hidden)[1](d_act)[0].astype(bf16)
     t_in = matmul_left(c_all, d_hidden).astype(bf16)
     g_in = sum_rows(t_in)
-    part_two, gain_grad_two = jax.vjp(normalize, h2, gains[2])[1](scatter_rows(matmul_right(d_hidden, w_in)))
+    part = matmul_right(d_hidden, w_in)
+    part_two, gain_grad_two = jax.vjp(normalize, h2, gains[2])[1](scatter_step(part))
     dh2 = grad_out + part_two
-    d_cross_out = gather_rows(after(dh2.astype(bf16), t_in, g_out))
+    d_cross_out = gather_step(after(dh2.astype(bf16), t_in))
     out_grads = to_owners(g_out, None)
     g_cross_out = matmul_left(cross_o, d_cross_out)
 
-    def through(weights, d_out, left, right, probs, probs_low, values):
-        d_mixed = split(matmul_right(d_out, weights).astype(bf16))
+    def through(d_mixed, left, right, probs, probs_low, values):
+        d_mixed = split(d_mixed.astype(bf16))
         d_probs = jnp.einsum("bqhd,bkhd->bhqk", d_mixed, values, preferred_element_type=f32)
         d_scores = (probs * (d_probs - jnp.sum(probs * d_probs, axis=-1, keepdims=True))).astype(bf16)
         d_left = joined(weighted(d_scores, right) * scale)
@@ -480,7 +496,9 @@
         d_values = joined(jnp.einsum("bhqk,bqhd->bkhd", probs_low, d_mixed, preferred_element_type=f32))
         return d_left, d_right, d_values
 
-    d_cq, d_ck, d_cv = through(w_cross_out, d_cross_out, cross_q, cross_k, cross_p, cross_low, cross_v)
+    d_cq, d_ck, d_cv = through(
+        matmul_right(d_cross_out, w_cross_out), cross_q, cross_k, cross_p, cross_low, cross_v
+    )
     d_ckv = jnp.concatenate([d_ck, d_cv], axis=1)
     t_cross = jnp.concatenate(
         [
@@ -490,9 +508,10 @@
         axis=1,
     )
     g_cross = sum_rows(t_cross)
-    part_one, gain_grad_one = jax.vjp(normalize, h1, gains[1])[1](scatter_rows(matmul_right(d_cq, w_cross_q)))
+    part = matmul_right(d_cq, w_cross_q)
+    part_one, gain_grad_one = jax.vjp(normalize, h1, gains[1])[1](scatter_step(part))
     dh1 = dh2 + part_one
-    d_self_out = gather_rows(after(dh1.astype(bf16), t_cross, g_in, out_grads))
+    d_self_out = gather_step(after(dh1.astype(bf16), t_cross, out_grads))
     g_self_out = matmul_left(attended, d_self_out)
     g_outer = sum_rows(
         jnp.concatenate(
@@ -503,14 +522,10 @@
             axis=0,
         )
     )
-    d_q, d_k, d_v = through(w_self_out, d_self_out, query, keys, probs, probs_low, values)
+    d_mixed = matmul_right(d_self_out, w_self_out)
+    d_q, d_k, d_v = through(d_mixed, query, keys, probs, probs_low, values)
     d_qkv = jnp.concatenate([d_q, d_k, d_v], axis=1)
     g_qkv = sum_rows(matmul_left(a_all, d_qkv).astype(bf16))
-    part_zero, gain_grad_zero = jax.vjp(normalize, h0, gains[0])[1](scatter_rows(matmul_right(d_qkv, w_qkv)))
-    grad_tokens = (dh1 + part_zero).astype(bf16)
-
-    gain_total = lax.psum(jnp.stack([gain_grad_zero, gain_grad_one, gain_grad_two]), ALL_AXES)
-
     group_of = np.array([0, 0, 0, 0, 0, 0, 0, 0, 0, 0, 1, 1, 1, 1, 0, 0, 0, 0], np.int32)
     column_of = np.array([0, 0, 0, 0, 0, 1, 3, 2, 4, 0, 0, 1, 2, 3, 0, 0, 0, 0], np.int32)
     group_at = jnp.sum(jnp.where(holds, group_of, 0), axis=2)
@@ -525,6 +540,12 @@
         cap,
     )
     early_grads = lax.all_to_all(sent, PLANE, 0, 0, tiled=True).reshape(8 * cap, rows, block)
+    part = matmul_right(after(d_qkv, sent), w_qkv)
+    part_zero, gain_grad_zero = jax.vjp(normalize, h0, gains[0])[1](scatter_step(part))
+    grad_tokens = (dh1 + part_zero).astype(bf16)
+
+    gain_total = sum_everywhere(jnp.stack([gain_grad_zero, gain_grad_one, gain_grad_two]))
+
     place = np.arange(8)
     source = (place % 2)[None, :] * 4 + ((place // 2)[None, :] - my_shift[:, None]) % 4
     row_source = ((z - my_shift) % 4) ^ f

time: 1260 us -> 1100 us (0.87)
  waiting for transfers between devices: 541 us -> 475 us
  blocking collectives: 51.6 us -> 0 us
  between operations: 66.6 us -> 36.5 us
  matrix products: 133 us -> 159 us
  local copies, waits for them, and re-layouts: 168 us -> 146 us
  other arithmetic: 73.9 us -> 52.3 us
    ppermute x68 -> x71, waiting for transfers between devices: 264 us -> 392 us  [swap(): return lax.ppermute(value, axis, [(0, 1), (1, 0)])]
    all_gather x4, waiting for transfers between devices: 94.5 us -> 0.08 us  [gather_z(): return lax.all_gather(value, 'z', axis=0, tiled=True)]
    psum x1 -> x0, blocking collectives: 51.6 us -> none  [plane_body(): lax.psum(jnp.stack([gain_grad_zero, gain_grad_one, gain_grad_two]), ALL_A...]
    ppermute x6, waiting for transfers between devices: 42 us -> 0.02 us  [to_owners(): lax.ppermute(value, ALL_AXES, flip_pairs(mask, keep_pair))]
    reduce_scatter x5, waiting for transfers between devices: 29.4 us -> 0.04 us  [sum_rows(): return lax.psum_scatter(value, 'z', scatter_dimension=0, tiled=True)]
    unnamed x234 -> x203, local copies, waits for them, and re-layouts: 65.2 us -> 44.4 us
    add x6, other arithmetic: 23.2 us -> 4.6 us  [scatter_rows(): chip = part[0] + swap(part[1], 'c')]
    ppermute x6, waiting for transfers between devices: 63.7 us -> 46.2 us  [take_rows(): got = lax.ppermute(got, ALL_AXES, flip_pairs(mask, keep_pair))]
  transfers between devices with their start and end apart: 96 -> 101, of which waited for: 61 -> 57; matrix products, arithmetic and copies ran while one was open for 23% -> 30% of each run, Pallas kernels for 6% -> 7%
where the time goes in v4:
time: 1100 us; the launch traced here: 1090 us
  waiting for transfers between devices  475 us (43%)
  matrix products  159 us (14%)
  local copies, waits for them, and re-layouts  146 us (13%)
  starting transfers between devices  114 us (10%)
  Pallas kernels  102 us (9%)
  other arithmetic  52.3 us (5%)
  between operations  36.5 us (3%)
    ppermute x71, waiting for transfers between devices, swap(): return lax.ppermute(value, axis, [(0, 1), (1, 0)])  392 us
    ppermute x71, starting transfers between devices, swap(): return lax.ppermute(value, axis, [(0, 1), (1, 0)])  71 us
    pallas_call x2, Pallas kernels, adam_tiles(): pl.pallas_call(kernel, out_shape=(shape, shape, shape), grid_spec=pltpu.P...  68.1 us
    dot_general x8, matrix products, matmul(): return jnp.dot(left, right, preferred_element_type=f32)  58.4 us
    dot_general x8, matrix products, matmul_left(): lax.dot_general(left, right, (((0,), (0,)), ((), ())), preferred_element_...  46.7 us
    ppermute x6, waiting for transfers between devices, take_rows(): got = lax.ppermute(got, ALL_AXES, flip_pairs(mask, keep_pair))  46.2 us
    unnamed x203, local copies, waits for them, and re-layouts  44.4 us
    dot_general x6, matrix products, matmul_right(): lax.dot_general(left, right, (((1,), (1,)), ((), ())), preferred_element_...  38.7 us
  transfers between devices with their start and end apart: 101, of which 57 were waited for; matrix products, arithmetic and copies ran while one was open for 30% of the time, Pallas kernels for 7%

profile of v4, /device:TPU:0, one launch (start us, length us, event | category | flops | bytes accessed | tf_op | source)
XLA Modules:
  0.0 1087.4 jit_solution(3489364502591833656)
XLA Ops:
  26.3 36.9 %all-to-all-done = bf16[8,3,256,256]{3,2,1,0:T(8,128)(2,1)S(1)} async-done(((bf16[8,3,256,256]{3,2,1,0:T(8,128)(2,1)}), bf16[8,3,256,256]{3,2,1,0:T(8,128)(2,1)S(1)}, u32[]{:S(2)}, u32[]{:S(2)}) %all-to-all-start) | async-done | bytes 3145760 | tf_op jit(solution)/shard_map/all_to_all | solution.py:340
  116.0 16.3 %collective-permute-done.58 = bf16[256,2048]{1,0:T(8,128)(2,1)} collective-permute-done((bf16[256,2048]{1,0:T(8,128)(2,1)}, bf16[256,2048]{1,0:T(8,128)(2,1)}, u32[]{:S(2)}, u32[]{:S(2)}) %collective-permute-start.58) | collective-permute-done | bytes 1048608 | tf_op jit(solution)/shard_map/ppermute | solution.py:367
  171.8 37.2 %collective-permute-done.63 = bf16[256,4096]{1,0:T(8,128)(2,1)} collective-permute-done((bf16[256,4096]{1,0:T(8,128)(2,1)}, bf16[256,4096]{1,0:T(8,128)(2,1)}, u32[]{:S(2)}, u32[]{:S(2)}) %collective-permute-start.63) | collective-permute-done | bytes 2097184 | tf_op jit(solution)/shard_map/ppermute | solution.py:240
  221.7 15.7 %collective-permute-done.64 = bf16[128,4096]{1,0:T(8,128)(2,1)S(1)} collective-permute-done((bf16[128,4096]{1,0:T(8,128)(2,1)S(1)}, bf16[128,4096]{1,0:T(8,128)(2,1)S(1)}, u32[]{:S(2)}, u32[]{:S(2)}) %collective-permute-start.64) | collective-permute-done | bytes 1048608 | tf_op jit(solution)/shard_map/ppermute | solution.py:240
  283.1 35.2 %conditional.10 = (f32[128,2048]{1,0:T(8,128)S(1)}) conditional(s32[]{:T(128)} %bitcast.60, () %tuple.88, f32[1024,2048]{1,0:T(8,128)} %fusion.113), branch_computations={%region_10.11_spmd, %region_11.12_spmd} | conditional | flops 2883584 | bytes 65536208 | solution.py:418
  319.2 27.0 %conditional.11 = (bf16[1024,2048]{1,0:T(8,128)(2,1)}) conditional(s32[]{:T(128)} %bitcast.60, () %tuple.98, bf16[128,2048]{1,0:T(8,128)(2,1)S(1)} %multiply_convert_fusion.5), branch_computations={%region_13.14_spmd, %region_14.15_spmd} | conditional | bytes 26214608 | solution.py:414
  384.7 22.6 %collective-permute-done.68 = bf16[256,2048]{1,0:T(8,128)(2,1)S(1)} collective-permute-done((bf16[256,2048]{1,0:T(8,128)(2,1)S(1)}, bf16[256,2048]{1,0:T(8,128)(2,1)S(1)}, u32[]{:S(2)}, u32[]{:S(2)}) %collective-permute-start.68) | collective-permute-done | bytes 1048608 | tf_op jit(solution)/shard_map/ppermute | solution.py:367
  449.4 35.1 %conditional.12 = (f32[128,2048]{1,0:T(8,128)S(1)}) conditional(s32[]{:T(128)} %bitcast.60, () %tuple.96, f32[1024,2048]{1,0:T(8,128)} %fusion.109), branch_computations={%region_17.18_spmd, %region_18.19_spmd} | conditional | flops 2883584 | bytes 65536208 | solution.py:418
  463.5 12.5 %collective-permute-done.28 = bf16[2,128,1024]{2,1,0:T(8,128)(2,1)S(1)} collective-permute-done((bf16[2,128,1024]{2,1,0:T(8,128)(2,1)S(1)}, bf16[2,128,1024]{2,1,0:T(8,128)(2,1)S(1)}, u32[]{:S(2)}, u32[]{:S(2)}) %collective-permute-start.28) | collective-permute-done | bytes 524320 | tf_op jit(solution)/shard_map/cond/branch_1_fun/ppermute | solution.py:240
  484.9 28.0 %conditional.13 = (bf16[1024,2048]{1,0:T(8,128)(2,1)}) conditional(s32[]{:T(128)} %bitcast.60, () %tuple.100, bf16[128,2048]{1,0:T(8,128)(2,1)S(1)} %multiply_convert_fusion.4), branch_computations={%region_20.21_spmd, %region_21.22_spmd} | conditional | bytes 26214608 | solution.py:414
  572.6 35.3 %conditional.14 = (f32[128,2048]{1,0:T(8,128)S(1)}) conditional(s32[]{:T(128)} %bitcast.60, () %tuple.99, f32[1024,2048]{1,0:T(8,128)} %fusion.173), branch_computations={%region_22.23_spmd, %region_23.24_spmd} | conditional | flops 2883584 | bytes 65536208 | solution.py:418
  607.9 35.3 %conditional.15 = (f32[128,2048]{1,0:T(8,128)S(1)}) conditional(s32[]{:T(128)} %bitcast.60, () %tuple.105, f32[1024,2048]{1,0:T(8,128)} %fusion.195), branch_computations={%region_24.25_spmd, %region_25.26_spmd} | conditional | flops 2883584 | bytes 65536208 | solution.py:418
  622.0 12.2 %collective-permute-done.38 = bf16[2,128,1024]{2,1,0:T(8,128)(2,1)S(1)} collective-permute-done((bf16[2,128,1024]{2,1,0:T(8,128)(2,1)S(1)}, bf16[2,128,1024]{2,1,0:T(8,128)(2,1)S(1)}, u32[]{:S(2)}, u32[]{:S(2)}) %collective-permute-start.38) | collective-permute-done | bytes 524320 | tf_op jit(solution)/shard_map/cond/branch_1_fun/ppermute | solution.py:240
  646.3 27.6 %conditional.16 = (bf16[1024,2048]{1,0:T(8,128)(2,1)}) conditional(s32[]{:T(128)} %bitcast.60, () %tuple.109, bf16[128,2048]{1,0:T(8,128)(2,1)} %get-tuple-element.87), branch_computations={%region_27.28_spmd, %region_28.29_spmd} | conditional | bytes 26214608 | solution.py:414
  714.3 59.5 %conditional.17 = (f32[128,2048]{1,0:T(8,128)S(1)}) conditional(s32[]{:T(128)} %bitcast.60, () %tuple.108, f32[1024,2048]{1,0:T(8,128)} %fusion.99), branch_computations={%region_30.31_spmd, %region_31.32_spmd} | conditional | flops 2883584 | bytes 65536208 | solution.py:418
  729.0 11.9 %collective-permute-done.43 = bf16[2,128,1024]{2,1,0:T(8,128)(2,1)S(1)} collective-permute-done((bf16[2,128,1024]{2,1,0:T(8,128)(2,1)S(1)}, bf16[2,128,1024]{2,1,0:T(8,128)(2,1)S(1)}, u32[]{:S(2)}, u32[]{:S(2)}) %collective-permute-start.43) | collective-permute-done | bytes 524320 | tf_op jit(solution)/shard_map/cond/branch_1_fun/ppermute | solution.py:240
  742.8 22.9 %collective-permute-done.41 = bf16[2,128,1024]{2,1,0:T(8,128)(2,1)S(1)} collective-permute-done((bf16[2,128,1024]{2,1,0:T(8,128)(2,1)S(1)}, bf16[2,128,1024]{2,1,0:T(8,128)(2,1)S(1)}, u32[]{:S(2)}, u32[]{:S(2)}) %collective-permute-start.41) | collective-permute-done | bytes 524320 | tf_op jit(solution)/shard_map/cond/branch_1_fun/ppermute | solution.py:240
  779.4 28.8 %conditional.18 = (bf16[1024,2048]{1,0:T(8,128)(2,1)}) conditional(s32[]{:T(128)} %bitcast.60, () %tuple.112, bf16[128,2048]{1,0:T(8,128)(2,1)S(1)} %copy-done.34), branch_computations={%region_34.35_spmd, %region_35.36_spmd} | conditional | bytes 26214608 | solution.py:414
  830.2 17.1 %pack_gradients.1 = bf16[8,6,256,256]{3,2,1,0:T(8,128)(2,1)} custom-call(s32[48]{0:T(128)S(1)} %tile.20.which_ref, s32[48]{0:T(128)S(1)} %tile.22.column_ref, bf16[512,1280]{1,0:T(8,128)(2,1)S(1)} %copy-done.6, bf16[512,1024]{1,0:T(8,128)(2,1)S(1)} %copy-done.7), custom_call_target="tpu_custom_call" | custom-call | tf_op jit(solution)/shard_map/pack_gradients/pallas_call | solution.py:152
  872.2 71.6 %conditional.19 = (f32[128,2048]{1,0:T(8,128)S(1)}) conditional(s32[]{:T(128)} %bitcast.60, () %tuple.111, f32[1024,2048]{1,0:T(8,128)} %fusion.196), branch_computations={%region_41.42_spmd, %region_42.43_spmd} | conditional | flops 2883584 | bytes 65536208 | solution.py:418
  887.9 46.0 %collective-permute-done.48 = bf16[2,128,1024]{2,1,0:T(8,128)(2,1)S(1)} collective-permute-done((bf16[2,128,1024]{2,1,0:T(8,128)(2,1)S(1)}, bf16[2,128,1024]{2,1,0:T(8,128)(2,1)S(1)}, u32[]{:S(2)}, u32[]{:S(2)}) %collective-permute-start.48) | collective-permute-done | bytes 524320 | tf_op jit(solution)/shard_map/cond/branch_1_fun/ppermute | solution.py:240
  956.4 34.2 %collective-permute-done.83 = f32[3,2048]{1,0:T(4,128)S(1)} collective-permute-done((f32[3,2048]{1,0:T(4,128)S(1)}, f32[3,2048]{1,0:T(4,128)S(1)}, u32[]{:S(2)}, u32[]{:S(2)}) %collective-permute-start.83) | collective-permute-done | bytes 24608 | tf_op jit(solution)/shard_map/ppermute | solution.py:240
  1009.7 46.3 %adam_tiles.2 = (f32[6,256,2048]{2,1,0:T(8,128)}, f32[6,256,2048]{2,1,0:T(8,128)}, f32[6,256,2048]{2,1,0:T(8,128)}) custom-call(s32[6]{0:T(128)S(1)} %call_exported.2.visit_ref, s32[6]{0:T(128)S(1)} %get-tuple-element.91.mode_ref, s32[48]{0:T(128)S(1)} %multiply_add_fusion.4.cp_ref, s32[6]{0:T(128)S(1)} %fusion.162.rp_ref, s32[6]{0:T(128)S(1)} %broadcast.521.hold_ref, ...), custom_call_target="tpu_custom_call" | custom-call | tf_op jit(solution)/shard_map/adam_tiles/pallas_call | solution.py:213
  1058.3 21.8 %adam_tiles.3 = (f32[6,256,2048]{2,1,0:T(8,128)}, f32[6,256,2048]{2,1,0:T(8,128)}, f32[6,256,2048]{2,1,0:T(8,128)}) custom-call(s32[5]{0:T(128)S(1)} %get-tuple-element.266.visit_ref, s32[5]{0:T(128)S(1)} %compare_select_fusion.17.mode_ref, s32[40]{0:T(128)S(1)} %select_n.408.cp_ref, ...), custom_call_target="tpu_custom_call", output_to_operand_aliasing={{0}: (12, {}), {1}: (13, {}), {2}: (14, {})} | custom-call | tf_op jit(solution)/shard_map/adam_tiles/pallas_call | solution.py:213
  (701 shorter events, 695.9 us)
Async XLA Ops:
  73.7 192.3 %all-gather.6.cloned.1.call-start = ((), (), s32[]{:S(2)}) async-start(), calls=%async_computation.9 | async-start | bytes 3932160 | tf_op jit(solution)/shard_map/all_gather | solution.py:351
  76.1 200.6 %all-gather.8.cloned.1.call-start = ((), (), s32[]{:S(2)}) async-start(), calls=%async_computation.10 | async-start | bytes 2621440 | tf_op jit(solution)/shard_map/all_gather | solution.py:387
  156.3 190.0 %all-gather.10.cloned.1.call-start = ((), (), s32[]{:S(2)}) async-start(), calls=%async_computation.11 | async-start | bytes 6553600 | tf_op jit(solution)/shard_map/all_gather | solution.py:351
  161.0 48.0 %collective-permute-start.63 = (bf16[256,4096]{1,0:T(8,128)(2,1)}, bf16[256,4096]{1,0:T(8,128)(2,1)}, u32[]{:S(2)}, u32[]{:S(2)}) collective-permute-start(bf16[256,4096]{1,0:T(8,128)(2,1)} %bitcast.77), channel_id=1, source_target_pairs={{0,4},{4,0},{1,5},{5,1},{2,6},{6,2},{3,7},{7,3},{8,12},{12,8},{9,1... | collective-permute-start | bytes 6291464 | tf_op jit(solution)/shard_map/ppermute | solution.py:240
  162.5 49.3 %collective-permute-start.62 = (bf16[256,4096]{1,0:T(8,128)(2,1)}, bf16[256,4096]{1,0:T(8,128)(2,1)}, u32[]{:S(2)}, u32[]{:S(2)}) collective-permute-start(bf16[256,4096]{1,0:T(8,128)(2,1)} %bitcast.77), channel_id=1, source_target_pairs={{0,2},{2,0},{1,3},{3,1},{4,6},{6,4},{5,7},{7,5},{8,10},{10,8},{9,1... | collective-permute-start | bytes 6291464 | tf_op jit(solution)/shard_map/ppermute | solution.py:240
  168.3 344.6 %all-gather.12.cloned.1.call-start = ((), (), s32[]{:S(2)}) async-start(), calls=%async_computation.12 | async-start | bytes 5242880 | tf_op jit(solution)/shard_map/all_gather | solution.py:351
  245.7 105.5 %collective-permute-start.66 = (bf16[1024,4096]{1,0:T(8,128)(2,1)}, bf16[1024,4096]{1,0:T(8,128)(2,1)}, u32[]{:S(2)}, u32[]{:S(2)}) collective-permute-start(bf16[1024,4096]{1,0:T(8,128)(2,1)} %get-tuple-element.208), channel_id=1, source_target_pairs={{0,1},{1,0},{2,3},{3,2},{4,5},{5,4},{6,7},{7,6},{8,9},{9,8},{10,11... | collective-permute-start | bytes 25165832 | tf_op jit(solution)/shard_map/ppermute | solution.py:240
  265.7 267.0 %all-gather.14.cloned.1.call-start = ((), (), s32[]{:S(2)}) async-start(), calls=%async_computation.13 | async-start | bytes 5242880 | tf_op jit(solution)/shard_map/all_gather | solution.py:351
  408.5 297.3 %reduce-scatter.6.cloned.1.call-start = ((), (), s32[]{:S(2)}) async-start(), calls=%async_computation.14 | async-start | bytes 5242880 | tf_op jit(solution)/shard_map/reduce_scatter | solution.py:470
  444.7 76.0 %collective-permute-start.74 = (bf16[512,2048]{1,0:T(8,128)(2,1)}, bf16[512,2048]{1,0:T(8,128)(2,1)}, u32[]{:S(2)}, u32[]{:S(2)}) collective-permute-start(bf16[512,2048]{1,0:T(8,128)(2,1)} %get-tuple-element.224), channel_id=1, source_target_pairs={{0,1},{1,0},{2,3},{3,2},{4,5},{5,4},{6,7},{7,6},{8,9},{9,8},{10,11... | collective-permute-start | bytes 6291464 | tf_op jit(solution)/shard_map/ppermute | solution.py:240
  532.6 295.0 %reduce-scatter.10.cloned.1.call-start = ((), (), s32[]{:S(2)}) async-start(), calls=%async_computation.16 | async-start | bytes 5242880 | tf_op jit(solution)/shard_map/reduce_scatter | solution.py:470
  553.7 274.0 %reduce-scatter.8.cloned.1.call-start = ((), (), s32[]{:S(2)}) async-start(), calls=%async_computation.15 | async-start | bytes 6553600 | tf_op jit(solution)/shard_map/reduce_scatter | solution.py:470
  705.6 239.5 %reduce-scatter.12.cloned.1.call-start = ((), (), s32[]{:S(2)}) async-start(), calls=%async_computation.17 | async-start | bytes 3932160 | tf_op jit(solution)/shard_map/reduce_scatter | solution.py:470
  705.9 69.8 %collective-permute-start.77 = (bf16[256,2048]{1,0:T(8,128)(2,1)}, bf16[256,2048]{1,0:T(8,128)(2,1)}, u32[]{:S(2)}, u32[]{:S(2)}) collective-permute-start(bf16[256,2048]{1,0:T(8,128)(2,1)} %reduce-scatter.6.cloned.1.call-done), channel_id=1, source_target_pairs={{0,3},{1,2},{2,1},{3,0},{4,7},{5,6},{6,5},{7,4},{8,11},{9,10},{10,... | collective-permute-start | bytes 3145736 | tf_op jit(solution)/shard_map/ppermute | solution.py:473
  707.5 68.1 %collective-permute-start.76 = (bf16[256,2048]{1,0:T(8,128)(2,1)}, bf16[256,2048]{1,0:T(8,128)(2,1)}, u32[]{:S(2)}, u32[]{:S(2)}) collective-permute-start(bf16[256,2048]{1,0:T(8,128)(2,1)} %reduce-scatter.6.cloned.1.call-done), channel_id=1, source_target_pairs={{0,2},{1,3},{2,0},{3,1},{4,6},{5,7},{6,4},{7,5},{8,10},{9,11},{10,... | collective-permute-start | bytes 3145736 | tf_op jit(solution)/shard_map/ppermute | solution.py:473
  707.9 67.7 %collective-permute-start.75 = (bf16[256,2048]{1,0:T(8,128)(2,1)}, bf16[256,2048]{1,0:T(8,128)(2,1)}, u32[]{:S(2)}, u32[]{:S(2)}) collective-permute-start(bf16[256,2048]{1,0:T(8,128)(2,1)} %reduce-scatter.6.cloned.1.call-done), channel_id=1, source_target_pairs={{0,1},{1,0},{2,3},{3,2},{4,5},{5,4},{6,7},{7,6},{8,9},{9,8},{10,11... | collective-permute-start | bytes 3145736 | tf_op jit(solution)/shard_map/ppermute | solution.py:473
  847.3 100.0 %all-to-all-start.2 = ((bf16[8,6,256,256]{3,2,1,0:T(8,128)(2,1)}), bf16[8,6,256,256]{3,2,1,0:T(8,128)(2,1)}, u32[]{:S(2)}, u32[]{:S(2)}) async-start(bf16[8,6,256,256]{3,2,1,0:T(8,128)(2,1)} %pack_gradients.1), calls=%async_computation.5 | async-start | bytes 12582912 | tf_op jit(solution)/shard_map/all_to_all | solution.py:542
  852.2 103.0 %reduce-scatter.14.cloned.1.call-start = ((), (), s32[]{:S(2)}) async-start(), calls=%async_computation.18 | async-start | bytes 2621440 | tf_op jit(solution)/shard_map/reduce_scatter | solution.py:470
  884.4 49.6 %collective-permute-start.48 = (bf16[2,128,1024]{2,1,0:T(8,128)(2,1)S(1)}, bf16[2,128,1024]{2,1,0:T(8,128)(2,1)S(1)}, u32[]{:S(2)}, u32[]{:S(2)}) collective-permute-start(bf16[2,128,1024]{2,1,0:T(8,128)(2,1)S(1)} %slice_bitcast_fusion.33), channel_id=1, source_target_pairs={{0,4},{4,0},{1,5},{5,1},{2,6},{6,2},{3,7},{7,3},{8,12},{12,8},{9,1... | collective-permute-start | bytes 1572872 | tf_op jit(solution)/shard_map/cond/branch_1_fun/ppermute | solution.py:240
  886.4 49.3 %collective-permute-start.46 = (bf16[2,128,1024]{2,1,0:T(8,128)(2,1)S(1)}, bf16[2,128,1024]{2,1,0:T(8,128)(2,1)S(1)}, u32[]{:S(2)}, u32[]{:S(2)}) collective-permute-start(bf16[2,128,1024]{2,1,0:T(8,128)(2,1)S(1)} %slice_bitcast_fusion.35), channel_id=1, source_target_pairs={{0,2},{2,0},{1,3},{3,1},{4,6},{6,4},{5,7},{7,5},{8,10},{10,8},{9,1... | collective-permute-start | bytes 1572872 | tf_op jit(solution)/shard_map/cond/branch_1_fun/ppermute | solution.py:240
  949.3 109.0 %all-to-all-start.3 = ((bf16[8,3,256,256]{3,2,1,0:T(8,128)(2,1)}), bf16[8,3,256,256]{3,2,1,0:T(8,128)(2,1)S(1)}, u32[]{:S(2)}, u32[]{:S(2)}) async-start(bf16[8,3,256,256]{3,2,1,0:T(8,128)(2,1)} %bitcast.357), calls=%async_computation.7 | async-start | bytes 6291456 | tf_op jit(solution)/shard_map/all_to_all | solution.py:577
  997.6 58.3 %collective-permute-start.81 = (bf16[256,2048]{1,0:T(8,128)(2,1)S(1)}, bf16[256,2048]{1,0:T(8,128)(2,1)S(1)}, u32[]{:S(2)}, u32[]{:S(2)}) collective-permute-start(bf16[256,2048]{1,0:T(8,128)(2,1)S(1)} %maximum_select_fusion), channel_id=1, source_target_pairs={{0,3},{2,1},{4,7},{6,5},{9,10},{11,8},{13,14},{15,12},{16,19},{18,... | collective-permute-start | bytes 3145736 | tf_op jit(solution)/shard_map/ppermute | solution.py:473
  999.0 57.0 %collective-permute-start.80 = (bf16[256,2048]{1,0:T(8,128)(2,1)S(1)}, bf16[256,2048]{1,0:T(8,128)(2,1)S(1)}, u32[]{:S(2)}, u32[]{:S(2)}) collective-permute-start(bf16[256,2048]{1,0:T(8,128)(2,1)S(1)} %maximum_select_fusion), channel_id=1, source_target_pairs={{0,2},{2,0},{4,6},{6,4},{9,11},{11,9},{13,15},{15,13},{16,18},{18,... | collective-permute-start | bytes 3145736 | tf_op jit(solution)/shard_map/ppermute | solution.py:473
  1001.4 54.6 %collective-permute-start.79 = (bf16[256,2048]{1,0:T(8,128)(2,1)S(1)}, bf16[256,2048]{1,0:T(8,128)(2,1)S(1)}, u32[]{:S(2)}, u32[]{:S(2)}) collective-permute-start(bf16[256,2048]{1,0:T(8,128)(2,1)S(1)} %maximum_select_fusion), channel_id=1, source_target_pairs={{0,1},{2,3},{4,5},{6,7},{9,8},{11,10},{13,12},{15,14},{16,17},{18,... | collective-permute-start | bytes 3145736 | tf_op jit(solution)/shard_map/ppermute | solution.py:473
  (170 other events, 2710.1 us)
Sparse Core Ops, SparseCore 0:
  76.2 65.1 all-gather.5
  156.4 47.3 all-gather.7
  205.4 96.7 all-gather.9
  303.6 79.1 all-gather.11
  408.7 82.0 all-gather.13
  532.7 77.9 reduce-scatter.5
  613.1 77.2 reduce-scatter.9
  705.8 95.2 reduce-scatter.7
  827.2 60.8 reduce-scatter.11
  890.8 43.8 reduce-scatter.13

commit v5 on v4

--- a/solution.py
+++ b/solution.py
@@ -3,6 +3,7 @@
 import numpy as np
 from jax import lax
 from jax.experimental import pallas as pl
+from jax.experimental.layout import Layout, with_layout_constraint
 from jax.experimental.pallas import tpu as pltpu
 from jax.sharding import Mesh
 from jax.sharding import PartitionSpec as P
@@ -130,39 +131,6 @@
     )(which, index, *sources)
 
 
-def pack_gradients(groups, which, column, rows, width, slots):
-    n_src = len(groups)
-
-    def kernel(which_ref, column_ref, *refs):
-        place = pl.program_id(0) * slots + pl.program_id(1)
-        out_ref = refs[n_src]
-        for number in range(n_src):
-
-            @pl.when(which_ref[place] == number)
-            def _():
-                out_ref[0, 0] = refs[number][...]
-
-    def spec(number):
-        def at(rank, k, which, column):
-            place = rank * slots + k
-            return (rank // 4, jnp.where(which[place] == number, column[place], 0))
-
-        return pl.BlockSpec((rows, width), at)
-
-    return pl.pallas_call(
-        kernel,
-        out_shape=jax.ShapeDtypeStruct((8, slots, rows, width), bf16),
-        grid_spec=pltpu.PrefetchScalarGridSpec(
-            num_scalar_prefetch=2,
-            grid=(8, slots),
-            in_specs=[spec(number) for number in range(n_src)],
-            out_specs=pl.BlockSpec((1, 1, rows, width), lambda rank, k, which, column: (rank, k, 0, 0)),
-        ),
-        compiler_params=pltpu.CompilerParams(vmem_limit_bytes=VMEM_LIMIT),
-        name="pack_gradients",
-    )(which, column, *groups)
-
-
 def adam_tiles(master, one, two, columns_from, rows_from, visit, mode, column_place, row_place, hold, previous=None):
     _, rows, columns = master.shape
     width = columns // 8
@@ -197,7 +165,8 @@
 
     def column_spec(number):
         def at(n, b, vi, mo, cp, rp, ho):
-            return (jnp.where(mo[n] == number + 2, cp[n * 8 + block_of(n, b, ho)], 0), 0, 0)
+            place = jnp.where(mo[n] == number + 2, cp[n * 8 + block_of(n, b, ho)], 0)
+            return (place // 8, 0, place % 8)
 
         return pl.BlockSpec((1, rows, width), at)
 
@@ -250,6 +219,15 @@
     return jnp.concatenate([four, swap(four, "c")], axis=0)
 
 
+def spread_columns(value):
+    rows = value.shape[0] // 2
+    low = lax.axis_index("x") == 0
+    upper, lower = value[:rows], value[rows:]
+    two = jnp.stack([jnp.where(low, upper, lower), swap(jnp.where(low, lower, upper), "x")])
+    four = jnp.concatenate([two, swap(two, "y")])
+    return jnp.concatenate([four, swap(four, "c")])
+
+
 def scatter_rows(part):
     rows, width = part.shape[0] // 8, part.shape[1]
     half = width // 2
@@ -340,8 +318,14 @@
         got = lax.all_to_all(pack_columns(weights, table, first, half_cap), PLANE, 0, 0, tiled=True)
         return got.reshape(8 * half_cap, rows, block)
 
+    def my_block(slot):
+        return lax.dynamic_index_in_dim(master, slot, 0, keepdims=False).astype(bf16)
+
+    h0 = tokens.astype(f32)
+    outer_blocks = [my_block(row_slots[mask]) for mask in range(4)]
+    a_in = normalize(h0, gains[0]).astype(bf16)
     received = [exchange_columns(0, after(master, column_part, column_place, row_slots, row_owners))]
-    received.append(exchange_columns(half_cap, after(master, received[0])))
+    received = [after(received[0], a_in, *outer_blocks)]
 
     def columns_here(first, count, parts):
         chosen = slice(2 * first, 2 * (first + count))
@@ -350,20 +334,17 @@
     def gather_z(value):
         return lax.all_gather(value, "z", axis=0, tiled=True)
 
-    w_qkv = gather_z(columns_here(0, 3, 1))
-
-    def my_block(slot):
-        return lax.dynamic_index_in_dim(master, slot, 0, keepdims=False).astype(bf16)
-
-    h0 = tokens.astype(f32)
-    a_all = gather_rows(after(normalize(h0, gains[0]).astype(bf16), received[1]))
-
-    def take_rows(kind, keep_pair, *earlier):
+    local = columns_here(0, 3, 1)
+    w_qkv = gather_z(local)
+    received.append(exchange_columns(half_cap, after(master, local)))
+    a_all = gather_rows(after(a_in, local))
+
+    def take_rows(kind, blocks, keep_pair, earlier):
         found = None
         source = row_owners[kind] ^ f
-        for mask in range(4):
-            got = after(my_block(row_slots[4 * kind + mask]), *earlier)
+        for mask, got in enumerate(blocks):
             if mask:
+                got = after(got, earlier)
                 got = lax.ppermute(got, ALL_AXES, flip_pairs(mask, keep_pair))
             found = got if found is None else jnp.where(source == mask, got, found)
         return found
@@ -371,7 +352,7 @@
     def needs_outer(zz, place, target):
         return target % 4 in (zz, (zz + 2) % 4)
 
-    outer = take_rows(0, needs_outer, received[0])
+    outer = take_rows(0, outer_blocks, needs_outer, local)
     half_rows = rows // 2
     odd = z % 2
     to_pair = lax.dynamic_slice_in_dim(outer, (1 - odd) * half_rows, half_rows, 0)
@@ -392,9 +373,9 @@
     w_cross = gather_z(columns_here(3, 5, 2))
     w_in = gather_z(columns_here(8, 4, 2))
     slots, ctx_len, ctx_width = context.shape
-    ctx_all = gather_rows(after(context.reshape(slots * ctx_len, ctx_width), a_all))
-    out_rows = take_rows(1, None, ctx_all)
-    w_out = gather_z(out_rows)
+    ctx = context.reshape(slots * ctx_len, ctx_width)
+    ctx_x = swap(after(ctx, a_all), "x")
+    ctx_y = swap(after(ctx, a_all), "y")
 
     seg = segments(lengths[0], count)
     live = keep == 1
@@ -405,17 +386,12 @@
     live_all = (code % 2 == 1).reshape(8, count)
 
     grad_out = cotangent.astype(f32) * live.astype(f32)[:, None]
-    d_ff = gather_rows(after(grad_out.astype(bf16), out_rows))
-
     present = owners[0] >= 0
 
-    def gather_step(value):
-        shape = jax.ShapeDtypeStruct((8 * value.shape[0], value.shape[1]), value.dtype)
-        return lax.cond(present, gather_rows, lambda _: jnp.zeros(shape.shape, shape.dtype), value)
-
-    def scatter_step(part):
-        shape = (part.shape[0] // 8, part.shape[1])
-        return lax.cond(present, scatter_rows, lambda _: jnp.zeros(shape, f32), part)
+    def chain_step(move, *values):
+        shapes = jax.eval_shape(move, *values)
+        idle = jax.tree.map(lambda leaf: jnp.zeros(leaf.shape, leaf.dtype), shapes)
+        return lax.cond(present, move, lambda *_: idle, *values)
 
     def split(value):
         return value.reshape(8, -1, heads_here, head_dim)
@@ -443,9 +419,20 @@
     probs = probabilities(query, keys, allowed)
     probs_low = probs.astype(bf16)
     attended = joined(weighted(probs_low, values))
-    part = matmul(attended, w_self_out)
-    h1 = h0 + scatter_step(part)
-    b_all = gather_step(normalize(h1, gains[1]).astype(bf16))
+    half = slots * ctx_len // 2
+    far_low = swap(after(ctx_y, attended)[:half], "x")
+    far_high = swap(after(ctx_x, attended)[half:], "y")
+    out_blocks = [my_block(row_slots[4 + mask]) for mask in range(4)]
+    out_rows = take_rows(1, out_blocks, None, attended)
+    w_out = gather_z(out_rows)
+    h1 = h0 + chain_step(scatter_rows, matmul(attended, w_self_out))
+    ctx_four = jnp.concatenate([ctx, ctx_y, ctx_x, far_low, far_high], axis=0)
+    ctx_all = jnp.concatenate([ctx_four, swap(ctx_four, "c")], axis=0)
+    b_all, d_ff = chain_step(
+        lambda one, two: (gather_rows(one), gather_rows(two)),
+        normalize(h1, gains[1]).astype(bf16),
+        grad_out.astype(bf16),
+    )
 
     w_cross_q = w_cross[:, :block]
     w_low = w_cross[:, block : 3 * block]
@@ -460,14 +447,16 @@
     cross_p = probabilities(cross_q, cross_k, own_item)
     cross_low = cross_p.astype(bf16)
     cross_o = joined(weighted(cross_low, cross_v))
-    h2 = h1 + scatter_step(matmul(cross_o, w_cross_out))
-    c_all = gather_step(normalize(h2, gains[2]).astype(bf16))
+    h2 = h1 + chain_step(scatter_rows, matmul(cross_o, w_cross_out))
+    c_all = chain_step(gather_rows, normalize(h2, gains[2]).astype(bf16))
 
     hidden = matmul(c_all, w_in)
     activated = gelu_tanh(hidden).astype(bf16)
 
     def sum_rows(value):
-        return lax.psum_scatter(value, "z", scatter_dimension=0, tiled=True)
+        value = with_layout_constraint(value, Layout(major_to_minor=(0, 1)))
+        value = lax.psum_scatter(value, "z", scatter_dimension=0, tiled=True)
+        return with_layout_constraint(value, Layout(major_to_minor=(0, 1)))
 
     def to_owners(value, keep_pair):
         moved = [lax.ppermute(value, ALL_AXES, flip_pairs(mask, keep_pair)) for mask in range(1, 4)]
@@ -476,14 +465,16 @@
     t_out = matmul_left(activated, d_ff).astype(bf16)
     g_out = sum_rows(t_out)
     d_act = matmul_right(after(d_ff, t_out), w_out)
-    layer_out = (h2 + scatter_step(matmul(activated, w_out))).astype(bf16)
     d_hidden = jax.vjp(gelu_tanh, hidden)[1](d_act)[0].astype(bf16)
     t_in = matmul_left(c_all, d_hidden).astype(bf16)
     g_in = sum_rows(t_in)
-    part = matmul_right(d_hidden, w_in)
-    part_two, gain_grad_two = jax.vjp(normalize, h2, gains[2])[1](scatter_step(part))
+    d_c, mixed = chain_step(
+        lambda one, two: (scatter_rows(one), scatter_rows(two)), matmul_right(d_hidden, w_in), matmul(activated, w_out)
+    )
+    layer_out = (h2 + mixed).astype(bf16)
+    part_two, gain_grad_two = jax.vjp(normalize, h2, gains[2])[1](d_c)
     dh2 = grad_out + part_two
-    d_cross_out = gather_step(after(dh2.astype(bf16), t_in))
+    d_cross_out = chain_step(gather_rows, after(dh2.astype(bf16), t_in))
     out_grads = to_owners(g_out, None)
     g_cross_out = matmul_left(cross_o, d_cross_out)
 
@@ -509,57 +500,56 @@
     )
     g_cross = sum_rows(t_cross)
     part = matmul_right(d_cq, w_cross_q)
-    part_one, gain_grad_one = jax.vjp(normalize, h1, gains[1])[1](scatter_step(part))
+    part_one, gain_grad_one = jax.vjp(normalize, h1, gains[1])[1](chain_step(scatter_rows, part))
     dh1 = dh2 + part_one
-    d_self_out = gather_step(after(dh1.astype(bf16), t_cross, out_grads))
+    d_self_out, in_grads = chain_step(
+        lambda one, two: (gather_rows(one), spread_columns(two)), after(dh1.astype(bf16), t_cross, out_grads), g_in
+    )
     g_self_out = matmul_left(attended, d_self_out)
-    g_outer = sum_rows(
-        jnp.concatenate(
-            [
-                jnp.where(low_y, g_self_out, g_cross_out).astype(bf16),
-                jnp.where(low_y, g_cross_out, g_self_out).astype(bf16),
-            ],
-            axis=0,
-        )
-    )
-    d_mixed = matmul_right(d_self_out, w_self_out)
+    t_outer = jnp.concatenate(
+        [
+            jnp.where(low_y, g_self_out, g_cross_out).astype(bf16),
+            jnp.where(low_y, g_cross_out, g_self_out).astype(bf16),
+        ],
+        axis=0,
+    )
+    g_outer = sum_rows(t_outer)
+    d_mixed = matmul_right(after(d_self_out, t_outer), w_self_out)
     d_q, d_k, d_v = through(d_mixed, query, keys, probs, probs_low, values)
     d_qkv = jnp.concatenate([d_q, d_k, d_v], axis=1)
     g_qkv = sum_rows(matmul_left(a_all, d_qkv).astype(bf16))
-    group_of = np.array([0, 0, 0, 0, 0, 0, 0, 0, 0, 0, 1, 1, 1, 1, 0, 0, 0, 0], np.int32)
-    column_of = np.array([0, 0, 0, 0, 0, 1, 3, 2, 4, 0, 0, 1, 2, 3, 0, 0, 0, 0], np.int32)
-    group_at = jnp.sum(jnp.where(holds, group_of, 0), axis=2)
-    column_at = jnp.sum(jnp.where(holds, column_of, 0), axis=2)
-    column_at = jnp.where(group_at == 1, (column_at + f) % 4, column_at)
-    sent = pack_gradients(
-        [g_cross, g_in],
-        jnp.tile(group_at.reshape(-1), 2),
-        jnp.tile(column_at.reshape(-1), 2),
-        rows,
-        block,
-        cap,
-    )
-    early_grads = lax.all_to_all(sent, PLANE, 0, 0, tiled=True).reshape(8 * cap, rows, block)
-    part = matmul_right(after(d_qkv, sent), w_qkv)
-    part_zero, gain_grad_zero = jax.vjp(normalize, h0, gains[0])[1](scatter_step(part))
+    d_a, cross_grads = chain_step(
+        lambda one, two: (scatter_rows(one), spread_columns(two)), matmul_right(d_qkv, w_qkv), g_cross
+    )
+    part_zero, gain_grad_zero = jax.vjp(normalize, h0, gains[0])[1](d_a)
     grad_tokens = (dh1 + part_zero).astype(bf16)
 
     gain_total = sum_everywhere(jnp.stack([gain_grad_zero, gain_grad_one, gain_grad_two]))
 
     place = np.arange(8)
-    source = (place % 2)[None, :] * 4 + ((place // 2)[None, :] - my_shift[:, None]) % 4
+    source_x, source_f = (place % 2)[None, :], ((place // 2)[None, :] - my_shift[:, None]) % 4
+    other = source_f ^ f
+    source = (other % 2) * 4 + (other // 2) * 2 + (source_x ^ x)
+    column_of = np.array([0, 1, 2, 0, 0, 1, 3, 2, 4, 0, 0, 0, 0, 0, 0, 0, 0, 0], np.int32)
+    my_column = jnp.sum(jnp.where(my_tile[:, None] == np.arange(n_tiles), column_of, 0), axis=1)
+    in_layer = (my_tile >= 10)[:, None]
+    column_place = source * 8 + jnp.where(in_layer, (place // 2)[None, :], my_column[:, None])
     row_source = ((z - my_shift) % 4) ^ f
     late = (my_used == 1) & ((my_tile < 4) | (my_tile == 9))
-    early_mode = jnp.where(my_used == 0, 1, jnp.where(late, 0, jnp.where(my_row == 1, 3, 2)))
+    early_mode = jnp.where(my_row == 1, 4, jnp.where(my_tile >= 10, 2, 3))
+    early_mode = jnp.where(my_used == 0, 1, jnp.where(late, 0, early_mode))
     states = (master, moment_one, moment_two)
     slot = np.arange(cap, dtype=np.int32)
+    by_tile = jnp.swapaxes(g_qkv.reshape(2, rows, 3, block), 1, 2)
+    sent = jnp.broadcast_to(by_tile[:, None], (2, 4, 3, rows, block)).reshape(8, 3, rows, block)
+    late_grads = lax.all_to_all(sent, PLANE, 0, 0, tiled=True).reshape(8 * 3, rows, block)
     early = adam_tiles(
         *states,
-        [early_grads],
+        [in_grads, cross_grads],
         [out_grads],
         slot,
-        after(early_mode, gain_total),
-        (source * cap + slot[:, None]).reshape(-1),
+        after(early_mode, gain_total, sent),
+        column_place.reshape(-1),
         row_source,
         np.zeros(cap, np.int32),
     )
@@ -571,11 +561,7 @@
         jnp.concatenate([g_outer, other_half], axis=0),
         jnp.concatenate([other_half, g_outer], axis=0),
     )
-    outer_grads = to_owners(after(outer_grad, early_grads), lambda zz, place, target: place % 4 in (zz, (zz + 2) % 4))
-    by_tile = jnp.swapaxes(g_qkv.reshape(2, rows, 3, block), 1, 2)
-    sent = jnp.broadcast_to(by_tile[:, None], (2, 4, 3, rows, block)).reshape(8, 3, rows, block)
-    late_grads = lax.all_to_all(sent, PLANE, 0, 0, tiled=True).reshape(8 * 3, rows, block)
-
+    outer_grads = to_owners(outer_grad, lambda zz, place, target: place % 4 in (zz, (zz + 2) % 4))
     n_late = 5
     order = jnp.sum(jnp.where(slot[None, :] < slot[:, None], late.astype(jnp.int32)[None, :], 0), axis=1)
     count_late = jnp.sum(late.astype(jnp.int32))
@@ -590,18 +576,18 @@
     tile = at_step(my_tile)
     some = count_late > 0
     visit = jnp.where(some, at_step(slot), 0)
-    first_mode = jnp.where(early_mode[0] == 3, 4, early_mode[0])
-    late_mode = jnp.where(at_step(my_row) == 1, 5, 3)
+    first_mode = jnp.where(early_mode[0] == 4, 5, early_mode[0])
+    late_mode = jnp.where(at_step(my_row) == 1, 6, 4)
     mode = jnp.where(hold == 1, 0, jnp.where(some, late_mode, first_mode))
-    late_place = (place % 2)[None, :] * 4 + (place // 2)[None, :]
-    column_place = jnp.where(some, late_place * 3 + tile[:, None], (source * cap + slot[:, None])[0][None, :])
+    late_place = ((place % 2)[None, :] * 4 + (place // 2)[None, :]) * 3 + tile[:, None]
+    late_place = jnp.where(some, late_place * 8, column_place[:1])
     new_w, new_m, new_v = adam_tiles(
         *states,
-        [early_grads, late_grads],
+        [in_grads, cross_grads, late_grads],
         [out_grads, outer_grads],
         visit,
         mode,
-        column_place.reshape(-1),
+        late_place.reshape(-1),
         jnp.where(some, at_step(row_source), row_source[0]),
         hold,
         early,

time: 1100 us -> 1180 us (1.073)
  waiting for transfers between devices: 475 us -> 543 us
  Pallas kernels: 102 us -> 77.8 us
  local copies, waits for them, and re-layouts: 146 us -> 159 us
    ppermute x6, waiting for transfers between devices: 0.02 us -> 52.4 us  [to_owners(): lax.ppermute(value, ALL_AXES, flip_pairs(mask, keep_pair))]
    all_to_all x2, waiting for transfers between devices: 36.9 us -> 10.6 us  [exchange_columns(): lax.all_to_all(pack_columns(weights, table, first, half_cap), PLANE, 0, 0...]
    ppermute x6, waiting for transfers between devices: 46.2 us -> 63.8 us  [take_rows(): got = lax.ppermute(got, ALL_AXES, flip_pairs(mask, keep_pair))]
    ppermute x1, waiting for transfers between devices: 0.01 us -> 17.4 us  [plane_body(): from_pair = lax.ppermute(to_pair, ALL_AXES, pair_swap)]
    pallas_call x1 -> x0, Pallas kernels: 17.1 us -> none  [pack_gradients(): pl.pallas_call(kernel, out_shape=jax.ShapeDtypeStruct((8, slots, rows, wi...]
    all_to_all x2, starting transfers between devices: 9.77 us -> 23.6 us  [exchange_columns(): lax.all_to_all(pack_columns(weights, table, first, half_cap), PLANE, 0, 0...]
    ppermute x71 -> x77, starting transfers between devices: 71 us -> 66.4 us  [swap(): return lax.ppermute(value, axis, [(0, 1), (1, 0)])]
    slice x6 -> x5, local copies, waits for them, and re-layouts: 24.7 us -> 27.3 us  [scatter_rows(): chip = part[0] + swap(part[1], 'c')]
  transfers between devices with their start and end apart: 101 -> 106, of which waited for: 57 -> 61; matrix products, arithmetic and copies ran while one was open for 30% -> 31% of each run, Pallas kernels for 7% -> 5%
where the time goes in v5:
time: 1180 us; the launch traced here: 1160 us
  waiting for transfers between devices  543 us (46%)
  matrix products  170 us (14%)
  local copies, waits for them, and re-layouts  159 us (13%)
  starting transfers between devices  116 us (10%)
  Pallas kernels  77.8 us (7%)
  other arithmetic  58.1 us (5%)
  between operations  36.6 us (3%)
    ppermute x77, waiting for transfers between devices, swap(): return lax.ppermute(value, axis, [(0, 1), (1, 0)])  394 us
    ppermute x77, starting transfers between devices, swap(): return lax.ppermute(value, axis, [(0, 1), (1, 0)])  66.4 us
    ppermute x6, waiting for transfers between devices, take_rows(): got = lax.ppermute(got, ALL_AXES, flip_pairs(mask, keep_pair))  63.8 us
    pallas_call x2, Pallas kernels, adam_tiles(): pl.pallas_call(kernel, out_shape=(shape, shape, shape), grid_spec=pltpu.P...  61 us
    dot_general x8, matrix products, matmul_left(): lax.dot_general(left, right, (((0,), (0,)), ((), ())), preferred_element_...  54.8 us
    dot_general x8, matrix products, matmul(): return jnp.dot(left, right, preferred_element_type=f32)  54.5 us
    ppermute x6, waiting for transfers between devices, to_owners(): lax.ppermute(value, ALL_AXES, flip_pairs(mask, keep_pair))  52.4 us
    unnamed x181, local copies, waits for them, and re-layouts  43 us
  transfers between devices with their start and end apart: 106, of which 61 were waited for; matrix products, arithmetic and copies ran while one was open for 31% of the time, Pallas kernels for 5%

profile of v5, /device:TPU:0, one launch (start us, length us, event | category | flops | bytes accessed | tf_op | source)
XLA Modules:
  0.0 1161.4 jit_solution(14105723632257256105)
XLA Ops:
  73.0 18.5 %collective-permute-done.69 = bf16[256,2048]{1,0:T(8,128)(2,1)} collective-permute-done((bf16[256,2048]{1,0:T(8,128)(2,1)}, bf16[256,2048]{1,0:T(8,128)(2,1)}, u32[]{:S(2)}, u32[]{:S(2)}) %collective-permute-start.69) | collective-permute-done | bytes 1048608 | tf_op jit(solution)/shard_map/ppermute | solution.py:348
  99.0 17.4 %collective-permute-done.72 = bf16[128,2048]{1,0:T(8,128)(2,1)} collective-permute-done((bf16[128,2048]{1,0:T(8,128)(2,1)}, bf16[128,2048]{1,0:T(8,128)(2,1)}, u32[]{:S(2)}, u32[]{:S(2)}) %collective-permute-start.72) | collective-permute-done | bytes 524320 | tf_op jit(solution)/shard_map/ppermute | solution.py:366
  124.5 18.3 %all-to-all-start.1 = ((bf16[8,3,256,256]{3,2,1,0:T(8,128)(2,1)}), bf16[8,3,256,256]{3,2,1,0:T(8,128)(2,1)}, u32[]{:S(2)}, u32[]{:S(2)}) async-start(bf16[8,3,256,256]{3,2,1,0:T(8,128)(2,1)} %copy-done.2), calls=%async_computation.1 | async-start | bytes 6291456 | tf_op jit(solution)/shard_map/all_to_all | solution.py:318
  148.3 43.1 %collective-permute-done.62 = bf16[128,2048]{1,0:T(8,128)(2,1)S(1)} collective-permute-done((bf16[128,2048]{1,0:T(8,128)(2,1)}, bf16[128,2048]{1,0:T(8,128)(2,1)S(1)}, u32[]{:S(2)}, u32[]{:S(2)}) %collective-permute-start.62) | collective-permute-done | bytes 524320 | tf_op jit(solution)/shard_map/ppermute | solution.py:209
  253.4 18.7 %collective-permute-done.74 = bf16[256,4096]{1,0:T(8,128)(2,1)} collective-permute-done((bf16[256,4096]{1,0:T(8,128)(2,1)}, bf16[256,4096]{1,0:T(8,128)(2,1)}, u32[]{:S(2)}, u32[]{:S(2)}) %collective-permute-start.74) | collective-permute-done | bytes 2097184 | tf_op jit(solution)/shard_map/ppermute | solution.py:209
  315.8 37.3 %conditional.9 = (f32[128,2048]{1,0:T(8,128)S(1)}) conditional(s32[]{:T(128)} %bitcast.64, () %tuple.89, f32[1024,2048]{1,0:T(8,128)} %fusion.125), branch_computations={%region_10.11_spmd, %region_11.12_spmd} | conditional | flops 2883584 | bytes 65536208 | solution.py:394
  353.9 42.6 %conditional.10 = (bf16[1024,2048]{1,0:T(8,128)(2,1)}, bf16[1024,2048]{1,0:T(8,128)(2,1)}) conditional(s32[]{:T(128)} %bitcast.64, () %tuple.101, (bf16[128,2048]{1,0:T(8,128)(2,1)S(1)}, bf16[128,2048]{1,0:T(8,128)(2,1)S(1)}) %tuple.102), branch_computations={%region_13.14_spmd, %region_14.15_spmd} | conditional | bytes 52429216 | solution.py:394
  401.6 20.3 %collective-permute-done.78 = bf16[256,2048]{1,0:T(8,128)(2,1)S(1)} collective-permute-done((bf16[256,2048]{1,0:T(8,128)(2,1)}, bf16[256,2048]{1,0:T(8,128)(2,1)S(1)}, u32[]{:S(2)}, u32[]{:S(2)}) %collective-permute-start.78) | collective-permute-done | bytes 1048608 | tf_op jit(solution)/shard_map/ppermute | solution.py:348
  421.9 23.1 %collective-permute-done.79 = bf16[256,2048]{1,0:T(8,128)(2,1)} collective-permute-done((bf16[256,2048]{1,0:T(8,128)(2,1)}, bf16[256,2048]{1,0:T(8,128)(2,1)}, u32[]{:S(2)}, u32[]{:S(2)}) %collective-permute-start.79) | collective-permute-done | bytes 1048608 | tf_op jit(solution)/shard_map/ppermute | solution.py:348
  493.8 35.4 %conditional.11 = (f32[128,2048]{1,0:T(8,128)S(1)}) conditional(s32[]{:T(128)} %bitcast.64, () %tuple.96, f32[1024,2048]{1,0:T(8,128)} %fusion.112), branch_computations={%region_17.18_spmd, %region_18.19_spmd} | conditional | flops 2883584 | bytes 65536208 | solution.py:394
  529.6 27.1 %conditional.12 = (bf16[1024,2048]{1,0:T(8,128)(2,1)}) conditional(s32[]{:T(128)} %bitcast.64, () %tuple.104, bf16[128,2048]{1,0:T(8,128)(2,1)S(1)} %multiply_convert_fusion.4), branch_computations={%region_20.21_spmd, %region_21.22_spmd} | conditional | bytes 26214608 | solution.py:394
  611.0 52.8 %conditional.13 = (f32[128,2048]{1,0:T(8,128)S(1)}, f32[128,2048]{1,0:T(8,128)S(1)}) conditional(s32[]{:T(128)} %bitcast.64, () %tuple.103, (f32[1024,2048]{1,0:T(8,128)}, f32[1024,2048]{1,0:T(8,128)S(1)}) %tuple.109), branch_computations={%region_22.23_spmd, %region_23.24_spmd} | conditional | flops 5767168 | bytes 131072416 | solution.py:394
  666.9 28.3 %conditional.14 = (bf16[1024,2048]{1,0:T(8,128)(2,1)}) conditional(s32[]{:T(128)} %bitcast.64, () %tuple.111, bf16[128,2048]{1,0:T(8,128)(2,1)} %get-tuple-element.102), branch_computations={%region_25.26_spmd, %region_26.27_spmd} | conditional | bytes 26214608 | solution.py:394
  743.3 34.9 %conditional.15 = (f32[128,2048]{1,0:T(8,128)S(1)}) conditional(s32[]{:T(128)} %bitcast.64, () %tuple.110, f32[1024,2048]{1,0:T(8,128)} %fusion.102), branch_computations={%region_28.29_spmd, %region_29.30_spmd} | conditional | flops 2883584 | bytes 65536208 | solution.py:394
  786.9 18.0 %collective-permute-done.82 = bf16[256,2048]{1,0:T(8,128)(2,1)S(1)} collective-permute-done((bf16[256,2048]{1,0:T(8,128)(2,1)}, bf16[256,2048]{1,0:T(8,128)(2,1)S(1)}, u32[]{:S(2)}, u32[]{:S(2)}) %collective-permute-start.82) | collective-permute-done | bytes 1048608 | tf_op jit(solution)/shard_map/ppermute | solution.py:462
  804.9 18.9 %collective-permute-done.83 = bf16[256,2048]{1,0:T(8,128)(2,1)S(1)} collective-permute-done((bf16[256,2048]{1,0:T(8,128)(2,1)}, bf16[256,2048]{1,0:T(8,128)(2,1)S(1)}, u32[]{:S(2)}, u32[]{:S(2)}) %collective-permute-start.83) | collective-permute-done | bytes 1048608 | tf_op jit(solution)/shard_map/ppermute | solution.py:462
  826.0 56.7 %conditional.16 = (bf16[1024,2048]{1,0:T(8,128)(2,1)}, bf16[8,256,1024]{2,1,0:T(8,128)(2,1)S(1)}) conditional(s32[]{:T(128)} %bitcast.64, () %tuple.114, (bf16[128,2048]{1,0:T(8,128)(2,1)S(1)}, bf16[512,1024]{1,0:T(8,128)(2,1)}) %tuple.262), branch_computations={%region_33.34_spmd, %region_34.35_spmd} | conditional | flops 9437188 | bytes 57672056 | solution.py:394
  859.4 18.3 %collective-permute-done.26 = bf16[2,256,1024]{2,1,0:T(8,128)(2,1)S(1)} collective-permute-done((bf16[2,256,1024]{2,1,0:T(8,128)(2,1)S(1)}, bf16[2,256,1024]{2,1,0:T(8,128)(2,1)S(1)}, u32[]{:S(2)}, u32[]{:S(2)}) %collective-permute-start.26) | collective-permute-done | bytes 1048608 | tf_op jit(solution)/shard_map/cond/branch_1_fun/ppermute | solution.py:209
  922.1 82.8 %conditional.17 = (f32[128,2048]{1,0:T(8,128)S(1)}, bf16[8,256,1280]{2,1,0:T(8,128)(2,1)S(1)}) conditional(s32[]{:T(128)} %bitcast.64, () %tuple.113, (f32[1024,2048]{1,0:T(8,128)}, bf16[512,1280]{1,0:T(8,128)(2,1)}) %tuple.118), branch_computations={%region_37.38_spmd, %region_38.39_spmd} | conditional | flops 14680068 | bytes 126878128 | solution.py:394
  930.7 17.1 %collective-permute-done.58 = bf16[256,1280]{1,0:T(8,128)(2,1)S(1)} collective-permute-done((bf16[256,1280]{1,0:T(8,128)(2,1)S(1)}, bf16[256,1280]{1,0:T(8,128)(2,1)S(1)}, u32[]{:S(2)}, u32[]{:S(2)}) %collective-permute-start.58) | collective-permute-done | bytes 655392 | tf_op jit(solution)/shard_map/cond/branch_1_fun/ppermute | solution.py:209
  947.9 30.4 %collective-permute-done.59 = bf16[2,256,1280]{2,1,0:T(8,128)(2,1)S(1)} collective-permute-done((bf16[2,256,1280]{2,1,0:T(8,128)(2,1)S(1)}, bf16[2,256,1280]{2,1,0:T(8,128)(2,1)S(1)}, u32[]{:S(2)}, u32[]{:S(2)}) %collective-permute-start.59) | collective-permute-done | bytes 1310752 | tf_op jit(solution)/shard_map/cond/branch_1_fun/ppermute | solution.py:209
  1020.6 34.0 %collective-permute-done.90 = f32[3,2048]{1,0:T(4,128)S(1)} collective-permute-done((f32[3,2048]{1,0:T(4,128)S(1)}, f32[3,2048]{1,0:T(4,128)S(1)}, u32[]{:S(2)}, u32[]{:S(2)}) %collective-permute-start.90) | collective-permute-done | bytes 24608 | tf_op jit(solution)/shard_map/ppermute | solution.py:209
  1093.1 41.2 %adam_tiles.2 = (f32[6,256,2048]{2,1,0:T(8,128)}, f32[6,256,2048]{2,1,0:T(8,128)}, f32[6,256,2048]{2,1,0:T(8,128)}) custom-call(s32[6]{0:T(128)S(1)} %call_exported.3.visit_ref, s32[6]{0:T(128)S(1)} %get-tuple-element.109.mode_ref, s32[48]{0:T(128)S(1)} %multiply_add_fusion.4.cp_ref, s32[6]{0:T(128)S(1)} %fusion.165.rp_ref, s32[6]{0:T(128)S(1)} %broadcast.529.hold_ref, ...), custom_call_target="tpu_custom_call" | custom-call | tf_op jit(solution)/shard_map/adam_tiles/pallas_call | solution.py:182
  1134.3 19.7 %adam_tiles.3 = (f32[6,256,2048]{2,1,0:T(8,128)}, f32[6,256,2048]{2,1,0:T(8,128)}, f32[6,256,2048]{2,1,0:T(8,128)}) custom-call(s32[5]{0:T(128)S(1)} %get-tuple-element.288.visit_ref, s32[5]{0:T(128)S(1)} %get-tuple-element.287.mode_ref, s32[40]{0:T(128)S(1)} %select_n.452.cp_ref, ...), custom_call_target="tpu_custom_call", output_to_operand_aliasing={{0}: (13, {}), {1}: (14, {}), {2}: (15, {})} | custom-call | tf_op jit(solution)/shard_map/adam_tiles/pallas_call | solution.py:182
  (694 shorter events, 765.9 us)
Async XLA Ops:
  21.7 42.2 %all-to-all-start = ((bf16[8,3,256,256]{3,2,1,0:T(8,128)(2,1)}), bf16[8,3,256,256]{3,2,1,0:T(8,128)(2,1)S(1)}, u32[]{:S(2)}, u32[]{:S(2)}) async-start(bf16[8,3,256,256]{3,2,1,0:T(8,128)(2,1)} %copy-done.1), calls=%async_computation | async-start | bytes 6291456 | tf_op jit(solution)/shard_map/all_to_all | solution.py:318
  27.0 199.7 %all-gather.6.cloned.1.call-start = ((), (), s32[]{:S(2)}) async-start(), calls=%async_computation.8 | async-start | bytes 3932160 | tf_op jit(solution)/shard_map/all_gather | solution.py:335
  65.7 243.8 %all-gather.8.cloned.1.call-start = ((), (), s32[]{:S(2)}) async-start(), calls=%async_computation.9 | async-start | bytes 2621440 | tf_op jit(solution)/shard_map/all_gather | solution.py:368
  124.5 80.2 %all-to-all-start.1 = ((bf16[8,3,256,256]{3,2,1,0:T(8,128)(2,1)}), bf16[8,3,256,256]{3,2,1,0:T(8,128)(2,1)}, u32[]{:S(2)}, u32[]{:S(2)}) async-start(bf16[8,3,256,256]{3,2,1,0:T(8,128)(2,1)} %copy-done.2), calls=%async_computation.1 | async-start | bytes 6291456 | tf_op jit(solution)/shard_map/all_to_all | solution.py:318
  142.8 305.1 %all-gather.10.cloned.1.call-start = ((), (), s32[]{:S(2)}) async-start(), calls=%async_computation.10 | async-start | bytes 6553600 | tf_op jit(solution)/shard_map/all_gather | solution.py:335
  142.8 48.5 %collective-permute-start.62 = (bf16[128,2048]{1,0:T(8,128)(2,1)}, bf16[128,2048]{1,0:T(8,128)(2,1)S(1)}, u32[]{:S(2)}, u32[]{:S(2)}) collective-permute-start(bf16[128,2048]{1,0:T(8,128)(2,1)} %fusion.79), channel_id=1, source_target_pairs={{0,4},{4,0},{1,5},{5,1},{2,6},{6,2},{3,7},{7,3},{8,12},{12,8},{9,1... | collective-permute-start | bytes 1572872 | tf_op jit(solution)/shard_map/ppermute | solution.py:209
  144.8 48.1 %collective-permute-start.61 = (bf16[128,2048]{1,0:T(8,128)(2,1)}, bf16[128,2048]{1,0:T(8,128)(2,1)S(1)}, u32[]{:S(2)}, u32[]{:S(2)}) collective-permute-start(bf16[128,2048]{1,0:T(8,128)(2,1)} %fusion.79), channel_id=1, source_target_pairs={{0,2},{2,0},{1,3},{3,1},{4,6},{6,4},{5,7},{7,5},{8,10},{10,8},{9,1... | collective-permute-start | bytes 1572872 | tf_op jit(solution)/shard_map/ppermute | solution.py:209
  209.5 347.2 %all-gather.12.cloned.1.call-start = ((), (), s32[]{:S(2)}) async-start(), calls=%async_computation.11 | async-start | bytes 5242880 | tf_op jit(solution)/shard_map/all_gather | solution.py:335
  224.0 48.1 %collective-permute-start.74 = (bf16[256,4096]{1,0:T(8,128)(2,1)}, bf16[256,4096]{1,0:T(8,128)(2,1)}, u32[]{:S(2)}, u32[]{:S(2)}) collective-permute-start(bf16[256,4096]{1,0:T(8,128)(2,1)} %bitcast.80), channel_id=1, source_target_pairs={{0,4},{4,0},{1,5},{5,1},{2,6},{6,2},{3,7},{7,3},{8,12},{12,8},{9,1... | collective-permute-start | bytes 6291464 | tf_op jit(solution)/shard_map/ppermute | solution.py:209
  226.0 48.0 %collective-permute-start.73 = (bf16[256,4096]{1,0:T(8,128)(2,1)}, bf16[256,4096]{1,0:T(8,128)(2,1)}, u32[]{:S(2)}, u32[]{:S(2)}) collective-permute-start(bf16[256,4096]{1,0:T(8,128)(2,1)} %bitcast.80), channel_id=1, source_target_pairs={{0,2},{2,0},{1,3},{3,1},{4,6},{6,4},{5,7},{7,5},{8,10},{10,8},{9,1... | collective-permute-start | bytes 6291464 | tf_op jit(solution)/shard_map/ppermute | solution.py:209
  303.1 149.7 %collective-permute-start.77 = (bf16[1024,4096]{1,0:T(8,128)(2,1)}, bf16[1024,4096]{1,0:T(8,128)(2,1)}, u32[]{:S(2)}, u32[]{:S(2)}) collective-permute-start(bf16[1024,4096]{1,0:T(8,128)(2,1)} %get-tuple-element.241), channel_id=1, source_target_pairs={{0,1},{1,0},{2,3},{3,2},{4,5},{5,4},{6,7},{7,6},{8,9},{9,8},{10,11... | collective-permute-start | bytes 25165832 | tf_op jit(solution)/shard_map/ppermute | solution.py:209
  308.1 267.1 %all-gather.14.cloned.1.call-start = ((), (), s32[]{:S(2)}) async-start(), calls=%async_computation.12 | async-start | bytes 5242880 | tf_op jit(solution)/shard_map/all_gather | solution.py:335
  397.8 47.1 %collective-permute-start.79 = (bf16[256,2048]{1,0:T(8,128)(2,1)}, bf16[256,2048]{1,0:T(8,128)(2,1)}, u32[]{:S(2)}, u32[]{:S(2)}) collective-permute-start(bf16[256,2048]{1,0:T(8,128)(2,1)} %get-tuple-element.98), channel_id=1, source_target_pairs={{0,2},{1,3},{2,0},{3,1},{4,6},{5,7},{6,4},{7,5},{8,10},{9,11},{10,... | collective-permute-start | bytes 3145736 | tf_op jit(solution)/shard_map/ppermute | solution.py:348
  447.8 330.7 %reduce-scatter.6.cloned.1.call-start = ((), (), s32[]{:S(2)}) async-start(), calls=%async_computation.13 | async-start | bytes 5242880 | tf_op jit(solution)/shard_map/reduce_scatter | solution.py:458
  574.9 251.1 %reduce-scatter.8.cloned.1.call-start = ((), (), s32[]{:S(2)}) async-start(), calls=%async_computation.14 | async-start | bytes 5242880 | tf_op jit(solution)/shard_map/reduce_scatter | solution.py:458
  596.1 326.0 %reduce-scatter.10.cloned.1.call-start = ((), (), s32[]{:S(2)}) async-start(), calls=%async_computation.15 | async-start | bytes 6553600 | tf_op jit(solution)/shard_map/reduce_scatter | solution.py:458
  736.0 273.1 %reduce-scatter.12.cloned.1.call-start = ((), (), s32[]{:S(2)}) async-start(), calls=%async_computation.16 | async-start | bytes 3932160 | tf_op jit(solution)/shard_map/reduce_scatter | solution.py:458
  780.0 43.7 %collective-permute-start.83 = (bf16[256,2048]{1,0:T(8,128)(2,1)}, bf16[256,2048]{1,0:T(8,128)(2,1)S(1)}, u32[]{:S(2)}, u32[]{:S(2)}) collective-permute-start(bf16[256,2048]{1,0:T(8,128)(2,1)} %reduce-scatter.6.cloned.1.call-done), channel_id=1, source_target_pairs={{0,3},{1,2},{2,1},{3,0},{4,7},{5,6},{6,5},{7,4},{8,11},{9,10},{10,... | collective-permute-start | bytes 3145736 | tf_op jit(solution)/shard_map/ppermute | solution.py:462
  909.1 108.1 %reduce-scatter.14.cloned.1.call-start = ((), (), s32[]{:S(2)}) async-start(), calls=%async_computation.17 | async-start | bytes 2621440 | tf_op jit(solution)/shard_map/reduce_scatter | solution.py:458
  930.4 48.3 %collective-permute-start.53 = (f32[2,2,128,2048]{3,2,1,0:T(8,128)}, f32[2,2,128,2048]{3,2,1,0:T(8,128)}, u32[]{:S(2)}, u32[]{:S(2)}) collective-permute-start(f32[2,2,128,2048]{3,2,1,0:T(8,128)} %bitcast.53), channel_id=1, source_target_pairs={{0,1},{1,0},{2,3},{3,2},{4,5},{5,4},{6,7},{7,6},{8,9},{9,8},{10,11... | collective-permute-start | bytes 12582920 | tf_op jit(solution)/shard_map/cond/branch_1_fun/ppermute | solution.py:209
  947.9 30.5 %collective-permute-start.59 = (bf16[2,256,1280]{2,1,0:T(8,128)(2,1)S(1)}, bf16[2,256,1280]{2,1,0:T(8,128)(2,1)S(1)}, u32[]{:S(2)}, u32[]{:S(2)}) collective-permute-start(bf16[2,256,1280]{2,1,0:T(8,128)(2,1)S(1)} %pad_maximum_fusion.10), channel_id=1, source_target_pairs={{0,2},{2,0},{1,3},{3,1},{4,6},{6,4},{5,7},{7,5},{8,10},{10,8},{9,1... | collective-permute-start | bytes 3932168 | tf_op jit(solution)/shard_map/cond/branch_1_fun/ppermute | solution.py:209
  1013.3 121.1 %all-to-all-start.2 = ((bf16[8,3,256,256]{3,2,1,0:T(8,128)(2,1)}), bf16[8,3,256,256]{3,2,1,0:T(8,128)(2,1)S(1)}, u32[]{:S(2)}, u32[]{:S(2)}) async-start(bf16[8,3,256,256]{3,2,1,0:T(8,128)(2,1)} %bitcast.371), calls=%async_computation.6 | async-start | bytes 6291456 | tf_op jit(solution)/shard_map/all_to_all | solution.py:545
  1017.2 42.3 %collective-permute-start.84 = (bf16[128,2048]{1,0:T(8,128)(2,1)}, bf16[128,2048]{1,0:T(8,128)(2,1)}, u32[]{:S(2)}, u32[]{:S(2)}) collective-permute-start(bf16[128,2048]{1,0:T(8,128)(2,1)} %reduce-scatter.14.cloned.1.call-done), channel_id=1, source_target_pairs={{8,0},{10,2},{12,4},{14,6},{1,9},{3,11},{5,13},{7,15},{24,16},{26,... | collective-permute-start | bytes 1572872 | tf_op jit(solution)/shard_map/ppermute | solution.py:558
  1018.6 36.1 %collective-permute-start.90 = (f32[3,2048]{1,0:T(4,128)S(1)}, f32[3,2048]{1,0:T(4,128)S(1)}, u32[]{:S(2)}, u32[]{:S(2)}) collective-permute-start(f32[3,2048]{1,0:T(4,128)S(1)} %fusion.247), channel_id=1, source_target_pairs={{0,4},{4,0},{1,5},{5,1},{2,6},{6,2},{3,7},{7,3},{8,12},{12,8},{9,1... | collective-permute-start | bytes 73736 | tf_op jit(solution)/shard_map/ppermute | solution.py:209
  (168 other events, 2644.9 us)
Sparse Core Ops, SparseCore 0:
  65.8 67.4 all-gather.5
  135.4 46.2 all-gather.7
  209.6 96.9 all-gather.9
  308.2 81.6 all-gather.11
  447.9 80.9 all-gather.13
  575.0 76.8 reduce-scatter.5
  654.3 77.2 reduce-scatter.7
  736.1 93.2 reduce-scatter.9
  909.2 59.9 reduce-scatter.11
  971.4 43.8 reduce-scatter.13

commit v6 on v5

--- a/solution.py
+++ b/solution.py
@@ -197,6 +197,9 @@
         ),
         input_output_aliases={n_before + n: n for n in range(len(kept))},
         compiler_params=pltpu.CompilerParams(vmem_limit_bytes=VMEM_LIMIT),
+        cost_estimate=pl.CostEstimate(
+            flops=30 * n_visit * rows * columns, bytes_accessed=26 * n_visit * rows * columns, transcendentals=0
+        ),
         name="adam_tiles",
     )(visit, mode, column_place, row_place, hold, master, one, two, *columns_from, *rows_from, *kept)
 
@@ -336,8 +339,8 @@
 
     local = columns_here(0, 3, 1)
     w_qkv = gather_z(local)
-    received.append(exchange_columns(half_cap, after(master, local)))
     a_all = gather_rows(after(a_in, local))
+    received.append(exchange_columns(half_cap, after(master, a_all)))
 
     def take_rows(kind, blocks, keep_pair, earlier):
         found = None
@@ -374,8 +377,8 @@
     w_in = gather_z(columns_here(8, 4, 2))
     slots, ctx_len, ctx_width = context.shape
     ctx = context.reshape(slots * ctx_len, ctx_width)
-    ctx_x = swap(after(ctx, a_all), "x")
-    ctx_y = swap(after(ctx, a_all), "y")
+    ctx_x = swap(after(ctx, received[1]), "x")
+    ctx_y = swap(after(ctx, received[1]), "y")
 
     seg = segments(lengths[0], count)
     live = keep == 1
@@ -419,20 +422,19 @@
     probs = probabilities(query, keys, allowed)
     probs_low = probs.astype(bf16)
     attended = joined(weighted(probs_low, values))
+    h1 = h0 + chain_step(scatter_rows, matmul(attended, w_self_out))
     half = slots * ctx_len // 2
-    far_low = swap(after(ctx_y, attended)[:half], "x")
-    far_high = swap(after(ctx_x, attended)[half:], "y")
-    out_blocks = [my_block(row_slots[4 + mask]) for mask in range(4)]
-    out_rows = take_rows(1, out_blocks, None, attended)
-    w_out = gather_z(out_rows)
-    h1 = h0 + chain_step(scatter_rows, matmul(attended, w_self_out))
-    ctx_four = jnp.concatenate([ctx, ctx_y, ctx_x, far_low, far_high], axis=0)
-    ctx_all = jnp.concatenate([ctx_four, swap(ctx_four, "c")], axis=0)
+    far_low = swap(after(ctx_y, h1)[:half], "x")
+    far_high = swap(after(ctx_x, h1)[half:], "y")
     b_all, d_ff = chain_step(
         lambda one, two: (gather_rows(one), gather_rows(two)),
         normalize(h1, gains[1]).astype(bf16),
         grad_out.astype(bf16),
     )
+    out_rows = take_rows(1, [my_block(row_slots[4 + mask]) for mask in range(4)], None, b_all)
+    w_out = gather_z(out_rows)
+    ctx_four = jnp.concatenate([ctx, ctx_y, ctx_x, far_low, far_high], axis=0)
+    ctx_all = jnp.concatenate([ctx_four, swap(ctx_four, "c")], axis=0)
 
     w_cross_q = w_cross[:, :block]
     w_low = w_cross[:, block : 3 * block]
@@ -458,9 +460,8 @@
         value = lax.psum_scatter(value, "z", scatter_dimension=0, tiled=True)
         return with_layout_constraint(value, Layout(major_to_minor=(0, 1)))
 
-    def to_owners(value, keep_pair):
-        moved = [lax.ppermute(value, ALL_AXES, flip_pairs(mask, keep_pair)) for mask in range(1, 4)]
-        return jnp.stack([value, *moved])
+    def from_other(value, mask, keep_pair=None):
+        return lax.ppermute(value, ALL_AXES, flip_pairs(mask, keep_pair))
 
     t_out = matmul_left(activated, d_ff).astype(bf16)
     g_out = sum_rows(t_out)
@@ -474,8 +475,11 @@
     layer_out = (h2 + mixed).astype(bf16)
     part_two, gain_grad_two = jax.vjp(normalize, h2, gains[2])[1](d_c)
     dh2 = grad_out + part_two
-    d_cross_out = chain_step(gather_rows, after(dh2.astype(bf16), t_in))
-    out_grads = to_owners(g_out, None)
+    d_cross_out, out_one, out_two = chain_step(
+        lambda one, two: (gather_rows(one), from_other(two, 1), from_other(two, 2)),
+        after(dh2.astype(bf16), t_in),
+        g_out,
+    )
     g_cross_out = matmul_left(cross_o, d_cross_out)
 
     def through(d_mixed, left, right, probs, probs_low, values):
@@ -500,10 +504,12 @@
     )
     g_cross = sum_rows(t_cross)
     part = matmul_right(d_cq, w_cross_q)
-    part_one, gain_grad_one = jax.vjp(normalize, h1, gains[1])[1](chain_step(scatter_rows, part))
+    d_b, out_three = chain_step(lambda one, two: (scatter_rows(one), from_other(two, 3)), part, g_out)
+    out_grads = jnp.stack([g_out, out_one, out_two, out_three])
+    part_one, gain_grad_one = jax.vjp(normalize, h1, gains[1])[1](d_b)
     dh1 = dh2 + part_one
     d_self_out, in_grads = chain_step(
-        lambda one, two: (gather_rows(one), spread_columns(two)), after(dh1.astype(bf16), t_cross, out_grads), g_in
+        lambda one, two: (gather_rows(one), spread_columns(two)), after(dh1.astype(bf16), t_cross), g_in
     )
     g_self_out = matmul_left(attended, d_self_out)
     t_outer = jnp.concatenate(
@@ -513,19 +519,32 @@
         ],
         axis=0,
     )
-    g_outer = sum_rows(t_outer)
-    d_mixed = matmul_right(after(d_self_out, t_outer), w_self_out)
+    g_outer = sum_rows(after(t_outer, g_cross))
+    d_mixed = matmul_right(after(d_self_out, t_outer, g_cross), w_self_out)
     d_q, d_k, d_v = through(d_mixed, query, keys, probs, probs_low, values)
     d_qkv = jnp.concatenate([d_q, d_k, d_v], axis=1)
     g_qkv = sum_rows(matmul_left(a_all, d_qkv).astype(bf16))
-    d_a, cross_grads = chain_step(
-        lambda one, two: (scatter_rows(one), spread_columns(two)), matmul_right(d_qkv, w_qkv), g_cross
-    )
-    part_zero, gain_grad_zero = jax.vjp(normalize, h0, gains[0])[1](d_a)
+
+    def last_step(part, grads, gain_grad_one, gain_grad_two):
+        part_zero, gain_grad_zero = jax.vjp(normalize, h0, gains[0])[1](scatter_rows(part))
+        gain_grads = jnp.stack([gain_grad_zero, gain_grad_one, gain_grad_two])
+        return part_zero, sum_everywhere(gain_grads), spread_columns(grads)
+
+    part_zero, gain_total, cross_grads = chain_step(
+        last_step, matmul_right(d_qkv, w_qkv), g_cross, gain_grad_one, gain_grad_two
+    )
     grad_tokens = (dh1 + part_zero).astype(bf16)
 
-    gain_total = sum_everywhere(jnp.stack([gain_grad_zero, gain_grad_one, gain_grad_two]))
-
+    back_swap = [(target, source) for source, target in pair_swap]
+    other_half = lax.ppermute(after(g_outer, cross_grads), ALL_AXES, back_swap)
+    outer_grad = jnp.where(
+        odd == 0,
+        jnp.concatenate([g_outer, other_half], axis=0),
+        jnp.concatenate([other_half, g_outer], axis=0),
+    )
+    by_tile = jnp.swapaxes(after(g_qkv, cross_grads).reshape(2, rows, 3, block), 1, 2)
+    sent = jnp.broadcast_to(by_tile[:, None], (2, 4, 3, rows, block)).reshape(8, 3, rows, block)
+    late_grads = lax.all_to_all(sent, PLANE, 0, 0, tiled=True).reshape(8 * 3, rows, block)
     place = np.arange(8)
     source_x, source_f = (place % 2)[None, :], ((place // 2)[None, :] - my_shift[:, None]) % 4
     other = source_f ^ f
@@ -540,28 +559,25 @@
     early_mode = jnp.where(my_used == 0, 1, jnp.where(late, 0, early_mode))
     states = (master, moment_one, moment_two)
     slot = np.arange(cap, dtype=np.int32)
-    by_tile = jnp.swapaxes(g_qkv.reshape(2, rows, 3, block), 1, 2)
-    sent = jnp.broadcast_to(by_tile[:, None], (2, 4, 3, rows, block)).reshape(8, 3, rows, block)
-    late_grads = lax.all_to_all(sent, PLANE, 0, 0, tiled=True).reshape(8 * 3, rows, block)
-    early = adam_tiles(
-        *states,
-        [in_grads, cross_grads],
-        [out_grads],
-        slot,
-        after(early_mode, gain_total, sent),
-        column_place.reshape(-1),
-        row_source,
-        np.zeros(cap, np.int32),
-    )
-
-    back_swap = [(target, source) for source, target in pair_swap]
-    other_half = lax.ppermute(g_outer, ALL_AXES, back_swap)
-    outer_grad = jnp.where(
-        odd == 0,
-        jnp.concatenate([g_outer, other_half], axis=0),
-        jnp.concatenate([other_half, g_outer], axis=0),
-    )
-    outer_grads = to_owners(outer_grad, lambda zz, place, target: place % 4 in (zz, (zz + 2) % 4))
+    early = None
+    for first in (0, half_cap):
+        chosen = slice(first, first + half_cap)
+        early = adam_tiles(
+            *states,
+            [in_grads, cross_grads],
+            [out_grads],
+            slot[chosen],
+            after(early_mode, outer_grad, sent)[chosen] if first else early_mode[chosen],
+            column_place[chosen].reshape(-1),
+            row_source[chosen],
+            np.zeros(half_cap, np.int32),
+            early,
+        )
+
+    outer_grads = jnp.stack(
+        [outer_grad]
+        + [from_other(outer_grad, mask, lambda zz, place, _: place % 4 in (zz, (zz + 2) % 4)) for mask in range(1, 4)]
+    )
     n_late = 5
     order = jnp.sum(jnp.where(slot[None, :] < slot[:, None], late.astype(jnp.int32)[None, :], 0), axis=1)
     count_late = jnp.sum(late.astype(jnp.int32))

time: 1180 us -> 1100 us (0.932)
  waiting for transfers between devices: 543 us -> 471 us
  other arithmetic: 58.1 us -> 70.9 us
    ppermute x77, waiting for transfers between devices: 394 us -> 330 us  [swap(): return lax.ppermute(value, axis, [(0, 1), (1, 0)])]
    all_to_all x2, waiting for transfers between devices: 10.6 us -> 46.6 us  [exchange_columns(): lax.all_to_all(pack_columns(weights, table, first, half_cap), PLANE, 0, 0...]
    ppermute x6, waiting for transfers between devices: 63.8 us -> 43.8 us  [take_rows(): got = lax.ppermute(got, ALL_AXES, flip_pairs(mask, keep_pair))]
    ppermute x7, waiting for transfers between devices: 52.4 us -> 34.6 us  [the longest x6 34.6 us: from_other(): return lax.ppermute(value, ALL_AXES, flip_pairs(mask, keep_pair))]
    all_to_all x2, starting transfers between devices: 23.6 us -> 10.4 us  [exchange_columns(): lax.all_to_all(pack_columns(weights, table, first, half_cap), PLANE, 0, 0...]
    unnamed x181 -> x161, local copies, waits for them, and re-layouts: 43 us -> 38 us
    pallas_call x2 -> x3, Pallas kernels: 61 us -> 64 us  [adam_tiles(): pl.pallas_call(kernel, out_shape=(shape, shape, shape), grid_spec=pltpu.P...]
where the time goes in v6:
time: 1100 us; the launch traced here: 1090 us
  waiting for transfers between devices  471 us (43%)
  matrix products  160 us (15%)
  local copies, waits for them, and re-layouts  153 us (14%)
  starting transfers between devices  115 us (10%)
  Pallas kernels  81.6 us (7%)
  other arithmetic  70.9 us (6%)
  between operations  35.8 us (3%)
    ppermute x77, waiting for transfers between devices, swap(): return lax.ppermute(value, axis, [(0, 1), (1, 0)])  330 us
    ppermute x77, starting transfers between devices, swap(): return lax.ppermute(value, axis, [(0, 1), (1, 0)])  69.7 us
    pallas_call x3, Pallas kernels, adam_tiles(): pl.pallas_call(kernel, out_shape=(shape, shape, shape), grid_spec=pltpu.P...  64 us
    dot_general x8, matrix products, matmul(): return jnp.dot(left, right, preferred_element_type=f32)  52.8 us
    dot_general x8, matrix products, matmul_left(): lax.dot_general(left, right, (((0,), (0,)), ((), ())), preferred_element_...  50.6 us
    all_to_all x2, waiting for transfers between devices, exchange_columns(): lax.all_to_all(pack_columns(weights, table, first, half_cap), PLANE, 0, 0...  46.6 us
    ppermute x6, waiting for transfers between devices, take_rows(): got = lax.ppermute(got, ALL_AXES, flip_pairs(mask, keep_pair))  43.8 us
    unnamed x161, local copies, waits for them, and re-layouts  38 us
  transfers between devices with their start and end apart: 106, of which 61 were waited for; matrix products, arithmetic and copies ran while one was open for 31% of the time, Pallas kernels for 5%

profile of v6, /device:TPU:0, one launch (start us, length us, event | category | flops | bytes accessed | tf_op | source)
XLA Modules:
  0.0 1089.0 jit_solution(732130867419031395)
XLA Ops:
  88.7 19.5 %collective-permute-done.72 = bf16[64,2048]{1,0:T(8,128)(2,1)S(1)} collective-permute-done((bf16[64,2048]{1,0:T(8,128)(2,1)S(1)}, bf16[64,2048]{1,0:T(8,128)(2,1)S(1)}, u32[]{:S(2)}, u32[]{:S(2)}) %collective-permute-start.72) | collective-permute-done | bytes 262176 | tf_op jit(solution)/shard_map/ppermute | solution.py:212
  119.8 12.1 %collective-permute-done.80 = bf16[128,2048]{1,0:T(8,128)(2,1)} collective-permute-done((bf16[128,2048]{1,0:T(8,128)(2,1)}, bf16[128,2048]{1,0:T(8,128)(2,1)}, u32[]{:S(2)}, u32[]{:S(2)}) %collective-permute-start.80) | collective-permute-done | bytes 524320 | tf_op jit(solution)/shard_map/ppermute | solution.py:369
  150.5 35.2 %all-to-all-done.1 = bf16[8,3,256,256]{3,2,1,0:T(8,128)(2,1)} async-done(((bf16[8,3,256,256]{3,2,1,0:T(8,128)(2,1)}), bf16[8,3,256,256]{3,2,1,0:T(8,128)(2,1)}, u32[]{:S(2)}, u32[]{:S(2)}) %all-to-all-start.1) | async-done | bytes 3145760 | tf_op jit(solution)/shard_map/all_to_all | solution.py:321
  238.2 35.7 %conditional.9 = (f32[128,2048]{1,0:T(8,128)}) conditional(s32[]{:T(128)} %bitcast.71, () %tuple.102, f32[1024,2048]{1,0:T(8,128)} %fusion.110), branch_computations={%region_10.11_spmd, %region_11.12_spmd} | conditional | flops 2883584 | bytes 65536208 | solution.py:397
  314.2 45.1 %conditional.10 = (bf16[1024,2048]{1,0:T(8,128)(2,1)}, bf16[1024,2048]{1,0:T(8,128)(2,1)}) conditional(s32[]{:T(128)} %bitcast.71, () %tuple.114, (bf16[128,2048]{1,0:T(8,128)(2,1)S(1)}, bf16[128,2048]{1,0:T(8,128)(2,1)S(1)}) %tuple.115), branch_computations={%region_13.14_spmd, %region_14.15_spmd} | conditional | bytes 52429216 | solution.py:397
  363.7 21.0 %collective-permute-done.86 = bf16[256,2048]{1,0:T(8,128)(2,1)S(1)} collective-permute-done((bf16[256,2048]{1,0:T(8,128)(2,1)}, bf16[256,2048]{1,0:T(8,128)(2,1)S(1)}, u32[]{:S(2)}, u32[]{:S(2)}) %collective-permute-start.86) | collective-permute-done | bytes 1048608 | tf_op jit(solution)/shard_map/ppermute | solution.py:351
  384.7 22.9 %collective-permute-done.87 = bf16[256,2048]{1,0:T(8,128)(2,1)} collective-permute-done((bf16[256,2048]{1,0:T(8,128)(2,1)S(1)}, bf16[256,2048]{1,0:T(8,128)(2,1)}, u32[]{:S(2)}, u32[]{:S(2)}) %collective-permute-start.87) | collective-permute-done | bytes 1048608 | tf_op jit(solution)/shard_map/ppermute | solution.py:351
  451.5 36.0 %conditional.11 = (f32[128,2048]{1,0:T(8,128)S(1)}) conditional(s32[]{:T(128)} %bitcast.71, () %tuple.109, f32[1024,2048]{1,0:T(8,128)} %fusion.106), branch_computations={%region_17.18_spmd, %region_18.19_spmd} | conditional | flops 2883584 | bytes 65536208 | solution.py:397
  466.0 12.1 %collective-permute-done.38 = bf16[2,128,1024]{2,1,0:T(8,128)(2,1)S(1)} collective-permute-done((bf16[2,128,1024]{2,1,0:T(8,128)(2,1)S(1)}, bf16[2,128,1024]{2,1,0:T(8,128)(2,1)S(1)}, u32[]{:S(2)}, u32[]{:S(2)}) %collective-permute-start.38) | collective-permute-done | bytes 524320 | tf_op jit(solution)/shard_map/cond/branch_1_fun/ppermute | solution.py:212
  489.0 25.7 %conditional.12 = (bf16[1024,2048]{1,0:T(8,128)(2,1)}) conditional(s32[]{:T(128)} %bitcast.71, () %tuple.117, bf16[128,2048]{1,0:T(8,128)(2,1)S(1)} %get-tuple-element.192), branch_computations={%region_20.21_spmd, %region_21.22_spmd} | conditional | bytes 26214608 | solution.py:397
  569.0 52.7 %conditional.13 = (f32[128,2048]{1,0:T(8,128)S(1)}, f32[128,2048]{1,0:T(8,128)S(1)}) conditional(s32[]{:T(128)} %bitcast.71, () %tuple.116, (f32[1024,2048]{1,0:T(8,128)}, f32[1024,2048]{1,0:T(8,128)S(1)}) %tuple.122), branch_computations={%region_22.23_spmd, %region_23.24_spmd} | conditional | flops 5767168 | bytes 131072416 | solution.py:397
  624.6 47.3 %conditional.14 = (bf16[1024,2048]{1,0:T(8,128)(2,1)}, bf16[1,256,2048]{2,1,0:T(8,128)(2,1)}, bf16[1,256,2048]{2,1,0:T(8,128)(2,1)}) conditional(s32[]{:T(128)} %bitcast.71, () %tuple.124, (bf16[128,2048]{1,0:T(8,128)(2,1)}, bf16[256,2048]{1,0:T(8,128)(2,1)}) %tuple.126), branch_computations={%region_26.27_spmd, %region_27.28_spmd} | conditional | bytes 34603312 | solution.py:397
  653.2 18.8 %collective-permute-done.21 = bf16[256,2048]{1,0:T(8,128)(2,1)} collective-permute-done((bf16[256,2048]{1,0:T(8,128)(2,1)}, bf16[256,2048]{1,0:T(8,128)(2,1)}, u32[]{:S(2)}, u32[]{:S(2)}) %collective-permute-start.21) | collective-permute-done | bytes 1048608 | tf_op jit(solution)/shard_map/cond/branch_1_fun/ppermute | solution.py:464
  712.9 56.3 %conditional.15 = (f32[128,2048]{1,0:T(8,128)S(1)}, bf16[1,256,2048]{2,1,0:T(8,128)(2,1)}) conditional(s32[]{:T(128)} %bitcast.71, () %tuple.123, (f32[1024,2048]{1,0:T(8,128)S(1)}, bf16[256,2048]{1,0:T(8,128)(2,1)}) %tuple.127), branch_computations={%region_29.30_spmd, %region_30.31_spmd} | conditional | flops 2883584 | bytes 69730560 | solution.py:397
  737.9 22.5 %collective-permute-done.51 = bf16[2,128,1024]{2,1,0:T(8,128)(2,1)S(1)} collective-permute-done((bf16[2,128,1024]{2,1,0:T(8,128)(2,1)S(1)}, bf16[2,128,1024]{2,1,0:T(8,128)(2,1)S(1)}, u32[]{:S(2)}, u32[]{:S(2)}) %collective-permute-start.51) | collective-permute-done | bytes 524320 | tf_op jit(solution)/shard_map/cond/branch_1_fun/ppermute | solution.py:212
  772.2 54.0 %conditional.16 = (bf16[1024,2048]{1,0:T(8,128)(2,1)}, bf16[8,256,1024]{2,1,0:T(8,128)(2,1)S(1)}) conditional(s32[]{:T(128)} %bitcast.71, () %tuple.129, (bf16[128,2048]{1,0:T(8,128)(2,1)}, bf16[512,1024]{1,0:T(8,128)(2,1)}) %tuple.131), branch_computations={%region_33.34_spmd, %region_34.35_spmd} | conditional | flops 9437188 | bytes 57672056 | solution.py:397
  805.1 16.0 %collective-permute-done.28 = bf16[2,256,1024]{2,1,0:T(8,128)(2,1)S(1)} collective-permute-done((bf16[2,256,1024]{2,1,0:T(8,128)(2,1)S(1)}, bf16[2,256,1024]{2,1,0:T(8,128)(2,1)S(1)}, u32[]{:S(2)}, u32[]{:S(2)}) %collective-permute-start.28) | collective-permute-done | bytes 1048608 | tf_op jit(solution)/shard_map/cond/branch_1_fun/ppermute | solution.py:212
  874.0 96.5 %conditional.17 = (f32[128,2048]{1,0:T(8,128)}, f32[3,2048]{1,0:T(4,128)S(1)}, bf16[8,256,1280]{2,1,0:T(8,128)(2,1)}) conditional(s32[]{:T(128)} %bitcast.71, () %tuple.128, (f32[1024,2048]{1,0:T(8,128)S(1)}, f32[3,2048]{1,0:T(4,128)S(1)}, f32[128,2048]{1,0:T(8,128)S(1)}, f32[128,2048]{1,0:T(8,128)}, f32[128,2048]{1,0:T(8,128)}, ...), branch_computations={%region_39.40_spmd, %region_40.44_spmd} | conditional | flops 19467012 | bytes 139409088 | solution.py:397
  881.3 15.5 %collective-permute-done.66 = bf16[256,1280]{1,0:T(8,128)(2,1)S(1)} collective-permute-done((bf16[256,1280]{1,0:T(8,128)(2,1)S(1)}, bf16[256,1280]{1,0:T(8,128)(2,1)S(1)}, u32[]{:S(2)}, u32[]{:S(2)}) %collective-permute-start.66) | collective-permute-done | bytes 655392 | tf_op jit(solution)/shard_map/cond/branch_1_fun/ppermute | solution.py:212
  902.3 25.0 %collective-permute-done.67 = bf16[2,256,1280]{2,1,0:T(8,128)(2,1)S(1)} collective-permute-done((bf16[2,256,1280]{2,1,0:T(8,128)(2,1)S(1)}, bf16[2,256,1280]{2,1,0:T(8,128)(2,1)S(1)}, u32[]{:S(2)}, u32[]{:S(2)}) %collective-permute-start.67) | collective-permute-done | bytes 1310752 | tf_op jit(solution)/shard_map/cond/branch_1_fun/ppermute | solution.py:212
  930.0 12.4 %collective-permute-done.57 = bf16[2,128,1024]{2,1,0:T(8,128)(2,1)S(1)} collective-permute-done((bf16[2,128,1024]{2,1,0:T(8,128)(2,1)S(1)}, bf16[2,128,1024]{2,1,0:T(8,128)(2,1)S(1)}, u32[]{:S(2)}, u32[]{:S(2)}) %collective-permute-start.57) | collective-permute-done | bytes 524320 | tf_op jit(solution)/shard_map/cond/branch_1_fun/ppermute | solution.py:212
  984.1 23.3 %adam_tiles.3 = (f32[6,256,2048]{2,1,0:T(8,128)}, f32[6,256,2048]{2,1,0:T(8,128)}, f32[6,256,2048]{2,1,0:T(8,128)}) custom-call(s32[3]{0:T(128)S(1)} %call_exported.3.visit_ref, s32[3]{0:T(128)S(1)} %bitcast.366, s32[24]{0:T(128)S(1)} %reshape.520.cp_ref, s32[3]{0:T(128)S(1)} %get-tuple-element.316.rp_ref, s32[3]{0:T(128)S(1)} %call_exported.4.hold_ref, ...), custom_call_target="tpu_custom_call" | custom-call | flops 47185920 | bytes 40894464 | tf_op jit(solution)/shard_map/adam_tiles/pallas_call | solution.py:182
  1041.0 20.8 %adam_tiles.4 = (f32[6,256,2048]{2,1,0:T(8,128)}, f32[6,256,2048]{2,1,0:T(8,128)}, f32[6,256,2048]{2,1,0:T(8,128)}) custom-call(s32[3]{0:T(128)S(1)} %copy-done.6, s32[3]{0:T(128)S(1)} %slice.529.mode_ref, s32[24]{0:T(128)S(1)} %reshape.519.cp_ref, s32[3]{0:T(128)S(1)} %get-tuple-element.317.rp_ref, ...), custom_call_target="tpu_custom_call", output_to_operand_aliasing={{0}: (11, {}), {1}: (12, {}), {2}: (13, {})} | custom-call | flops 47185920 | bytes 40894464 | tf_op jit(solution)/shard_map/adam_tiles/pallas_call | solution.py:182
  1061.8 19.8 %adam_tiles.5 = (f32[6,256,2048]{2,1,0:T(8,128)}, f32[6,256,2048]{2,1,0:T(8,128)}, f32[6,256,2048]{2,1,0:T(8,128)}) custom-call(s32[5]{0:T(128)S(1)} %get-tuple-element.342.visit_ref, s32[5]{0:T(128)S(1)} %get-tuple-element.341.mode_ref, s32[40]{0:T(128)S(1)} %select_n.439.cp_ref, ...), custom_call_target="tpu_custom_call", output_to_operand_aliasing={{0}: (13, {}), {1}: (14, {}), {2}: (15, {})} | custom-call | flops 78643200 | bytes 68157440 | tf_op jit(solution)/shard_map/adam_tiles/pallas_call | solution.py:182
  (684 shorter events, 754.6 us)
Async XLA Ops:
  22.3 42.2 %all-to-all-start = ((bf16[8,3,256,256]{3,2,1,0:T(8,128)(2,1)}), bf16[8,3,256,256]{3,2,1,0:T(8,128)(2,1)S(1)}, u32[]{:S(2)}, u32[]{:S(2)}) async-start(bf16[8,3,256,256]{3,2,1,0:T(8,128)(2,1)} %copy-done.1), calls=%async_computation | async-start | bytes 6291456 | tf_op jit(solution)/shard_map/all_to_all | solution.py:321
  27.6 177.6 %all-gather.6.cloned.1.call-start = ((), (), s32[]{:S(2)}) async-start(), calls=%async_computation.8 | async-start | bytes 3932160 | tf_op jit(solution)/shard_map/all_gather | solution.py:338
  66.3 165.6 %all-gather.8.cloned.1.call-start = ((), (), s32[]{:S(2)}) async-start(), calls=%async_computation.9 | async-start | bytes 2621440 | tf_op jit(solution)/shard_map/all_gather | solution.py:371
  68.4 43.8 %collective-permute-start.77 = (bf16[256,2048]{1,0:T(8,128)(2,1)}, bf16[256,2048]{1,0:T(8,128)(2,1)}, u32[]{:S(2)}, u32[]{:S(2)}) collective-permute-start(bf16[256,2048]{1,0:T(8,128)(2,1)} %get-tuple-element.118), channel_id=1, source_target_pairs={{1,2},{3,0},{5,6},{7,4},{8,11},{10,9},{12,15},{14,13},{17,18},{19,... | collective-permute-start | bytes 3145736 | tf_op jit(solution)/shard_map/ppermute | solution.py:351
  69.7 42.5 %collective-permute-start.78 = (bf16[256,2048]{1,0:T(8,128)(2,1)}, bf16[256,2048]{1,0:T(8,128)(2,1)}, u32[]{:S(2)}, u32[]{:S(2)}) collective-permute-start(bf16[256,2048]{1,0:T(8,128)(2,1)} %get-tuple-element.119), channel_id=1, source_target_pairs={{0,2},{2,0},{4,6},{6,4},{9,11},{11,9},{13,15},{15,13},{16,18},{18,... | collective-permute-start | bytes 3145736 | tf_op jit(solution)/shard_map/ppermute | solution.py:351
  73.1 39.2 %collective-permute-start.79 = (bf16[256,2048]{1,0:T(8,128)(2,1)}, bf16[256,2048]{1,0:T(8,128)(2,1)}, u32[]{:S(2)}, u32[]{:S(2)}) collective-permute-start(bf16[256,2048]{1,0:T(8,128)(2,1)} %get-tuple-element.120), channel_id=1, source_target_pairs={{1,0},{3,2},{5,4},{7,6},{8,9},{10,11},{12,13},{14,15},{17,16},{19,... | collective-permute-start | bytes 3145736 | tf_op jit(solution)/shard_map/ppermute | solution.py:351
  143.2 42.6 %all-to-all-start.1 = ((bf16[8,3,256,256]{3,2,1,0:T(8,128)(2,1)}), bf16[8,3,256,256]{3,2,1,0:T(8,128)(2,1)}, u32[]{:S(2)}, u32[]{:S(2)}) async-start(bf16[8,3,256,256]{3,2,1,0:T(8,128)(2,1)} %copy-done.2), calls=%async_computation.1 | async-start | bytes 6291456 | tf_op jit(solution)/shard_map/all_to_all | solution.py:321
  148.3 262.5 %all-gather.10.cloned.1.call-start = ((), (), s32[]{:S(2)}) async-start(), calls=%async_computation.10 | async-start | bytes 6553600 | tf_op jit(solution)/shard_map/all_gather | solution.py:338
  191.4 323.3 %all-gather.12.cloned.1.call-start = ((), (), s32[]{:S(2)}) async-start(), calls=%async_computation.11 | async-start | bytes 5242880 | tf_op jit(solution)/shard_map/all_gather | solution.py:338
  203.3 73.1 %collective-permute-start.81 = (bf16[256,4096]{1,0:T(8,128)(2,1)}, bf16[256,4096]{1,0:T(8,128)(2,1)}, u32[]{:S(2)}, u32[]{:S(2)}) collective-permute-start(bf16[256,4096]{1,0:T(8,128)(2,1)} %bitcast.393), channel_id=1, source_target_pairs={{0,2},{2,0},{1,3},{3,1},{4,6},{6,4},{5,7},{7,5},{8,10},{10,8},{9,1... | collective-permute-start | bytes 6291464 | tf_op jit(solution)/shard_map/ppermute | solution.py:212
  203.7 75.7 %collective-permute-start.82 = (bf16[256,4096]{1,0:T(8,128)(2,1)}, bf16[256,4096]{1,0:T(8,128)(2,1)}, u32[]{:S(2)}, u32[]{:S(2)}) collective-permute-start(bf16[256,4096]{1,0:T(8,128)(2,1)} %bitcast.394), channel_id=1, source_target_pairs={{0,4},{4,0},{1,5},{5,1},{2,6},{6,2},{3,7},{7,3},{8,12},{12,8},{9,1... | collective-permute-start | bytes 6291464 | tf_op jit(solution)/shard_map/ppermute | solution.py:212
  305.5 109.6 %collective-permute-start.85 = (bf16[1024,4096]{1,0:T(8,128)(2,1)}, bf16[1024,4096]{1,0:T(8,128)(2,1)}, u32[]{:S(2)}, u32[]{:S(2)}) collective-permute-start(bf16[1024,4096]{1,0:T(8,128)(2,1)} %get-tuple-element.293), channel_id=1, source_target_pairs={{0,1},{1,0},{2,3},{3,2},{4,5},{5,4},{6,7},{7,6},{8,9},{9,8},{10,11... | collective-permute-start | bytes 25165832 | tf_op jit(solution)/shard_map/ppermute | solution.py:212
  310.5 222.6 %all-gather.14.cloned.1.call-start = ((), (), s32[]{:S(2)}) async-start(), calls=%async_computation.12 | async-start | bytes 5242880 | tf_op jit(solution)/shard_map/all_gather | solution.py:338
  360.7 46.8 %collective-permute-start.87 = (bf16[256,2048]{1,0:T(8,128)(2,1)S(1)}, bf16[256,2048]{1,0:T(8,128)(2,1)}, u32[]{:S(2)}, u32[]{:S(2)}) collective-permute-start(bf16[256,2048]{1,0:T(8,128)(2,1)S(1)} %copy-done.34), channel_id=1, source_target_pairs={{0,2},{1,3},{2,0},{3,1},{4,6},{5,7},{6,4},{7,5},{8,10},{9,11},{10,... | collective-permute-start | bytes 3145736 | tf_op jit(solution)/shard_map/ppermute | solution.py:351
  361.1 46.4 %collective-permute-start.88 = (bf16[256,2048]{1,0:T(8,128)(2,1)S(1)}, bf16[256,2048]{1,0:T(8,128)(2,1)}, u32[]{:S(2)}, u32[]{:S(2)}) collective-permute-start(bf16[256,2048]{1,0:T(8,128)(2,1)S(1)} %copy-done.33), channel_id=1, source_target_pairs={{0,1},{1,0},{2,3},{3,2},{4,5},{5,4},{6,7},{7,6},{8,9},{9,8},{10,11... | collective-permute-start | bytes 3145736 | tf_op jit(solution)/shard_map/ppermute | solution.py:351
  410.7 213.9 %reduce-scatter.6.cloned.1.call-start = ((), (), s32[]{:S(2)}) async-start(), calls=%async_computation.13 | async-start | bytes 5242880 | tf_op jit(solution)/shard_map/reduce_scatter | solution.py:460
  532.9 239.3 %reduce-scatter.8.cloned.1.call-start = ((), (), s32[]{:S(2)}) async-start(), calls=%async_computation.14 | async-start | bytes 5242880 | tf_op jit(solution)/shard_map/reduce_scatter | solution.py:460
  554.0 282.3 %reduce-scatter.10.cloned.1.call-start = ((), (), s32[]{:S(2)}) async-start(), calls=%async_computation.15 | async-start | bytes 6553600 | tf_op jit(solution)/shard_map/reduce_scatter | solution.py:460
  710.1 260.5 %reduce-scatter.12.cloned.1.call-start = ((), (), s32[]{:S(2)}) async-start(), calls=%async_computation.16 | async-start | bytes 3932160 | tf_op jit(solution)/shard_map/reduce_scatter | solution.py:460
  723.5 45.8 %collective-permute-start.55 = (bf16[256,2048]{1,0:T(8,128)(2,1)}, bf16[256,2048]{1,0:T(8,128)(2,1)}, u32[]{:S(2)}, u32[]{:S(2)}) collective-permute-start(bf16[256,2048]{1,0:T(8,128)(2,1)} %get-tuple-element.54), channel_id=1, source_target_pairs={{0,3},{1,2},{2,1},{3,0},{4,7},{5,6},{6,5},{7,4},{8,11},{9,10},{10,... | collective-permute-start | bytes 3145736 | tf_op jit(solution)/shard_map/cond/branch_1_fun/ppermute | solution.py:464
  724.0 36.4 %collective-permute-start.51 = (bf16[2,128,1024]{2,1,0:T(8,128)(2,1)S(1)}, bf16[2,128,1024]{2,1,0:T(8,128)(2,1)S(1)}, u32[]{:S(2)}, u32[]{:S(2)}) collective-permute-start(bf16[2,128,1024]{2,1,0:T(8,128)(2,1)S(1)} %slice_bitcast_fusion.29), channel_id=1, source_target_pairs={{0,2},{2,0},{1,3},{3,1},{4,6},{6,4},{5,7},{7,5},{8,10},{10,8},{9,1... | collective-permute-start | bytes 1572872 | tf_op jit(solution)/shard_map/cond/branch_1_fun/ppermute | solution.py:212
  862.2 116.5 %reduce-scatter.14.cloned.1.call-start = ((), (), s32[]{:S(2)}) async-start(), calls=%async_computation.17 | async-start | bytes 2621440 | tf_op jit(solution)/shard_map/reduce_scatter | solution.py:460
  896.9 30.3 %collective-permute-start.67 = (bf16[2,256,1280]{2,1,0:T(8,128)(2,1)S(1)}, bf16[2,256,1280]{2,1,0:T(8,128)(2,1)S(1)}, u32[]{:S(2)}, u32[]{:S(2)}) collective-permute-start(bf16[2,256,1280]{2,1,0:T(8,128)(2,1)S(1)} %pad_maximum_fusion.10), channel_id=1, source_target_pairs={{0,2},{2,0},{1,3},{3,1},{4,6},{6,4},{5,7},{7,5},{8,10},{10,8},{9,1... | collective-permute-start | bytes 3932168 | tf_op jit(solution)/shard_map/cond/branch_1_fun/ppermute | solution.py:212
  974.8 87.0 %all-to-all-start.2 = ((bf16[8,3,256,256]{3,2,1,0:T(8,128)(2,1)}), bf16[8,3,256,256]{3,2,1,0:T(8,128)(2,1)S(1)}, u32[]{:S(2)}, u32[]{:S(2)}) async-start(bf16[8,3,256,256]{3,2,1,0:T(8,128)(2,1)} %bitcast.373), calls=%async_computation.6 | async-start | bytes 6291456 | tf_op jit(solution)/shard_map/all_to_all | solution.py:547
  (159 other events, 2425.0 us)
Sparse Core Ops, SparseCore 0:
  66.4 63.1 all-gather.5
  134.1 47.7 all-gather.7
  191.5 97.9 all-gather.9
  310.6 80.8 all-gather.11
  410.8 80.8 all-gather.13
  533.0 77.0 reduce-scatter.5
  612.6 77.2 reduce-scatter.7
  710.2 94.0 reduce-scatter.9
  862.4 60.1 reduce-scatter.11
  924.7 44.5 reduce-scatter.13

commit v7 on v6

--- a/solution.py
+++ b/solution.py
@@ -314,7 +314,7 @@
     outer_tiles = jnp.where(other_f == z, 3, 9)
     out_tiles = 14 + (z - other_f) % 4
     row_slots = of_tiles(jnp.concatenate([outer_tiles, out_tiles]), rank)
-    row_owners = of_tiles(jnp.stack([outer_tiles[0], out_tiles[0]]), owners)
+    row_owners = of_tiles(jnp.stack([outer_tiles[0], outer_tiles[2], out_tiles[0], out_tiles[2]]), owners)
 
     def exchange_columns(first, weights):
         table = column_table[first : first + half_cap].reshape(-1)
@@ -326,9 +326,10 @@
 
     h0 = tokens.astype(f32)
     outer_blocks = [my_block(row_slots[mask]) for mask in range(4)]
+    out_blocks = [my_block(row_slots[4 + mask]) for mask in range(4)]
     a_in = normalize(h0, gains[0]).astype(bf16)
     received = [exchange_columns(0, after(master, column_part, column_place, row_slots, row_owners))]
-    received = [after(received[0], a_in, *outer_blocks)]
+    received = [after(received[0], a_in, *outer_blocks, *out_blocks)]
 
     def columns_here(first, count, parts):
         chosen = slice(2 * first, 2 * (first + count))
@@ -342,20 +343,19 @@
     a_all = gather_rows(after(a_in, local))
     received.append(exchange_columns(half_cap, after(master, a_all)))
 
-    def take_rows(kind, blocks, keep_pair, earlier):
-        found = None
-        source = row_owners[kind] ^ f
-        for mask, got in enumerate(blocks):
-            if mask:
-                got = after(got, earlier)
-                got = lax.ppermute(got, ALL_AXES, flip_pairs(mask, keep_pair))
-            found = got if found is None else jnp.where(source == mask, got, found)
-        return found
+    def take_rows(kind, blocks, keep_pair):
+        here, there = row_owners[2 * kind], row_owners[2 * kind + 1]
+        core = f % 2
+        from_core = swap(jnp.stack([blocks[1], blocks[3]]), "c")
+        mine = jnp.where(here % 2 == core, blocks[0], from_core[0])
+        across = jnp.where(there % 2 == core, blocks[2], from_core[1])
+        from_y = lax.ppermute(across, ALL_AXES, flip_pairs(2, keep_pair))
+        return jnp.where(here // 2 == f // 2, mine, from_y)
 
     def needs_outer(zz, place, target):
         return target % 4 in (zz, (zz + 2) % 4)
 
-    outer = take_rows(0, outer_blocks, needs_outer, local)
+    outer = take_rows(0, [after(value, local) for value in outer_blocks], needs_outer)
     half_rows = rows // 2
     odd = z % 2
     to_pair = lax.dynamic_slice_in_dim(outer, (1 - odd) * half_rows, half_rows, 0)
@@ -373,13 +373,6 @@
     w_self_out = jnp.where(low_y, outer_all[:rows], outer_all[rows:])
     w_cross_out = jnp.where(low_y, outer_all[rows:], outer_all[:rows])
 
-    w_cross = gather_z(columns_here(3, 5, 2))
-    w_in = gather_z(columns_here(8, 4, 2))
-    slots, ctx_len, ctx_width = context.shape
-    ctx = context.reshape(slots * ctx_len, ctx_width)
-    ctx_x = swap(after(ctx, received[1]), "x")
-    ctx_y = swap(after(ctx, received[1]), "y")
-
     seg = segments(lengths[0], count)
     live = keep == 1
     code = seg * 2 + live.astype(jnp.int32)
@@ -422,6 +415,15 @@
     probs = probabilities(query, keys, allowed)
     probs_low = probs.astype(bf16)
     attended = joined(weighted(probs_low, values))
+    received[1] = after(received[1], attended)
+    local_cross, local_in = columns_here(3, 5, 2), columns_here(8, 4, 2)
+    w_cross = gather_z(local_cross)
+    w_in = gather_z(local_in)
+    slots, ctx_len, ctx_width = context.shape
+    ctx = after(context.reshape(slots * ctx_len, ctx_width), local_cross, local_in)
+    ctx_x, ctx_y = swap(ctx, "x"), swap(ctx, "y")
+    out_rows = take_rows(1, [after(value, local_cross, local_in) for value in out_blocks], None)
+    w_out = gather_z(out_rows)
     h1 = h0 + chain_step(scatter_rows, matmul(attended, w_self_out))
     half = slots * ctx_len // 2
     far_low = swap(after(ctx_y, h1)[:half], "x")
@@ -431,8 +433,6 @@
         normalize(h1, gains[1]).astype(bf16),
         grad_out.astype(bf16),
     )
-    out_rows = take_rows(1, [my_block(row_slots[4 + mask]) for mask in range(4)], None, b_all)
-    w_out = gather_z(out_rows)
     ctx_four = jnp.concatenate([ctx, ctx_y, ctx_x, far_low, far_high], axis=0)
     ctx_all = jnp.concatenate([ctx_four, swap(ctx_four, "c")], axis=0)
 
@@ -460,8 +460,11 @@
         value = lax.psum_scatter(value, "z", scatter_dimension=0, tiled=True)
         return with_layout_constraint(value, Layout(major_to_minor=(0, 1)))
 
-    def from_other(value, mask, keep_pair=None):
-        return lax.ppermute(value, ALL_AXES, flip_pairs(mask, keep_pair))
+    def from_y(value, keep_pair=None):
+        return jnp.stack([value, lax.ppermute(value, ALL_AXES, flip_pairs(2, keep_pair))])
+
+    def with_core(pair):
+        return jnp.concatenate([pair, swap(pair, "c")])
 
     t_out = matmul_left(activated, d_ff).astype(bf16)
     g_out = sum_rows(t_out)
@@ -475,11 +478,7 @@
     layer_out = (h2 + mixed).astype(bf16)
     part_two, gain_grad_two = jax.vjp(normalize, h2, gains[2])[1](d_c)
     dh2 = grad_out + part_two
-    d_cross_out, out_one, out_two = chain_step(
-        lambda one, two: (gather_rows(one), from_other(two, 1), from_other(two, 2)),
-        after(dh2.astype(bf16), t_in),
-        g_out,
-    )
+    d_cross_out = chain_step(gather_rows, after(dh2.astype(bf16), t_in))
     g_cross_out = matmul_left(cross_o, d_cross_out)
 
     def through(d_mixed, left, right, probs, probs_low, values):
@@ -491,8 +490,13 @@
         d_values = joined(jnp.einsum("bhqk,bqhd->bkhd", probs_low, d_mixed, preferred_element_type=f32))
         return d_left, d_right, d_values
 
-    d_cq, d_ck, d_cv = through(
-        matmul_right(d_cross_out, w_cross_out), cross_q, cross_k, cross_p, cross_low, cross_v
+    (d_cq, d_ck, d_cv), out_grads = chain_step(
+        lambda one, two: (
+            through(matmul_right(one, w_cross_out), cross_q, cross_k, cross_p, cross_low, cross_v),
+            from_y(two),
+        ),
+        d_cross_out,
+        g_out,
     )
     d_ckv = jnp.concatenate([d_ck, d_cv], axis=1)
     t_cross = jnp.concatenate(
@@ -504,13 +508,10 @@
     )
     g_cross = sum_rows(t_cross)
     part = matmul_right(d_cq, w_cross_q)
-    d_b, out_three = chain_step(lambda one, two: (scatter_rows(one), from_other(two, 3)), part, g_out)
-    out_grads = jnp.stack([g_out, out_one, out_two, out_three])
+    d_b = chain_step(scatter_rows, part)
     part_one, gain_grad_one = jax.vjp(normalize, h1, gains[1])[1](d_b)
     dh1 = dh2 + part_one
-    d_self_out, in_grads = chain_step(
-        lambda one, two: (gather_rows(one), spread_columns(two)), after(dh1.astype(bf16), t_cross), g_in
-    )
+    d_self_out = chain_step(gather_rows, after(dh1.astype(bf16), t_cross, g_in))
     g_self_out = matmul_left(attended, d_self_out)
     t_outer = jnp.concatenate(
         [
@@ -525,13 +526,14 @@
     d_qkv = jnp.concatenate([d_q, d_k, d_v], axis=1)
     g_qkv = sum_rows(matmul_left(a_all, d_qkv).astype(bf16))
 
-    def last_step(part, grads, gain_grad_one, gain_grad_two):
+    def last_step(part, in_sum, cross_sum, out_pair, gain_grad_one, gain_grad_two):
         part_zero, gain_grad_zero = jax.vjp(normalize, h0, gains[0])[1](scatter_rows(part))
         gain_grads = jnp.stack([gain_grad_zero, gain_grad_one, gain_grad_two])
-        return part_zero, sum_everywhere(gain_grads), spread_columns(grads)
-
-    part_zero, gain_total, cross_grads = chain_step(
-        last_step, matmul_right(d_qkv, w_qkv), g_cross, gain_grad_one, gain_grad_two
+        moved = spread_columns(in_sum), spread_columns(cross_sum), with_core(out_pair)
+        return part_zero, sum_everywhere(gain_grads), *moved
+
+    part_zero, gain_total, in_grads, cross_grads, out_grads = chain_step(
+        last_step, matmul_right(d_qkv, w_qkv), g_in, g_cross, out_grads, gain_grad_one, gain_grad_two
     )
     grad_tokens = (dh1 + part_zero).astype(bf16)
 
@@ -553,7 +555,8 @@
     my_column = jnp.sum(jnp.where(my_tile[:, None] == np.arange(n_tiles), column_of, 0), axis=1)
     in_layer = (my_tile >= 10)[:, None]
     column_place = source * 8 + jnp.where(in_layer, (place // 2)[None, :], my_column[:, None])
-    row_source = ((z - my_shift) % 4) ^ f
+    other_row = ((z - my_shift) % 4) ^ f
+    row_source = (other_row % 2) * 2 + other_row // 2
     late = (my_used == 1) & ((my_tile < 4) | (my_tile == 9))
     early_mode = jnp.where(my_row == 1, 4, jnp.where(my_tile >= 10, 2, 3))
     early_mode = jnp.where(my_used == 0, 1, jnp.where(late, 0, early_mode))
@@ -574,10 +577,8 @@
             early,
         )
 
-    outer_grads = jnp.stack(
-        [outer_grad]
-        + [from_other(outer_grad, mask, lambda zz, place, _: place % 4 in (zz, (zz + 2) % 4)) for mask in range(1, 4)]
-    )
+    outer_grads = with_core(from_y(outer_grad, lambda zz, place, _: place % 4 in (zz, (zz + 2) % 4)))
+
     n_late = 5
     order = jnp.sum(jnp.where(slot[None, :] < slot[:, None], late.astype(jnp.int32)[None, :], 0), axis=1)
     count_late = jnp.sum(late.astype(jnp.int32))

time: 1100 us -> 1090 us (level)
  waiting for transfers between devices: 471 us -> 415 us
  other arithmetic: 70.9 us -> 93.7 us
    ppermute x12 -> x4, waiting for transfers between devices: 78.4 us -> 30.2 us  [the longest x2 24.3 us: take_rows(): from_y = lax.ppermute(across, ALL_AXES, flip_pairs(2, keep_pair))]
    ppermute x77 -> x81, waiting for transfers between devices: 330 us -> 299 us  [swap(): return lax.ppermute(value, axis, [(0, 1), (1, 0)])]
    reduce_scatter x5, waiting for transfers between devices: 0.03 us -> 12.7 us  [sum_rows(): value = lax.psum_scatter(value, 'z', scatter_dimension=0, tiled=True)]
    ppermute x12 -> x4, starting transfers between devices: 19.6 us -> 8.43 us  [the longest x2 4.43 us: take_rows(): from_y = lax.ppermute(across, ALL_AXES, flip_pairs(2, keep_pair))]
    cond x25 -> x34, local copies, waits for them, and re-layouts: 19.9 us -> 22.5 us
    ppermute x77 -> x81, starting transfers between devices: 69.7 us -> 70.4 us  [swap(): return lax.ppermute(value, axis, [(0, 1), (1, 0)])]
    unnamed x161 -> x163, local copies, waits for them, and re-layouts: 38 us -> 37.3 us
  transfers between devices with their start and end apart: 106 -> 102, of which waited for: 61 -> 59; matrix products, arithmetic and copies ran while one was open for 31% -> 36% of each run, Pallas kernels for 5% -> 5%
where the time goes in v7:
time: 1090 us; the launch traced here: 1080 us
  waiting for transfers between devices  415 us (38%)
  local copies, waits for them, and re-layouts  161 us (15%)
  matrix products  161 us (15%)
  starting transfers between devices  107 us (10%)
  other arithmetic  93.7 us (9%)
  Pallas kernels  92.3 us (8%)
  between operations  43.6 us (4%)
    ppermute x81, waiting for transfers between devices, swap(): return lax.ppermute(value, axis, [(0, 1), (1, 0)])  299 us
    pallas_call x3, Pallas kernels, adam_tiles(): pl.pallas_call(kernel, out_shape=(shape, shape, shape), grid_spec=pltpu.P...  74.2 us
    ppermute x81, starting transfers between devices, swap(): return lax.ppermute(value, axis, [(0, 1), (1, 0)])  70.4 us
    dot_general x8, matrix products, matmul(): return jnp.dot(left, right, preferred_element_type=f32)  53.9 us
    dot_general x8, matrix products, matmul_left(): lax.dot_general(left, right, (((0,), (0,)), ((), ())), preferred_element_...  50 us
    all_to_all x2, waiting for transfers between devices, exchange_columns(): lax.all_to_all(pack_columns(weights, table, first, half_cap), PLANE, 0, 0...  42.5 us
    dot_general x6, matrix products, matmul_right(): lax.dot_general(left, right, (((1,), (1,)), ((), ())), preferred_element_...  39.5 us
    unnamed x163, local copies, waits for them, and re-layouts  37.3 us
  transfers between devices with their start and end apart: 102, of which 59 were waited for; matrix products, arithmetic and copies ran while one was open for 36% of the time, Pallas kernels for 5%

profile of v7, /device:TPU:0, one launch (start us, length us, event | category | flops | bytes accessed | tf_op | source)
XLA Modules:
  0.0 1076.3 jit_solution(2438608283604552361)
XLA Ops:
  116.6 17.4 %collective-permute-done.78 = bf16[128,2048]{1,0:T(8,128)(2,1)} collective-permute-done((bf16[128,2048]{1,0:T(8,128)(2,1)}, bf16[128,2048]{1,0:T(8,128)(2,1)}, u32[]{:S(2)}, u32[]{:S(2)}) %collective-permute-start.78) | collective-permute-done | bytes 524320 | tf_op jit(solution)/shard_map/ppermute | solution.py:369
  156.9 35.2 %all-to-all-done.1 = bf16[8,3,256,256]{3,2,1,0:T(8,128)(2,1)} async-done(((bf16[8,3,256,256]{3,2,1,0:T(8,128)(2,1)}), bf16[8,3,256,256]{3,2,1,0:T(8,128)(2,1)}, u32[]{:S(2)}, u32[]{:S(2)}) %all-to-all-start.1) | async-done | bytes 3145760 | tf_op jit(solution)/shard_map/all_to_all | solution.py:321
  248.3 49.3 %conditional.10 = (f32[128,2048]{1,0:T(8,128)S(1)}) conditional(s32[]{:T(128)} %bitcast.73, () %tuple.101, f32[1024,2048]{1,0:T(8,128)} %fusion.121), branch_computations={%region_10.11_spmd, %region_11.12_spmd} | conditional | flops 2883584 | bytes 65536208 | solution.py:390
  262.5 25.9 %collective-permute-done.29 = bf16[2,128,1024]{2,1,0:T(8,128)(2,1)S(1)} collective-permute-done((bf16[2,128,1024]{2,1,0:T(8,128)(2,1)S(1)}, bf16[2,128,1024]{2,1,0:T(8,128)(2,1)S(1)}, u32[]{:S(2)}, u32[]{:S(2)}) %collective-permute-start.29) | collective-permute-done | bytes 524320 | tf_op jit(solution)/shard_map/cond/branch_1_fun/ppermute | solution.py:212
  311.3 12.9 %collective-permute-done.81 = bf16[128,4096]{1,0:T(8,128)(2,1)S(1)} collective-permute-done((bf16[128,4096]{1,0:T(8,128)(2,1)S(1)}, bf16[128,4096]{1,0:T(8,128)(2,1)S(1)}, u32[]{:S(2)}, u32[]{:S(2)}) %collective-permute-start.81) | collective-permute-done | bytes 1048608 | tf_op jit(solution)/shard_map/ppermute | solution.py:212
  331.5 44.3 %conditional.11 = (bf16[1024,2048]{1,0:T(8,128)(2,1)}, bf16[1024,2048]{1,0:T(8,128)(2,1)}) conditional(s32[]{:T(128)} %bitcast.73, () %tuple.115, (bf16[128,2048]{1,0:T(8,128)(2,1)S(1)}, bf16[128,2048]{1,0:T(8,128)(2,1)S(1)}) %tuple.116), branch_computations={%region_13.14_spmd, %region_14.15_spmd} | conditional | bytes 52429216 | solution.py:390
  387.6 20.6 %collective-permute-done.85 = bf16[256,2048]{1,0:T(8,128)(2,1)} collective-permute-done((bf16[256,2048]{1,0:T(8,128)(2,1)}, bf16[256,2048]{1,0:T(8,128)(2,1)}, u32[]{:S(2)}, u32[]{:S(2)}) %collective-permute-start.85) | collective-permute-done | bytes 1048608 | tf_op jit(solution)/shard_map/ppermute | solution.py:352
  453.9 36.4 %conditional.12 = (f32[128,2048]{1,0:T(8,128)}) conditional(s32[]{:T(128)} %bitcast.73, () %tuple.109, f32[1024,2048]{1,0:T(8,128)} %fusion.111), branch_computations={%region_17.18_spmd, %region_18.19_spmd} | conditional | flops 2883584 | bytes 65536208 | solution.py:390
  468.5 12.0 %collective-permute-done.34 = bf16[2,128,1024]{2,1,0:T(8,128)(2,1)S(1)} collective-permute-done((bf16[2,128,1024]{2,1,0:T(8,128)(2,1)S(1)}, bf16[2,128,1024]{2,1,0:T(8,128)(2,1)S(1)}, u32[]{:S(2)}, u32[]{:S(2)}) %collective-permute-start.34) | collective-permute-done | bytes 524320 | tf_op jit(solution)/shard_map/cond/branch_1_fun/ppermute | solution.py:212
  493.9 27.0 %conditional.13 = (bf16[1024,2048]{1,0:T(8,128)(2,1)}) conditional(s32[]{:T(128)} %bitcast.73, () %tuple.118, bf16[128,2048]{1,0:T(8,128)(2,1)S(1)} %get-tuple-element.241), branch_computations={%region_20.21_spmd, %region_21.22_spmd} | conditional | bytes 26214608 | solution.py:390
  574.8 52.7 %conditional.14 = (f32[128,2048]{1,0:T(8,128)S(1)}, f32[128,2048]{1,0:T(8,128)S(1)}) conditional(s32[]{:T(128)} %bitcast.73, () %tuple.117, (f32[1024,2048]{1,0:T(8,128)S(1)}, f32[1024,2048]{1,0:T(8,128)}) %tuple.124), branch_computations={%region_22.23_spmd, %region_23.24_spmd} | conditional | flops 5767168 | bytes 131072416 | solution.py:390
  630.6 28.2 %conditional.15 = (bf16[1024,2048]{1,0:T(8,128)(2,1)}) conditional(s32[]{:T(128)} %bitcast.73, () %tuple.127, bf16[128,2048]{1,0:T(8,128)(2,1)} %get-tuple-element.159), branch_computations={%region_25.26_spmd, %region_26.27_spmd} | conditional | bytes 26214608 | solution.py:390
  658.9 28.7 %conditional.16 = (bf16[1024,256]{0,1:T(8,128)(2,1)}, bf16[2048,256]{0,1:T(8,128)(2,1)}, bf16[2048,256]{0,1:T(8,128)(2,1)}, bf16[2,256,2048]{2,1,0:T(8,128)(2,1)}) conditional(s32[]{:T(128)} %bitcast.73, () %tuple.126, (bf16[1024,2048]{1,0:T(8,128)(2,1)}, bf16[256,2048]{1,0:T(8,128)(2,1)}, bf16[8,256,2,128]{3,2,1,0:T(2,128)(2,1)}, ...), branch_computations={%region_28.29_spmd, %region_29.31_spmd} | conditional | flops 1616640000 | bytes 54018204 | solution.py:390
  722.5 34.8 %conditional.17 = (f32[128,2048]{1,0:T(8,128)S(1)}) conditional(s32[]{:T(128)} %bitcast.73, () %tuple.125, f32[1024,2048]{1,0:T(8,128)} %fusion.106), branch_computations={%region_31.32_spmd, %region_32.33_spmd} | conditional | flops 2883584 | bytes 65536208 | solution.py:390
  736.6 12.3 %collective-permute-done.49 = bf16[2,128,1024]{2,1,0:T(8,128)(2,1)S(1)} collective-permute-done((bf16[2,128,1024]{2,1,0:T(8,128)(2,1)S(1)}, bf16[2,128,1024]{2,1,0:T(8,128)(2,1)S(1)}, u32[]{:S(2)}, u32[]{:S(2)}) %collective-permute-start.49) | collective-permute-done | bytes 524320 | tf_op jit(solution)/shard_map/cond/branch_1_fun/ppermute | solution.py:212
  759.1 27.8 %conditional.18 = (bf16[1024,2048]{1,0:T(8,128)(2,1)}) conditional(s32[]{:T(128)} %bitcast.73, () %tuple.131, bf16[128,2048]{1,0:T(8,128)(2,1)} %get-tuple-element.163), branch_computations={%region_35.36_spmd, %region_36.37_spmd} | conditional | bytes 26214608 | solution.py:390
  791.9 12.7 %reduce-scatter.10.cloned.1.call-done = bf16[512,1280]{1,0:T(8,128)(2,1)} async-done(((bf16[2048,1280]{1,0:T(8,128)(2,1)}), bf16[512,1280]{1,0:T(8,128)(2,1)}) %reduce-scatter.10.cloned.1.call-update) | async-done | bytes 1310736 | tf_op jit(solution)/shard_map/reduce_scatter | solution.py:460
  835.0 117.8 %conditional.19 = (f32[128,2048]{1,0:T(8,128)}, f32[3,2048]{1,0:T(4,128)S(1)}, bf16[8,256,1024]{2,1,0:T(8,128)(2,1)}, bf16[8,256,1280]{2,1,0:T(8,128)(2,1)}, bf16[4,256,2048]{2,1,0:T(8,128)(2,1)}) conditional(s32[]{:T(128)} %bitcast.73, () %tuple.130, (f32[1024,2048]{1,0:T(8,128)S(1)}, f32[3,2048]{1,0:T(4,128)S(1)}, f32[128,2048]{1,0:T(8,128)S(1)}, ...), branch_computations={%region_41.42_spmd, %region_42.46_spmd} | conditional | flops 31001348 | bytes 187643712 | solution.py:390
  857.1 11.9 %collective-permute-done.64 = bf16[256,1280]{1,0:T(8,128)(2,1)S(1)} collective-permute-done((bf16[256,1280]{1,0:T(8,128)(2,1)S(1)}, bf16[256,1280]{1,0:T(8,128)(2,1)S(1)}, u32[]{:S(2)}, u32[]{:S(2)}) %collective-permute-start.64) | collective-permute-done | bytes 655392 | tf_op jit(solution)/shard_map/cond/branch_1_fun/ppermute | solution.py:212
  886.6 21.4 %collective-permute-done.65 = bf16[2,256,1280]{2,1,0:T(8,128)(2,1)S(1)} collective-permute-done((bf16[2,256,1280]{2,1,0:T(8,128)(2,1)S(1)}, bf16[2,256,1280]{2,1,0:T(8,128)(2,1)S(1)}, u32[]{:S(2)}, u32[]{:S(2)}) %collective-permute-start.65) | collective-permute-done | bytes 1310752 | tf_op jit(solution)/shard_map/cond/branch_1_fun/ppermute | solution.py:212
  910.8 12.4 %collective-permute-done.52 = bf16[2,128,1024]{2,1,0:T(8,128)(2,1)S(1)} collective-permute-done((bf16[2,128,1024]{2,1,0:T(8,128)(2,1)S(1)}, bf16[2,128,1024]{2,1,0:T(8,128)(2,1)S(1)}, u32[]{:S(2)}, u32[]{:S(2)}) %collective-permute-start.52) | collective-permute-done | bytes 524320 | tf_op jit(solution)/shard_map/cond/branch_1_fun/ppermute | solution.py:212
  988.4 22.9 %adam_tiles.3 = (f32[6,256,2048]{2,1,0:T(8,128)}, f32[6,256,2048]{2,1,0:T(8,128)}, f32[6,256,2048]{2,1,0:T(8,128)}) custom-call(s32[3]{0:T(128)S(1)} %call_exported.3.visit_ref, s32[3]{0:T(128)S(1)} %bitcast.379, s32[24]{0:T(128)S(1)} %reshape.544.cp_ref, s32[3]{0:T(128)S(1)} %get-tuple-element.370.rp_ref, s32[3]{0:T(128)S(1)} %call_exported.4.hold_ref, ...), custom_call_target="tpu_custom_call" | custom-call | flops 47185920 | bytes 40894464 | tf_op jit(solution)/shard_map/adam_tiles/pallas_call | solution.py:182
  1014.3 23.2 %adam_tiles.4 = (f32[6,256,2048]{2,1,0:T(8,128)}, f32[6,256,2048]{2,1,0:T(8,128)}, f32[6,256,2048]{2,1,0:T(8,128)}) custom-call(s32[3]{0:T(128)S(1)} %copy-done.4, s32[3]{0:T(128)S(1)} %slice.561.mode_ref, s32[24]{0:T(128)S(1)} %reshape.543.cp_ref, s32[3]{0:T(128)S(1)} %get-tuple-element.371.rp_ref, ...), custom_call_target="tpu_custom_call", output_to_operand_aliasing={{0}: (11, {}), {1}: (12, {}), {2}: (13, {})} | custom-call | flops 47185920 | bytes 40894464 | tf_op jit(solution)/shard_map/adam_tiles/pallas_call | solution.py:182
  1041.1 28.1 %adam_tiles.5 = (f32[6,256,2048]{2,1,0:T(8,128)}, f32[6,256,2048]{2,1,0:T(8,128)}, f32[6,256,2048]{2,1,0:T(8,128)}) custom-call(s32[5]{0:T(128)S(1)} %get-tuple-element.400.visit_ref, s32[5]{0:T(128)S(1)} %get-tuple-element.399.mode_ref, s32[40]{0:T(128)S(1)} %select_n.497.cp_ref, ...), custom_call_target="tpu_custom_call", output_to_operand_aliasing={{0}: (13, {}), {1}: (14, {}), {2}: (15, {})} | custom-call | flops 78643200 | bytes 68157440 | tf_op jit(solution)/shard_map/adam_tiles/pallas_call | solution.py:182
  (695 shorter events, 761.7 us)
Async XLA Ops:
  25.4 42.2 %all-to-all-start = ((bf16[8,3,256,256]{3,2,1,0:T(8,128)(2,1)}), bf16[8,3,256,256]{3,2,1,0:T(8,128)(2,1)S(1)}, u32[]{:S(2)}, u32[]{:S(2)}) async-start(bf16[8,3,256,256]{3,2,1,0:T(8,128)(2,1)} %copy-done), calls=%async_computation | async-start | bytes 6291456 | tf_op jit(solution)/shard_map/all_to_all | solution.py:321
  30.7 175.0 %all-gather.6.cloned.1.call-start = ((), (), s32[]{:S(2)}) async-start(), calls=%async_computation.8 | async-start | bytes 3932160 | tf_op jit(solution)/shard_map/all_gather | solution.py:339
  72.5 169.4 %all-gather.8.cloned.1.call-start = ((), (), s32[]{:S(2)}) async-start(), calls=%async_computation.9 | async-start | bytes 2621440 | tf_op jit(solution)/shard_map/all_gather | solution.py:371
  104.8 31.3 %collective-permute-start.72 = (bf16[512,2048]{1,0:T(8,128)(2,1)}, bf16[512,2048]{1,0:T(8,128)(2,1)}, u32[]{:S(2)}, u32[]{:S(2)}) collective-permute-start(bf16[512,2048]{1,0:T(8,128)(2,1)} %get-tuple-element.357), channel_id=1, source_target_pairs={{0,1},{1,0},{2,3},{3,2},{4,5},{5,4},{6,7},{7,6},{8,9},{9,8},{10,11... | collective-permute-start | bytes 6291464 | tf_op jit(solution)/shard_map/ppermute | solution.py:212
  145.2 46.9 %all-to-all-start.1 = ((bf16[8,3,256,256]{3,2,1,0:T(8,128)(2,1)}), bf16[8,3,256,256]{3,2,1,0:T(8,128)(2,1)}, u32[]{:S(2)}, u32[]{:S(2)}) async-start(bf16[8,3,256,256]{3,2,1,0:T(8,128)(2,1)} %copy-done.1), calls=%async_computation.1 | async-start | bytes 6291456 | tf_op jit(solution)/shard_map/all_to_all | solution.py:321
  154.7 256.0 %all-gather.10.cloned.1.call-start = ((), (), s32[]{:S(2)}) async-start(), calls=%async_computation.10 | async-start | bytes 6553600 | tf_op jit(solution)/shard_map/all_gather | solution.py:339
  196.1 324.8 %all-gather.12.cloned.1.call-start = ((), (), s32[]{:S(2)}) async-start(), calls=%async_computation.11 | async-start | bytes 5242880 | tf_op jit(solution)/shard_map/all_gather | solution.py:339
  229.6 68.3 %collective-permute-start.80 = (bf16[256,4096]{1,0:T(8,128)(2,1)}, bf16[256,4096]{1,0:T(8,128)(2,1)}, u32[]{:S(2)}, u32[]{:S(2)}) collective-permute-start(bf16[256,4096]{1,0:T(8,128)(2,1)} %bitcast.405), channel_id=1, source_target_pairs={{0,4},{4,0},{1,5},{5,1},{2,6},{6,2},{3,7},{7,3},{8,12},{12,8},{9,1... | collective-permute-start | bytes 6291464 | tf_op jit(solution)/shard_map/ppermute | solution.py:212
  231.1 66.8 %collective-permute-start.79 = (bf16[256,4096]{1,0:T(8,128)(2,1)}, bf16[256,4096]{1,0:T(8,128)(2,1)}, u32[]{:S(2)}, u32[]{:S(2)}) collective-permute-start(bf16[256,4096]{1,0:T(8,128)(2,1)} %bitcast.406), channel_id=1, source_target_pairs={{0,2},{2,0},{1,3},{3,1},{4,6},{6,4},{5,7},{7,5},{8,10},{10,8},{9,1... | collective-permute-start | bytes 6291464 | tf_op jit(solution)/shard_map/ppermute | solution.py:212
  262.0 28.2 %collective-permute-start.27 = (bf16[2,128,1024]{2,1,0:T(8,128)(2,1)S(1)}, bf16[2,128,1024]{2,1,0:T(8,128)(2,1)S(1)}, u32[]{:S(2)}, u32[]{:S(2)}) collective-permute-start(bf16[2,128,1024]{2,1,0:T(8,128)(2,1)S(1)} %slice_bitcast_fusion.5), channel_id=1, source_target_pairs={{0,2},{2,0},{1,3},{3,1},{4,6},{6,4},{5,7},{7,5},{8,10},{10,8},{9,1... | collective-permute-start | bytes 1572872 | tf_op jit(solution)/shard_map/cond/branch_1_fun/ppermute | solution.py:212
  327.4 88.0 %collective-permute-start.83 = (bf16[1024,4096]{1,0:T(8,128)(2,1)}, bf16[1024,4096]{1,0:T(8,128)(2,1)}, u32[]{:S(2)}, u32[]{:S(2)}) collective-permute-start(bf16[1024,4096]{1,0:T(8,128)(2,1)} %get-tuple-element.347), channel_id=1, source_target_pairs={{0,1},{1,0},{2,3},{3,2},{4,5},{5,4},{6,7},{7,6},{8,9},{9,8},{10,11... | collective-permute-start | bytes 25165832 | tf_op jit(solution)/shard_map/ppermute | solution.py:212
  327.4 212.1 %all-gather.14.cloned.1.call-start = ((), (), s32[]{:S(2)}) async-start(), calls=%async_computation.12 | async-start | bytes 5242880 | tf_op jit(solution)/shard_map/all_gather | solution.py:339
  410.6 248.3 %reduce-scatter.6.cloned.1.call-start = ((), (), s32[]{:S(2)}) async-start(), calls=%async_computation.13 | async-start | bytes 5242880 | tf_op jit(solution)/shard_map/reduce_scatter | solution.py:460
  539.2 219.9 %reduce-scatter.8.cloned.1.call-start = ((), (), s32[]{:S(2)}) async-start(), calls=%async_computation.14 | async-start | bytes 5242880 | tf_op jit(solution)/shard_map/reduce_scatter | solution.py:460
  560.3 244.2 %reduce-scatter.10.cloned.1.call-start = ((), (), s32[]{:S(2)}) async-start(), calls=%async_computation.15 | async-start | bytes 6553600 | tf_op jit(solution)/shard_map/reduce_scatter | solution.py:460
  710.5 242.4 %reduce-scatter.14.cloned.1.call-start = ((), (), s32[]{:S(2)}) async-start(), calls=%async_computation.17 | async-start | bytes 2621440 | tf_op jit(solution)/shard_map/reduce_scatter | solution.py:460
  804.6 169.4 %reduce-scatter.12.cloned.1.call-start = ((), (), s32[]{:S(2)}) async-start(), calls=%async_computation.16 | async-start | bytes 3932160 | tf_op jit(solution)/shard_map/reduce_scatter | solution.py:460
  839.3 42.6 %collective-permute-start.51 = (f32[2,2,128,2048]{3,2,1,0:T(8,128)}, f32[2,2,128,2048]{3,2,1,0:T(8,128)}, u32[]{:S(2)}, u32[]{:S(2)}) collective-permute-start(f32[2,2,128,2048]{3,2,1,0:T(8,128)} %bitcast.56), channel_id=1, source_target_pairs={{0,1},{1,0},{2,3},{3,2},{4,5},{5,4},{6,7},{7,6},{8,9},{9,8},{10,11... | collective-permute-start | bytes 12582920 | tf_op jit(solution)/shard_map/cond/branch_1_fun/ppermute | solution.py:212
  869.1 38.8 %collective-permute-start.65 = (bf16[2,256,1280]{2,1,0:T(8,128)(2,1)S(1)}, bf16[2,256,1280]{2,1,0:T(8,128)(2,1)S(1)}, u32[]{:S(2)}, u32[]{:S(2)}) collective-permute-start(bf16[2,256,1280]{2,1,0:T(8,128)(2,1)S(1)} %pad_maximum_fusion.11), channel_id=1, source_target_pairs={{0,2},{2,0},{1,3},{3,1},{4,6},{6,4},{5,7},{7,5},{8,10},{10,8},{9,1... | collective-permute-start | bytes 3932168 | tf_op jit(solution)/shard_map/cond/branch_1_fun/ppermute | solution.py:212
  870.7 60.7 %collective-permute-start.67 = (bf16[2,256,2048]{2,1,0:T(8,128)(2,1)}, bf16[2,256,2048]{2,1,0:T(8,128)(2,1)S(1)}, u32[]{:S(2)}, u32[]{:S(2)}) collective-permute-start(bf16[2,256,2048]{2,1,0:T(8,128)(2,1)} %get-tuple-element.83), channel_id=1, source_target_pairs={{0,1},{1,0},{2,3},{3,2},{4,5},{5,4},{6,7},{7,6},{8,9},{9,8},{10,11... | collective-permute-start | bytes 6291464 | tf_op jit(solution)/shard_map/cond/branch_1_fun/ppermute | solution.py:212
  881.8 55.2 %collective-permute-start.63 = (bf16[4,256,1024]{2,1,0:T(8,128)(2,1)S(1)}, bf16[4,256,1024]{2,1,0:T(8,128)(2,1)S(1)}, u32[]{:S(2)}, u32[]{:S(2)}) collective-permute-start(bf16[4,256,1024]{2,1,0:T(8,128)(2,1)S(1)} %pad_maximum_fusion.10), channel_id=1, source_target_pairs={{0,1},{1,0},{2,3},{3,2},{4,5},{5,4},{6,7},{7,6},{8,9},{9,8},{10,11... | collective-permute-start | bytes 6291464 | tf_op jit(solution)/shard_map/cond/branch_1_fun/ppermute | solution.py:212
  908.2 32.9 %collective-permute-start.66 = (bf16[4,256,1280]{2,1,0:T(8,128)(2,1)S(1)}, bf16[4,256,1280]{2,1,0:T(8,128)(2,1)S(1)}, u32[]{:S(2)}, u32[]{:S(2)}) collective-permute-start(bf16[4,256,1280]{2,1,0:T(8,128)(2,1)S(1)} %pad_maximum_fusion.9), channel_id=1, source_target_pairs={{0,1},{1,0},{2,3},{3,2},{4,5},{5,4},{6,7},{7,6},{8,9},{9,8},{10,11... | collective-permute-start | bytes 7864328 | tf_op jit(solution)/shard_map/cond/branch_1_fun/ppermute | solution.py:212
  978.2 62.9 %all-to-all-start.2 = ((bf16[8,3,256,256]{3,2,1,0:T(8,128)(2,1)}), bf16[8,3,256,256]{3,2,1,0:T(8,128)(2,1)S(1)}, u32[]{:S(2)}, u32[]{:S(2)}) async-start(bf16[8,3,256,256]{3,2,1,0:T(8,128)(2,1)} %bitcast.386), calls=%async_computation.6 | async-start | bytes 6291456 | tf_op jit(solution)/shard_map/all_to_all | solution.py:549
  987.4 50.2 %collective-permute-start.88 = (bf16[2,256,2048]{2,1,0:T(8,128)(2,1)}, bf16[2,256,2048]{2,1,0:T(8,128)(2,1)}, u32[]{:S(2)}, u32[]{:S(2)}) collective-permute-start(bf16[2,256,2048]{2,1,0:T(8,128)(2,1)} %pad_maximum_fusion.20), channel_id=1, source_target_pairs={{0,1},{1,0},{2,3},{3,2},{4,5},{5,4},{6,7},{7,6},{8,9},{9,8},{10,11... | collective-permute-start | bytes 6291464 | tf_op jit(solution)/shard_map/ppermute | solution.py:212
  (160 other events, 3260.2 us)
Sparse Core Ops, SparseCore 0:
  72.6 66.4 all-gather.5
  141.3 47.5 all-gather.7
  196.3 97.9 all-gather.9
  327.5 80.8 all-gather.11
  410.7 81.2 all-gather.13
  539.3 77.7 reduce-scatter.5
  619.5 77.2 reduce-scatter.7
  710.7 93.8 reduce-scatter.9
  806.9 44.3 reduce-scatter.13
  853.6 59.5 reduce-scatter.11

commit v8 on v7

--- a/solution.py
+++ b/solution.py
@@ -213,9 +213,11 @@
 
 
 def gather_rows(value):
+    return gather_rest(value, swap(value, "x"), swap(value, "y"))
+
+
+def gather_rest(value, over_x, over_y):
     half = value.shape[0] // 2
-    over_x = swap(value, "x")
-    over_y = swap(value, "y")
     far_low = swap(over_y[:half], "x")
     far_high = swap(over_x[half:], "y")
     four = jnp.concatenate([value, over_y, over_x, far_low, far_high], axis=0)
@@ -356,9 +358,10 @@
         return target % 4 in (zz, (zz + 2) % 4)
 
     outer = take_rows(0, [after(value, local) for value in outer_blocks], needs_outer)
+    out_rows = take_rows(1, [after(value, local) for value in out_blocks], None)
     half_rows = rows // 2
     odd = z % 2
-    to_pair = lax.dynamic_slice_in_dim(outer, (1 - odd) * half_rows, half_rows, 0)
+    to_pair = lax.dynamic_slice_in_dim(after(outer, a_all), (1 - odd) * half_rows, half_rows, 0)
     own_half = lax.dynamic_slice_in_dim(outer, odd * half_rows, half_rows, 0)
     pair_swap = [
         (zz * 8 + place, (zz ^ 1) * 8 + place)
@@ -414,27 +417,27 @@
 
     probs = probabilities(query, keys, allowed)
     probs_low = probs.astype(bf16)
-    attended = joined(weighted(probs_low, values))
-    received[1] = after(received[1], attended)
+    mixed = weighted(probs_low, values).astype(bf16)
+    attended = mixed.reshape(-1, block)
+    received[1] = after(received[1], mixed)
     local_cross, local_in = columns_here(3, 5, 2), columns_here(8, 4, 2)
     w_cross = gather_z(local_cross)
     w_in = gather_z(local_in)
+    w_out = gather_z(after(out_rows, local_cross, local_in))
     slots, ctx_len, ctx_width = context.shape
-    ctx = after(context.reshape(slots * ctx_len, ctx_width), local_cross, local_in)
-    ctx_x, ctx_y = swap(ctx, "x"), swap(ctx, "y")
-    out_rows = take_rows(1, [after(value, local_cross, local_in) for value in out_blocks], None)
-    w_out = gather_z(out_rows)
-    h1 = h0 + chain_step(scatter_rows, matmul(attended, w_self_out))
-    half = slots * ctx_len // 2
-    far_low = swap(after(ctx_y, h1)[:half], "x")
-    far_high = swap(after(ctx_x, h1)[half:], "y")
-    b_all, d_ff = chain_step(
-        lambda one, two: (gather_rows(one), gather_rows(two)),
-        normalize(h1, gains[1]).astype(bf16),
-        grad_out.astype(bf16),
-    )
-    ctx_four = jnp.concatenate([ctx, ctx_y, ctx_x, far_low, far_high], axis=0)
-    ctx_all = jnp.concatenate([ctx_four, swap(ctx_four, "c")], axis=0)
+    ctx = context.reshape(slots * ctx_len, ctx_width)
+    part = matmul(attended, w_self_out)
+    h1, ctx_x, ctx_y = chain_step(
+        lambda one, two: (scatter_rows(one), swap(two, "x"), swap(two, "y")), part, after(ctx, local_cross, local_in)
+    )
+    h1 = h0 + h1
+
+    def with_context(one, two, own, over_x, over_y):
+        return gather_rows(one), gather_rows(two), gather_rest(own, over_x, over_y)
+
+    b_all, d_ff, ctx_all = chain_step(
+        with_context, normalize(h1, gains[1]).astype(bf16), grad_out.astype(bf16), ctx, ctx_x, ctx_y
+    )
 
     w_cross_q = w_cross[:, :block]
     w_low = w_cross[:, block : 3 * block]
@@ -472,10 +475,10 @@
     d_hidden = jax.vjp(gelu_tanh, hidden)[1](d_act)[0].astype(bf16)
     t_in = matmul_left(c_all, d_hidden).astype(bf16)
     g_in = sum_rows(t_in)
-    d_c, mixed = chain_step(
+    d_c, out_sum = chain_step(
         lambda one, two: (scatter_rows(one), scatter_rows(two)), matmul_right(d_hidden, w_in), matmul(activated, w_out)
     )
-    layer_out = (h2 + mixed).astype(bf16)
+    layer_out = (h2 + out_sum).astype(bf16)
     part_two, gain_grad_two = jax.vjp(normalize, h2, gains[2])[1](d_c)
     dh2 = grad_out + part_two
     d_cross_out = chain_step(gather_rows, after(dh2.astype(bf16), t_in))
@@ -521,29 +524,33 @@
         axis=0,
     )
     g_outer = sum_rows(after(t_outer, g_cross))
-    d_mixed = matmul_right(after(d_self_out, t_outer, g_cross), w_self_out)
-    d_q, d_k, d_v = through(d_mixed, query, keys, probs, probs_low, values)
+    (d_q, d_k, d_v), in_grads = chain_step(
+        lambda one, two: (
+            through(matmul_right(one, w_self_out), query, keys, probs, probs_low, values),
+            spread_columns(two),
+        ),
+        after(d_self_out, t_outer, g_cross),
+        g_in,
+    )
     d_qkv = jnp.concatenate([d_q, d_k, d_v], axis=1)
     g_qkv = sum_rows(matmul_left(a_all, d_qkv).astype(bf16))
 
-    def last_step(part, in_sum, cross_sum, out_pair, gain_grad_one, gain_grad_two):
+    back_swap = [(target, source) for source, target in pair_swap]
+
+    def last_step(part, cross_sum, out_pair, half, gain_grad_one, gain_grad_two):
         part_zero, gain_grad_zero = jax.vjp(normalize, h0, gains[0])[1](scatter_rows(part))
         gain_grads = jnp.stack([gain_grad_zero, gain_grad_one, gain_grad_two])
-        moved = spread_columns(in_sum), spread_columns(cross_sum), with_core(out_pair)
+        other_half = lax.ppermute(half, ALL_AXES, back_swap)
+        in_order = jnp.where(odd == 0, jnp.stack([half, other_half]), jnp.stack([other_half, half]))
+        outer_pair = from_y(in_order.reshape(rows, width), lambda zz, place, _: place % 4 in (zz, (zz + 2) % 4))
+        moved = spread_columns(cross_sum), with_core(out_pair), with_core(outer_pair)
         return part_zero, sum_everywhere(gain_grads), *moved
 
-    part_zero, gain_total, in_grads, cross_grads, out_grads = chain_step(
-        last_step, matmul_right(d_qkv, w_qkv), g_in, g_cross, out_grads, gain_grad_one, gain_grad_two
+    part_zero, gain_total, cross_grads, out_grads, outer_grads = chain_step(
+        last_step, matmul_right(d_qkv, w_qkv), g_cross, out_grads, g_outer, gain_grad_one, gain_grad_two
     )
     grad_tokens = (dh1 + part_zero).astype(bf16)
 
-    back_swap = [(target, source) for source, target in pair_swap]
-    other_half = lax.ppermute(after(g_outer, cross_grads), ALL_AXES, back_swap)
-    outer_grad = jnp.where(
-        odd == 0,
-        jnp.concatenate([g_outer, other_half], axis=0),
-        jnp.concatenate([other_half, g_outer], axis=0),
-    )
     by_tile = jnp.swapaxes(after(g_qkv, cross_grads).reshape(2, rows, 3, block), 1, 2)
     sent = jnp.broadcast_to(by_tile[:, None], (2, 4, 3, rows, block)).reshape(8, 3, rows, block)
     late_grads = lax.all_to_all(sent, PLANE, 0, 0, tiled=True).reshape(8 * 3, rows, block)
@@ -570,14 +577,12 @@
             [in_grads, cross_grads],
             [out_grads],
             slot[chosen],
-            after(early_mode, outer_grad, sent)[chosen] if first else early_mode[chosen],
+            after(early_mode, sent)[chosen] if first else early_mode[chosen],
             column_place[chosen].reshape(-1),
             row_source[chosen],
             np.zeros(half_cap, np.int32),
             early,
         )
-
-    outer_grads = with_core(from_y(outer_grad, lambda zz, place, _: place % 4 in (zz, (zz + 2) % 4)))
 
     n_late = 5
     order = jnp.sum(jnp.where(slot[None, :] < slot[:, None], late.astype(jnp.int32)[None, :], 0), axis=1)

time: 1090 us -> 1160 us (1.064)
  waiting for transfers between devices: 415 us -> 459 us
  local copies, waits for them, and re-layouts: 161 us -> 184 us
    ppermute x81, waiting for transfers between devices: 299 us -> 348 us  [swap(): return lax.ppermute(value, axis, [(0, 1), (1, 0)])]
    all_to_all x2, waiting for transfers between devices: 42.5 us -> 7.74 us  [exchange_columns(): lax.all_to_all(pack_columns(weights, table, first, half_cap), PLANE, 0, 0...]
    ppermute x1, waiting for transfers between devices: 9.98 us -> 30.2 us  [last_step(): other_half = lax.ppermute(half, ALL_AXES, back_swap)]
    cond x34 -> x57, local copies, waits for them, and re-layouts: 22.5 us -> 37.9 us
    slice x15 -> x16, local copies, waits for them, and re-layouts: 5.15 us -> 16.8 us  [the longest x1 12 us: plane_body(): ctx_low, ctx_high = (ctx_all[:, :width], ctx_all[:, width:])]
    unnamed x163 -> x139, local copies, waits for them, and re-layouts: 37.3 us -> 27.7 us
  transfers between devices with their start and end apart: 102 -> 102, of which waited for: 59 -> 64; matrix products, arithmetic and copies ran while one was open for 36% -> 36% of each run, Pallas kernels for 5% -> 5%
where the time goes in v8:
time: 1160 us; the launch traced here: 1140 us
  waiting for transfers between devices  459 us (40%)
  local copies, waits for them, and re-layouts  184 us (16%)
  matrix products  165 us (14%)
  other arithmetic  101 us (9%)
  starting transfers between devices  101 us (9%)
  Pallas kernels  86.4 us (7%)
  between operations  43.2 us (4%)
    ppermute x81, waiting for transfers between devices, swap(): return lax.ppermute(value, axis, [(0, 1), (1, 0)])  348 us
    ppermute x81, starting transfers between devices, swap(): return lax.ppermute(value, axis, [(0, 1), (1, 0)])  72.2 us
    pallas_call x3, Pallas kernels, adam_tiles(): pl.pallas_call(kernel, out_shape=(shape, shape, shape), grid_spec=pltpu.P...  69.7 us
    dot_general x8, matrix products, matmul_left(): lax.dot_general(left, right, (((0,), (0,)), ((), ())), preferred_element_...  53.6 us
    dot_general x8, matrix products, matmul(): return jnp.dot(left, right, preferred_element_type=f32)  47.4 us
    dot_general x6, matrix products, matmul_right(): lax.dot_general(left, right, (((1,), (1,)), ((), ())), preferred_element_...  42.6 us
    cond x57, local copies, waits for them, and re-layouts  37.9 us
    ppermute x1, waiting for transfers between devices, last_step(): other_half = lax.ppermute(half, ALL_AXES, back_swap)  30.2 us
  transfers between devices with their start and end apart: 102, of which 64 were waited for; matrix products, arithmetic and copies ran while one was open for 36% of the time, Pallas kernels for 5%

profile of v8, /device:TPU:0, one launch (start us, length us, event | category | flops | bytes accessed | tf_op | source)
XLA Modules:
  0.0 1141.8 jit_solution(8140392391390085823)
XLA Ops:
  123.1 17.4 %collective-permute-done.86 = bf16[128,2048]{1,0:T(8,128)(2,1)} collective-permute-done((bf16[128,2048]{1,0:T(8,128)(2,1)}, bf16[128,2048]{1,0:T(8,128)(2,1)}, u32[]{:S(2)}, u32[]{:S(2)}) %collective-permute-start.86) | collective-permute-done | bytes 524320 | tf_op jit(solution)/shard_map/ppermute | solution.py:372
  159.3 35.2 %collective-permute-done.82 = s32[256]{0:T(256)S(1)} collective-permute-done((s32[256]{0:T(256)S(1)}, s32[256]{0:T(256)S(1)}, u32[]{:S(2)}, u32[]{:S(2)}) %collective-permute-start.82) | collective-permute-done | bytes 1056 | tf_op jit(solution)/shard_map/ppermute | solution.py:212
  241.9 21.7 %collective-permute-done.88 = bf16[256,2048]{1,0:T(8,128)(2,1)} collective-permute-done((bf16[256,2048]{1,0:T(8,128)(2,1)}, bf16[256,2048]{1,0:T(8,128)(2,1)}, u32[]{:S(2)}, u32[]{:S(2)}) %collective-permute-start.88) | collective-permute-done | bytes 1048608 | tf_op jit(solution)/shard_map/ppermute | solution.py:354
  270.9 76.6 %conditional.11 = (f32[128,2048]{1,0:T(8,128)S(1)}, bf16[256,4096]{1,0:T(8,128)(2,1)}, bf16[256,4096]{1,0:T(8,128)(2,1)}) conditional(s32[]{:T(128)} %bitcast.81, () %tuple.112, (f32[1024,2048]{1,0:T(8,128)S(1)}, bf16[256,4096]{1,0:T(8,128)(2,1)}) %tuple.124), branch_computations={%region_10.11_spmd, %region_11.12_spmd} | conditional | flops 2883584 | bytes 82313520 | solution.py:393
  295.2 44.9 %collective-permute-done.35 = bf16[2,128,1024]{2,1,0:T(8,128)(2,1)S(1)} collective-permute-done((bf16[2,128,1024]{2,1,0:T(8,128)(2,1)S(1)}, bf16[2,128,1024]{2,1,0:T(8,128)(2,1)S(1)}, u32[]{:S(2)}, u32[]{:S(2)}) %collective-permute-start.35) | collective-permute-done | bytes 524320 | tf_op jit(solution)/shard_map/cond/branch_1_fun/ppermute | solution.py:212
  349.0 92.2 %conditional.12 = (bf16[1024,2048]{1,0:T(8,128)(2,1)}, bf16[1024,2048]{1,0:T(8,128)(2,1)}, bf16[2048,4096]{1,0:T(8,128)(2,1)}, bf16[2048,2048]{1,0:T(8,128)(2,1)}, bf16[2048,2048]{1,0:T(8,128)(2,1)}) conditional(s32[]{:T(128)} %bitcast.81, () %tuple.126, (bf16[128,2048]{1,0:T(8,128)(2,1)S(1)}, bf16[128,2048]{1,0:T(8,128)(2,1)S(1)}, ...), branch_computations={%region_13.14_spmd, %region_14.15_spmd} | conditional | bytes 174064160 | solution.py:393
  429.0 12.0 %fusion.182 = (bf16[2048,2048]{1,0:T(8,128)(2,1)}, bf16[2048,2048]{1,0:T(8,128)(2,1)}) fusion(bf16[2048,4096]{1,0:T(8,128)(2,1)} %constant_dynamic-update-slice_fusion.27), kind=kLoop, calls=%fused_computation.517 | loop fusion | bytes 33554432 | tf_op jit(solution)/shard_map/slice | solution.py:445
  477.9 35.5 %conditional.13 = (f32[128,2048]{1,0:T(8,128)S(1)}) conditional(s32[]{:T(128)} %bitcast.81, () %tuple.125, f32[1024,2048]{1,0:T(8,128)} %fusion.100), branch_computations={%region_17.18_spmd, %region_18.19_spmd} | conditional | flops 2883584 | bytes 65536208 | solution.py:393
  492.8 11.7 %collective-permute-done.40 = bf16[2,128,1024]{2,1,0:T(8,128)(2,1)S(1)} collective-permute-done((bf16[2,128,1024]{2,1,0:T(8,128)(2,1)S(1)}, bf16[2,128,1024]{2,1,0:T(8,128)(2,1)S(1)}, u32[]{:S(2)}, u32[]{:S(2)}) %collective-permute-start.40) | collective-permute-done | bytes 524320 | tf_op jit(solution)/shard_map/cond/branch_1_fun/ppermute | solution.py:212
  515.9 26.5 %conditional.14 = (bf16[1024,2048]{1,0:T(8,128)(2,1)}) conditional(s32[]{:T(128)} %bitcast.81, () %tuple.129, bf16[128,2048]{1,0:T(8,128)(2,1)S(1)} %get-tuple-element.321), branch_computations={%region_20.21_spmd, %region_21.22_spmd} | conditional | bytes 26214608 | solution.py:393
  596.1 52.2 %conditional.15 = (f32[128,2048]{1,0:T(8,128)S(1)}, f32[128,2048]{1,0:T(8,128)S(1)}) conditional(s32[]{:T(128)} %bitcast.81, () %tuple.128, (f32[1024,2048]{1,0:T(8,128)S(1)}, f32[1024,2048]{1,0:T(8,128)}) %tuple.136), branch_computations={%region_22.23_spmd, %region_23.24_spmd} | conditional | flops 5767168 | bytes 131072416 | solution.py:393
  651.3 27.7 %conditional.16 = (bf16[1024,2048]{1,0:T(8,128)(2,1)}) conditional(s32[]{:T(128)} %bitcast.81, () %tuple.139, bf16[128,2048]{1,0:T(8,128)(2,1)} %get-tuple-element.212), branch_computations={%region_25.26_spmd, %region_26.27_spmd} | conditional | bytes 26214608 | solution.py:393
  679.0 29.6 %conditional.17 = (bf16[1024,256]{0,1:T(8,128)(2,1)}, bf16[2048,256]{0,1:T(8,128)(2,1)}, bf16[2048,256]{0,1:T(8,128)(2,1)}, bf16[2,256,2048]{2,1,0:T(8,128)(2,1)}) conditional(s32[]{:T(128)} %bitcast.81, () %tuple.138, (bf16[1024,2048]{1,0:T(8,128)(2,1)}, bf16[256,2048]{1,0:T(8,128)(2,1)}, bf16[8,256,2,128]{3,2,1,0:T(2,128)(2,1)}, ...), branch_computations={%region_28.29_spmd, %region_29.31_spmd} | conditional | flops 1616640000 | bytes 62406868 | solution.py:393
  746.4 36.7 %conditional.18 = (f32[128,2048]{1,0:T(8,128)}) conditional(s32[]{:T(128)} %bitcast.81, () %tuple.137, f32[1024,2048]{1,0:T(8,128)} %fusion.95), branch_computations={%region_31.32_spmd, %region_32.33_spmd} | conditional | flops 2883584 | bytes 65536208 | solution.py:393
  787.6 26.3 %conditional.19 = (bf16[1024,2048]{1,0:T(8,128)(2,1)}) conditional(s32[]{:T(128)} %bitcast.81, () %tuple.144, bf16[128,2048]{1,0:T(8,128)(2,1)S(1)} %get-tuple-element.216), branch_computations={%region_35.36_spmd, %region_36.37_spmd} | conditional | bytes 26214608 | solution.py:393
  830.3 67.0 %conditional.20 = (bf16[1024,256]{0,1:T(8,128)(2,1)}, bf16[1024,256]{0,1:T(8,128)(2,1)}, bf16[1024,256]{0,1:T(8,128)(2,1)}, bf16[8,256,1024]{2,1,0:T(8,128)(2,1)}) conditional(s32[]{:T(128)} %bitcast.81, () %tuple.143, (bf16[1024,2048]{1,0:T(8,128)(2,1)}, bf16[256,2048]{1,0:T(8,128)(2,1)}, bf16[8,128,2,128]{3,2,1,0:T(2,128)(2,1)}, ...), branch_computations={%region_38.39_spmd, %region_39.41_spmd} | conditional | flops 1354496000 | bytes 72892776 | solution.py:393
  833.2 12.3 %collective-permute-done.29 = bf16[256,1024]{1,0:T(8,128)(2,1)S(1)} collective-permute-done((bf16[256,1024]{1,0:T(8,128)(2,1)S(1)}, bf16[256,1024]{1,0:T(8,128)(2,1)S(1)}, u32[]{:S(2)}, u32[]{:S(2)}) %collective-permute-start.29) | collective-permute-done | bytes 524320 | tf_op jit(solution)/shard_map/cond/branch_1_fun/ppermute | solution.py:212
  847.1 22.7 %collective-permute-done.30 = bf16[2,256,1024]{2,1,0:T(8,128)(2,1)S(1)} collective-permute-done((bf16[2,256,1024]{2,1,0:T(8,128)(2,1)S(1)}, bf16[2,256,1024]{2,1,0:T(8,128)(2,1)S(1)}, u32[]{:S(2)}, u32[]{:S(2)}) %collective-permute-start.30) | collective-permute-done | bytes 1048608 | tf_op jit(solution)/shard_map/cond/branch_1_fun/ppermute | solution.py:212
  922.7 129.9 %conditional.21 = (f32[128,2048]{1,0:T(8,128)}, f32[3,2048]{1,0:T(4,128)S(1)}, bf16[8,256,1280]{2,1,0:T(8,128)(2,1)}, bf16[4,256,2048]{2,1,0:T(8,128)(2,1)}, bf16[4,256,2048]{2,1,0:T(8,128)(2,1)}) conditional(s32[]{:T(128)} %bitcast.81, () %tuple.142, (f32[1024,2048]{1,0:T(8,128)}, f32[3,2048]{1,0:T(4,128)S(1)}, f32[128,2048]{1,0:T(8,128)S(1)}, ...), branch_computations={%region_44.45_spmd, %region_45.49_spmd} | conditional | flops 28379908 | bytes 188168064 | solution.py:393
  936.4 30.2 %collective-permute-done.73 = bf16[128,2048]{1,0:T(8,128)(2,1)} collective-permute-done((bf16[128,2048]{1,0:T(8,128)(2,1)}, bf16[128,2048]{1,0:T(8,128)(2,1)}, u32[]{:S(2)}, u32[]{:S(2)}) %collective-permute-start.73) | collective-permute-done | bytes 524320 | tf_op jit(solution)/shard_map/cond/branch_1_fun/ppermute | solution.py:543
  989.9 14.7 %collective-permute-done.70 = bf16[2,256,1280]{2,1,0:T(8,128)(2,1)S(1)} collective-permute-done((bf16[2,256,1280]{2,1,0:T(8,128)(2,1)S(1)}, bf16[2,256,1280]{2,1,0:T(8,128)(2,1)S(1)}, u32[]{:S(2)}, u32[]{:S(2)}) %collective-permute-start.70) | collective-permute-done | bytes 1310752 | tf_op jit(solution)/shard_map/cond/branch_1_fun/ppermute | solution.py:212
  1061.9 22.9 %adam_tiles.3 = (f32[6,256,2048]{2,1,0:T(8,128)}, f32[6,256,2048]{2,1,0:T(8,128)}, f32[6,256,2048]{2,1,0:T(8,128)}) custom-call(s32[3]{0:T(128)S(1)} %call_exported.3.visit_ref, s32[3]{0:T(128)S(1)} %bitcast.384, s32[24]{0:T(128)S(1)} %reshape.510.cp_ref, s32[3]{0:T(128)S(1)} %get-tuple-element.458.rp_ref, s32[3]{0:T(128)S(1)} %call_exported.4.hold_ref, ...), custom_call_target="tpu_custom_call" | custom-call | flops 47185920 | bytes 40894464 | tf_op jit(solution)/shard_map/adam_tiles/pallas_call | solution.py:182
  1087.7 22.9 %adam_tiles.4 = (f32[6,256,2048]{2,1,0:T(8,128)}, f32[6,256,2048]{2,1,0:T(8,128)}, f32[6,256,2048]{2,1,0:T(8,128)}) custom-call(s32[3]{0:T(128)S(1)} %copy-done.5, s32[3]{0:T(128)S(1)} %slice.563.mode_ref, s32[24]{0:T(128)S(1)} %reshape.509.cp_ref, s32[3]{0:T(128)S(1)} %get-tuple-element.459.rp_ref, ...), custom_call_target="tpu_custom_call", output_to_operand_aliasing={{0}: (11, {}), {1}: (12, {}), {2}: (13, {})} | custom-call | flops 47185920 | bytes 40894464 | tf_op jit(solution)/shard_map/adam_tiles/pallas_call | solution.py:182
  1110.6 23.9 %adam_tiles.5 = (f32[6,256,2048]{2,1,0:T(8,128)}, f32[6,256,2048]{2,1,0:T(8,128)}, f32[6,256,2048]{2,1,0:T(8,128)}) custom-call(s32[5]{0:T(128)S(1)} %broadcast_select_fusion.6.visit_ref, s32[5]{0:T(128)S(1)} %compare_select_fusion.11.mode_ref, s32[40]{0:T(128)S(1)} %select_n.502.cp_ref, ...), custom_call_target="tpu_custom_call", output_to_operand_aliasing={{0}: (13, {}), {1}: (14, {}), {2}: (15, {})} | custom-call | flops 78643200 | bytes 68157440 | tf_op jit(solution)/shard_map/adam_tiles/pallas_call | solution.py:182
  (693 shorter events, 803.4 us)
Async XLA Ops:
  25.9 42.2 %all-to-all-start = ((bf16[8,3,256,256]{3,2,1,0:T(8,128)(2,1)}), bf16[8,3,256,256]{3,2,1,0:T(8,128)(2,1)S(1)}, u32[]{:S(2)}, u32[]{:S(2)}) async-start(bf16[8,3,256,256]{3,2,1,0:T(8,128)(2,1)} %copy-done), calls=%async_computation | async-start | bytes 6291456 | tf_op jit(solution)/shard_map/all_to_all | solution.py:323
  31.2 164.8 %all-gather.6.cloned.1.call-start = ((), (), s32[]{:S(2)}) async-start(), calls=%async_computation.8 | async-start | bytes 3932160 | tf_op jit(solution)/shard_map/all_gather | solution.py:341
  75.0 191.8 %all-gather.8.cloned.1.call-start = ((), (), s32[]{:S(2)}) async-start(), calls=%async_computation.9 | async-start | bytes 2621440 | tf_op jit(solution)/shard_map/all_gather | solution.py:374
  152.8 65.1 %all-to-all-start.1 = ((bf16[8,3,256,256]{3,2,1,0:T(8,128)(2,1)}), bf16[8,3,256,256]{3,2,1,0:T(8,128)(2,1)}, u32[]{:S(2)}, u32[]{:S(2)}) async-start(bf16[8,3,256,256]{3,2,1,0:T(8,128)(2,1)} %copy-done.1), calls=%async_computation.1 | async-start | bytes 6291456 | tf_op jit(solution)/shard_map/all_to_all | solution.py:323
  157.2 284.0 %all-gather.10.cloned.1.call-start = ((), (), s32[]{:S(2)}) async-start(), calls=%async_computation.10 | async-start | bytes 6553600 | tf_op jit(solution)/shard_map/all_gather | solution.py:341
  157.3 37.1 %collective-permute-start.82 = (s32[256]{0:T(256)S(1)}, s32[256]{0:T(256)S(1)}, u32[]{:S(2)}, u32[]{:S(2)}) collective-permute-start(s32[256]{0:T(256)S(1)} %pad_add_fusion.1), channel_id=1, source_target_pairs={{0,4},{4,0},{1,5},{5,1},{2,6},{6,2},{3,7},{7,3},{8,12},{12,8},{9,1... | collective-permute-start | bytes 3080 | tf_op jit(solution)/shard_map/ppermute | solution.py:212
  221.9 320.5 %all-gather.12.cloned.1.call-start = ((), (), s32[]{:S(2)}) async-start(), calls=%async_computation.11 | async-start | bytes 5242880 | tf_op jit(solution)/shard_map/all_gather | solution.py:341
  227.7 333.1 %all-gather.14.cloned.1.call-start = ((), (), s32[]{:S(2)}) async-start(), calls=%async_computation.12 | async-start | bytes 5242880 | tf_op jit(solution)/shard_map/all_gather | solution.py:341
  266.7 412.3 %reduce-scatter.6.cloned.1.call-start = ((), (), s32[]{:S(2)}) async-start(), calls=%async_computation.13 | async-start | bytes 5242880 | tf_op jit(solution)/shard_map/reduce_scatter | solution.py:463
  280.1 67.3 %collective-permute-start.37 = (bf16[256,4096]{1,0:T(8,128)(2,1)}, bf16[256,4096]{1,0:T(8,128)(2,1)}, u32[]{:S(2)}, u32[]{:S(2)}) collective-permute-start(bf16[256,4096]{1,0:T(8,128)(2,1)} %get-tuple-element.91), channel_id=1, source_target_pairs={{0,4},{4,0},{1,5},{5,1},{2,6},{6,2},{3,7},{7,3},{8,12},{12,8},{9,1... | collective-permute-start | bytes 6291464 | tf_op jit(solution)/shard_map/cond/branch_1_fun/ppermute | solution.py:212
  280.7 66.7 %collective-permute-start.38 = (bf16[256,4096]{1,0:T(8,128)(2,1)}, bf16[256,4096]{1,0:T(8,128)(2,1)}, u32[]{:S(2)}, u32[]{:S(2)}) collective-permute-start(bf16[256,4096]{1,0:T(8,128)(2,1)} %get-tuple-element.91), channel_id=1, source_target_pairs={{0,2},{2,0},{1,3},{3,1},{4,6},{6,4},{5,7},{7,5},{8,10},{10,8},{9,1... | collective-permute-start | bytes 6291464 | tf_op jit(solution)/shard_map/cond/branch_1_fun/ppermute | solution.py:212
  282.2 57.9 %collective-permute-start.35 = (bf16[2,128,1024]{2,1,0:T(8,128)(2,1)S(1)}, bf16[2,128,1024]{2,1,0:T(8,128)(2,1)S(1)}, u32[]{:S(2)}, u32[]{:S(2)}) collective-permute-start(bf16[2,128,1024]{2,1,0:T(8,128)(2,1)S(1)} %slice_bitcast_fusion.3), channel_id=1, source_target_pairs={{0,4},{4,0},{1,5},{5,1},{2,6},{6,2},{3,7},{7,3},{8,12},{12,8},{9,1... | collective-permute-start | bytes 1572872 | tf_op jit(solution)/shard_map/cond/branch_1_fun/ppermute | solution.py:212
  295.1 49.8 %collective-permute-start.34 = (bf16[128,1024]{1,0:T(8,128)(2,1)S(1)}, bf16[128,1024]{1,0:T(8,128)(2,1)S(1)}, u32[]{:S(2)}, u32[]{:S(2)}) collective-permute-start(bf16[128,1024]{1,0:T(8,128)(2,1)S(1)} %fusion.4), channel_id=1, source_target_pairs={{0,4},{4,0},{1,5},{5,1},{2,6},{6,2},{3,7},{7,3},{8,12},{12,8},{9,1... | collective-permute-start | bytes 786440 | tf_op jit(solution)/shard_map/cond/branch_1_fun/ppermute | solution.py:212
  375.8 45.3 %collective-permute-start.27 = (bf16[1024,4096]{1,0:T(8,128)(2,1)S(1)}, bf16[1024,4096]{1,0:T(8,128)(2,1)}, u32[]{:S(2)}, u32[]{:S(2)}) collective-permute-start(bf16[1024,4096]{1,0:T(8,128)(2,1)S(1)} %get-tuple-element.341), channel_id=1, source_target_pairs={{0,1},{1,0},{2,3},{3,2},{4,5},{5,4},{6,7},{7,6},{8,9},{9,8},{10,11... | collective-permute-start | bytes 25165832 | tf_op jit(solution)/shard_map/cond/branch_1_fun/ppermute | solution.py:212
  560.5 227.0 %reduce-scatter.8.cloned.1.call-start = ((), (), s32[]{:S(2)}) async-start(), calls=%async_computation.14 | async-start | bytes 5242880 | tf_op jit(solution)/shard_map/reduce_scatter | solution.py:463
  581.7 248.5 %reduce-scatter.10.cloned.1.call-start = ((), (), s32[]{:S(2)}) async-start(), calls=%async_computation.15 | async-start | bytes 6553600 | tf_op jit(solution)/shard_map/reduce_scatter | solution.py:463
  734.8 187.8 %reduce-scatter.12.cloned.1.call-start = ((), (), s32[]{:S(2)}) async-start(), calls=%async_computation.16 | async-start | bytes 2621440 | tf_op jit(solution)/shard_map/reduce_scatter | solution.py:463
  830.2 222.3 %reduce-scatter.14.cloned.1.call-start = ((), (), s32[]{:S(2)}) async-start(), calls=%async_computation.17 | async-start | bytes 3932160 | tf_op jit(solution)/shard_map/reduce_scatter | solution.py:463
  930.7 54.6 %collective-permute-start.59 = (f32[2,2,128,2048]{3,2,1,0:T(8,128)}, f32[2,2,128,2048]{3,2,1,0:T(8,128)}, u32[]{:S(2)}, u32[]{:S(2)}) collective-permute-start(f32[2,2,128,2048]{3,2,1,0:T(8,128)} %bitcast.61), channel_id=1, source_target_pairs={{0,1},{1,0},{2,3},{3,2},{4,5},{5,4},{6,7},{7,6},{8,9},{9,8},{10,11... | collective-permute-start | bytes 12582920 | tf_op jit(solution)/shard_map/cond/branch_1_fun/ppermute | solution.py:212
  931.2 35.4 %collective-permute-start.73 = (bf16[128,2048]{1,0:T(8,128)(2,1)}, bf16[128,2048]{1,0:T(8,128)(2,1)}, u32[]{:S(2)}, u32[]{:S(2)}) collective-permute-start(bf16[128,2048]{1,0:T(8,128)(2,1)} %get-tuple-element.123), channel_id=1, source_target_pairs={{8,0},{10,2},{12,4},{14,6},{1,9},{3,11},{5,13},{7,15},{24,16},{26,... | collective-permute-start | bytes 1572872 | tf_op jit(solution)/shard_map/cond/branch_1_fun/ppermute | solution.py:543
  934.9 36.8 %collective-permute-start.69 = (bf16[256,1280]{1,0:T(8,128)(2,1)}, bf16[256,1280]{1,0:T(8,128)(2,1)}, u32[]{:S(2)}, u32[]{:S(2)}) collective-permute-start(bf16[256,1280]{1,0:T(8,128)(2,1)} %get-tuple-element.418), channel_id=1, source_target_pairs={{0,4},{4,0},{1,5},{5,1},{2,6},{6,2},{3,7},{7,3},{8,12},{12,8},{9,1... | collective-permute-start | bytes 1966088 | tf_op jit(solution)/shard_map/cond/branch_1_fun/ppermute | solution.py:212
  973.8 55.5 %collective-permute-start.72 = (bf16[2,256,2048]{2,1,0:T(8,128)(2,1)}, bf16[2,256,2048]{2,1,0:T(8,128)(2,1)S(1)}, u32[]{:S(2)}, u32[]{:S(2)}) collective-permute-start(bf16[2,256,2048]{2,1,0:T(8,128)(2,1)} %get-tuple-element.121), channel_id=1, source_target_pairs={{0,1},{1,0},{2,3},{3,2},{4,5},{5,4},{6,7},{7,6},{8,9},{9,8},{10,11... | collective-permute-start | bytes 6291464 | tf_op jit(solution)/shard_map/cond/branch_1_fun/ppermute | solution.py:212
  985.2 49.6 %collective-permute-start.75 = (bf16[2,256,2048]{2,1,0:T(8,128)(2,1)S(1)}, bf16[2,256,2048]{2,1,0:T(8,128)(2,1)S(1)}, u32[]{:S(2)}, u32[]{:S(2)}) collective-permute-start(bf16[2,256,2048]{2,1,0:T(8,128)(2,1)S(1)} %pad_maximum_fusion.13), channel_id=1, source_target_pairs={{0,1},{1,0},{2,3},{3,2},{4,5},{5,4},{6,7},{7,6},{8,9},{9,8},{10,11... | collective-permute-start | bytes 6291464 | tf_op jit(solution)/shard_map/cond/branch_1_fun/ppermute | solution.py:212
  1056.8 53.8 %all-to-all-start.2 = ((bf16[8,3,256,256]{3,2,1,0:T(8,128)(2,1)}), bf16[8,3,256,256]{3,2,1,0:T(8,128)(2,1)S(1)}, u32[]{:S(2)}, u32[]{:S(2)}) async-start(bf16[8,3,256,256]{3,2,1,0:T(8,128)(2,1)} %bitcast.391), calls=%async_computation.7 | async-start | bytes 6291456 | tf_op jit(solution)/shard_map/all_to_all | solution.py:556
  (159 other events, 2545.6 us)
Sparse Core Ops, SparseCore 0:
  75.1 65.6 all-gather.5
  142.9 48.3 all-gather.7
  222.0 98.8 all-gather.9
  322.3 79.1 all-gather.11
  402.9 79.2 all-gather.13
  560.7 77.6 reduce-scatter.5
  640.8 77.2 reduce-scatter.7
  734.9 95.2 reduce-scatter.9
  833.1 44.3 reduce-scatter.11
  909.4 66.2 reduce-scatter.13

commit v9 on v7

--- a/solution.py
+++ b/solution.py
@@ -131,6 +131,39 @@
     )(which, index, *sources)
 
 
+def pack_gradients(groups, which, column, rows, width, slots):
+    n_src = len(groups)
+
+    def kernel(which_ref, column_ref, *refs):
+        place = pl.program_id(0) * slots + pl.program_id(1)
+        out_ref = refs[n_src]
+        for number in range(n_src):
+
+            @pl.when(which_ref[place] == number)
+            def _():
+                out_ref[0, 0] = refs[number][...]
+
+    def spec(number):
+        def at(rank, k, which, column):
+            place = rank * slots + k
+            return (rank // 4, jnp.where(which[place] == number, column[place], 0))
+
+        return pl.BlockSpec((rows, width), at)
+
+    return pl.pallas_call(
+        kernel,
+        out_shape=jax.ShapeDtypeStruct((8, slots, rows, width), bf16),
+        grid_spec=pltpu.PrefetchScalarGridSpec(
+            num_scalar_prefetch=2,
+            grid=(8, slots),
+            in_specs=[spec(number) for number in range(n_src)],
+            out_specs=pl.BlockSpec((1, 1, rows, width), lambda rank, k, which, column: (rank, k, 0, 0)),
+        ),
+        compiler_params=pltpu.CompilerParams(vmem_limit_bytes=VMEM_LIMIT),
+        name="pack_gradients",
+    )(which, column, *groups)
+
+
 def adam_tiles(master, one, two, columns_from, rows_from, visit, mode, column_place, row_place, hold, previous=None):
     _, rows, columns = master.shape
     width = columns // 8
@@ -165,8 +198,7 @@
 
     def column_spec(number):
         def at(n, b, vi, mo, cp, rp, ho):
-            place = jnp.where(mo[n] == number + 2, cp[n * 8 + block_of(n, b, ho)], 0)
-            return (place // 8, 0, place % 8)
+            return (jnp.where(mo[n] == number + 2, cp[n * 8 + block_of(n, b, ho)], 0), 0, 0)
 
         return pl.BlockSpec((1, rows, width), at)
 
@@ -222,15 +254,6 @@
     return jnp.concatenate([four, swap(four, "c")], axis=0)
 
 
-def spread_columns(value):
-    rows = value.shape[0] // 2
-    low = lax.axis_index("x") == 0
-    upper, lower = value[:rows], value[rows:]
-    two = jnp.stack([jnp.where(low, upper, lower), swap(jnp.where(low, lower, upper), "x")])
-    four = jnp.concatenate([two, swap(two, "y")])
-    return jnp.concatenate([four, swap(four, "c")])
-
-
 def scatter_rows(part):
     rows, width = part.shape[0] // 8, part.shape[1]
     half = width // 2
@@ -316,10 +339,11 @@
     row_slots = of_tiles(jnp.concatenate([outer_tiles, out_tiles]), rank)
     row_owners = of_tiles(jnp.stack([outer_tiles[0], outer_tiles[2], out_tiles[0], out_tiles[2]]), owners)
 
-    def exchange_columns(first, weights):
-        table = column_table[first : first + half_cap].reshape(-1)
-        got = lax.all_to_all(pack_columns(weights, table, first, half_cap), PLANE, 0, 0, tiled=True)
-        return got.reshape(8 * half_cap, rows, block)
+    def pack_first(weights):
+        return pack_columns(weights, column_table[:half_cap].reshape(-1), 0, half_cap)
+
+    def pack_second(weights):
+        return pack_columns(weights, column_table[half_cap:].reshape(-1), half_cap, half_cap)
 
     def my_block(slot):
         return lax.dynamic_index_in_dim(master, slot, 0, keepdims=False).astype(bf16)
@@ -328,8 +352,17 @@
     outer_blocks = [my_block(row_slots[mask]) for mask in range(4)]
     out_blocks = [my_block(row_slots[4 + mask]) for mask in range(4)]
     a_in = normalize(h0, gains[0]).astype(bf16)
-    received = [exchange_columns(0, after(master, column_part, column_place, row_slots, row_owners))]
-    received = [after(received[0], a_in, *outer_blocks, *out_blocks)]
+    sent = pack_first(after(master, column_part, column_place, row_slots, row_owners))
+    received = [lax.all_to_all(sent, PLANE, 0, 0, tiled=True).reshape(8 * half_cap, rows, block)]
+    seg = segments(lengths[0], count)
+    live = keep == 1
+    code = seg * 2 + live.astype(jnp.int32)
+    for axis in ("y", "x", "c"):
+        code = jnp.concatenate([code, swap(code, axis)])
+    seg_all = (code // 2).reshape(8, count)
+    live_all = (code % 2 == 1).reshape(8, count)
+    grad_out = cotangent.astype(f32) * live.astype(f32)[:, None]
+    received = [after(received[0], a_in, code, *outer_blocks, *out_blocks)]
 
     def columns_here(first, count, parts):
         chosen = slice(2 * first, 2 * (first + count))
@@ -341,7 +374,9 @@
     local = columns_here(0, 3, 1)
     w_qkv = gather_z(local)
     a_all = gather_rows(after(a_in, local))
-    received.append(exchange_columns(half_cap, after(master, a_all)))
+    d_ff = gather_rows(after(grad_out.astype(bf16), local))
+    sent = pack_second(after(master, a_all, d_ff))
+    received.append(lax.all_to_all(sent, PLANE, 0, 0, tiled=True).reshape(8 * half_cap, rows, block))
 
     def take_rows(kind, blocks, keep_pair):
         here, there = row_owners[2 * kind], row_owners[2 * kind + 1]
@@ -356,9 +391,10 @@
         return target % 4 in (zz, (zz + 2) % 4)
 
     outer = take_rows(0, [after(value, local) for value in outer_blocks], needs_outer)
+    out_rows = take_rows(1, [after(value, local) for value in out_blocks], None)
     half_rows = rows // 2
     odd = z % 2
-    to_pair = lax.dynamic_slice_in_dim(outer, (1 - odd) * half_rows, half_rows, 0)
+    to_pair = lax.dynamic_slice_in_dim(after(outer, sent), (1 - odd) * half_rows, half_rows, 0)
     own_half = lax.dynamic_slice_in_dim(outer, odd * half_rows, half_rows, 0)
     pair_swap = [
         (zz * 8 + place, (zz ^ 1) * 8 + place)
@@ -373,15 +409,6 @@
     w_self_out = jnp.where(low_y, outer_all[:rows], outer_all[rows:])
     w_cross_out = jnp.where(low_y, outer_all[rows:], outer_all[:rows])
 
-    seg = segments(lengths[0], count)
-    live = keep == 1
-    code = seg * 2 + live.astype(jnp.int32)
-    for axis in ("y", "x", "c"):
-        code = jnp.concatenate([code, swap(code, axis)])
-    seg_all = (code // 2).reshape(8, count)
-    live_all = (code % 2 == 1).reshape(8, count)
-
-    grad_out = cotangent.astype(f32) * live.astype(f32)[:, None]
     present = owners[0] >= 0
 
     def chain_step(move, *values):
@@ -414,25 +441,25 @@
 
     probs = probabilities(query, keys, allowed)
     probs_low = probs.astype(bf16)
-    attended = joined(weighted(probs_low, values))
-    received[1] = after(received[1], attended)
+    mixed = weighted(probs_low, values).astype(bf16)
+    attended = mixed.reshape(-1, block)
+    received[1] = after(received[1], mixed)
     local_cross, local_in = columns_here(3, 5, 2), columns_here(8, 4, 2)
     w_cross = gather_z(local_cross)
-    w_in = gather_z(local_in)
+    middle = width // 2
+    halves = jnp.concatenate([out_rows[:, :middle], out_rows[:, middle:]], axis=0)
+    w_layer = gather_z(jnp.concatenate([local_in, halves], axis=1))
+    w_in = w_layer[:, : 4 * block]
+    w_out = jnp.swapaxes(w_layer[:, 4 * block :].reshape(4, 2, rows, middle), 1, 2).reshape(4 * rows, width)
+
     slots, ctx_len, ctx_width = context.shape
     ctx = after(context.reshape(slots * ctx_len, ctx_width), local_cross, local_in)
     ctx_x, ctx_y = swap(ctx, "x"), swap(ctx, "y")
-    out_rows = take_rows(1, [after(value, local_cross, local_in) for value in out_blocks], None)
-    w_out = gather_z(out_rows)
     h1 = h0 + chain_step(scatter_rows, matmul(attended, w_self_out))
     half = slots * ctx_len // 2
     far_low = swap(after(ctx_y, h1)[:half], "x")
     far_high = swap(after(ctx_x, h1)[half:], "y")
-    b_all, d_ff = chain_step(
-        lambda one, two: (gather_rows(one), gather_rows(two)),
-        normalize(h1, gains[1]).astype(bf16),
-        grad_out.astype(bf16),
-    )
+    b_all = chain_step(gather_rows, normalize(h1, gains[1]).astype(bf16))
     ctx_four = jnp.concatenate([ctx, ctx_y, ctx_x, far_low, far_high], axis=0)
     ctx_all = jnp.concatenate([ctx_four, swap(ctx_four, "c")], axis=0)
 
@@ -472,10 +499,10 @@
     d_hidden = jax.vjp(gelu_tanh, hidden)[1](d_act)[0].astype(bf16)
     t_in = matmul_left(c_all, d_hidden).astype(bf16)
     g_in = sum_rows(t_in)
-    d_c, mixed = chain_step(
+    d_c, out_sum = chain_step(
         lambda one, two: (scatter_rows(one), scatter_rows(two)), matmul_right(d_hidden, w_in), matmul(activated, w_out)
     )
-    layer_out = (h2 + mixed).astype(bf16)
+    layer_out = (h2 + out_sum).astype(bf16)
     part_two, gain_grad_two = jax.vjp(normalize, h2, gains[2])[1](d_c)
     dh2 = grad_out + part_two
     d_cross_out = chain_step(gather_rows, after(dh2.astype(bf16), t_in))
@@ -521,53 +548,58 @@
         axis=0,
     )
     g_outer = sum_rows(after(t_outer, g_cross))
-    d_mixed = matmul_right(after(d_self_out, t_outer, g_cross), w_self_out)
+    group_of = np.array([0, 0, 0, 0, 0, 0, 0, 0, 0, 0, 1, 1, 1, 1, 0, 0, 0, 0], np.int32)
+    column_of = np.array([0, 0, 0, 0, 0, 1, 3, 2, 4, 0, 0, 1, 2, 3, 0, 0, 0, 0], np.int32)
+    group_at = jnp.sum(jnp.where(holds, group_of, 0), axis=2)
+    column_at = jnp.sum(jnp.where(holds, column_of, 0), axis=2)
+    column_at = jnp.where(group_at == 1, (column_at + f) % 4, column_at)
+    sent = pack_gradients(
+        [g_cross, g_in], jnp.tile(group_at.reshape(-1), 2), jnp.tile(column_at.reshape(-1), 2), rows, block, cap
+    )
+    early_grads = lax.all_to_all(sent, PLANE, 0, 0, tiled=True).reshape(8 * cap, rows, block)
+    d_mixed = matmul_right(after(d_self_out, t_outer, sent), w_self_out)
     d_q, d_k, d_v = through(d_mixed, query, keys, probs, probs_low, values)
     d_qkv = jnp.concatenate([d_q, d_k, d_v], axis=1)
     g_qkv = sum_rows(matmul_left(a_all, d_qkv).astype(bf16))
 
-    def last_step(part, in_sum, cross_sum, out_pair, gain_grad_one, gain_grad_two):
+    def last_step(part, out_pair, gain_grad_one, gain_grad_two):
         part_zero, gain_grad_zero = jax.vjp(normalize, h0, gains[0])[1](scatter_rows(part))
         gain_grads = jnp.stack([gain_grad_zero, gain_grad_one, gain_grad_two])
-        moved = spread_columns(in_sum), spread_columns(cross_sum), with_core(out_pair)
-        return part_zero, sum_everywhere(gain_grads), *moved
-
-    part_zero, gain_total, in_grads, cross_grads, out_grads = chain_step(
-        last_step, matmul_right(d_qkv, w_qkv), g_in, g_cross, out_grads, gain_grad_one, gain_grad_two
+        return part_zero, sum_everywhere(gain_grads), with_core(out_pair)
+
+    part_zero, gain_total, out_grads = chain_step(
+        last_step, matmul_right(d_qkv, w_qkv), out_grads, gain_grad_one, gain_grad_two
     )
     grad_tokens = (dh1 + part_zero).astype(bf16)
 
+    by_tile = jnp.swapaxes(after(g_qkv, out_grads).reshape(2, rows, 3, block), 1, 2)
+    sent = jnp.broadcast_to(by_tile[:, None], (2, 4, 3, rows, block)).reshape(8, 3, rows, block)
+    late_grads = lax.all_to_all(sent, PLANE, 0, 0, tiled=True).reshape(8 * 3, rows, block)
     back_swap = [(target, source) for source, target in pair_swap]
-    other_half = lax.ppermute(after(g_outer, cross_grads), ALL_AXES, back_swap)
+    other_half = lax.ppermute(after(g_outer, out_grads), ALL_AXES, back_swap)
     outer_grad = jnp.where(
         odd == 0,
         jnp.concatenate([g_outer, other_half], axis=0),
         jnp.concatenate([other_half, g_outer], axis=0),
     )
-    by_tile = jnp.swapaxes(after(g_qkv, cross_grads).reshape(2, rows, 3, block), 1, 2)
-    sent = jnp.broadcast_to(by_tile[:, None], (2, 4, 3, rows, block)).reshape(8, 3, rows, block)
-    late_grads = lax.all_to_all(sent, PLANE, 0, 0, tiled=True).reshape(8 * 3, rows, block)
+    outer_pair = from_y(outer_grad, lambda zz, place, _: place % 4 in (zz, (zz + 2) % 4))
+    outer_grads = with_core(outer_pair)
+
     place = np.arange(8)
     source_x, source_f = (place % 2)[None, :], ((place // 2)[None, :] - my_shift[:, None]) % 4
-    other = source_f ^ f
-    source = (other % 2) * 4 + (other // 2) * 2 + (source_x ^ x)
-    column_of = np.array([0, 1, 2, 0, 0, 1, 3, 2, 4, 0, 0, 0, 0, 0, 0, 0, 0, 0], np.int32)
-    my_column = jnp.sum(jnp.where(my_tile[:, None] == np.arange(n_tiles), column_of, 0), axis=1)
-    in_layer = (my_tile >= 10)[:, None]
-    column_place = source * 8 + jnp.where(in_layer, (place // 2)[None, :], my_column[:, None])
+    slot = np.arange(cap, dtype=np.int32)
+    column_place = (source_x * 4 + source_f) * cap + slot[:, None]
     other_row = ((z - my_shift) % 4) ^ f
     row_source = (other_row % 2) * 2 + other_row // 2
     late = (my_used == 1) & ((my_tile < 4) | (my_tile == 9))
-    early_mode = jnp.where(my_row == 1, 4, jnp.where(my_tile >= 10, 2, 3))
-    early_mode = jnp.where(my_used == 0, 1, jnp.where(late, 0, early_mode))
+    early_mode = jnp.where(my_used == 0, 1, jnp.where(late, 0, jnp.where(my_row == 1, 3, 2)))
     states = (master, moment_one, moment_two)
-    slot = np.arange(cap, dtype=np.int32)
     early = None
     for first in (0, half_cap):
         chosen = slice(first, first + half_cap)
         early = adam_tiles(
             *states,
-            [in_grads, cross_grads],
+            [early_grads],
             [out_grads],
             slot[chosen],
             after(early_mode, outer_grad, sent)[chosen] if first else early_mode[chosen],
@@ -577,8 +609,6 @@
             early,
         )
 
-    outer_grads = with_core(from_y(outer_grad, lambda zz, place, _: place % 4 in (zz, (zz + 2) % 4)))
-
     n_late = 5
     order = jnp.sum(jnp.where(slot[None, :] < slot[:, None], late.astype(jnp.int32)[None, :], 0), axis=1)
     count_late = jnp.sum(late.astype(jnp.int32))
@@ -593,14 +623,14 @@
     tile = at_step(my_tile)
     some = count_late > 0
     visit = jnp.where(some, at_step(slot), 0)
-    first_mode = jnp.where(early_mode[0] == 4, 5, early_mode[0])
-    late_mode = jnp.where(at_step(my_row) == 1, 6, 4)
+    first_mode = jnp.where(early_mode[0] == 3, 4, early_mode[0])
+    late_mode = jnp.where(at_step(my_row) == 1, 5, 3)
     mode = jnp.where(hold == 1, 0, jnp.where(some, late_mode, first_mode))
     late_place = ((place % 2)[None, :] * 4 + (place // 2)[None, :]) * 3 + tile[:, None]
-    late_place = jnp.where(some, late_place * 8, column_place[:1])
+    late_place = jnp.where(some, late_place, column_place[:1])
     new_w, new_m, new_v = adam_tiles(
         *states,
-        [in_grads, cross_grads, late_grads],
+        [early_grads, late_grads],
         [out_grads, outer_grads],
         visit,
         mode,

time: 1090 us -> 1070 us (0.982)
  waiting for transfers between devices: 415 us -> 370 us
  local copies, waits for them, and re-layouts: 161 us -> 191 us
  Pallas kernels: 92.3 us -> 108 us
    all_to_all x2 -> x3, waiting for transfers between devices: 42.5 us -> 13.9 us  [the longest x2 13.9 us: plane_body(): lax.all_to_all(sent, PLANE, 0, 0, tiled=True)]
    ppermute x2, waiting for transfers between devices: 24.3 us -> 0.01 us  [take_rows(): from_y = lax.ppermute(across, ALL_AXES, flip_pairs(2, keep_pair))]
    ppermute x81 -> x75, waiting for transfers between devices: 299 us -> 319 us  [swap(): return lax.ppermute(value, axis, [(0, 1), (1, 0)])]
    pallas_call x0 -> x1, Pallas kernels: none -> 17 us  [pack_gradients(): pl.pallas_call(kernel, out_shape=jax.ShapeDtypeStruct((8, slots, rows, wi...]
    ppermute x1, waiting for transfers between devices: 17.4 us -> 4.31 us  [plane_body(): from_pair = lax.ppermute(to_pair, ALL_AXES, pair_swap)]
    unnamed x163 -> x184, local copies, waits for them, and re-layouts: 37.3 us -> 48.7 us
    ppermute x81 -> x75, starting transfers between devices: 70.4 us -> 67.8 us  [swap(): return lax.ppermute(value, axis, [(0, 1), (1, 0)])]
    cond x34 -> x29, local copies, waits for them, and re-layouts: 22.5 us -> 22 us
  transfers between devices with their start and end apart: 102 -> 96, of which waited for: 59 -> 55; matrix products, arithmetic and copies ran while one was open for 36% -> 37% of each run, Pallas kernels for 5% -> 7%
where the time goes in v9:
time: 1070 us; the launch traced here: 1060 us
  waiting for transfers between devices  370 us (35%)
  local copies, waits for them, and re-layouts  191 us (18%)
  matrix products  154 us (14%)
  Pallas kernels  108 us (10%)
  starting transfers between devices  104 us (10%)
  other arithmetic  86.6 us (8%)
  between operations  42.9 us (4%)
    ppermute x75, waiting for transfers between devices, swap(): return lax.ppermute(value, axis, [(0, 1), (1, 0)])  319 us
    pallas_call x3, Pallas kernels, adam_tiles(): pl.pallas_call(kernel, out_shape=(shape, shape, shape), grid_spec=pltpu.P...  73.9 us
    ppermute x75, starting transfers between devices, swap(): return lax.ppermute(value, axis, [(0, 1), (1, 0)])  67.8 us
    dot_general x8, matrix products, matmul(): return jnp.dot(left, right, preferred_element_type=f32)  50.3 us
    unnamed x184, local copies, waits for them, and re-layouts  48.7 us
    dot_general x8, matrix products, matmul_left(): lax.dot_general(left, right, (((0,), (0,)), ((), ())), preferred_element_...  48.1 us
    dot_general x6, matrix products, matmul_right(): lax.dot_general(left, right, (((1,), (1,)), ((), ())), preferred_element_...  34.5 us
    cond x29, local copies, waits for them, and re-layouts  22 us
  transfers between devices with their start and end apart: 96, of which 55 were waited for; matrix products, arithmetic and copies ran while one was open for 37% of the time, Pallas kernels for 7%

profile of v9, /device:TPU:0, one launch (start us, length us, event | category | flops | bytes accessed | tf_op | source)
XLA Modules:
  0.0 1057.7 jit_solution(2391645327531788430)
XLA Ops:
  228.2 69.7 %conditional.10 = (f32[128,2048]{1,0:T(8,128)S(1)}) conditional(s32[]{:T(128)} %bitcast.69, () %tuple.101, f32[1024,2048]{1,0:T(8,128)} %fusion.119), branch_computations={%region_10.11_spmd, %region_11.12_spmd} | conditional | flops 2883584 | bytes 65536208 | solution.py:417
  242.6 46.8 %collective-permute-done.22 = bf16[2,128,1024]{2,1,0:T(8,128)(2,1)S(1)} collective-permute-done((bf16[2,128,1024]{2,1,0:T(8,128)(2,1)S(1)}, bf16[2,128,1024]{2,1,0:T(8,128)(2,1)S(1)}, u32[]{:S(2)}, u32[]{:S(2)}) %collective-permute-start.22) | collective-permute-done | bytes 524320 | tf_op jit(solution)/shard_map/cond/branch_1_fun/ppermute | solution.py:244
  312.2 12.8 %collective-permute-done.75 = bf16[128,4096]{1,0:T(8,128)(2,1)S(1)} collective-permute-done((bf16[128,4096]{1,0:T(8,128)(2,1)S(1)}, bf16[128,4096]{1,0:T(8,128)(2,1)S(1)}, u32[]{:S(2)}, u32[]{:S(2)}) %collective-permute-start.75) | collective-permute-done | bytes 1048608 | tf_op jit(solution)/shard_map/ppermute | solution.py:244
  335.7 30.3 %conditional.11 = (bf16[1024,2048]{1,0:T(8,128)(2,1)}) conditional(s32[]{:T(128)} %bitcast.69, () %tuple.117, bf16[128,2048]{1,0:T(8,128)(2,1)S(1)} %get-tuple-element.237), branch_computations={%region_13.14_spmd, %region_14.15_spmd} | conditional | bytes 26214608 | solution.py:417
  337.8 12.2 %collective-permute-done = bf16[128,2048]{1,0:T(8,128)(2,1)S(1)} collective-permute-done((bf16[128,2048]{1,0:T(8,128)(2,1)S(1)}, bf16[128,2048]{1,0:T(8,128)(2,1)S(1)}, u32[]{:S(2)}, u32[]{:S(2)}) %collective-permute-start) | collective-permute-done | bytes 524320 | tf_op jit(solution)/shard_map/cond/branch_1_fun/ppermute | solution.py:244
  412.3 35.2 %conditional.12 = (f32[128,2048]{1,0:T(8,128)S(1)}) conditional(s32[]{:T(128)} %bitcast.69, () %tuple.112, f32[1024,2048]{1,0:T(8,128)} %fusion.115), branch_computations={%region_17.18_spmd, %region_18.19_spmd} | conditional | flops 2883584 | bytes 65536208 | solution.py:417
  426.2 12.2 %collective-permute-done.27 = bf16[2,128,1024]{2,1,0:T(8,128)(2,1)S(1)} collective-permute-done((bf16[2,128,1024]{2,1,0:T(8,128)(2,1)S(1)}, bf16[2,128,1024]{2,1,0:T(8,128)(2,1)S(1)}, u32[]{:S(2)}, u32[]{:S(2)}) %collective-permute-start.27) | collective-permute-done | bytes 524320 | tf_op jit(solution)/shard_map/cond/branch_1_fun/ppermute | solution.py:244
  448.9 26.4 %conditional.13 = (bf16[1024,2048]{1,0:T(8,128)(2,1)}) conditional(s32[]{:T(128)} %bitcast.69, () %tuple.119, bf16[128,2048]{1,0:T(8,128)(2,1)S(1)} %get-tuple-element.231), branch_computations={%region_20.21_spmd, %region_21.22_spmd} | conditional | bytes 26214608 | solution.py:417
  451.6 9.6 collective-permute-done.5
  475.3 9.9 all-gather.11.cloned.1.call-done
  549.6 53.3 %conditional.14 = (f32[128,2048]{1,0:T(8,128)S(1)}, f32[128,2048]{1,0:T(8,128)S(1)}) conditional(s32[]{:T(128)} %bitcast.69, () %tuple.118, (f32[1024,2048]{1,0:T(8,128)S(1)}, f32[1024,2048]{1,0:T(8,128)}) %tuple.125), branch_computations={%region_22.23_spmd, %region_23.24_spmd} | conditional | flops 5767168 | bytes 131072416 | solution.py:417
  605.9 27.5 %conditional.15 = (bf16[1024,2048]{1,0:T(8,128)(2,1)}) conditional(s32[]{:T(128)} %bitcast.69, () %tuple.128, bf16[128,2048]{1,0:T(8,128)(2,1)} %get-tuple-element.149), branch_computations={%region_25.26_spmd, %region_26.27_spmd} | conditional | bytes 26214608 | solution.py:417
  633.4 29.6 %conditional.16 = (bf16[1024,256]{0,1:T(8,128)(2,1)}, bf16[2048,256]{0,1:T(8,128)(2,1)}, bf16[2048,256]{0,1:T(8,128)(2,1)}, bf16[2,256,2048]{2,1,0:T(8,128)(2,1)}) conditional(s32[]{:T(128)} %bitcast.69, () %tuple.127, (bf16[1024,2048]{1,0:T(8,128)(2,1)}, bf16[256,2048]{1,0:T(8,128)(2,1)}, bf16[8,256,2,128]{3,2,1,0:T(2,128)(2,1)}, ...), branch_computations={%region_28.29_spmd, %region_29.31_spmd} | conditional | flops 1616640000 | bytes 62406868 | solution.py:417
  697.3 35.9 %conditional.17 = (f32[128,2048]{1,0:T(8,128)S(1)}) conditional(s32[]{:T(128)} %bitcast.69, () %tuple.126, f32[1024,2048]{1,0:T(8,128)} %fusion.110), branch_computations={%region_31.32_spmd, %region_32.33_spmd} | conditional | flops 2883584 | bytes 65536208 | solution.py:417
  712.2 11.4 %collective-permute-done.42 = bf16[2,128,1024]{2,1,0:T(8,128)(2,1)S(1)} collective-permute-done((bf16[2,128,1024]{2,1,0:T(8,128)(2,1)S(1)}, bf16[2,128,1024]{2,1,0:T(8,128)(2,1)S(1)}, u32[]{:S(2)}, u32[]{:S(2)}) %collective-permute-start.42) | collective-permute-done | bytes 524320 | tf_op jit(solution)/shard_map/cond/branch_1_fun/ppermute | solution.py:244
  736.2 26.7 %conditional.18 = (bf16[1024,2048]{1,0:T(8,128)(2,1)}) conditional(s32[]{:T(128)} %bitcast.69, () %tuple.132, bf16[128,2048]{1,0:T(8,128)(2,1)} %get-tuple-element.153), branch_computations={%region_35.36_spmd, %region_36.37_spmd} | conditional | bytes 26214608 | solution.py:417
  779.6 17.0 %pack_gradients.1 = bf16[8,6,256,256]{3,2,1,0:T(8,128)(2,1)} custom-call(s32[48]{0:T(128)S(1)} %tile.20.which_ref, s32[48]{0:T(128)S(1)} %tile.22.column_ref, bf16[512,1280]{1,0:T(8,128)(2,1)S(1)} %copy-done.6, bf16[512,1024]{1,0:T(8,128)(2,1)S(1)} %copy-done.7), custom_call_target="tpu_custom_call" | custom-call | tf_op jit(solution)/shard_map/pack_gradients/pallas_call | solution.py:153
  831.1 104.5 %conditional.19 = (f32[128,2048]{1,0:T(8,128)}, f32[3,2048]{1,0:T(4,128)S(1)}, bf16[4,256,2048]{2,1,0:T(8,128)(2,1)}) conditional(s32[]{:T(128)} %bitcast.69, () %tuple.131, (f32[1024,2048]{1,0:T(8,128)S(1)}, f32[3,2048]{1,0:T(4,128)S(1)}, f32[128,2048]{1,0:T(8,128)S(1)}, f32[128,2048]{1,0:T(8,128)S(1)}, f32[128,2048]{1,0:T(8,128)S(1)}, ...), branch_computations={%region_43.44_spmd, %region_44.48_spmd} | conditional | flops 9767680 | bytes 91698648 | solution.py:417
  832.9 9.7 collective-permute-done.46
  847.6 59.1 %collective-permute-done.47 = bf16[2,128,1024]{2,1,0:T(8,128)(2,1)S(1)} collective-permute-done((bf16[2,128,1024]{2,1,0:T(8,128)(2,1)S(1)}, bf16[2,128,1024]{2,1,0:T(8,128)(2,1)S(1)}, u32[]{:S(2)}, u32[]{:S(2)}) %collective-permute-start.47) | collective-permute-done | bytes 524320 | tf_op jit(solution)/shard_map/cond/branch_1_fun/ppermute | solution.py:244
  937.0 10.0 collective-permute-done.80
  973.4 23.3 %adam_tiles.3 = (f32[6,256,2048]{2,1,0:T(8,128)}, f32[6,256,2048]{2,1,0:T(8,128)}, f32[6,256,2048]{2,1,0:T(8,128)}) custom-call(s32[3]{0:T(128)S(1)} %call_exported.2.visit_ref, s32[3]{0:T(128)S(1)} %bitcast.392, s32[24]{0:T(128)S(1)} %reshape.574.cp_ref, s32[3]{0:T(128)S(1)} %get-tuple-element.356.rp_ref, s32[3]{0:T(128)S(1)} %call_exported.3.hold_ref, ...), custom_call_target="tpu_custom_call" | custom-call | flops 47185920 | bytes 40894464 | tf_op jit(solution)/shard_map/adam_tiles/pallas_call | solution.py:214
  996.7 24.2 %adam_tiles.4 = (f32[6,256,2048]{2,1,0:T(8,128)}, f32[6,256,2048]{2,1,0:T(8,128)}, f32[6,256,2048]{2,1,0:T(8,128)}) custom-call(s32[3]{0:T(128)S(1)} %copy-done.8, s32[3]{0:T(128)S(1)} %slice.567.mode_ref, s32[24]{0:T(128)S(1)} %reshape.573.cp_ref, s32[3]{0:T(128)S(1)} %get-tuple-element.357.rp_ref, ...), custom_call_target="tpu_custom_call", output_to_operand_aliasing={{0}: (10, {}), {1}: (11, {}), {2}: (12, {})} | custom-call | flops 47185920 | bytes 40894464 | tf_op jit(solution)/shard_map/adam_tiles/pallas_call | solution.py:214
  1024.5 26.5 %adam_tiles.5 = (f32[6,256,2048]{2,1,0:T(8,128)}, f32[6,256,2048]{2,1,0:T(8,128)}, f32[6,256,2048]{2,1,0:T(8,128)}) custom-call(s32[5]{0:T(128)S(1)} %get-tuple-element.386.visit_ref, s32[5]{0:T(128)S(1)} %get-tuple-element.385.mode_ref, s32[40]{0:T(128)S(1)} %select_n.476.cp_ref, ...), custom_call_target="tpu_custom_call", output_to_operand_aliasing={{0}: (12, {}), {1}: (13, {}), {2}: (14, {})} | custom-call | flops 78643200 | bytes 68157440 | tf_op jit(solution)/shard_map/adam_tiles/pallas_call | solution.py:214
  (701 shorter events, 728.1 us)
Async XLA Ops:
  24.8 42.2 %all-to-all-start = ((bf16[8,3,256,256]{3,2,1,0:T(8,128)(2,1)}), bf16[8,3,256,256]{3,2,1,0:T(8,128)(2,1)S(1)}, u32[]{:S(2)}, u32[]{:S(2)}) async-start(bf16[8,3,256,256]{3,2,1,0:T(8,128)(2,1)} %copy-done.1), calls=%async_computation | async-start | bytes 6291456 | tf_op jit(solution)/shard_map/all_to_all | solution.py:356
  30.1 135.6 %all-gather.5.cloned.1.call-start = ((), (), s32[]{:S(2)}) async-start(), calls=%async_computation.9 | async-start | bytes 3932160 | tf_op jit(solution)/shard_map/all_gather | solution.py:372
  72.8 149.1 %all-gather.7.cloned.1.call-start = ((), (), s32[]{:S(2)}) async-start(), calls=%async_computation.10 | async-start | bytes 2621440 | tf_op jit(solution)/shard_map/all_gather | solution.py:407
  156.7 41.6 %all-to-all-start.1 = ((bf16[8,3,256,256]{3,2,1,0:T(8,128)(2,1)}), bf16[8,3,256,256]{3,2,1,0:T(8,128)(2,1)}, u32[]{:S(2)}, u32[]{:S(2)}) async-start(bf16[8,3,256,256]{3,2,1,0:T(8,128)(2,1)} %copy-done), calls=%async_computation.1 | async-start | bytes 6291456 | tf_op jit(solution)/shard_map/all_to_all | solution.py:379
  161.2 206.5 %all-gather.9.cloned.1.call-start = ((), (), s32[]{:S(2)}) async-start(), calls=%async_computation.11 | async-start | bytes 6553600 | tf_op jit(solution)/shard_map/all_gather | solution.py:372
  165.2 46.8 %collective-permute-start.78 = (bf16[2,256,2048]{2,1,0:T(8,128)(2,1)}, bf16[2,256,2048]{2,1,0:T(8,128)(2,1)}, u32[]{:S(2)}, u32[]{:S(2)}) collective-permute-start(bf16[2,256,2048]{2,1,0:T(8,128)(2,1)} %pad_maximum_fusion.12), channel_id=1, source_target_pairs={{0,1},{1,0},{2,3},{3,2},{4,5},{5,4},{6,7},{7,6},{8,9},{9,8},{10,11... | collective-permute-start | bytes 6291464 | tf_op jit(solution)/shard_map/ppermute | solution.py:244
  202.3 282.9 %all-gather.11.cloned.1.call-start = ((), (), s32[]{:S(2)}) async-start(), calls=%async_computation.12 | async-start | bytes 10485760 | tf_op jit(solution)/shard_map/all_gather | solution.py:372
  208.1 90.0 %collective-permute-start.74 = (bf16[256,4096]{1,0:T(8,128)(2,1)}, bf16[256,4096]{1,0:T(8,128)(2,1)}, u32[]{:S(2)}, u32[]{:S(2)}) collective-permute-start(bf16[256,4096]{1,0:T(8,128)(2,1)} %bitcast.98), channel_id=1, source_target_pairs={{0,4},{4,0},{1,5},{5,1},{2,6},{6,2},{3,7},{7,3},{8,12},{12,8},{9,1... | collective-permute-start | bytes 6291464 | tf_op jit(solution)/shard_map/ppermute | solution.py:244
  209.4 92.0 %collective-permute-start.73 = (bf16[256,4096]{1,0:T(8,128)(2,1)}, bf16[256,4096]{1,0:T(8,128)(2,1)}, u32[]{:S(2)}, u32[]{:S(2)}) collective-permute-start(bf16[256,4096]{1,0:T(8,128)(2,1)} %bitcast.98), channel_id=1, source_target_pairs={{0,2},{2,0},{1,3},{3,1},{4,6},{6,4},{5,7},{7,5},{8,10},{10,8},{9,1... | collective-permute-start | bytes 6291464 | tf_op jit(solution)/shard_map/ppermute | solution.py:244
  214.8 116.0 %collective-permute-start.79 = (bf16[256,2048]{1,0:T(8,128)(2,1)}, bf16[256,2048]{1,0:T(8,128)(2,1)}, u32[]{:S(2)}, u32[]{:S(2)}) collective-permute-start(bf16[256,2048]{1,0:T(8,128)(2,1)} %fusion.97), channel_id=1, source_target_pairs={{0,2},{1,3},{2,0},{3,1},{4,6},{5,7},{6,4},{7,5},{8,10},{9,11},{10,... | collective-permute-start | bytes 3145736 | tf_op jit(solution)/shard_map/ppermute | solution.py:387
  240.3 49.1 %collective-permute-start.22 = (bf16[2,128,1024]{2,1,0:T(8,128)(2,1)S(1)}, bf16[2,128,1024]{2,1,0:T(8,128)(2,1)S(1)}, u32[]{:S(2)}, u32[]{:S(2)}) collective-permute-start(bf16[2,128,1024]{2,1,0:T(8,128)(2,1)S(1)} %slice_bitcast_fusion.5), channel_id=1, source_target_pairs={{0,2},{2,0},{1,3},{3,1},{4,6},{6,4},{5,7},{7,5},{8,10},{10,8},{9,1... | collective-permute-start | bytes 1572872 | tf_op jit(solution)/shard_map/cond/branch_1_fun/ppermute | solution.py:244
  241.1 50.0 %collective-permute-start.24 = (bf16[2,128,1024]{2,1,0:T(8,128)(2,1)S(1)}, bf16[2,128,1024]{2,1,0:T(8,128)(2,1)S(1)}, u32[]{:S(2)}, u32[]{:S(2)}) collective-permute-start(bf16[2,128,1024]{2,1,0:T(8,128)(2,1)S(1)} %slice_bitcast_fusion.3), channel_id=1, source_target_pairs={{0,4},{4,0},{1,5},{5,1},{2,6},{6,2},{3,7},{7,3},{8,12},{12,8},{9,1... | collective-permute-start | bytes 1572872 | tf_op jit(solution)/shard_map/cond/branch_1_fun/ppermute | solution.py:244
  328.2 44.5 %collective-permute-start.77 = (bf16[1024,4096]{1,0:T(8,128)(2,1)}, bf16[1024,4096]{1,0:T(8,128)(2,1)}, u32[]{:S(2)}, u32[]{:S(2)}) collective-permute-start(bf16[1024,4096]{1,0:T(8,128)(2,1)} %get-tuple-element.323), channel_id=1, source_target_pairs={{0,1},{1,0},{2,3},{3,2},{4,5},{5,4},{6,7},{7,6},{8,9},{9,8},{10,11... | collective-permute-start | bytes 25165832 | tf_op jit(solution)/shard_map/ppermute | solution.py:244
  334.2 299.2 %reduce-scatter.6.cloned.1.call-start = ((), (), s32[]{:S(2)}) async-start(), calls=%async_computation.13 | async-start | bytes 5242880 | tf_op jit(solution)/shard_map/reduce_scatter | solution.py:487
  501.6 234.7 %reduce-scatter.8.cloned.1.call-start = ((), (), s32[]{:S(2)}) async-start(), calls=%async_computation.14 | async-start | bytes 5242880 | tf_op jit(solution)/shard_map/reduce_scatter | solution.py:487
  535.9 241.7 %reduce-scatter.10.cloned.1.call-start = ((), (), s32[]{:S(2)}) async-start(), calls=%async_computation.15 | async-start | bytes 6553600 | tf_op jit(solution)/shard_map/reduce_scatter | solution.py:487
  685.8 249.9 %reduce-scatter.14.cloned.1.call-start = ((), (), s32[]{:S(2)}) async-start(), calls=%async_computation.17 | async-start | bytes 2621440 | tf_op jit(solution)/shard_map/reduce_scatter | solution.py:487
  777.6 178.3 %reduce-scatter.12.cloned.1.call-start = ((), (), s32[]{:S(2)}) async-start(), calls=%async_computation.16 | async-start | bytes 3932160 | tf_op jit(solution)/shard_map/reduce_scatter | solution.py:487
  819.6 138.6 %all-to-all-start.2 = ((bf16[8,6,256,256]{3,2,1,0:T(8,128)(2,1)}), bf16[8,6,256,256]{3,2,1,0:T(8,128)(2,1)}, u32[]{:S(2)}, u32[]{:S(2)}) async-start(bf16[8,6,256,256]{3,2,1,0:T(8,128)(2,1)} %pack_gradients.1), calls=%async_computation.5 | async-start | bytes 12582912 | tf_op jit(solution)/shard_map/all_to_all | solution.py:559
  832.8 89.8 %collective-permute-start.56 = (bf16[2,256,2048]{2,1,0:T(8,128)(2,1)}, bf16[2,256,2048]{2,1,0:T(8,128)(2,1)S(1)}, u32[]{:S(2)}, u32[]{:S(2)}) collective-permute-start(bf16[2,256,2048]{2,1,0:T(8,128)(2,1)} %get-tuple-element.75), channel_id=1, source_target_pairs={{0,1},{1,0},{2,3},{3,2},{4,5},{5,4},{6,7},{7,6},{8,9},{9,8},{10,11... | collective-permute-start | bytes 6291464 | tf_op jit(solution)/shard_map/cond/branch_1_fun/ppermute | solution.py:244
  843.4 63.2 %collective-permute-start.47 = (bf16[2,128,1024]{2,1,0:T(8,128)(2,1)S(1)}, bf16[2,128,1024]{2,1,0:T(8,128)(2,1)S(1)}, u32[]{:S(2)}, u32[]{:S(2)}) collective-permute-start(bf16[2,128,1024]{2,1,0:T(8,128)(2,1)S(1)} %slice_bitcast_fusion.35), channel_id=1, source_target_pairs={{0,2},{2,0},{1,3},{3,1},{4,6},{6,4},{5,7},{7,5},{8,10},{10,8},{9,1... | collective-permute-start | bytes 1572872 | tf_op jit(solution)/shard_map/cond/branch_1_fun/ppermute | solution.py:244
  846.0 62.4 %collective-permute-start.49 = (bf16[2,128,1024]{2,1,0:T(8,128)(2,1)S(1)}, bf16[2,128,1024]{2,1,0:T(8,128)(2,1)S(1)}, u32[]{:S(2)}, u32[]{:S(2)}) collective-permute-start(bf16[2,128,1024]{2,1,0:T(8,128)(2,1)S(1)} %slice_bitcast_fusion.33), channel_id=1, source_target_pairs={{0,4},{4,0},{1,5},{5,1},{2,6},{6,2},{3,7},{7,3},{8,12},{12,8},{9,1... | collective-permute-start | bytes 1572872 | tf_op jit(solution)/shard_map/cond/branch_1_fun/ppermute | solution.py:244
  960.1 64.3 %all-to-all-start.3 = ((bf16[8,3,256,256]{3,2,1,0:T(8,128)(2,1)}), bf16[8,3,256,256]{3,2,1,0:T(8,128)(2,1)S(1)}, u32[]{:S(2)}, u32[]{:S(2)}) async-start(bf16[8,3,256,256]{3,2,1,0:T(8,128)(2,1)} %bitcast.401), calls=%async_computation.7 | async-start | bytes 6291456 | tf_op jit(solution)/shard_map/all_to_all | solution.py:577
  969.5 51.4 %collective-permute-start.82 = (bf16[2,256,2048]{2,1,0:T(8,128)(2,1)}, bf16[2,256,2048]{2,1,0:T(8,128)(2,1)}, u32[]{:S(2)}, u32[]{:S(2)}) collective-permute-start(bf16[2,256,2048]{2,1,0:T(8,128)(2,1)} %pad_maximum_fusion.14), channel_id=1, source_target_pairs={{0,1},{1,0},{2,3},{3,2},{4,5},{5,4},{6,7},{7,6},{8,9},{9,8},{10,11... | collective-permute-start | bytes 6291464 | tf_op jit(solution)/shard_map/ppermute | solution.py:244
  (161 other events, 3005.3 us)
Sparse Core Ops, SparseCore 0:
  72.9 63.7 all-gather.4
  148.9 47.5 all-gather.6
  202.4 99.3 all-gather.8
  334.3 150.8 all-gather.10
  501.7 74.9 reduce-scatter.5
  579.0 77.2 reduce-scatter.7
  685.9 91.6 reduce-scatter.9
  779.9 44.3 reduce-scatter.13
  827.3 59.5 reduce-scatter.11

commit v10 on v9

--- a/solution.py
+++ b/solution.py
@@ -132,34 +132,29 @@
 
 
 def pack_gradients(groups, which, column, rows, width, slots):
-    n_src = len(groups)
+    places = [(rank, k) for rank in range(8) for k in range(slots)]
 
     def kernel(which_ref, column_ref, *refs):
-        place = pl.program_id(0) * slots + pl.program_id(1)
-        out_ref = refs[n_src]
-        for number in range(n_src):
-
-            @pl.when(which_ref[place] == number)
-            def _():
-                out_ref[0, 0] = refs[number][...]
-
-    def spec(number):
-        def at(rank, k, which, column):
-            place = rank * slots + k
-            return (rank // 4, jnp.where(which[place] == number, column[place], 0))
-
-        return pl.BlockSpec((rows, width), at)
+        out_ref, sems = refs[len(groups)], refs[len(groups) + 1]
+        for place, (rank, k) in enumerate(places):
+            for number in range(len(groups)):
+
+                @pl.when(which_ref[place] == number)
+                def _():
+                    start = pl.multiple_of(column_ref[place] * width, width)
+                    source = refs[number].at[pl.ds(rank // 4 * rows, rows), pl.ds(start, width)]
+                    pltpu.make_async_copy(source, out_ref.at[rank, k], sems.at[place]).start()
+
+        for place, (rank, k) in enumerate(places):
+            source = refs[0].at[pl.ds(0, rows), pl.ds(0, width)]
+            pltpu.make_async_copy(source, out_ref.at[rank, k], sems.at[place]).wait()
 
     return pl.pallas_call(
         kernel,
         out_shape=jax.ShapeDtypeStruct((8, slots, rows, width), bf16),
-        grid_spec=pltpu.PrefetchScalarGridSpec(
-            num_scalar_prefetch=2,
-            grid=(8, slots),
-            in_specs=[spec(number) for number in range(n_src)],
-            out_specs=pl.BlockSpec((1, 1, rows, width), lambda rank, k, which, column: (rank, k, 0, 0)),
-        ),
-        compiler_params=pltpu.CompilerParams(vmem_limit_bytes=VMEM_LIMIT),
+        in_specs=[pl.BlockSpec(memory_space=pltpu.SMEM)] * 2 + [pl.BlockSpec(memory_space=pl.ANY)] * len(groups),
+        out_specs=pl.BlockSpec(memory_space=pl.ANY),
+        scratch_shapes=[pltpu.SemaphoreType.DMA((len(places),))],
         name="pack_gradients",
     )(which, column, *groups)
 
@@ -373,10 +368,6 @@
 
     local = columns_here(0, 3, 1)
     w_qkv = gather_z(local)
-    a_all = gather_rows(after(a_in, local))
-    d_ff = gather_rows(after(grad_out.astype(bf16), local))
-    sent = pack_second(after(master, a_all, d_ff))
-    received.append(lax.all_to_all(sent, PLANE, 0, 0, tiled=True).reshape(8 * half_cap, rows, block))
 
     def take_rows(kind, blocks, keep_pair):
         here, there = row_owners[2 * kind], row_owners[2 * kind + 1]
@@ -391,10 +382,14 @@
         return target % 4 in (zz, (zz + 2) % 4)
 
     outer = take_rows(0, [after(value, local) for value in outer_blocks], needs_outer)
-    out_rows = take_rows(1, [after(value, local) for value in out_blocks], None)
+    a_all = gather_rows(after(a_in, outer))
+    d_ff = gather_rows(after(grad_out.astype(bf16), outer))
+    out_rows = take_rows(1, [after(value, outer) for value in out_blocks], None)
+    sent = pack_second(after(master, a_all, d_ff, out_rows))
+    received.append(lax.all_to_all(sent, PLANE, 0, 0, tiled=True).reshape(8 * half_cap, rows, block))
     half_rows = rows // 2
     odd = z % 2
-    to_pair = lax.dynamic_slice_in_dim(after(outer, sent), (1 - odd) * half_rows, half_rows, 0)
+    to_pair = lax.dynamic_slice_in_dim(outer, (1 - odd) * half_rows, half_rows, 0)
     own_half = lax.dynamic_slice_in_dim(outer, odd * half_rows, half_rows, 0)
     pair_swap = [
         (zz * 8 + place, (zz ^ 1) * 8 + place)
@@ -446,28 +441,29 @@
     received[1] = after(received[1], mixed)
     local_cross, local_in = columns_here(3, 5, 2), columns_here(8, 4, 2)
     w_cross = gather_z(local_cross)
-    middle = width // 2
-    halves = jnp.concatenate([out_rows[:, :middle], out_rows[:, middle:]], axis=0)
-    w_layer = gather_z(jnp.concatenate([local_in, halves], axis=1))
-    w_in = w_layer[:, : 4 * block]
-    w_out = jnp.swapaxes(w_layer[:, 4 * block :].reshape(4, 2, rows, middle), 1, 2).reshape(4 * rows, width)
+    w_in = gather_z(local_in)
+    w_out = gather_z(after(out_rows, local_cross, local_in))
 
     slots, ctx_len, ctx_width = context.shape
     ctx = after(context.reshape(slots * ctx_len, ctx_width), local_cross, local_in)
     ctx_x, ctx_y = swap(ctx, "x"), swap(ctx, "y")
     h1 = h0 + chain_step(scatter_rows, matmul(attended, w_self_out))
-    half = slots * ctx_len // 2
-    far_low = swap(after(ctx_y, h1)[:half], "x")
-    far_high = swap(after(ctx_x, h1)[half:], "y")
-    b_all = chain_step(gather_rows, normalize(h1, gains[1]).astype(bf16))
-    ctx_four = jnp.concatenate([ctx, ctx_y, ctx_x, far_low, far_high], axis=0)
-    ctx_all = jnp.concatenate([ctx_four, swap(ctx_four, "c")], axis=0)
-
+
+    def with_context(one, over_x, over_y):
+        half = over_x.shape[0] // 2
+        return gather_rows(one), swap(over_y[:half], "x"), swap(over_x[half:], "y")
+
+    b_all, far_low, far_high = chain_step(with_context, normalize(h1, gains[1]).astype(bf16), ctx_x, ctx_y)
+
+    def context_step(weights, *pieces):
+        four = jnp.concatenate(pieces, axis=0)
+        every = jnp.concatenate([four, swap(four, "c")], axis=0)
+        low = matmul(every[:, :width], weights[:, block : 3 * block])
+        return every, (low + matmul(every[:, width:], weights[:, 3 * block :])).astype(bf16)
+
+    ctx_all, ctx_kv = chain_step(context_step, w_cross, ctx, ctx_y, ctx_x, far_low, far_high)
     w_cross_q = w_cross[:, :block]
-    w_low = w_cross[:, block : 3 * block]
-    w_high = w_cross[:, 3 * block :]
     ctx_low, ctx_high = ctx_all[:, :width], ctx_all[:, width:]
-    ctx_kv = (matmul(ctx_low, w_low) + matmul(ctx_high, w_high)).astype(bf16)
     cross_q = matmul(b_all, w_cross_q)
     cross_q = split(cross_q.astype(bf16))
     cross_k, cross_v = split(ctx_kv[:, :block]), split(ctx_kv[:, block:])
@@ -557,10 +553,14 @@
         [g_cross, g_in], jnp.tile(group_at.reshape(-1), 2), jnp.tile(column_at.reshape(-1), 2), rows, block, cap
     )
     early_grads = lax.all_to_all(sent, PLANE, 0, 0, tiled=True).reshape(8 * cap, rows, block)
-    d_mixed = matmul_right(after(d_self_out, t_outer, sent), w_self_out)
-    d_q, d_k, d_v = through(d_mixed, query, keys, probs, probs_low, values)
-    d_qkv = jnp.concatenate([d_q, d_k, d_v], axis=1)
-    g_qkv = sum_rows(matmul_left(a_all, d_qkv).astype(bf16))
+
+    def self_back(d_out):
+        d_mixed = matmul_right(d_out, w_self_out)
+        d_qkv = jnp.concatenate(through(d_mixed, query, keys, probs, probs_low, values), axis=1)
+        return d_qkv, matmul_left(a_all, d_qkv).astype(bf16)
+
+    d_qkv, t_qkv = chain_step(self_back, after(d_self_out, t_outer, sent))
+    g_qkv = sum_rows(t_qkv)
 
     def last_step(part, out_pair, gain_grad_one, gain_grad_two):
         part_zero, gain_grad_zero = jax.vjp(normalize, h0, gains[0])[1](scatter_rows(part))

time: 1070 us -> 1290 us (1.21)
  Pallas kernels: 108 us -> 277 us
  waiting for transfers between devices: 370 us -> 417 us
  local copies, waits for them, and re-layouts: 191 us -> 176 us
  matrix products: 154 us -> 167 us
    pallas_call x1, Pallas kernels: 17 us -> 193 us  [pack_gradients(): pl.pallas_call(kernel, out_shape=jax.ShapeDtypeStruct((8, slots, rows, wi...]
    ppermute x75, waiting for transfers between devices: 319 us -> 361 us  [swap(): return lax.ppermute(value, axis, [(0, 1), (1, 0)])]
    unnamed x184 -> x145, local copies, waits for them, and re-layouts: 48.7 us -> 22.5 us
    cond x29 -> x44, local copies, waits for them, and re-layouts: 22 us -> 45.1 us
    ppermute x2, waiting for transfers between devices: 0.01 us -> 22.5 us  [take_rows(): from_y = lax.ppermute(across, ALL_AXES, flip_pairs(2, keep_pair))]
  transfers between devices with their start and end apart: 96 -> 97, of which waited for: 55 -> 59; matrix products, arithmetic and copies ran while one was open for 37% -> 32% of each run, Pallas kernels for 7% -> 20%
where the time goes in v10:
time: 1290 us; the launch traced here: 1270 us
  waiting for transfers between devices  417 us (32%)
  Pallas kernels  277 us (21%)
  local copies, waits for them, and re-layouts  176 us (14%)
  matrix products  167 us (13%)
  starting transfers between devices  98.4 us (8%)
  other arithmetic  89.2 us (7%)
  between operations  43.4 us (3%)
    ppermute x75, waiting for transfers between devices, swap(): return lax.ppermute(value, axis, [(0, 1), (1, 0)])  361 us
    pallas_call x1, Pallas kernels, pack_gradients(): pl.pallas_call(kernel, out_shape=jax.ShapeDtypeStruct((8, slots, rows, wi...  193 us
    pallas_call x3, Pallas kernels, adam_tiles(): pl.pallas_call(kernel, out_shape=(shape, shape, shape), grid_spec=pltpu.P...  68.6 us
    ppermute x75, starting transfers between devices, swap(): return lax.ppermute(value, axis, [(0, 1), (1, 0)])  62.4 us
    dot_general x8, matrix products, matmul_left(): lax.dot_general(left, right, (((0,), (0,)), ((), ())), preferred_element_...  53.9 us
    dot_general x8, matrix products, matmul(): return jnp.dot(left, right, preferred_element_type=f32)  52.5 us
    dot_general x6, matrix products, matmul_right(): lax.dot_general(left, right, (((1,), (1,)), ((), ())), preferred_element_...  40.3 us
    cond x41, local copies, waits for them, and re-layouts  34.4 us
  transfers between devices with their start and end apart: 97, of which 59 were waited for; matrix products, arithmetic and copies ran while one was open for 32% of the time, Pallas kernels for 20%

profile of v10, /device:TPU:0, one launch (start us, length us, event | category | flops | bytes accessed | tf_op | source)
XLA Modules:
  0.0 1270.7 jit_solution(3344632014028993067)
XLA Ops:
  87.0 13.1 %collective-permute-done.64 = bf16[256,2048]{1,0:T(8,128)(2,1)} collective-permute-done((bf16[256,2048]{1,0:T(8,128)(2,1)}, bf16[256,2048]{1,0:T(8,128)(2,1)}, u32[]{:S(2)}, u32[]{:S(2)}) %collective-permute-start.64) | collective-permute-done | bytes 1048608 | tf_op jit(solution)/shard_map/ppermute | solution.py:378
  184.6 34.6 %collective-permute-done.61 = s32[256]{0:T(256)S(1)} collective-permute-done((s32[256]{0:T(256)S(1)}, s32[256]{0:T(256)S(1)}, u32[]{:S(2)}, u32[]{:S(2)}) %collective-permute-start.61) | collective-permute-done | bytes 1056 | tf_op jit(solution)/shard_map/ppermute | solution.py:239
  262.3 58.2 %conditional.12 = (f32[128,2048]{1,0:T(8,128)S(1)}) conditional(s32[]{:T(128)} %bitcast.73, () %tuple.119, f32[1024,2048]{1,0:T(8,128)} %fusion.117), branch_computations={%region_10.11_spmd, %region_11.12_spmd} | conditional | flops 2883584 | bytes 65536208 | solution.py:412
  276.7 34.2 %collective-permute-done.27 = bf16[2,128,1024]{2,1,0:T(8,128)(2,1)S(1)} collective-permute-done((bf16[2,128,1024]{2,1,0:T(8,128)(2,1)S(1)}, bf16[2,128,1024]{2,1,0:T(8,128)(2,1)S(1)}, u32[]{:S(2)}, u32[]{:S(2)}) %collective-permute-start.27) | collective-permute-done | bytes 524320 | tf_op jit(solution)/shard_map/cond/branch_1_fun/ppermute | solution.py:239
  322.6 51.0 %conditional.13 = (bf16[1024,2048]{1,0:T(8,128)(2,1)}, bf16[128,4096]{1,0:T(8,128)(2,1)}, bf16[128,4096]{1,0:T(8,128)(2,1)}) conditional(s32[]{:T(128)} %bitcast.73, () %tuple.137, (bf16[128,2048]{1,0:T(8,128)(2,1)S(1)}, bf16[256,4096]{1,0:T(8,128)(2,1)}, bf16[256,4096]{1,0:T(8,128)(2,1)}) %tuple.138), branch_computations={%region_13.14_spmd, %region_14.15_spmd} | conditional | bytes 38797616 | solution.py:412
  350.1 20.5 %collective-permute-done.6 = bf16[128,4096]{1,0:T(8,128)(2,1)} collective-permute-done((bf16[128,4096]{1,0:T(8,128)(2,1)S(1)}, bf16[128,4096]{1,0:T(8,128)(2,1)}, u32[]{:S(2)}, u32[]{:S(2)}) %collective-permute-start.6) | collective-permute-done | bytes 1048608 | tf_op jit(solution)/shard_map/cond/branch_1_fun/ppermute | solution.py:239
  379.3 67.8 %conditional.14 = (bf16[2048,4096]{1,0:T(8,128)(2,1)}, bf16[2048,512]{1,0:T(8,128)(2,1)}, bf16[2048,256]{1,0:T(8,128)(2,1)}, bf16[2048,256]{1,0:T(8,128)(2,1)}, ...) conditional(s32[]{:T(128)} %bitcast.73, () %tuple.128, ...), branch_computations={%region_15.16_spmd, %region_16.17_spmd} | conditional | flops 8592031744 | bytes 119537768 | solution.py:412
  394.9 13.3 %collective-permute-done.22 = bf16[1024,4096]{1,0:T(8,128)(2,1)} collective-permute-done((bf16[1024,4096]{1,0:T(8,128)(2,1)S(1)}, bf16[1024,4096]{1,0:T(8,128)(2,1)}, u32[]{:S(2)}, u32[]{:S(2)}) %collective-permute-start.22) | collective-permute-done | bytes 8388640 | tf_op jit(solution)/shard_map/cond/branch_1_fun/ppermute | solution.py:239
  461.0 35.0 %conditional.15 = (f32[128,2048]{1,0:T(8,128)S(1)}) conditional(s32[]{:T(128)} %bitcast.73, () %tuple.127, f32[1024,2048]{1,0:T(8,128)} %fusion.113), branch_computations={%region_19.20_spmd, %region_20.21_spmd} | conditional | flops 2883584 | bytes 65536208 | solution.py:412
  475.8 11.4 collective-permute-done.32
  498.5 28.3 %conditional.16 = (bf16[1024,2048]{1,0:T(8,128)(2,1)}) conditional(s32[]{:T(128)} %bitcast.73, () %tuple.141, bf16[128,2048]{1,0:T(8,128)(2,1)S(1)} %get-tuple-element.320), branch_computations={%region_22.23_spmd, %region_23.24_spmd} | conditional | bytes 26214608 | solution.py:412
  580.5 51.8 %conditional.17 = (f32[128,2048]{1,0:T(8,128)S(1)}, f32[128,2048]{1,0:T(8,128)S(1)}) conditional(s32[]{:T(128)} %bitcast.73, () %tuple.140, (f32[1024,2048]{1,0:T(8,128)S(1)}, f32[1024,2048]{1,0:T(8,128)}) %tuple.144), branch_computations={%region_24.25_spmd, %region_25.26_spmd} | conditional | flops 5767168 | bytes 131072416 | solution.py:412
  635.3 28.3 %conditional.18 = (bf16[1024,2048]{1,0:T(8,128)(2,1)}) conditional(s32[]{:T(128)} %bitcast.73, () %tuple.147, bf16[128,2048]{1,0:T(8,128)(2,1)} %get-tuple-element.209), branch_computations={%region_27.28_spmd, %region_28.29_spmd} | conditional | bytes 26214608 | solution.py:412
  663.6 28.5 %conditional.19 = (bf16[1024,256]{0,1:T(8,128)(2,1)}, bf16[2048,256]{0,1:T(8,128)(2,1)}, bf16[2048,256]{0,1:T(8,128)(2,1)}, bf16[2,256,2048]{2,1,0:T(8,128)(2,1)}) conditional(s32[]{:T(128)} %bitcast.73, () %tuple.146, (bf16[1024,2048]{1,0:T(8,128)(2,1)}, bf16[256,2048]{1,0:T(8,128)(2,1)}, bf16[8,256,2,128]{3,2,1,0:T(2,128)(2,1)}, ...), branch_computations={%region_30.31_spmd, %region_31.33_spmd} | conditional | flops 1616640000 | bytes 66601200 | solution.py:412
  730.1 35.9 %conditional.20 = (f32[128,2048]{1,0:T(8,128)}) conditional(s32[]{:T(128)} %bitcast.73, () %tuple.145, f32[1024,2048]{1,0:T(8,128)} %fusion.108), branch_computations={%region_33.34_spmd, %region_34.35_spmd} | conditional | flops 2883584 | bytes 65536208 | solution.py:412
  744.5 11.9 collective-permute-done.47
  770.5 28.0 %conditional.21 = (bf16[1024,2048]{1,0:T(8,128)(2,1)}) conditional(s32[]{:T(128)} %bitcast.73, () %tuple.152, bf16[128,2048]{1,0:T(8,128)(2,1)S(1)} %get-tuple-element.214), branch_computations={%region_37.38_spmd, %region_38.39_spmd} | conditional | bytes 26214608 | solution.py:412
  814.6 192.9 %pack_gradients.1 = bf16[8,6,256,256]{3,2,1,0:T(8,128)(2,1)} custom-call(s32[48]{0:T(128)} %tile.20.which_ref, s32[48]{0:T(128)} %tile.22.column_ref, bf16[512,1280]{1,0:T(8,128)(2,1)} %reduce-scatter.10.cloned.1.call-done.refs_0_, bf16[512,1024]{1,0:T(8,128)(2,1)} %reduce-scatter.8.cloned.1.call-done.refs_1_), custom_call_target="tpu_custom_call" | custom-call | tf_op jit(solution)/shard_map/pack_gradients/pallas_call | solution.py:152
  1007.5 25.7 %conditional.22 = (bf16[1024,768]{0,1:T(8,128)(2,1)}, bf16[2048,768]{0,1:T(8,128)(2,1)}) conditional(s32[]{:T(128)} %bitcast.73, () %tuple.151, (bf16[1024,2048]{1,0:T(8,128)(2,1)}, bf16[256,2048]{1,0:T(8,128)(2,1)}, bf16[8,128,2,128]{3,2,1,0:T(2,128)(2,1)}, f32[8,2,128,128]{2,3,1,0:T(8,128)S(1)}, bf16[8,128,2,128]{3,2,1,0:T(2,128)(2,1)}, ...), branch_computations={%region_42.43_spmd, %region_43.45_spmd} | conditional | flops 4567857152 | bytes 37765192 | solution.py:412
  1049.9 103.9 %conditional.23 = (f32[128,2048]{1,0:T(8,128)}, f32[3,2048]{1,0:T(4,128)S(1)}, bf16[4,256,2048]{2,1,0:T(8,128)(2,1)}) conditional(s32[]{:T(128)} %bitcast.73, () %tuple.150, (f32[1024,2048]{1,0:T(8,128)S(1)}, f32[3,2048]{1,0:T(4,128)S(1)}, f32[128,2048]{1,0:T(8,128)S(1)}, f32[128,2048]{1,0:T(8,128)S(1)}, f32[128,2048]{1,0:T(8,128)S(1)}, ...), branch_computations={%region_47.48_spmd, %region_48.52_spmd} | conditional | flops 9767680 | bytes 91698648 | solution.py:412
  1066.3 58.5 %collective-permute-done.52 = bf16[2,128,1024]{2,1,0:T(8,128)(2,1)S(1)} collective-permute-done((bf16[2,128,1024]{2,1,0:T(8,128)(2,1)S(1)}, bf16[2,128,1024]{2,1,0:T(8,128)(2,1)S(1)}, u32[]{:S(2)}, u32[]{:S(2)}) %collective-permute-start.52) | collective-permute-done | bytes 524320 | tf_op jit(solution)/shard_map/cond/branch_1_fun/ppermute | solution.py:239
  1191.5 23.3 %adam_tiles.3 = (f32[6,256,2048]{2,1,0:T(8,128)}, f32[6,256,2048]{2,1,0:T(8,128)}, f32[6,256,2048]{2,1,0:T(8,128)}) custom-call(s32[3]{0:T(128)S(1)} %call_exported.2.visit_ref, s32[3]{0:T(128)S(1)} %bitcast.390, s32[24]{0:T(128)S(1)} %reshape.566.cp_ref, s32[3]{0:T(128)S(1)} %get-tuple-element.447.rp_ref, s32[3]{0:T(128)S(1)} %call_exported.3.hold_ref, ...), custom_call_target="tpu_custom_call" | custom-call | flops 47185920 | bytes 40894464 | tf_op jit(solution)/shard_map/adam_tiles/pallas_call | solution.py:209
  1214.8 23.5 %adam_tiles.4 = (f32[6,256,2048]{2,1,0:T(8,128)}, f32[6,256,2048]{2,1,0:T(8,128)}, f32[6,256,2048]{2,1,0:T(8,128)}) custom-call(s32[3]{0:T(128)S(1)} %copy-done.5, s32[3]{0:T(128)S(1)} %slice.557.mode_ref, s32[24]{0:T(128)S(1)} %reshape.565.cp_ref, s32[3]{0:T(128)S(1)} %get-tuple-element.448.rp_ref, ...), custom_call_target="tpu_custom_call", output_to_operand_aliasing={{0}: (10, {}), {1}: (11, {}), {2}: (12, {})} | custom-call | flops 47185920 | bytes 40894464 | tf_op jit(solution)/shard_map/adam_tiles/pallas_call | solution.py:209
  1241.9 21.8 %adam_tiles.5 = (f32[6,256,2048]{2,1,0:T(8,128)}, f32[6,256,2048]{2,1,0:T(8,128)}, f32[6,256,2048]{2,1,0:T(8,128)}) custom-call(s32[5]{0:T(128)S(1)} %get-tuple-element.475.visit_ref, s32[5]{0:T(128)S(1)} %get-tuple-element.474.mode_ref, s32[40]{0:T(128)S(1)} %select_n.476.cp_ref, ...), custom_call_target="tpu_custom_call", output_to_operand_aliasing={{0}: (12, {}), {1}: (13, {}), {2}: (14, {})} | custom-call | flops 78643200 | bytes 68157440 | tf_op jit(solution)/shard_map/adam_tiles/pallas_call | solution.py:209
  (675 shorter events, 766.1 us)
Async XLA Ops:
  24.7 42.2 %all-to-all-start = ((bf16[8,3,256,256]{3,2,1,0:T(8,128)(2,1)}), bf16[8,3,256,256]{3,2,1,0:T(8,128)(2,1)S(1)}, u32[]{:S(2)}, u32[]{:S(2)}) async-start(bf16[8,3,256,256]{3,2,1,0:T(8,128)(2,1)} %copy-done), calls=%async_computation | async-start | bytes 6291456 | tf_op jit(solution)/shard_map/all_to_all | solution.py:351
  30.0 190.8 %all-gather.6.cloned.1.call-start = ((), (), s32[]{:S(2)}) async-start(), calls=%async_computation.9 | async-start | bytes 3932160 | tf_op jit(solution)/shard_map/all_gather | solution.py:367
  86.9 168.6 %all-gather.8.cloned.1.call-start = ((), (), s32[]{:S(2)}) async-start(), calls=%async_computation.10 | async-start | bytes 2621440 | tf_op jit(solution)/shard_map/all_gather | solution.py:402
  146.5 36.1 %collective-permute-start.60 = (s32[128]{0:T(128)S(1)}, s32[128]{0:T(128)S(1)}, u32[]{:S(2)}, u32[]{:S(2)}) collective-permute-start(s32[128]{0:T(128)S(1)} %fusion.161), channel_id=1, source_target_pairs={{0,2},{2,0},{1,3},{3,1},{4,6},{6,4},{5,7},{7,5},{8,10},{10,8},{9,1... | collective-permute-start | bytes 1544 | tf_op jit(solution)/shard_map/ppermute | solution.py:239
  177.8 64.7 %all-to-all-start.1 = ((bf16[8,3,256,256]{3,2,1,0:T(8,128)(2,1)}), bf16[8,3,256,256]{3,2,1,0:T(8,128)(2,1)}, u32[]{:S(2)}, u32[]{:S(2)}) async-start(bf16[8,3,256,256]{3,2,1,0:T(8,128)(2,1)} %copy-done.1), calls=%async_computation.1 | async-start | bytes 6291456 | tf_op jit(solution)/shard_map/all_to_all | solution.py:389
  182.3 191.3 %all-gather.10.cloned.1.call-start = ((), (), s32[]{:S(2)}) async-start(), calls=%async_computation.11 | async-start | bytes 6553600 | tf_op jit(solution)/shard_map/all_gather | solution.py:367
  182.7 36.6 %collective-permute-start.61 = (s32[256]{0:T(256)S(1)}, s32[256]{0:T(256)S(1)}, u32[]{:S(2)}, u32[]{:S(2)}) collective-permute-start(s32[256]{0:T(256)S(1)} %pad_add_fusion.2), channel_id=1, source_target_pairs={{0,4},{4,0},{1,5},{5,1},{2,6},{6,2},{3,7},{7,3},{8,12},{12,8},{9,1... | collective-permute-start | bytes 3080 | tf_op jit(solution)/shard_map/ppermute | solution.py:239
  245.7 281.1 %all-gather.12.cloned.1.call-start = ((), (), s32[]{:S(2)}) async-start(), calls=%async_computation.12 | async-start | bytes 5242880 | tf_op jit(solution)/shard_map/all_gather | solution.py:367
  251.6 293.6 %all-gather.14.cloned.1.call-start = ((), (), s32[]{:S(2)}) async-start(), calls=%async_computation.13 | async-start | bytes 5242880 | tf_op jit(solution)/shard_map/all_gather | solution.py:367
  251.7 70.9 %collective-permute-start.79 = (bf16[256,4096]{1,0:T(8,128)(2,1)}, bf16[256,4096]{1,0:T(8,128)(2,1)}, u32[]{:S(2)}, u32[]{:S(2)}) collective-permute-start(bf16[256,4096]{1,0:T(8,128)(2,1)} %bitcast.411), channel_id=1, source_target_pairs={{0,4},{4,0},{1,5},{5,1},{2,6},{6,2},{3,7},{7,3},{8,12},{12,8},{9,1... | collective-permute-start | bytes 6291464 | tf_op jit(solution)/shard_map/ppermute | solution.py:239
  252.1 70.4 %collective-permute-start.78 = (bf16[256,4096]{1,0:T(8,128)(2,1)}, bf16[256,4096]{1,0:T(8,128)(2,1)}, u32[]{:S(2)}, u32[]{:S(2)}) collective-permute-start(bf16[256,4096]{1,0:T(8,128)(2,1)} %bitcast.412), channel_id=1, source_target_pairs={{0,2},{2,0},{1,3},{3,1},{4,6},{6,4},{5,7},{7,5},{8,10},{10,8},{9,1... | collective-permute-start | bytes 6291464 | tf_op jit(solution)/shard_map/ppermute | solution.py:239
  257.5 406.0 %reduce-scatter.6.cloned.1.call-start = ((), (), s32[]{:S(2)}) async-start(), calls=%async_computation.14 | async-start | bytes 5242880 | tf_op jit(solution)/shard_map/reduce_scatter | solution.py:483
  274.5 36.5 %collective-permute-start.27 = (bf16[2,128,1024]{2,1,0:T(8,128)(2,1)S(1)}, bf16[2,128,1024]{2,1,0:T(8,128)(2,1)S(1)}, u32[]{:S(2)}, u32[]{:S(2)}) collective-permute-start(bf16[2,128,1024]{2,1,0:T(8,128)(2,1)S(1)} %slice_bitcast_fusion.3), channel_id=1, source_target_pairs={{0,4},{4,0},{1,5},{5,1},{2,6},{6,2},{3,7},{7,3},{8,12},{12,8},{9,1... | collective-permute-start | bytes 1572872 | tf_op jit(solution)/shard_map/cond/branch_1_fun/ppermute | solution.py:239
  276.2 36.5 %collective-permute-start.25 = (bf16[2,128,1024]{2,1,0:T(8,128)(2,1)S(1)}, bf16[2,128,1024]{2,1,0:T(8,128)(2,1)S(1)}, u32[]{:S(2)}, u32[]{:S(2)}) collective-permute-start(bf16[2,128,1024]{2,1,0:T(8,128)(2,1)S(1)} %slice_bitcast_fusion.5), channel_id=1, source_target_pairs={{0,2},{2,0},{1,3},{3,1},{4,6},{6,4},{5,7},{7,5},{8,10},{10,8},{9,1... | collective-permute-start | bytes 1572872 | tf_op jit(solution)/shard_map/cond/branch_1_fun/ppermute | solution.py:239
  544.9 225.6 %reduce-scatter.8.cloned.1.call-start = ((), (), s32[]{:S(2)}) async-start(), calls=%async_computation.15 | async-start | bytes 5242880 | tf_op jit(solution)/shard_map/reduce_scatter | solution.py:483
  566.1 246.8 %reduce-scatter.10.cloned.1.call-start = ((), (), s32[]{:S(2)}) async-start(), calls=%async_computation.16 | async-start | bytes 6553600 | tf_op jit(solution)/shard_map/reduce_scatter | solution.py:483
  718.3 435.5 %reduce-scatter.14.cloned.1.call-start = ((), (), s32[]{:S(2)}) async-start(), calls=%async_computation.18 | async-start | bytes 2621440 | tf_op jit(solution)/shard_map/reduce_scatter | solution.py:483
  812.9 361.2 %reduce-scatter.12.cloned.1.call-start = ((), (), s32[]{:S(2)}) async-start(), calls=%async_computation.17 | async-start | bytes 3932160 | tf_op jit(solution)/shard_map/reduce_scatter | solution.py:483
  1037.8 138.5 %all-to-all-start.2 = ((bf16[8,6,256,256]{3,2,1,0:T(8,128)(2,1)}), bf16[8,6,256,256]{3,2,1,0:T(8,128)(2,1)}, u32[]{:S(2)}, u32[]{:S(2)}) async-start(bf16[8,6,256,256]{3,2,1,0:T(8,128)(2,1)} %pack_gradients.1), calls=%async_computation.5 | async-start | bytes 12582912 | tf_op jit(solution)/shard_map/all_to_all | solution.py:555
  1051.5 89.2 %collective-permute-start.59 = (bf16[2,256,2048]{2,1,0:T(8,128)(2,1)}, bf16[2,256,2048]{2,1,0:T(8,128)(2,1)S(1)}, u32[]{:S(2)}, u32[]{:S(2)}) collective-permute-start(bf16[2,256,2048]{2,1,0:T(8,128)(2,1)} %get-tuple-element.126), channel_id=1, source_target_pairs={{0,1},{1,0},{2,3},{3,2},{4,5},{5,4},{6,7},{7,6},{8,9},{9,8},{10,11... | collective-permute-start | bytes 6291464 | tf_op jit(solution)/shard_map/cond/branch_1_fun/ppermute | solution.py:239
  1062.1 62.7 %collective-permute-start.52 = (bf16[2,128,1024]{2,1,0:T(8,128)(2,1)S(1)}, bf16[2,128,1024]{2,1,0:T(8,128)(2,1)S(1)}, u32[]{:S(2)}, u32[]{:S(2)}) collective-permute-start(bf16[2,128,1024]{2,1,0:T(8,128)(2,1)S(1)} %slice_bitcast_fusion.33), channel_id=1, source_target_pairs={{0,4},{4,0},{1,5},{5,1},{2,6},{6,2},{3,7},{7,3},{8,12},{12,8},{9,1... | collective-permute-start | bytes 1572872 | tf_op jit(solution)/shard_map/cond/branch_1_fun/ppermute | solution.py:239
  1064.7 61.8 %collective-permute-start.50 = (bf16[2,128,1024]{2,1,0:T(8,128)(2,1)S(1)}, bf16[2,128,1024]{2,1,0:T(8,128)(2,1)S(1)}, u32[]{:S(2)}, u32[]{:S(2)}) collective-permute-start(bf16[2,128,1024]{2,1,0:T(8,128)(2,1)S(1)} %slice_bitcast_fusion.35), channel_id=1, source_target_pairs={{0,2},{2,0},{1,3},{3,1},{4,6},{6,4},{5,7},{7,5},{8,10},{10,8},{9,1... | collective-permute-start | bytes 1572872 | tf_op jit(solution)/shard_map/cond/branch_1_fun/ppermute | solution.py:239
  1178.3 63.6 %all-to-all-start.3 = ((bf16[8,3,256,256]{3,2,1,0:T(8,128)(2,1)}), bf16[8,3,256,256]{3,2,1,0:T(8,128)(2,1)S(1)}, u32[]{:S(2)}, u32[]{:S(2)}) async-start(bf16[8,3,256,256]{3,2,1,0:T(8,128)(2,1)} %bitcast.397), calls=%async_computation.7 | async-start | bytes 6291456 | tf_op jit(solution)/shard_map/all_to_all | solution.py:577
  1187.6 50.6 %collective-permute-start.82 = (bf16[2,256,2048]{2,1,0:T(8,128)(2,1)}, bf16[2,256,2048]{2,1,0:T(8,128)(2,1)}, u32[]{:S(2)}, u32[]{:S(2)}) collective-permute-start(bf16[2,256,2048]{2,1,0:T(8,128)(2,1)} %pad_maximum_fusion.14), channel_id=1, source_target_pairs={{0,1},{1,0},{2,3},{3,2},{4,5},{5,4},{6,7},{7,6},{8,9},{9,8},{10,11... | collective-permute-start | bytes 6291464 | tf_op jit(solution)/shard_map/ppermute | solution.py:239
  (149 other events, 3585.1 us)
Sparse Core Ops, SparseCore 0:
  87.0 63.0 all-gather.5
  153.8 48.0 all-gather.7
  245.9 97.9 all-gather.9
  345.3 79.1 all-gather.11
  425.9 79.2 all-gather.13
  545.0 76.2 reduce-scatter.5
  623.7 77.2 reduce-scatter.7
  718.5 94.3 reduce-scatter.9
  815.2 44.3 reduce-scatter.13
  1038.0 60.7 reduce-scatter.11

commit v11 on v9

--- a/solution.py
+++ b/solution.py
@@ -135,29 +135,26 @@
     n_src = len(groups)
 
     def kernel(which_ref, column_ref, *refs):
-        place = pl.program_id(0) * slots + pl.program_id(1)
+        rank = pl.program_id(0)
         out_ref = refs[n_src]
-        for number in range(n_src):
-
-            @pl.when(which_ref[place] == number)
-            def _():
-                out_ref[0, 0] = refs[number][...]
-
-    def spec(number):
-        def at(rank, k, which, column):
-            place = rank * slots + k
-            return (rank // 4, jnp.where(which[place] == number, column[place], 0))
-
-        return pl.BlockSpec((rows, width), at)
+        for k in range(slots):
+            start = pl.multiple_of(column_ref[rank * slots + k] * width, width)
+            for number in range(n_src):
+
+                @pl.when(which_ref[rank * slots + k] == number)
+                def _():
+                    out_ref[0, k] = refs[number][:, pl.ds(start, width)]
 
     return pl.pallas_call(
         kernel,
         out_shape=jax.ShapeDtypeStruct((8, slots, rows, width), bf16),
         grid_spec=pltpu.PrefetchScalarGridSpec(
             num_scalar_prefetch=2,
-            grid=(8, slots),
-            in_specs=[spec(number) for number in range(n_src)],
-            out_specs=pl.BlockSpec((1, 1, rows, width), lambda rank, k, which, column: (rank, k, 0, 0)),
+            grid=(8,),
+            in_specs=[
+                pl.BlockSpec((rows, group.shape[1]), lambda rank, which, column: (rank // 4, 0)) for group in groups
+            ],
+            out_specs=pl.BlockSpec((1, slots, rows, width), lambda rank, which, column: (rank, 0, 0, 0)),
         ),
         compiler_params=pltpu.CompilerParams(vmem_limit_bytes=VMEM_LIMIT),
         name="pack_gradients",
@@ -348,21 +345,33 @@
     def my_block(slot):
         return lax.dynamic_index_in_dim(master, slot, 0, keepdims=False).astype(bf16)
 
+    present = owners[0] >= 0
+
+    def chain_step(move, *values):
+        shapes = jax.eval_shape(move, *values)
+        idle = jax.tree.map(lambda leaf: jnp.zeros(leaf.shape, leaf.dtype), shapes)
+        return lax.cond(present, move, lambda *_: idle, *values)
+
+    seg = segments(lengths[0], count)
+    live = keep == 1
+    code = seg * 2 + live.astype(jnp.int32)
+
+    def spread_code(code):
+        for axis in ("y", "x", "c"):
+            code = jnp.concatenate([code, swap(code, axis)])
+        return code
+
+    code = chain_step(spread_code, code)
+    seg_all = (code // 2).reshape(8, count)
+    live_all = (code % 2 == 1).reshape(8, count)
+    grad_out = cotangent.astype(f32) * live.astype(f32)[:, None]
     h0 = tokens.astype(f32)
     outer_blocks = [my_block(row_slots[mask]) for mask in range(4)]
     out_blocks = [my_block(row_slots[4 + mask]) for mask in range(4)]
     a_in = normalize(h0, gains[0]).astype(bf16)
-    sent = pack_first(after(master, column_part, column_place, row_slots, row_owners))
+    sent = pack_first(after(master, row_slots, row_owners))
     received = [lax.all_to_all(sent, PLANE, 0, 0, tiled=True).reshape(8 * half_cap, rows, block)]
-    seg = segments(lengths[0], count)
-    live = keep == 1
-    code = seg * 2 + live.astype(jnp.int32)
-    for axis in ("y", "x", "c"):
-        code = jnp.concatenate([code, swap(code, axis)])
-    seg_all = (code // 2).reshape(8, count)
-    live_all = (code % 2 == 1).reshape(8, count)
-    grad_out = cotangent.astype(f32) * live.astype(f32)[:, None]
-    received = [after(received[0], a_in, code, *outer_blocks, *out_blocks)]
+    received = [after(received[0], code, a_in, *outer_blocks, *out_blocks)]
 
     def columns_here(first, count, parts):
         chosen = slice(2 * first, 2 * (first + count))
@@ -374,9 +383,11 @@
     local = columns_here(0, 3, 1)
     w_qkv = gather_z(local)
     a_all = gather_rows(after(a_in, local))
-    d_ff = gather_rows(after(grad_out.astype(bf16), local))
-    sent = pack_second(after(master, a_all, d_ff))
+    sent = pack_second(after(master, a_all))
     received.append(lax.all_to_all(sent, PLANE, 0, 0, tiled=True).reshape(8 * half_cap, rows, block))
+    slots, ctx_len, ctx_width = context.shape
+    ctx = after(context.reshape(slots * ctx_len, ctx_width), sent)
+    ctx_x, ctx_y = swap(ctx, "x"), swap(ctx, "y")
 
     def take_rows(kind, blocks, keep_pair):
         here, there = row_owners[2 * kind], row_owners[2 * kind + 1]
@@ -391,10 +402,9 @@
         return target % 4 in (zz, (zz + 2) % 4)
 
     outer = take_rows(0, [after(value, local) for value in outer_blocks], needs_outer)
-    out_rows = take_rows(1, [after(value, local) for value in out_blocks], None)
     half_rows = rows // 2
     odd = z % 2
-    to_pair = lax.dynamic_slice_in_dim(after(outer, sent), (1 - odd) * half_rows, half_rows, 0)
+    to_pair = lax.dynamic_slice_in_dim(outer, (1 - odd) * half_rows, half_rows, 0)
     own_half = lax.dynamic_slice_in_dim(outer, odd * half_rows, half_rows, 0)
     pair_swap = [
         (zz * 8 + place, (zz ^ 1) * 8 + place)
@@ -409,13 +419,6 @@
     w_self_out = jnp.where(low_y, outer_all[:rows], outer_all[rows:])
     w_cross_out = jnp.where(low_y, outer_all[rows:], outer_all[:rows])
 
-    present = owners[0] >= 0
-
-    def chain_step(move, *values):
-        shapes = jax.eval_shape(move, *values)
-        idle = jax.tree.map(lambda leaf: jnp.zeros(leaf.shape, leaf.dtype), shapes)
-        return lax.cond(present, move, lambda *_: idle, *values)
-
     def split(value):
         return value.reshape(8, -1, heads_here, head_dim)
 
@@ -446,28 +449,38 @@
     received[1] = after(received[1], mixed)
     local_cross, local_in = columns_here(3, 5, 2), columns_here(8, 4, 2)
     w_cross = gather_z(local_cross)
-    middle = width // 2
-    halves = jnp.concatenate([out_rows[:, :middle], out_rows[:, middle:]], axis=0)
-    w_layer = gather_z(jnp.concatenate([local_in, halves], axis=1))
-    w_in = w_layer[:, : 4 * block]
-    w_out = jnp.swapaxes(w_layer[:, 4 * block :].reshape(4, 2, rows, middle), 1, 2).reshape(4 * rows, width)
-
-    slots, ctx_len, ctx_width = context.shape
-    ctx = after(context.reshape(slots * ctx_len, ctx_width), local_cross, local_in)
-    ctx_x, ctx_y = swap(ctx, "x"), swap(ctx, "y")
-    h1 = h0 + chain_step(scatter_rows, matmul(attended, w_self_out))
-    half = slots * ctx_len // 2
-    far_low = swap(after(ctx_y, h1)[:half], "x")
-    far_high = swap(after(ctx_x, h1)[half:], "y")
-    b_all = chain_step(gather_rows, normalize(h1, gains[1]).astype(bf16))
-    ctx_four = jnp.concatenate([ctx, ctx_y, ctx_x, far_low, far_high], axis=0)
-    ctx_all = jnp.concatenate([ctx_four, swap(ctx_four, "c")], axis=0)
+    w_in = gather_z(local_in)
+
+    def first_step(one, over_x, over_y):
+        half = over_x.shape[0] // 2
+        return scatter_rows(one), swap(over_y[:half], "x"), swap(over_x[half:], "y")
+
+    h1, far_low, far_high = chain_step(
+        first_step, matmul(attended, w_self_out), after(ctx_x, local_in), after(ctx_y, local_in)
+    )
+    h1 = h0 + h1
+
+    def second_step(one, *pieces):
+        four = jnp.concatenate(pieces, axis=0)
+        return gather_rows(one), four, swap(four, "c")
+
+    b_all, ctx_here, ctx_there = chain_step(
+        second_step, normalize(h1, gains[1]).astype(bf16), ctx, ctx_y, ctx_x, far_low, far_high
+    )
+    out_rows = take_rows(1, [after(value, b_all) for value in out_blocks], None)
+    w_out = gather_z(out_rows)
+    d_ff = gather_rows(after(grad_out.astype(bf16), b_all))
 
     w_cross_q = w_cross[:, :block]
     w_low = w_cross[:, block : 3 * block]
     w_high = w_cross[:, 3 * block :]
-    ctx_low, ctx_high = ctx_all[:, :width], ctx_all[:, width:]
-    ctx_kv = (matmul(ctx_low, w_low) + matmul(ctx_high, w_high)).astype(bf16)
+    ctx_kv = jnp.concatenate(
+        [
+            (matmul(part[:, :width], w_low) + matmul(part[:, width:], w_high)).astype(bf16)
+            for part in (ctx_here, ctx_there)
+        ],
+        axis=0,
+    )
     cross_q = matmul(b_all, w_cross_q)
     cross_q = split(cross_q.astype(bf16))
     cross_k, cross_v = split(ctx_kv[:, :block]), split(ctx_kv[:, block:])
@@ -476,7 +489,14 @@
     cross_p = probabilities(cross_q, cross_k, own_item)
     cross_low = cross_p.astype(bf16)
     cross_o = joined(weighted(cross_low, cross_v))
-    h2 = h1 + chain_step(scatter_rows, matmul(cross_o, w_cross_out))
+    h2, ctx_all = chain_step(
+        lambda one, *pieces: (scatter_rows(one), jnp.concatenate(pieces, axis=0)),
+        matmul(cross_o, w_cross_out),
+        ctx_here,
+        ctx_there,
+    )
+    ctx_low, ctx_high = ctx_all[:, :width], ctx_all[:, width:]
+    h2 = h1 + h2
     c_all = chain_step(gather_rows, normalize(h2, gains[2]).astype(bf16))
 
     hidden = matmul(c_all, w_in)
@@ -548,19 +568,20 @@
         axis=0,
     )
     g_outer = sum_rows(after(t_outer, g_cross))
+    d_mixed = matmul_right(after(d_self_out, t_outer), w_self_out)
+    d_q, d_k, d_v = through(d_mixed, query, keys, probs, probs_low, values)
+    d_qkv = jnp.concatenate([d_q, d_k, d_v], axis=1)
+    t_qkv = matmul_left(a_all, d_qkv).astype(bf16)
+    g_qkv = sum_rows(t_qkv)
     group_of = np.array([0, 0, 0, 0, 0, 0, 0, 0, 0, 0, 1, 1, 1, 1, 0, 0, 0, 0], np.int32)
     column_of = np.array([0, 0, 0, 0, 0, 1, 3, 2, 4, 0, 0, 1, 2, 3, 0, 0, 0, 0], np.int32)
     group_at = jnp.sum(jnp.where(holds, group_of, 0), axis=2)
     column_at = jnp.sum(jnp.where(holds, column_of, 0), axis=2)
     column_at = jnp.where(group_at == 1, (column_at + f) % 4, column_at)
     sent = pack_gradients(
-        [g_cross, g_in], jnp.tile(group_at.reshape(-1), 2), jnp.tile(column_at.reshape(-1), 2), rows, block, cap
+        [after(g_cross, t_qkv), g_in], jnp.tile(group_at.reshape(-1), 2), jnp.tile(column_at.reshape(-1), 2), rows, block, cap
     )
     early_grads = lax.all_to_all(sent, PLANE, 0, 0, tiled=True).reshape(8 * cap, rows, block)
-    d_mixed = matmul_right(after(d_self_out, t_outer, sent), w_self_out)
-    d_q, d_k, d_v = through(d_mixed, query, keys, probs, probs_low, values)
-    d_qkv = jnp.concatenate([d_q, d_k, d_v], axis=1)
-    g_qkv = sum_rows(matmul_left(a_all, d_qkv).astype(bf16))
 
     def last_step(part, out_pair, gain_grad_one, gain_grad_two):
         part_zero, gain_grad_zero = jax.vjp(normalize, h0, gains[0])[1](scatter_rows(part))
@@ -568,7 +589,7 @@
         return part_zero, sum_everywhere(gain_grads), with_core(out_pair)
 
     part_zero, gain_total, out_grads = chain_step(
-        last_step, matmul_right(d_qkv, w_qkv), out_grads, gain_grad_one, gain_grad_two
+        last_step, matmul_right(after(d_qkv, sent), w_qkv), out_grads, gain_grad_one, gain_grad_two
     )
     grad_tokens = (dh1 + part_zero).astype(bf16)
 

time: 1070 us -> 1090 us (1.019)
  waiting for transfers between devices: 370 us -> 434 us
  local copies, waits for them, and re-layouts: 191 us -> 148 us
  Pallas kernels: 108 us -> 85.5 us
  other arithmetic: 86.6 us -> 100 us
    ppermute x75, waiting for transfers between devices: 319 us -> 355 us  [swap(): return lax.ppermute(value, axis, [(0, 1), (1, 0)])]
    ppermute x2, waiting for transfers between devices: 0.01 us -> 21 us  [take_rows(): from_y = lax.ppermute(across, ALL_AXES, flip_pairs(2, keep_pair))]
    unnamed x184 -> x177, local copies, waits for them, and re-layouts: 48.7 us -> 31.1 us
    concatenate x3 -> x5, other arithmetic: 1.57 us -> 14.8 us  [the longest x1 13.7 us: plane_body(): jnp.concatenate(pieces, axis=0)]
    ppermute x1, waiting for transfers between devices: 4.31 us -> 17.4 us  [plane_body(): from_pair = lax.ppermute(to_pair, ALL_AXES, pair_swap)]
    pallas_call x1, Pallas kernels: 17 us -> 4.88 us  [pack_gradients(): pl.pallas_call(kernel, out_shape=jax.ShapeDtypeStruct((8, slots, rows, wi...]
    cond x29 -> x33, local copies, waits for them, and re-layouts: 22 us -> 30.9 us
    dot_general x8 -> x10, matrix products: 50.3 us -> 48.5 us  [matmul(): return jnp.dot(left, right, preferred_element_type=f32)]
  transfers between devices with their start and end apart: 96 -> 97, of which waited for: 55 -> 61; matrix products, arithmetic and copies ran while one was open for 37% -> 35% of each run, Pallas kernels for 7% -> 6%
where the time goes in v11:
time: 1090 us; the launch traced here: 1070 us
  waiting for transfers between devices  434 us (40%)
  matrix products  156 us (14%)
  local copies, waits for them, and re-layouts  148 us (14%)
  other arithmetic  100 us (9%)
  starting transfers between devices  99.3 us (9%)
  Pallas kernels  85.5 us (8%)
  between operations  43.4 us (4%)
    ppermute x75, waiting for transfers between devices, swap(): return lax.ppermute(value, axis, [(0, 1), (1, 0)])  355 us
    pallas_call x3, Pallas kernels, adam_tiles(): pl.pallas_call(kernel, out_shape=(shape, shape, shape), grid_spec=pltpu.P...  64.6 us
    ppermute x75, starting transfers between devices, swap(): return lax.ppermute(value, axis, [(0, 1), (1, 0)])  58.5 us
    dot_general x8, matrix products, matmul_left(): lax.dot_general(left, right, (((0,), (0,)), ((), ())), preferred_element_...  48.9 us
    dot_general x10, matrix products, matmul(): return jnp.dot(left, right, preferred_element_type=f32)  48.5 us
    dot_general x6, matrix products, matmul_right(): lax.dot_general(left, right, (((1,), (1,)), ((), ())), preferred_element_...  39.8 us
    unnamed x177, local copies, waits for them, and re-layouts  31.1 us
    cond x33, local copies, waits for them, and re-layouts  30.9 us
  transfers between devices with their start and end apart: 97, of which 61 were waited for; matrix products, arithmetic and copies ran while one was open for 35% of the time, Pallas kernels for 6%

profile of v11, /device:TPU:0, one launch (start us, length us, event | category | flops | bytes accessed | tf_op | source)
XLA Modules:
  0.0 1067.2 jit_solution(13519578915756908923)
XLA Ops:
  49.2 22.6 %conditional.11 = (s32[1024]{0:T(1024)S(1)}) conditional(s32[]{:T(128)} %bitcast.69, () %tuple.116, (s32[128]{0:T(128)S(1)}, s32[128]{0:T(128)S(1)}, s32[128]{0:T(128)S(1)}) %tuple.117), branch_computations={%region_8.9_spmd, %region_9.10_spmd} | conditional | flops 4736 | bytes 30848 | solution.py:353
  51.3 15.8 %collective-permute-done = s32[128]{0:T(128)S(1)} collective-permute-done((s32[128]{0:T(128)S(1)}, s32[128]{0:T(128)S(1)}, u32[]{:S(2)}, u32[]{:S(2)}) %collective-permute-start) | collective-permute-done | bytes 544 | tf_op jit(solution)/shard_map/cond/branch_1_fun/ppermute | solution.py:241
  133.4 17.4 %collective-permute-done.70 = bf16[128,2048]{1,0:T(8,128)(2,1)} collective-permute-done((bf16[128,2048]{1,0:T(8,128)(2,1)}, bf16[128,2048]{1,0:T(8,128)(2,1)}, u32[]{:S(2)}, u32[]{:S(2)}) %collective-permute-start.70) | collective-permute-done | bytes 524320 | tf_op jit(solution)/shard_map/ppermute | solution.py:415
  196.8 12.4 %all-to-all-done.1 = bf16[8,3,256,256]{3,2,1,0:T(8,128)(2,1)} async-done(((bf16[8,3,256,256]{3,2,1,0:T(8,128)(2,1)}), bf16[8,3,256,256]{3,2,1,0:T(8,128)(2,1)}, u32[]{:S(2)}, u32[]{:S(2)}) %all-to-all-start.1) | async-done | bytes 3145760 | tf_op jit(solution)/shard_map/all_to_all | solution.py:387
  223.4 36.9 %collective-permute-done.71 = bf16[256,4096]{1,0:T(8,128)(2,1)} collective-permute-done((bf16[256,4096]{1,0:T(8,128)(2,1)}, bf16[256,4096]{1,0:T(8,128)(2,1)}, u32[]{:S(2)}, u32[]{:S(2)}) %collective-permute-start.71) | collective-permute-done | bytes 2097184 | tf_op jit(solution)/shard_map/ppermute | solution.py:241
  264.4 58.2 %conditional.12 = (f32[128,2048]{1,0:T(8,128)S(1)}, bf16[128,4096]{1,0:T(8,128)(2,1)}, bf16[128,4096]{1,0:T(8,128)(2,1)}) conditional(s32[]{:T(128)} %bitcast.69, () %tuple.114, (f32[1024,2048]{1,0:T(8,128)S(1)}, bf16[256,4096]{1,0:T(8,128)(2,1)}, bf16[256,4096]{1,0:T(8,128)(2,1)}) %tuple.129), branch_computations={%region_12.13_spmd, %region_13.14_spmd} | conditional | flops 2883584 | bytes 78119216 | solution.py:353
  289.3 26.5 %collective-permute-done.26 = bf16[2,128,1024]{2,1,0:T(8,128)(2,1)S(1)} collective-permute-done((bf16[2,128,1024]{2,1,0:T(8,128)(2,1)S(1)}, bf16[2,128,1024]{2,1,0:T(8,128)(2,1)S(1)}, u32[]{:S(2)}, u32[]{:S(2)}) %collective-permute-start.26) | collective-permute-done | bytes 524320 | tf_op jit(solution)/shard_map/cond/branch_1_fun/ppermute | solution.py:241
  325.0 41.9 %conditional.13 = (bf16[1024,2048]{1,0:T(8,128)(2,1)}, bf16[1024,4096]{1,0:T(8,128)(2,1)}, bf16[1024,4096]{1,0:T(8,128)(2,1)}) conditional(s32[]{:T(128)} %bitcast.69, () %tuple.131, (bf16[128,2048]{1,0:T(8,128)(2,1)S(1)}, bf16[256,4096]{1,0:T(8,128)(2,1)S(1)}, bf16[256,4096]{1,0:T(8,128)(2,1)}, bf16[256,4096]{1,0:T(8,128)(2,1)}, ...), branch_computations={%region_15.16_spmd, %region_16.17_spmd} | conditional | bytes 76546312 | solution.py:353
  339.1 12.5 %collective-permute-done.3 = bf16[128,2048]{1,0:T(8,128)(2,1)S(1)} collective-permute-done((bf16[128,2048]{1,0:T(8,128)(2,1)S(1)}, bf16[128,2048]{1,0:T(8,128)(2,1)S(1)}, u32[]{:S(2)}, u32[]{:S(2)}) %collective-permute-start.3) | collective-permute-done | bytes 524320 | tf_op jit(solution)/shard_map/cond/branch_1_fun/ppermute | solution.py:241
  405.5 17.0 %collective-permute-done.79 = bf16[256,2048]{1,0:T(8,128)(2,1)} collective-permute-done((bf16[256,2048]{1,0:T(8,128)(2,1)}, bf16[256,2048]{1,0:T(8,128)(2,1)}, u32[]{:S(2)}, u32[]{:S(2)}) %collective-permute-start.79) | collective-permute-done | bytes 1048608 | tf_op jit(solution)/shard_map/ppermute | solution.py:398
  461.8 39.5 %conditional.14 = (f32[128,2048]{1,0:T(8,128)S(1)}, bf16[2048,4096]{1,0:T(8,128)(2,1)}) conditional(s32[]{:T(128)} %bitcast.69, () %tuple.130, (f32[1024,2048]{1,0:T(8,128)S(1)}, bf16[1024,4096]{1,0:T(8,128)(2,1)}, bf16[1024,4096]{1,0:T(8,128)(2,1)}) %tuple.133), branch_computations={%region_19.20_spmd, %region_20.21_spmd} | conditional | flops 36438016 | bytes 99090648 | solution.py:353
  472.9 12.2 %collective-permute-done.35 = bf16[2,128,1024]{2,1,0:T(8,128)(2,1)S(1)} collective-permute-done((bf16[2,128,1024]{2,1,0:T(8,128)(2,1)S(1)}, bf16[2,128,1024]{2,1,0:T(8,128)(2,1)S(1)}, u32[]{:S(2)}, u32[]{:S(2)}) %collective-permute-start.35) | collective-permute-done | bytes 524320 | tf_op jit(solution)/shard_map/cond/branch_1_fun/ppermute | solution.py:241
  487.4 13.7 %pad_maximum_fusion.1 = bf16[2048,4096]{1,0:T(8,128)(2,1)} fusion(bf16[1024,4096]{1,0:T(8,128)(2,1)} %get-tuple-element.100, bf16[1024,4096]{1,0:T(8,128)(2,1)} %get-tuple-element.99), kind=kLoop, calls=%fused_computation.36 | loop fusion | flops 33554432 | bytes 33554432 | tf_op jit(solution)/shard_map/cond/branch_1_fun/concatenate | solution.py:493
  502.8 27.0 %conditional.15 = (bf16[1024,2048]{1,0:T(8,128)(2,1)}) conditional(s32[]{:T(128)} %bitcast.69, () %tuple.135, bf16[128,2048]{1,0:T(8,128)(2,1)S(1)} %get-tuple-element.290), branch_computations={%region_22.23_spmd, %region_23.24_spmd} | conditional | bytes 26214608 | solution.py:353
  581.7 52.8 %conditional.16 = (f32[128,2048]{1,0:T(8,128)S(1)}, f32[128,2048]{1,0:T(8,128)S(1)}) conditional(s32[]{:T(128)} %bitcast.69, () %tuple.134, (f32[1024,2048]{1,0:T(8,128)S(1)}, f32[1024,2048]{1,0:T(8,128)}) %tuple.142), branch_computations={%region_24.25_spmd, %region_25.26_spmd} | conditional | flops 5767168 | bytes 131072416 | solution.py:353
  636.5 26.8 %conditional.17 = (bf16[1024,2048]{1,0:T(8,128)(2,1)}) conditional(s32[]{:T(128)} %bitcast.69, () %tuple.145, bf16[128,2048]{1,0:T(8,128)(2,1)} %get-tuple-element.205), branch_computations={%region_27.28_spmd, %region_28.29_spmd} | conditional | bytes 26214608 | solution.py:353
  663.2 28.6 %conditional.18 = (bf16[1024,256]{0,1:T(8,128)(2,1)}, bf16[2048,256]{0,1:T(8,128)(2,1)}, bf16[2048,256]{0,1:T(8,128)(2,1)}, bf16[2,256,2048]{2,1,0:T(8,128)(2,1)}) conditional(s32[]{:T(128)} %bitcast.69, () %tuple.144, (bf16[1024,2048]{1,0:T(8,128)(2,1)}, bf16[256,2048]{1,0:T(8,128)(2,1)}, bf16[8,256,2,128]{3,2,1,0:T(2,128)(2,1)}, ...), branch_computations={%region_30.31_spmd, %region_31.33_spmd} | conditional | flops 1616640000 | bytes 62406868 | solution.py:353
  729.9 35.3 %conditional.19 = (f32[128,2048]{1,0:T(8,128)S(1)}) conditional(s32[]{:T(128)} %bitcast.69, () %tuple.143, f32[1024,2048]{1,0:T(8,128)} %fusion.119), branch_computations={%region_33.34_spmd, %region_34.35_spmd} | conditional | flops 2883584 | bytes 65536208 | solution.py:353
  768.2 26.8 %conditional.20 = (bf16[1024,2048]{1,0:T(8,128)(2,1)}) conditional(s32[]{:T(128)} %bitcast.69, () %tuple.149, bf16[128,2048]{1,0:T(8,128)(2,1)S(1)} %get-tuple-element.210), branch_computations={%region_37.38_spmd, %region_38.39_spmd} | conditional | bytes 26214608 | solution.py:353
  849.5 104.5 %conditional.21 = (f32[128,2048]{1,0:T(8,128)}, f32[3,2048]{1,0:T(4,128)S(1)}, bf16[4,256,2048]{2,1,0:T(8,128)(2,1)}) conditional(s32[]{:T(128)} %bitcast.69, () %tuple.148, (f32[1024,2048]{1,0:T(8,128)S(1)}, f32[3,2048]{1,0:T(4,128)S(1)}, f32[128,2048]{1,0:T(8,128)S(1)}, f32[128,2048]{1,0:T(8,128)S(1)}, f32[128,2048]{1,0:T(8,128)S(1)}, ...), branch_computations={%region_45.46_spmd, %region_46.50_spmd} | conditional | flops 9767680 | bytes 91698648 | solution.py:353
  865.9 59.1 %collective-permute-done.55 = bf16[2,128,1024]{2,1,0:T(8,128)(2,1)S(1)} collective-permute-done((bf16[2,128,1024]{2,1,0:T(8,128)(2,1)S(1)}, bf16[2,128,1024]{2,1,0:T(8,128)(2,1)S(1)}, u32[]{:S(2)}, u32[]{:S(2)}) %collective-permute-start.55) | collective-permute-done | bytes 524320 | tf_op jit(solution)/shard_map/cond/branch_1_fun/ppermute | solution.py:241
  992.0 24.1 %adam_tiles.3 = (f32[6,256,2048]{2,1,0:T(8,128)}, f32[6,256,2048]{2,1,0:T(8,128)}, f32[6,256,2048]{2,1,0:T(8,128)}) custom-call(s32[3]{0:T(128)S(1)} %call_exported.2.visit_ref, s32[3]{0:T(128)S(1)} %bitcast.367, s32[24]{0:T(128)S(1)} %reshape.489.cp_ref, s32[3]{0:T(128)S(1)} %get-tuple-element.401.rp_ref, s32[3]{0:T(128)S(1)} %call_exported.3.hold_ref, ...), custom_call_target="tpu_custom_call" | custom-call | flops 47185920 | bytes 40894464 | tf_op jit(solution)/shard_map/adam_tiles/pallas_call | solution.py:211
  1016.2 23.4 %adam_tiles.4 = (f32[6,256,2048]{2,1,0:T(8,128)}, f32[6,256,2048]{2,1,0:T(8,128)}, f32[6,256,2048]{2,1,0:T(8,128)}) custom-call(s32[3]{0:T(128)S(1)} %copy-done.7, s32[3]{0:T(128)S(1)} %slice.565.mode_ref, s32[24]{0:T(128)S(1)} %reshape.488.cp_ref, s32[3]{0:T(128)S(1)} %get-tuple-element.402.rp_ref, ...), custom_call_target="tpu_custom_call", output_to_operand_aliasing={{0}: (10, {}), {1}: (11, {}), {2}: (12, {})} | custom-call | flops 47185920 | bytes 40894464 | tf_op jit(solution)/shard_map/adam_tiles/pallas_call | solution.py:211
  1043.2 17.0 %adam_tiles.5 = (f32[6,256,2048]{2,1,0:T(8,128)}, f32[6,256,2048]{2,1,0:T(8,128)}, f32[6,256,2048]{2,1,0:T(8,128)}) custom-call(s32[5]{0:T(128)S(1)} %get-tuple-element.433.visit_ref, s32[5]{0:T(128)S(1)} %get-tuple-element.432.mode_ref, s32[40]{0:T(128)S(1)} %select_n.464.cp_ref, ...), custom_call_target="tpu_custom_call", output_to_operand_aliasing={{0}: (12, {}), {1}: (13, {}), {2}: (14, {})} | custom-call | flops 78643200 | bytes 68157440 | tf_op jit(solution)/shard_map/adam_tiles/pallas_call | solution.py:211
  (701 shorter events, 734.0 us)
Async XLA Ops:
  24.7 60.2 %all-to-all-start = ((bf16[8,3,256,256]{3,2,1,0:T(8,128)(2,1)}), bf16[8,3,256,256]{3,2,1,0:T(8,128)(2,1)S(1)}, u32[]{:S(2)}, u32[]{:S(2)}) async-start(bf16[8,3,256,256]{3,2,1,0:T(8,128)(2,1)} %copy-done), calls=%async_computation | async-start | bytes 6291456 | tf_op jit(solution)/shard_map/all_to_all | solution.py:373
  30.0 142.4 %all-gather.6.cloned.1.call-start = ((), (), s32[]{:S(2)}) async-start(), calls=%async_computation.9 | async-start | bytes 3932160 | tf_op jit(solution)/shard_map/all_gather | solution.py:381
  89.8 171.7 %all-gather.8.cloned.1.call-start = ((), (), s32[]{:S(2)}) async-start(), calls=%async_computation.10 | async-start | bytes 2621440 | tf_op jit(solution)/shard_map/all_gather | solution.py:417
  121.6 31.3 %collective-permute-start.67 = (bf16[512,2048]{1,0:T(8,128)(2,1)}, bf16[512,2048]{1,0:T(8,128)(2,1)}, u32[]{:S(2)}, u32[]{:S(2)}) collective-permute-start(bf16[512,2048]{1,0:T(8,128)(2,1)} %get-tuple-element.388), channel_id=1, source_target_pairs={{0,1},{1,0},{2,3},{3,2},{4,5},{5,4},{6,7},{7,6},{8,9},{9,8},{10,11... | collective-permute-start | bytes 6291464 | tf_op jit(solution)/shard_map/ppermute | solution.py:241
  162.0 47.1 %all-to-all-start.1 = ((bf16[8,3,256,256]{3,2,1,0:T(8,128)(2,1)}), bf16[8,3,256,256]{3,2,1,0:T(8,128)(2,1)}, u32[]{:S(2)}, u32[]{:S(2)}) async-start(bf16[8,3,256,256]{3,2,1,0:T(8,128)(2,1)} %copy-done.1), calls=%async_computation.1 | async-start | bytes 6291456 | tf_op jit(solution)/shard_map/all_to_all | solution.py:387
  171.7 253.7 %all-gather.10.cloned.1.call-start = ((), (), s32[]{:S(2)}) async-start(), calls=%async_computation.11 | async-start | bytes 6553600 | tf_op jit(solution)/shard_map/all_gather | solution.py:381
  212.4 317.4 %all-gather.12.cloned.1.call-start = ((), (), s32[]{:S(2)}) async-start(), calls=%async_computation.12 | async-start | bytes 5242880 | tf_op jit(solution)/shard_map/all_gather | solution.py:381
  212.4 47.9 %collective-permute-start.71 = (bf16[256,4096]{1,0:T(8,128)(2,1)}, bf16[256,4096]{1,0:T(8,128)(2,1)}, u32[]{:S(2)}, u32[]{:S(2)}) collective-permute-start(bf16[256,4096]{1,0:T(8,128)(2,1)} %bitcast.394), channel_id=1, source_target_pairs={{0,2},{2,0},{1,3},{3,1},{4,6},{6,4},{5,7},{7,5},{8,10},{10,8},{9,1... | collective-permute-start | bytes 6291464 | tf_op jit(solution)/shard_map/ppermute | solution.py:241
  214.0 47.5 %collective-permute-start.72 = (bf16[256,4096]{1,0:T(8,128)(2,1)}, bf16[256,4096]{1,0:T(8,128)(2,1)}, u32[]{:S(2)}, u32[]{:S(2)}) collective-permute-start(bf16[256,4096]{1,0:T(8,128)(2,1)} %bitcast.395), channel_id=1, source_target_pairs={{0,4},{4,0},{1,5},{5,1},{2,6},{6,2},{3,7},{7,3},{8,12},{12,8},{9,1... | collective-permute-start | bytes 6291464 | tf_op jit(solution)/shard_map/ppermute | solution.py:241
  220.4 326.0 %all-gather.14.cloned.1.call-start = ((), (), s32[]{:S(2)}) async-start(), calls=%async_computation.13 | async-start | bytes 5242880 | tf_op jit(solution)/shard_map/all_gather | solution.py:381
  275.6 47.0 %collective-permute-start.30 = (bf16[128,4096]{1,0:T(8,128)(2,1)S(1)}, bf16[128,4096]{1,0:T(8,128)(2,1)}, u32[]{:S(2)}, u32[]{:S(2)}) collective-permute-start(bf16[128,4096]{1,0:T(8,128)(2,1)S(1)} %slice.372), channel_id=1, source_target_pairs={{0,4},{4,0},{1,5},{5,1},{2,6},{6,2},{3,7},{7,3},{8,12},{12,8},{9,1... | collective-permute-start | bytes 3145736 | tf_op jit(solution)/shard_map/cond/branch_1_fun/ppermute | solution.py:241
  278.4 44.2 %collective-permute-start.31 = (bf16[128,4096]{1,0:T(8,128)(2,1)S(1)}, bf16[128,4096]{1,0:T(8,128)(2,1)}, u32[]{:S(2)}, u32[]{:S(2)}) collective-permute-start(bf16[128,4096]{1,0:T(8,128)(2,1)S(1)} %slice.373), channel_id=1, source_target_pairs={{0,2},{2,0},{1,3},{3,1},{4,6},{6,4},{5,7},{7,5},{8,10},{10,8},{9,1... | collective-permute-start | bytes 3145736 | tf_op jit(solution)/shard_map/cond/branch_1_fun/ppermute | solution.py:241
  279.0 36.7 %collective-permute-start.26 = (bf16[2,128,1024]{2,1,0:T(8,128)(2,1)S(1)}, bf16[2,128,1024]{2,1,0:T(8,128)(2,1)S(1)}, u32[]{:S(2)}, u32[]{:S(2)}) collective-permute-start(bf16[2,128,1024]{2,1,0:T(8,128)(2,1)S(1)} %slice_bitcast_fusion.5), channel_id=1, source_target_pairs={{0,2},{2,0},{1,3},{3,1},{4,6},{6,4},{5,7},{7,5},{8,10},{10,8},{9,1... | collective-permute-start | bytes 1572872 | tf_op jit(solution)/shard_map/cond/branch_1_fun/ppermute | solution.py:241
  424.9 238.4 %reduce-scatter.6.cloned.1.call-start = ((), (), s32[]{:S(2)}) async-start(), calls=%async_computation.14 | async-start | bytes 5242880 | tf_op jit(solution)/shard_map/reduce_scatter | solution.py:507
  546.1 222.1 %reduce-scatter.8.cloned.1.call-start = ((), (), s32[]{:S(2)}) async-start(), calls=%async_computation.15 | async-start | bytes 5242880 | tf_op jit(solution)/shard_map/reduce_scatter | solution.py:507
  567.3 244.4 %reduce-scatter.10.cloned.1.call-start = ((), (), s32[]{:S(2)}) async-start(), calls=%async_computation.16 | async-start | bytes 6553600 | tf_op jit(solution)/shard_map/reduce_scatter | solution.py:507
  717.9 236.2 %reduce-scatter.14.cloned.1.call-start = ((), (), s32[]{:S(2)}) async-start(), calls=%async_computation.18 | async-start | bytes 2621440 | tf_op jit(solution)/shard_map/reduce_scatter | solution.py:507
  811.7 162.4 %reduce-scatter.12.cloned.1.call-start = ((), (), s32[]{:S(2)}) async-start(), calls=%async_computation.17 | async-start | bytes 3932160 | tf_op jit(solution)/shard_map/reduce_scatter | solution.py:507
  838.2 138.1 %all-to-all-start.2 = ((bf16[8,6,256,256]{3,2,1,0:T(8,128)(2,1)}), bf16[8,6,256,256]{3,2,1,0:T(8,128)(2,1)}, u32[]{:S(2)}, u32[]{:S(2)}) async-start(bf16[8,6,256,256]{3,2,1,0:T(8,128)(2,1)} %pack_gradients.1), calls=%async_computation.5 | async-start | bytes 12582912 | tf_op jit(solution)/shard_map/all_to_all | solution.py:584
  851.1 89.8 %collective-permute-start.62 = (bf16[2,256,2048]{2,1,0:T(8,128)(2,1)}, bf16[2,256,2048]{2,1,0:T(8,128)(2,1)S(1)}, u32[]{:S(2)}, u32[]{:S(2)}) collective-permute-start(bf16[2,256,2048]{2,1,0:T(8,128)(2,1)} %get-tuple-element.116), channel_id=1, source_target_pairs={{0,1},{1,0},{2,3},{3,2},{4,5},{5,4},{6,7},{7,6},{8,9},{9,8},{10,11... | collective-permute-start | bytes 6291464 | tf_op jit(solution)/shard_map/cond/branch_1_fun/ppermute | solution.py:241
  861.8 63.2 %collective-permute-start.55 = (bf16[2,128,1024]{2,1,0:T(8,128)(2,1)S(1)}, bf16[2,128,1024]{2,1,0:T(8,128)(2,1)S(1)}, u32[]{:S(2)}, u32[]{:S(2)}) collective-permute-start(bf16[2,128,1024]{2,1,0:T(8,128)(2,1)S(1)} %slice_bitcast_fusion.33), channel_id=1, source_target_pairs={{0,4},{4,0},{1,5},{5,1},{2,6},{6,2},{3,7},{7,3},{8,12},{12,8},{9,1... | collective-permute-start | bytes 1572872 | tf_op jit(solution)/shard_map/cond/branch_1_fun/ppermute | solution.py:241
  864.4 62.4 %collective-permute-start.53 = (bf16[2,128,1024]{2,1,0:T(8,128)(2,1)S(1)}, bf16[2,128,1024]{2,1,0:T(8,128)(2,1)S(1)}, u32[]{:S(2)}, u32[]{:S(2)}) collective-permute-start(bf16[2,128,1024]{2,1,0:T(8,128)(2,1)S(1)} %slice_bitcast_fusion.35), channel_id=1, source_target_pairs={{0,2},{2,0},{1,3},{3,1},{4,6},{6,4},{5,7},{7,5},{8,10},{10,8},{9,1... | collective-permute-start | bytes 1572872 | tf_op jit(solution)/shard_map/cond/branch_1_fun/ppermute | solution.py:241
  978.3 64.8 %all-to-all-start.3 = ((bf16[8,3,256,256]{3,2,1,0:T(8,128)(2,1)}), bf16[8,3,256,256]{3,2,1,0:T(8,128)(2,1)S(1)}, u32[]{:S(2)}, u32[]{:S(2)}) async-start(bf16[8,3,256,256]{3,2,1,0:T(8,128)(2,1)} %bitcast.374), calls=%async_computation.7 | async-start | bytes 6291456 | tf_op jit(solution)/shard_map/all_to_all | solution.py:598
  987.8 51.8 %collective-permute-start.82 = (bf16[2,256,2048]{2,1,0:T(8,128)(2,1)}, bf16[2,256,2048]{2,1,0:T(8,128)(2,1)}, u32[]{:S(2)}, u32[]{:S(2)}) collective-permute-start(bf16[2,256,2048]{2,1,0:T(8,128)(2,1)} %pad_maximum_fusion.15), channel_id=1, source_target_pairs={{0,1},{1,0},{2,3},{3,2},{4,5},{5,4},{6,7},{7,6},{8,9},{9,8},{10,11... | collective-permute-start | bytes 6291464 | tf_op jit(solution)/shard_map/ppermute | solution.py:241
  (161 other events, 3011.5 us)
Sparse Core Ops, SparseCore 0:
  90.0 65.7 all-gather.5
  157.9 48.0 all-gather.7
  212.5 97.9 all-gather.9
  311.9 79.1 all-gather.11
  425.0 80.1 all-gather.13
  546.2 76.5 reduce-scatter.5
  625.2 77.2 reduce-scatter.7
  718.0 93.6 reduce-scatter.9
  814.0 44.3 reduce-scatter.13
  861.2 59.5 reduce-scatter.11

commit v12 on v11

--- a/solution.py
+++ b/solution.py
@@ -195,7 +195,8 @@
 
     def column_spec(number):
         def at(n, b, vi, mo, cp, rp, ho):
-            return (jnp.where(mo[n] == number + 2, cp[n * 8 + block_of(n, b, ho)], 0), 0, 0)
+            place = jnp.where(mo[n] == number + 2, cp[n * 8 + block_of(n, b, ho)], 0)
+            return (place // 8, 0, place % 8)
 
         return pl.BlockSpec((1, rows, width), at)
 
@@ -242,9 +243,11 @@
 
 
 def gather_rows(value):
+    return gather_rest(value, swap(value, "x"), swap(value, "y"))
+
+
+def gather_rest(value, over_x, over_y):
     half = value.shape[0] // 2
-    over_x = swap(value, "x")
-    over_y = swap(value, "y")
     far_low = swap(over_y[:half], "x")
     far_high = swap(over_x[half:], "y")
     four = jnp.concatenate([value, over_y, over_x, far_low, far_high], axis=0)
@@ -265,11 +268,14 @@
 
 
 def sum_everywhere(value):
-    for axis in ("c", "y", "x"):
-        value = value + swap(value, axis)
-    for step in (1, 2):
-        value = value + lax.ppermute(value, "z", [(z, z ^ step) for z in range(4)])
-    return value
+    def add_up(terms):
+        while len(terms) > 1:
+            terms = [terms[n] + terms[n + 1] for n in range(0, len(terms), 2)]
+        return terms[0]
+
+    value = add_up([value] + [lax.ppermute(value, ALL_AXES, flip_pairs(mask)) for mask in range(1, 8)])
+    flips = [[(z, z ^ mask) for z in range(4)] for mask in range(1, 4)]
+    return add_up([value] + [lax.ppermute(value, "z", pairs) for pairs in flips])
 
 
 def flip_pairs(mask, keep=None):
@@ -361,9 +367,6 @@
             code = jnp.concatenate([code, swap(code, axis)])
         return code
 
-    code = chain_step(spread_code, code)
-    seg_all = (code // 2).reshape(8, count)
-    live_all = (code % 2 == 1).reshape(8, count)
     grad_out = cotangent.astype(f32) * live.astype(f32)[:, None]
     h0 = tokens.astype(f32)
     outer_blocks = [my_block(row_slots[mask]) for mask in range(4)]
@@ -371,7 +374,10 @@
     a_in = normalize(h0, gains[0]).astype(bf16)
     sent = pack_first(after(master, row_slots, row_owners))
     received = [lax.all_to_all(sent, PLANE, 0, 0, tiled=True).reshape(8 * half_cap, rows, block)]
+    code = chain_step(spread_code, after(code, a_in, *outer_blocks, *out_blocks))
     received = [after(received[0], code, a_in, *outer_blocks, *out_blocks)]
+    seg_all = (code // 2).reshape(8, count)
+    live_all = (code % 2 == 1).reshape(8, count)
 
     def columns_here(first, count, parts):
         chosen = slice(2 * first, 2 * (first + count))
@@ -382,8 +388,10 @@
 
     local = columns_here(0, 3, 1)
     w_qkv = gather_z(local)
-    a_all = gather_rows(after(a_in, local))
-    sent = pack_second(after(master, a_all))
+    a_ready = after(a_in, local)
+    a_x, a_y = swap(a_ready, "x"), swap(a_ready, "y")
+    a_all = gather_rest(a_in, a_x, a_y)
+    sent = pack_second(after(master, a_x, a_y))
     received.append(lax.all_to_all(sent, PLANE, 0, 0, tiled=True).reshape(8 * half_cap, rows, block))
     slots, ctx_len, ctx_width = context.shape
     ctx = after(context.reshape(slots * ctx_len, ctx_width), sent)
@@ -422,7 +430,7 @@
     def split(value):
         return value.reshape(8, -1, heads_here, head_dim)
 
-    qkv = matmul(a_all, w_qkv)
+    qkv = matmul(after(a_all, received[1]), w_qkv)
     qkv = qkv.astype(bf16)
     query, keys, values = (split(qkv[:, n * block : (n + 1) * block]) for n in range(3))
     places = jnp.arange(count)
@@ -446,7 +454,6 @@
     probs_low = probs.astype(bf16)
     mixed = weighted(probs_low, values).astype(bf16)
     attended = mixed.reshape(-1, block)
-    received[1] = after(received[1], mixed)
     local_cross, local_in = columns_here(3, 5, 2), columns_here(8, 4, 2)
     w_cross = gather_z(local_cross)
     w_in = gather_z(local_in)
@@ -460,16 +467,14 @@
     )
     h1 = h0 + h1
 
-    def second_step(one, *pieces):
+    def second_step(one, blocks, pieces):
         four = jnp.concatenate(pieces, axis=0)
-        return gather_rows(one), four, swap(four, "c")
-
-    b_all, ctx_here, ctx_there = chain_step(
-        second_step, normalize(h1, gains[1]).astype(bf16), ctx, ctx_y, ctx_x, far_low, far_high
-    )
-    out_rows = take_rows(1, [after(value, b_all) for value in out_blocks], None)
+        return gather_rows(one), take_rows(1, blocks, None), four, swap(four, "c")
+
+    b_all, out_rows, ctx_here, ctx_there = chain_step(
+        second_step, normalize(h1, gains[1]).astype(bf16), out_blocks, (ctx, ctx_y, ctx_x, far_low, far_high)
+    )
     w_out = gather_z(out_rows)
-    d_ff = gather_rows(after(grad_out.astype(bf16), b_all))
 
     w_cross_q = w_cross[:, :block]
     w_low = w_cross[:, block : 3 * block]
@@ -497,7 +502,11 @@
     )
     ctx_low, ctx_high = ctx_all[:, :width], ctx_all[:, width:]
     h2 = h1 + h2
-    c_all = chain_step(gather_rows, normalize(h2, gains[2]).astype(bf16))
+    c_all, d_ff = chain_step(
+        lambda one, two: (gather_rows(one), gather_rows(two)),
+        normalize(h2, gains[2]).astype(bf16),
+        grad_out.astype(bf16),
+    )
 
     hidden = matmul(c_all, w_in)
     activated = gelu_tanh(hidden).astype(bf16)
@@ -593,9 +602,11 @@
     )
     grad_tokens = (dh1 + part_zero).astype(bf16)
 
-    by_tile = jnp.swapaxes(after(g_qkv, out_grads).reshape(2, rows, 3, block), 1, 2)
-    sent = jnp.broadcast_to(by_tile[:, None], (2, 4, 3, rows, block)).reshape(8, 3, rows, block)
-    late_grads = lax.all_to_all(sent, PLANE, 0, 0, tiled=True).reshape(8 * 3, rows, block)
+    upper, lower = g_qkv[:rows], g_qkv[rows:]
+    same_x = jnp.where(x == 0, upper, lower)
+    other_x = jnp.where(x == 0, lower, upper)
+    moved = [lax.ppermute(same_x if mask < 4 else other_x, ALL_AXES, flip_pairs(mask)) for mask in range(1, 8)]
+    late_grads = jnp.stack([same_x, *moved])
     back_swap = [(target, source) for source, target in pair_swap]
     other_half = lax.ppermute(after(g_outer, out_grads), ALL_AXES, back_swap)
     outer_grad = jnp.where(
@@ -609,7 +620,7 @@
     place = np.arange(8)
     source_x, source_f = (place % 2)[None, :], ((place // 2)[None, :] - my_shift[:, None]) % 4
     slot = np.arange(cap, dtype=np.int32)
-    column_place = (source_x * 4 + source_f) * cap + slot[:, None]
+    column_place = ((source_x * 4 + source_f) * cap + slot[:, None]) * 8
     other_row = ((z - my_shift) % 4) ^ f
     row_source = (other_row % 2) * 2 + other_row // 2
     late = (my_used == 1) & ((my_tile < 4) | (my_tile == 9))
@@ -623,7 +634,7 @@
             [early_grads],
             [out_grads],
             slot[chosen],
-            after(early_mode, outer_grad, sent)[chosen] if first else early_mode[chosen],
+            after(early_mode, outer_grad)[chosen] if first else early_mode[chosen],
             column_place[chosen].reshape(-1),
             row_source[chosen],
             np.zeros(half_cap, np.int32),
@@ -647,7 +658,7 @@
     first_mode = jnp.where(early_mode[0] == 3, 4, early_mode[0])
     late_mode = jnp.where(at_step(my_row) == 1, 5, 3)
     mode = jnp.where(hold == 1, 0, jnp.where(some, late_mode, first_mode))
-    late_place = ((place % 2)[None, :] * 4 + (place // 2)[None, :]) * 3 + tile[:, None]
+    late_place = (((place % 2)[None, :] ^ x) * 4 + ((place // 2)[None, :] ^ f)) * 8 + tile[:, None]
     late_place = jnp.where(some, late_place, column_place[:1])
     new_w, new_m, new_v = adam_tiles(
         *states,

time: 1090 us -> 1120 us (1.028)
  starting transfers between devices: 99.3 us -> 126 us
  waiting for transfers between devices: 434 us -> 459 us
  local copies, waits for them, and re-layouts: 148 us -> 132 us
    ppermute x75 -> x72, waiting for transfers between devices: 355 us -> 318 us  [swap(): return lax.ppermute(value, axis, [(0, 1), (1, 0)])]
    ppermute x2 -> x17, waiting for transfers between devices: 3.22 us -> 34.1 us  [the longest x7 28.4 us: plane_body(): lax.ppermute(same_x if mask < 4 else other_x, ALL_AXES, flip_pairs(mask))]
    all_to_all x2, waiting for transfers between devices: 12.4 us -> 37.1 us  [plane_body(): lax.all_to_all(sent, PLANE, 0, 0, tiled=True)]
    ppermute x2 -> x17, starting transfers between devices: 4.72 us -> 20.8 us  [the longest x7 10 us: plane_body(): lax.ppermute(same_x if mask < 4 else other_x, ALL_AXES, flip_pairs(mask))]
    ppermute x2, waiting for transfers between devices: 21 us -> 35 us  [take_rows(): from_y = lax.ppermute(across, ALL_AXES, flip_pairs(2, keep_pair))]
    unnamed x177 -> x197, local copies, waits for them, and re-layouts: 31.1 us -> 23.9 us
    cond x33 -> x36, local copies, waits for them, and re-layouts: 30.9 us -> 35.8 us
    ppermute x75 -> x72, starting transfers between devices: 58.5 us -> 62.6 us  [swap(): return lax.ppermute(value, axis, [(0, 1), (1, 0)])]
  transfers between devices with their start and end apart: 97 -> 108, of which waited for: 61 -> 60; matrix products, arithmetic and copies ran while one was open for 35% -> 32% of each run, Pallas kernels for 6% -> 6%
where the time goes in v12:
time: 1120 us; the launch traced here: 1100 us
  waiting for transfers between devices  459 us (41%)
  matrix products  157 us (14%)
  local copies, waits for them, and re-layouts  132 us (12%)
  starting transfers between devices  126 us (11%)
  other arithmetic  96.7 us (9%)
  Pallas kernels  87.6 us (8%)
  between operations  39.9 us (4%)
    ppermute x72, waiting for transfers between devices, swap(): return lax.ppermute(value, axis, [(0, 1), (1, 0)])  318 us
    pallas_call x3, Pallas kernels, adam_tiles(): pl.pallas_call(kernel, out_shape=(shape, shape, shape), grid_spec=pltpu.P...  65.1 us
    ppermute x72, starting transfers between devices, swap(): return lax.ppermute(value, axis, [(0, 1), (1, 0)])  62.6 us
    dot_general x8, matrix products, matmul_left(): lax.dot_general(left, right, (((0,), (0,)), ((), ())), preferred_element_...  53.5 us
    dot_general x10, matrix products, matmul(): return jnp.dot(left, right, preferred_element_type=f32)  49.4 us
    dot_general x6, matrix products, matmul_right(): lax.dot_general(left, right, (((1,), (1,)), ((), ())), preferred_element_...  38.9 us
    all_to_all x2, waiting for transfers between devices, plane_body(): lax.all_to_all(sent, PLANE, 0, 0, tiled=True)  37.1 us
    cond x36, local copies, waits for them, and re-layouts  35.8 us
  transfers between devices with their start and end apart: 108, of which 60 were waited for; matrix products, arithmetic and copies ran while one was open for 32% of the time, Pallas kernels for 6%

profile of v12, /device:TPU:0, one launch (start us, length us, event | category | flops | bytes accessed | tf_op | source)
XLA Modules:
  0.0 1104.2 jit_solution(10263330541990607825)
XLA Ops:
  89.5 14.9 %collective-permute-done.81 = bf16[256,2048]{1,0:T(8,128)(2,1)} collective-permute-done((bf16[256,2048]{1,0:T(8,128)(2,1)}, bf16[256,2048]{1,0:T(8,128)(2,1)}, u32[]{:S(2)}, u32[]{:S(2)}) %collective-permute-start.81) | collective-permute-done | bytes 1048608 | tf_op jit(solution)/shard_map/ppermute | solution.py:406
  113.0 14.1 %collective-permute-done.82 = bf16[128,2048]{1,0:T(8,128)(2,1)} collective-permute-done((bf16[128,2048]{1,0:T(8,128)(2,1)}, bf16[128,2048]{1,0:T(8,128)(2,1)}, u32[]{:S(2)}, u32[]{:S(2)}) %collective-permute-start.82) | collective-permute-done | bytes 524320 | tf_op jit(solution)/shard_map/ppermute | solution.py:423
  135.2 19.6 %all-to-all-start.1 = ((bf16[8,3,256,256]{3,2,1,0:T(8,128)(2,1)}), bf16[8,3,256,256]{3,2,1,0:T(8,128)(2,1)}, u32[]{:S(2)}, u32[]{:S(2)}) async-start(bf16[8,3,256,256]{3,2,1,0:T(8,128)(2,1)} %copy-done.1), calls=%async_computation.1 | async-start | bytes 6291456 | tf_op jit(solution)/shard_map/all_to_all | solution.py:395
  155.2 37.1 %all-to-all-done.1 = bf16[8,3,256,256]{3,2,1,0:T(8,128)(2,1)} async-done(((bf16[8,3,256,256]{3,2,1,0:T(8,128)(2,1)}), bf16[8,3,256,256]{3,2,1,0:T(8,128)(2,1)}, u32[]{:S(2)}, u32[]{:S(2)}) %all-to-all-start.1) | async-done | bytes 3145760 | tf_op jit(solution)/shard_map/all_to_all | solution.py:395
  225.3 40.5 %collective-permute-done.84 = bf16[256,4096]{1,0:T(8,128)(2,1)} collective-permute-done((bf16[256,4096]{1,0:T(8,128)(2,1)S(1)}, bf16[256,4096]{1,0:T(8,128)(2,1)}, u32[]{:S(2)}, u32[]{:S(2)}) %collective-permute-start.84) | collective-permute-done | bytes 2097184 | tf_op jit(solution)/shard_map/ppermute | solution.py:242
  280.7 56.1 %conditional.12 = (f32[128,2048]{1,0:T(8,128)S(1)}, bf16[128,4096]{1,0:T(8,128)(2,1)}, bf16[128,4096]{1,0:T(8,128)(2,1)}) conditional(s32[]{:T(128)} %bitcast.75, () %tuple.110, (f32[1024,2048]{1,0:T(8,128)S(1)}, bf16[256,4096]{1,0:T(8,128)(2,1)}, bf16[256,4096]{1,0:T(8,128)(2,1)}) %tuple.125), branch_computations={%region_12.13_spmd, %region_13.14_spmd} | conditional | flops 2883584 | bytes 78119216 | solution.py:359
  306.1 23.9 %collective-permute-done.35 = bf16[2,128,1024]{2,1,0:T(8,128)(2,1)S(1)} collective-permute-done((bf16[2,128,1024]{2,1,0:T(8,128)(2,1)S(1)}, bf16[2,128,1024]{2,1,0:T(8,128)(2,1)S(1)}, u32[]{:S(2)}, u32[]{:S(2)}) %collective-permute-start.35) | collective-permute-done | bytes 524320 | tf_op jit(solution)/shard_map/cond/branch_1_fun/ppermute | solution.py:242
  339.5 72.1 %conditional.13 = (bf16[1024,2048]{1,0:T(8,128)(2,1)}, bf16[256,2048]{1,0:T(8,128)(2,1)}, bf16[1024,4096]{1,0:T(8,128)(2,1)}, bf16[1024,4096]{1,0:T(8,128)(2,1)}) conditional(s32[]{:T(128)} %bitcast.75, () %tuple.127, (bf16[128,2048]{1,0:T(8,128)(2,1)S(1)}, s32[4]{0:T(128)S(1)}, s32[]{:T(128)}, bf16[256,2048]{1,0:T(8,128)(2,1)S(1)}, ...), branch_computations={%region_15.16_spmd, %region_16.17_spmd} | conditional | flops 2621492 | bytes 100664152 | solution.py:359
  388.8 20.1 %collective-permute-done.29 = bf16[256,2048]{1,0:T(8,128)(2,1)} collective-permute-done((bf16[256,2048]{1,0:T(8,128)(2,1)}, bf16[256,2048]{1,0:T(8,128)(2,1)}, u32[]{:S(2)}, u32[]{:S(2)}) %collective-permute-start.29) | collective-permute-done | bytes 1048608 | tf_op jit(solution)/shard_map/cond/branch_1_fun/ppermute | solution.py:406
  451.8 39.5 %conditional.14 = (f32[128,2048]{1,0:T(8,128)S(1)}, bf16[2048,4096]{1,0:T(8,128)(2,1)}) conditional(s32[]{:T(128)} %bitcast.75, () %tuple.126, (f32[1024,2048]{1,0:T(8,128)S(1)}, bf16[1024,4096]{1,0:T(8,128)(2,1)}, bf16[1024,4096]{1,0:T(8,128)(2,1)}) %tuple.129), branch_computations={%region_19.20_spmd, %region_20.21_spmd} | conditional | flops 36438016 | bytes 99090648 | solution.py:359
  462.8 12.4 %collective-permute-done.40 = bf16[2,128,1024]{2,1,0:T(8,128)(2,1)S(1)} collective-permute-done((bf16[2,128,1024]{2,1,0:T(8,128)(2,1)S(1)}, bf16[2,128,1024]{2,1,0:T(8,128)(2,1)S(1)}, u32[]{:S(2)}, u32[]{:S(2)}) %collective-permute-start.40) | collective-permute-done | bytes 524320 | tf_op jit(solution)/shard_map/cond/branch_1_fun/ppermute | solution.py:242
  477.4 13.7 %pad_maximum_fusion.2 = bf16[2048,4096]{1,0:T(8,128)(2,1)} fusion(bf16[1024,4096]{1,0:T(8,128)(2,1)} %get-tuple-element.105, bf16[1024,4096]{1,0:T(8,128)(2,1)} %get-tuple-element.104), kind=kLoop, calls=%fused_computation.41 | loop fusion | flops 33554432 | bytes 33554432 | tf_op jit(solution)/shard_map/cond/branch_1_fun/concatenate | solution.py:498
  492.9 43.4 %conditional.15 = (bf16[1024,2048]{1,0:T(8,128)(2,1)}, bf16[1024,2048]{1,0:T(8,128)(2,1)}) conditional(s32[]{:T(128)} %bitcast.75, () %tuple.131, (bf16[128,2048]{1,0:T(8,128)(2,1)S(1)}, bf16[128,2048]{1,0:T(8,128)(2,1)S(1)}) %tuple.313), branch_computations={%region_22.23_spmd, %region_23.24_spmd} | conditional | bytes 52429216 | solution.py:359
  589.9 52.1 %conditional.16 = (f32[128,2048]{1,0:T(8,128)S(1)}, f32[128,2048]{1,0:T(8,128)S(1)}) conditional(s32[]{:T(128)} %bitcast.75, () %tuple.130, (f32[1024,2048]{1,0:T(8,128)S(1)}, f32[1024,2048]{1,0:T(8,128)}) %tuple.134), branch_computations={%region_24.25_spmd, %region_25.26_spmd} | conditional | flops 5767168 | bytes 131072416 | solution.py:359
  644.1 27.4 %conditional.17 = (bf16[1024,2048]{1,0:T(8,128)(2,1)}) conditional(s32[]{:T(128)} %bitcast.75, () %tuple.137, bf16[128,2048]{1,0:T(8,128)(2,1)} %get-tuple-element.209), branch_computations={%region_27.28_spmd, %region_28.29_spmd} | conditional | bytes 26214608 | solution.py:359
  671.5 28.6 %conditional.18 = (bf16[1024,256]{0,1:T(8,128)(2,1)}, bf16[2048,256]{0,1:T(8,128)(2,1)}, bf16[2048,256]{0,1:T(8,128)(2,1)}, bf16[2,256,2048]{2,1,0:T(8,128)(2,1)}) conditional(s32[]{:T(128)} %bitcast.75, () %tuple.136, (bf16[1024,2048]{1,0:T(8,128)(2,1)}, bf16[256,2048]{1,0:T(8,128)(2,1)}, bf16[8,256,2,128]{3,2,1,0:T(2,128)(2,1)}, ...), branch_computations={%region_30.31_spmd, %region_31.33_spmd} | conditional | flops 1616640000 | bytes 62406868 | solution.py:359
  738.1 35.0 %conditional.19 = (f32[128,2048]{1,0:T(8,128)S(1)}) conditional(s32[]{:T(128)} %bitcast.75, () %tuple.135, f32[1024,2048]{1,0:T(8,128)} %fusion.118), branch_computations={%region_33.34_spmd, %region_34.35_spmd} | conditional | flops 2883584 | bytes 65536208 | solution.py:359
  776.1 26.6 %conditional.20 = (bf16[1024,2048]{1,0:T(8,128)(2,1)}) conditional(s32[]{:T(128)} %bitcast.75, () %tuple.141, bf16[128,2048]{1,0:T(8,128)(2,1)S(1)} %get-tuple-element.214), branch_computations={%region_37.38_spmd, %region_38.39_spmd} | conditional | bytes 26214608 | solution.py:359
  859.6 106.4 %conditional.21 = (f32[128,2048]{1,0:T(8,128)}, f32[3,2048]{1,0:T(4,128)S(1)}, bf16[4,256,2048]{2,1,0:T(8,128)(2,1)}) conditional(s32[]{:T(128)} %bitcast.75, () %tuple.140, (f32[1024,2048]{1,0:T(8,128)S(1)}, f32[3,2048]{1,0:T(4,128)S(1)}, f32[128,2048]{1,0:T(8,128)S(1)}, f32[128,2048]{1,0:T(8,128)S(1)}, f32[128,2048]{1,0:T(8,128)S(1)}, ...), branch_computations={%region_45.46_spmd, %region_46.50_spmd} | conditional | flops 9779968 | bytes 92141216 | solution.py:359
  876.0 58.3 %collective-permute-done.60 = bf16[2,128,1024]{2,1,0:T(8,128)(2,1)S(1)} collective-permute-done((bf16[2,128,1024]{2,1,0:T(8,128)(2,1)S(1)}, bf16[2,128,1024]{2,1,0:T(8,128)(2,1)S(1)}, u32[]{:S(2)}, u32[]{:S(2)}) %collective-permute-start.60) | collective-permute-done | bytes 524320 | tf_op jit(solution)/shard_map/cond/branch_1_fun/ppermute | solution.py:242
  986.2 18.2 %collective-permute-done.86 = bf16[256,768]{1,0:T(8,128)(2,1)S(1)} collective-permute-done((bf16[256,768]{1,0:T(8,128)(2,1)S(1)}, bf16[256,768]{1,0:T(8,128)(2,1)S(1)}, u32[]{:S(2)}, u32[]{:S(2)}) %collective-permute-start.86) | collective-permute-done | bytes 393248 | tf_op jit(solution)/shard_map/ppermute | solution.py:608
  1028.5 24.2 %adam_tiles.3 = (f32[6,256,2048]{2,1,0:T(8,128)}, f32[6,256,2048]{2,1,0:T(8,128)}, f32[6,256,2048]{2,1,0:T(8,128)}) custom-call(s32[3]{0:T(128)S(1)} %call_exported.2.visit_ref, s32[3]{0:T(128)S(1)} %bitcast.379, s32[24]{0:T(128)S(1)} %reshape.476.cp_ref, s32[3]{0:T(128)S(1)} %get-tuple-element.411.rp_ref, s32[3]{0:T(128)S(1)} %call_exported.3.hold_ref, ...), custom_call_target="tpu_custom_call" | custom-call | flops 47185920 | bytes 40894464 | tf_op jit(solution)/shard_map/adam_tiles/pallas_call | solution.py:212
  1052.7 22.7 %adam_tiles.4 = (f32[6,256,2048]{2,1,0:T(8,128)}, f32[6,256,2048]{2,1,0:T(8,128)}, f32[6,256,2048]{2,1,0:T(8,128)}) custom-call(s32[3]{0:T(128)S(1)} %copy-done.7, s32[3]{0:T(128)S(1)} %slice.567.mode_ref, s32[24]{0:T(128)S(1)} %reshape.475.cp_ref, s32[3]{0:T(128)S(1)} %get-tuple-element.412.rp_ref, ...), custom_call_target="tpu_custom_call", output_to_operand_aliasing={{0}: (10, {}), {1}: (11, {}), {2}: (12, {})} | custom-call | flops 47185920 | bytes 40894464 | tf_op jit(solution)/shard_map/adam_tiles/pallas_call | solution.py:212
  1079.0 18.2 %adam_tiles.5 = (f32[6,256,2048]{2,1,0:T(8,128)}, f32[6,256,2048]{2,1,0:T(8,128)}, f32[6,256,2048]{2,1,0:T(8,128)}) custom-call(s32[5]{0:T(128)S(1)} %get-tuple-element.439.visit_ref, s32[5]{0:T(128)S(1)} %get-tuple-element.438.mode_ref, s32[40]{0:T(128)S(1)} %select_n.471.cp_ref, ...), custom_call_target="tpu_custom_call", output_to_operand_aliasing={{0}: (12, {}), {1}: (13, {}), {2}: (14, {})} | custom-call | flops 78643200 | bytes 68157440 | tf_op jit(solution)/shard_map/adam_tiles/pallas_call | solution.py:212
  (743 shorter events, 729.1 us)
Async XLA Ops:
  24.8 47.1 %all-to-all-start = ((bf16[8,3,256,256]{3,2,1,0:T(8,128)(2,1)}), bf16[8,3,256,256]{3,2,1,0:T(8,128)(2,1)S(1)}, u32[]{:S(2)}, u32[]{:S(2)}) async-start(bf16[8,3,256,256]{3,2,1,0:T(8,128)(2,1)} %copy-done), calls=%async_computation | async-start | bytes 6291456 | tf_op jit(solution)/shard_map/all_to_all | solution.py:376
  30.1 236.9 %all-gather.6.cloned.1.call-start = ((), (), s32[]{:S(2)}) async-start(), calls=%async_computation.8 | async-start | bytes 3932160 | tf_op jit(solution)/shard_map/all_gather | solution.py:387
  76.8 200.8 %all-gather.8.cloned.1.call-start = ((), (), s32[]{:S(2)}) async-start(), calls=%async_computation.9 | async-start | bytes 2621440 | tf_op jit(solution)/shard_map/all_gather | solution.py:425
  135.2 57.1 %all-to-all-start.1 = ((bf16[8,3,256,256]{3,2,1,0:T(8,128)(2,1)}), bf16[8,3,256,256]{3,2,1,0:T(8,128)(2,1)}, u32[]{:S(2)}, u32[]{:S(2)}) async-start(bf16[8,3,256,256]{3,2,1,0:T(8,128)(2,1)} %copy-done.1), calls=%async_computation.1 | async-start | bytes 6291456 | tf_op jit(solution)/shard_map/all_to_all | solution.py:395
  154.8 259.8 %all-gather.10.cloned.1.call-start = ((), (), s32[]{:S(2)}) async-start(), calls=%async_computation.10 | async-start | bytes 6553600 | tf_op jit(solution)/shard_map/all_gather | solution.py:387
  198.8 337.5 %all-gather.12.cloned.1.call-start = ((), (), s32[]{:S(2)}) async-start(), calls=%async_computation.11 | async-start | bytes 5242880 | tf_op jit(solution)/shard_map/all_gather | solution.py:387
  212.5 342.1 %all-gather.14.cloned.1.call-start = ((), (), s32[]{:S(2)}) async-start(), calls=%async_computation.12 | async-start | bytes 5242880 | tf_op jit(solution)/shard_map/all_gather | solution.py:387
  217.7 48.1 %collective-permute-start.84 = (bf16[256,4096]{1,0:T(8,128)(2,1)S(1)}, bf16[256,4096]{1,0:T(8,128)(2,1)}, u32[]{:S(2)}, u32[]{:S(2)}) collective-permute-start(bf16[256,4096]{1,0:T(8,128)(2,1)S(1)} %bitcast.406), channel_id=1, source_target_pairs={{0,4},{4,0},{1,5},{5,1},{2,6},{6,2},{3,7},{7,3},{8,12},{12,8},{9,1... | collective-permute-start | bytes 6291464 | tf_op jit(solution)/shard_map/ppermute | solution.py:242
  219.1 47.9 %collective-permute-start.83 = (bf16[256,4096]{1,0:T(8,128)(2,1)S(1)}, bf16[256,4096]{1,0:T(8,128)(2,1)}, u32[]{:S(2)}, u32[]{:S(2)}) collective-permute-start(bf16[256,4096]{1,0:T(8,128)(2,1)S(1)} %bitcast.407), channel_id=1, source_target_pairs={{0,2},{2,0},{1,3},{3,1},{4,6},{6,4},{5,7},{7,5},{8,10},{10,8},{9,1... | collective-permute-start | bytes 6291464 | tf_op jit(solution)/shard_map/ppermute | solution.py:242
  292.6 44.2 %collective-permute-start.37 = (bf16[128,4096]{1,0:T(8,128)(2,1)S(1)}, bf16[128,4096]{1,0:T(8,128)(2,1)}, u32[]{:S(2)}, u32[]{:S(2)}) collective-permute-start(bf16[128,4096]{1,0:T(8,128)(2,1)S(1)} %slice.376), channel_id=1, source_target_pairs={{0,4},{4,0},{1,5},{5,1},{2,6},{6,2},{3,7},{7,3},{8,12},{12,8},{9,1... | collective-permute-start | bytes 3145736 | tf_op jit(solution)/shard_map/cond/branch_1_fun/ppermute | solution.py:242
  295.5 41.4 %collective-permute-start.38 = (bf16[128,4096]{1,0:T(8,128)(2,1)S(1)}, bf16[128,4096]{1,0:T(8,128)(2,1)}, u32[]{:S(2)}, u32[]{:S(2)}) collective-permute-start(bf16[128,4096]{1,0:T(8,128)(2,1)S(1)} %slice.377), channel_id=1, source_target_pairs={{0,2},{2,0},{1,3},{3,1},{4,6},{6,4},{5,7},{7,5},{8,10},{10,8},{9,1... | collective-permute-start | bytes 3145736 | tf_op jit(solution)/shard_map/cond/branch_1_fun/ppermute | solution.py:242
  353.5 58.0 %collective-permute-start.30 = (bf16[1024,4096]{1,0:T(8,128)(2,1)}, bf16[1024,4096]{1,0:T(8,128)(2,1)}, u32[]{:S(2)}, u32[]{:S(2)}) collective-permute-start(bf16[1024,4096]{1,0:T(8,128)(2,1)} %constant_dynamic-update-slice_fusion.11), channel_id=1, source_target_pairs={{0,1},{1,0},{2,3},{3,2},{4,5},{5,4},{6,7},{7,6},{8,9},{9,8},{10,11... | collective-permute-start | bytes 25165832 | tf_op jit(solution)/shard_map/cond/branch_1_fun/ppermute | solution.py:242
  411.6 259.9 %reduce-scatter.6.cloned.1.call-start = ((), (), s32[]{:S(2)}) async-start(), calls=%async_computation.13 | async-start | bytes 5242880 | tf_op jit(solution)/shard_map/reduce_scatter | solution.py:516
  554.4 221.7 %reduce-scatter.8.cloned.1.call-start = ((), (), s32[]{:S(2)}) async-start(), calls=%async_computation.14 | async-start | bytes 5242880 | tf_op jit(solution)/shard_map/reduce_scatter | solution.py:516
  575.6 244.7 %reduce-scatter.10.cloned.1.call-start = ((), (), s32[]{:S(2)}) async-start(), calls=%async_computation.15 | async-start | bytes 6553600 | tf_op jit(solution)/shard_map/reduce_scatter | solution.py:516
  726.1 239.9 %reduce-scatter.14.cloned.1.call-start = ((), (), s32[]{:S(2)}) async-start(), calls=%async_computation.17 | async-start | bytes 2621440 | tf_op jit(solution)/shard_map/reduce_scatter | solution.py:516
  820.3 148.0 %reduce-scatter.12.cloned.1.call-start = ((), (), s32[]{:S(2)}) async-start(), calls=%async_computation.16 | async-start | bytes 3932160 | tf_op jit(solution)/shard_map/reduce_scatter | solution.py:516
  847.3 181.2 %all-to-all-start.2 = ((bf16[8,6,256,256]{3,2,1,0:T(8,128)(2,1)}), bf16[8,6,256,256]{3,2,1,0:T(8,128)(2,1)}, u32[]{:S(2)}, u32[]{:S(2)}) async-start(bf16[8,6,256,256]{3,2,1,0:T(8,128)(2,1)} %pack_gradients.1), calls=%async_computation.5 | async-start | bytes 12582912 | tf_op jit(solution)/shard_map/all_to_all | solution.py:593
  861.2 84.0 %collective-permute-start.74 = (bf16[2,256,2048]{2,1,0:T(8,128)(2,1)}, bf16[2,256,2048]{2,1,0:T(8,128)(2,1)S(1)}, u32[]{:S(2)}, u32[]{:S(2)}) collective-permute-start(bf16[2,256,2048]{2,1,0:T(8,128)(2,1)} %get-tuple-element.123), channel_id=1, source_target_pairs={{0,1},{1,0},{2,3},{3,2},{4,5},{5,4},{6,7},{7,6},{8,9},{9,8},{10,11... | collective-permute-start | bytes 6291464 | tf_op jit(solution)/shard_map/cond/branch_1_fun/ppermute | solution.py:242
  871.8 62.4 %collective-permute-start.60 = (bf16[2,128,1024]{2,1,0:T(8,128)(2,1)S(1)}, bf16[2,128,1024]{2,1,0:T(8,128)(2,1)S(1)}, u32[]{:S(2)}, u32[]{:S(2)}) collective-permute-start(bf16[2,128,1024]{2,1,0:T(8,128)(2,1)S(1)} %slice_bitcast_fusion.37), channel_id=1, source_target_pairs={{0,2},{2,0},{1,3},{3,1},{4,6},{6,4},{5,7},{7,5},{8,10},{10,8},{9,1... | collective-permute-start | bytes 1572872 | tf_op jit(solution)/shard_map/cond/branch_1_fun/ppermute | solution.py:242
  874.4 61.6 %collective-permute-start.62 = (bf16[2,128,1024]{2,1,0:T(8,128)(2,1)S(1)}, bf16[2,128,1024]{2,1,0:T(8,128)(2,1)S(1)}, u32[]{:S(2)}, u32[]{:S(2)}) collective-permute-start(bf16[2,128,1024]{2,1,0:T(8,128)(2,1)S(1)} %slice_bitcast_fusion.35), channel_id=1, source_target_pairs={{0,4},{4,0},{1,5},{5,1},{2,6},{6,2},{3,7},{7,3},{8,12},{12,8},{9,1... | collective-permute-start | bytes 1572872 | tf_op jit(solution)/shard_map/cond/branch_1_fun/ppermute | solution.py:242
  983.5 40.6 %collective-permute-start.87 = (bf16[256,768]{1,0:T(8,128)(2,1)S(1)}, bf16[256,768]{1,0:T(8,128)(2,1)S(1)}, u32[]{:S(2)}, u32[]{:S(2)}) collective-permute-start(bf16[256,768]{1,0:T(8,128)(2,1)S(1)} %get-tuple-element.288), channel_id=1, source_target_pairs={{0,3},{1,2},{2,1},{3,0},{4,7},{5,6},{6,5},{7,4},{8,11},{9,10},{10,... | collective-permute-start | bytes 1179656 | tf_op jit(solution)/shard_map/ppermute | solution.py:608
  983.6 41.8 %collective-permute-start.88 = (bf16[256,768]{1,0:T(8,128)(2,1)S(1)}, bf16[256,768]{1,0:T(8,128)(2,1)S(1)}, u32[]{:S(2)}, u32[]{:S(2)}) collective-permute-start(bf16[256,768]{1,0:T(8,128)(2,1)S(1)} %broadcast_select_fusion.2), channel_id=1, source_target_pairs={{0,4},{1,5},{2,6},{3,7},{4,0},{5,1},{6,2},{7,3},{8,12},{9,13},{10,... | collective-permute-start | bytes 1179656 | tf_op jit(solution)/shard_map/ppermute | solution.py:608
  1024.1 51.3 %collective-permute-start.94 = (bf16[2,256,2048]{2,1,0:T(8,128)(2,1)}, bf16[2,256,2048]{2,1,0:T(8,128)(2,1)}, u32[]{:S(2)}, u32[]{:S(2)}) collective-permute-start(bf16[2,256,2048]{2,1,0:T(8,128)(2,1)} %pad_maximum_fusion.15), channel_id=1, source_target_pairs={{0,1},{1,0},{2,3},{3,2},{4,5},{5,4},{6,7},{7,6},{8,9},{9,8},{10,11... | collective-permute-start | bytes 6291464 | tf_op jit(solution)/shard_map/ppermute | solution.py:242
  (181 other events, 2790.9 us)
Sparse Core Ops, SparseCore 0:
  76.9 68.4 all-gather.5
  147.5 46.1 all-gather.7
  199.0 98.1 all-gather.9
  298.6 79.1 all-gather.11
  411.7 80.4 all-gather.13
  554.5 76.4 reduce-scatter.5
  633.4 77.2 reduce-scatter.7
  726.2 94.0 reduce-scatter.9
  822.6 44.3 reduce-scatter.13
  869.9 59.5 reduce-scatter.11

commit v13 on v11

--- a/solution.py
+++ b/solution.py
@@ -166,12 +166,13 @@
     width = columns // 8
     n_visit = visit.shape[0]
     n_col, n_row = len(columns_from), len(rows_from)
-    kept = () if previous is None else tuple(previous)
+    kept = () if previous is None else tuple(previous[:3])
 
     def kernel(visit_ref, mode_ref, cp_ref, rp_ref, hold_ref, *refs):
         w_ref, m_ref, v_ref = refs[:3]
         grads = refs[3 : 3 + n_col + n_row]
-        outs = refs[3 + n_col + n_row + len(kept) :]
+        outs = refs[3 + n_col + n_row + len(kept) : -1]
+        refs[-1][...] = jnp.zeros_like(refs[-1])
         how = mode_ref[pl.program_id(0)]
 
         @pl.when(how == 1)
@@ -210,7 +211,7 @@
     n_before = 5 + 3 + n_col + n_row
     return pl.pallas_call(
         kernel,
-        out_shape=(shape, shape, shape),
+        out_shape=(shape, shape, shape, jax.ShapeDtypeStruct((8, 128), f32)),
         grid_spec=pltpu.PrefetchScalarGridSpec(
             num_scalar_prefetch=5,
             grid=(n_visit, 8),
@@ -222,7 +223,7 @@
                 *(row_spec(n_col + number) for number in range(n_row)),
                 *(pl.BlockSpec(memory_space=pl.ANY) for _ in kept),
             ],
-            out_specs=(state, state, state),
+            out_specs=(state, state, state, pl.BlockSpec((8, 128), lambda *_: (0, 0))),
         ),
         input_output_aliases={n_before + n: n for n in range(len(kept))},
         compiler_params=pltpu.CompilerParams(vmem_limit_bytes=VMEM_LIMIT),
@@ -352,6 +353,12 @@
         idle = jax.tree.map(lambda leaf: jnp.zeros(leaf.shape, leaf.dtype), shapes)
         return lax.cond(present, move, lambda *_: idle, *values)
 
+    h0 = tokens.astype(f32)
+    outer_blocks = [my_block(row_slots[mask]) for mask in range(4)]
+    out_blocks = [my_block(row_slots[4 + mask]) for mask in range(4)]
+    a_in = normalize(h0, gains[0]).astype(bf16)
+    sent = pack_first(after(master, column_part, column_place, row_slots, row_owners))
+    received = [lax.all_to_all(sent, PLANE, 0, 0, tiled=True).reshape(8 * half_cap, rows, block)]
     seg = segments(lengths[0], count)
     live = keep == 1
     code = seg * 2 + live.astype(jnp.int32)
@@ -361,17 +368,11 @@
             code = jnp.concatenate([code, swap(code, axis)])
         return code
 
-    code = chain_step(spread_code, code)
+    code = chain_step(spread_code, after(code, a_in, *outer_blocks, *out_blocks))
     seg_all = (code // 2).reshape(8, count)
     live_all = (code % 2 == 1).reshape(8, count)
     grad_out = cotangent.astype(f32) * live.astype(f32)[:, None]
-    h0 = tokens.astype(f32)
-    outer_blocks = [my_block(row_slots[mask]) for mask in range(4)]
-    out_blocks = [my_block(row_slots[4 + mask]) for mask in range(4)]
-    a_in = normalize(h0, gains[0]).astype(bf16)
-    sent = pack_first(after(master, row_slots, row_owners))
-    received = [lax.all_to_all(sent, PLANE, 0, 0, tiled=True).reshape(8 * half_cap, rows, block)]
-    received = [after(received[0], code, a_in, *outer_blocks, *out_blocks)]
+    received = [after(received[0], a_in, code, *outer_blocks, *out_blocks)]
 
     def columns_here(first, count, parts):
         chosen = slice(2 * first, 2 * (first + count))
@@ -383,11 +384,9 @@
     local = columns_here(0, 3, 1)
     w_qkv = gather_z(local)
     a_all = gather_rows(after(a_in, local))
-    sent = pack_second(after(master, a_all))
+    d_ff = gather_rows(after(grad_out.astype(bf16), local))
+    sent = pack_second(after(master, a_all, d_ff))
     received.append(lax.all_to_all(sent, PLANE, 0, 0, tiled=True).reshape(8 * half_cap, rows, block))
-    slots, ctx_len, ctx_width = context.shape
-    ctx = after(context.reshape(slots * ctx_len, ctx_width), sent)
-    ctx_x, ctx_y = swap(ctx, "x"), swap(ctx, "y")
 
     def take_rows(kind, blocks, keep_pair):
         here, there = row_owners[2 * kind], row_owners[2 * kind + 1]
@@ -402,9 +401,10 @@
         return target % 4 in (zz, (zz + 2) % 4)
 
     outer = take_rows(0, [after(value, local) for value in outer_blocks], needs_outer)
+    out_rows = take_rows(1, [after(value, local) for value in out_blocks], None)
     half_rows = rows // 2
     odd = z % 2
-    to_pair = lax.dynamic_slice_in_dim(outer, (1 - odd) * half_rows, half_rows, 0)
+    to_pair = lax.dynamic_slice_in_dim(after(outer, sent), (1 - odd) * half_rows, half_rows, 0)
     own_half = lax.dynamic_slice_in_dim(outer, odd * half_rows, half_rows, 0)
     pair_swap = [
         (zz * 8 + place, (zz ^ 1) * 8 + place)
@@ -451,25 +451,21 @@
     w_cross = gather_z(local_cross)
     w_in = gather_z(local_in)
 
-    def first_step(one, over_x, over_y):
+    w_out = gather_z(after(out_rows, local_cross, local_in))
+    slots, ctx_len, ctx_width = context.shape
+    ctx = after(context.reshape(slots * ctx_len, ctx_width), local_cross, local_in, out_rows)
+    ctx_x, ctx_y = swap(ctx, "x"), swap(ctx, "y")
+    h1 = h0 + chain_step(scatter_rows, matmul(after(attended, local_in), w_self_out))
+
+    def second_step(one, own, over_x, over_y):
         half = over_x.shape[0] // 2
-        return scatter_rows(one), swap(over_y[:half], "x"), swap(over_x[half:], "y")
-
-    h1, far_low, far_high = chain_step(
-        first_step, matmul(attended, w_self_out), after(ctx_x, local_in), after(ctx_y, local_in)
-    )
-    h1 = h0 + h1
-
-    def second_step(one, *pieces):
-        four = jnp.concatenate(pieces, axis=0)
+        far_low, far_high = swap(over_y[:half], "x"), swap(over_x[half:], "y")
+        four = jnp.concatenate([own, over_y, over_x, far_low, far_high], axis=0)
         return gather_rows(one), four, swap(four, "c")
 
     b_all, ctx_here, ctx_there = chain_step(
-        second_step, normalize(h1, gains[1]).astype(bf16), ctx, ctx_y, ctx_x, far_low, far_high
-    )
-    out_rows = take_rows(1, [after(value, b_all) for value in out_blocks], None)
-    w_out = gather_z(out_rows)
-    d_ff = gather_rows(after(grad_out.astype(bf16), b_all))
+        second_step, normalize(h1, gains[1]).astype(bf16), ctx, ctx_x, ctx_y
+    )
 
     w_cross_q = w_cross[:, :block]
     w_low = w_cross[:, block : 3 * block]
@@ -597,15 +593,7 @@
     sent = jnp.broadcast_to(by_tile[:, None], (2, 4, 3, rows, block)).reshape(8, 3, rows, block)
     late_grads = lax.all_to_all(sent, PLANE, 0, 0, tiled=True).reshape(8 * 3, rows, block)
     back_swap = [(target, source) for source, target in pair_swap]
-    other_half = lax.ppermute(after(g_outer, out_grads), ALL_AXES, back_swap)
-    outer_grad = jnp.where(
-        odd == 0,
-        jnp.concatenate([g_outer, other_half], axis=0),
-        jnp.concatenate([other_half, g_outer], axis=0),
-    )
-    outer_pair = from_y(outer_grad, lambda zz, place, _: place % 4 in (zz, (zz + 2) % 4))
-    outer_grads = with_core(outer_pair)
-
+    other_half = lax.ppermute(after(g_outer, sent), ALL_AXES, back_swap)
     place = np.arange(8)
     source_x, source_f = (place % 2)[None, :], ((place // 2)[None, :] - my_shift[:, None]) % 4
     slot = np.arange(cap, dtype=np.int32)
@@ -615,20 +603,31 @@
     late = (my_used == 1) & ((my_tile < 4) | (my_tile == 9))
     early_mode = jnp.where(my_used == 0, 1, jnp.where(late, 0, jnp.where(my_row == 1, 3, 2)))
     states = (master, moment_one, moment_two)
-    early = None
-    for first in (0, half_cap):
+
+    def adam_early(first, mode, previous):
         chosen = slice(first, first + half_cap)
-        early = adam_tiles(
+        return adam_tiles(
             *states,
             [early_grads],
             [out_grads],
             slot[chosen],
-            after(early_mode, outer_grad, sent)[chosen] if first else early_mode[chosen],
+            mode[chosen],
             column_place[chosen].reshape(-1),
             row_source[chosen],
             np.zeros(half_cap, np.int32),
-            early,
+            previous,
         )
+
+    early = adam_early(0, early_mode, None)
+    other_half = after(other_half, early[3])
+    outer_grad = jnp.where(
+        odd == 0,
+        jnp.concatenate([g_outer, other_half], axis=0),
+        jnp.concatenate([other_half, g_outer], axis=0),
+    )
+    outer_pair = from_y(outer_grad, lambda zz, place, _: place % 4 in (zz, (zz + 2) % 4))
+    early = adam_early(half_cap, after(early_mode, outer_grad), early)
+    outer_grads = with_core(outer_pair)
 
     n_late = 5
     order = jnp.sum(jnp.where(slot[None, :] < slot[:, None], late.astype(jnp.int32)[None, :], 0), axis=1)
@@ -649,7 +648,7 @@
     mode = jnp.where(hold == 1, 0, jnp.where(some, late_mode, first_mode))
     late_place = ((place % 2)[None, :] * 4 + (place // 2)[None, :]) * 3 + tile[:, None]
     late_place = jnp.where(some, late_place, column_place[:1])
-    new_w, new_m, new_v = adam_tiles(
+    new_w, new_m, new_v, _ = adam_tiles(
         *states,
         [early_grads, late_grads],
         [out_grads, outer_grads],

time: 1090 us -> 1060 us (0.972)
  waiting for transfers between devices: 434 us -> 382 us
  local copies, waits for them, and re-layouts: 148 us -> 159 us
    ppermute x75, waiting for transfers between devices: 355 us -> 306 us  [swap(): return lax.ppermute(value, axis, [(0, 1), (1, 0)])]
    ppermute x2, waiting for transfers between devices: 3.01 us -> 23.8 us  [from_y(): lax.ppermute(value, ALL_AXES, flip_pairs(2, keep_pair))]
    reduce_scatter x5, waiting for transfers between devices: 11.4 us -> 0.06 us  [sum_rows(): value = lax.psum_scatter(value, 'z', scatter_dimension=0, tiled=True)]
    ppermute x1, waiting for transfers between devices: 17.4 us -> 6.2 us  [plane_body(): from_pair = lax.ppermute(to_pair, ALL_AXES, pair_swap)]
    cond x33 -> x35, local copies, waits for them, and re-layouts: 30.9 us -> 33.6 us
    unnamed x177 -> x170, local copies, waits for them, and re-layouts: 31.1 us -> 30.8 us
  transfers between devices with their start and end apart: 97 -> 97, of which waited for: 61 -> 54; matrix products, arithmetic and copies ran while one was open for 35% -> 38% of each run, Pallas kernels for 6% -> 6%
where the time goes in v13:
time: 1060 us; the launch traced here: 1040 us
  waiting for transfers between devices  382 us (36%)
  matrix products  164 us (15%)
  local copies, waits for them, and re-layouts  159 us (15%)
  other arithmetic  103 us (10%)
  starting transfers between devices  102 us (10%)
  Pallas kernels  89.5 us (8%)
  between operations  43.5 us (4%)
    ppermute x75, waiting for transfers between devices, swap(): return lax.ppermute(value, axis, [(0, 1), (1, 0)])  306 us
    pallas_call x3, Pallas kernels, adam_tiles(): pl.pallas_call(kernel, out_shape=(shape, shape, shape, jax.ShapeDtypeStru...  70.3 us
    ppermute x75, starting transfers between devices, swap(): return lax.ppermute(value, axis, [(0, 1), (1, 0)])  63.4 us
    dot_general x10, matrix products, matmul(): return jnp.dot(left, right, preferred_element_type=f32)  51.5 us
    dot_general x8, matrix products, matmul_left(): lax.dot_general(left, right, (((0,), (0,)), ((), ())), preferred_element_...  51 us
    dot_general x6, matrix products, matmul_right(): lax.dot_general(left, right, (((1,), (1,)), ((), ())), preferred_element_...  39.1 us
    cond x35, local copies, waits for them, and re-layouts  33.6 us
    unnamed x170, local copies, waits for them, and re-layouts  30.8 us
  transfers between devices with their start and end apart: 97, of which 54 were waited for; matrix products, arithmetic and copies ran while one was open for 38% of the time, Pallas kernels for 6%

profile of v13, /device:TPU:0, one launch (start us, length us, event | category | flops | bytes accessed | tf_op | source)
XLA Modules:
  0.0 1044.6 jit_solution(10727763260500891377)
XLA Ops:
  186.0 11.4 %all-to-all-done.1 = bf16[8,3,256,256]{3,2,1,0:T(8,128)(2,1)} async-done(((bf16[8,3,256,256]{3,2,1,0:T(8,128)(2,1)}), bf16[8,3,256,256]{3,2,1,0:T(8,128)(2,1)}, u32[]{:S(2)}, u32[]{:S(2)}) %all-to-all-start.1) | async-done | bytes 3145760 | tf_op jit(solution)/shard_map/all_to_all | solution.py:389
  219.1 20.6 %collective-permute-done.77 = bf16[256,2048]{1,0:T(8,128)(2,1)S(1)} collective-permute-done((bf16[256,2048]{1,0:T(8,128)(2,1)S(1)}, bf16[256,2048]{1,0:T(8,128)(2,1)S(1)}, u32[]{:S(2)}, u32[]{:S(2)}) %collective-permute-start.77) | collective-permute-done | bytes 1048608 | tf_op jit(solution)/shard_map/ppermute | solution.py:397
  252.3 57.4 %conditional.12 = (f32[128,2048]{1,0:T(8,128)S(1)}) conditional(s32[]{:T(128)} %bitcast.69, () %tuple.115, f32[1024,2048]{1,0:T(8,128)} %fusion.134), branch_computations={%region_12.13_spmd, %region_13.14_spmd} | conditional | flops 2883584 | bytes 65536208 | solution.py:354
  266.4 35.5 %collective-permute-done.30 = bf16[2,128,1024]{2,1,0:T(8,128)(2,1)S(1)} collective-permute-done((bf16[2,128,1024]{2,1,0:T(8,128)(2,1)S(1)}, bf16[2,128,1024]{2,1,0:T(8,128)(2,1)S(1)}, u32[]{:S(2)}, u32[]{:S(2)}) %collective-permute-start.30) | collective-permute-done | bytes 524320 | tf_op jit(solution)/shard_map/cond/branch_1_fun/ppermute | solution.py:242
  314.2 57.2 %conditional.13 = (bf16[1024,2048]{1,0:T(8,128)(2,1)}, bf16[1024,4096]{1,0:T(8,128)(2,1)}, bf16[1024,4096]{1,0:T(8,128)(2,1)}) conditional(s32[]{:T(128)} %bitcast.69, () %tuple.131, (bf16[128,2048]{1,0:T(8,128)(2,1)S(1)}, bf16[256,4096]{1,0:T(8,128)(2,1)}, bf16[256,4096]{1,0:T(8,128)(2,1)}, bf16[256,4096]{1,0:T(8,128)(2,1)}) %tuple.137), branch_computations={%region_15.16_spmd, %region_16.17_spmd} | conditional | bytes 89129304 | solution.py:354
  344.1 10.9 %collective-permute-done.3 = bf16[128,2048]{1,0:T(8,128)(2,1)S(1)} collective-permute-done((bf16[128,2048]{1,0:T(8,128)(2,1)S(1)}, bf16[128,2048]{1,0:T(8,128)(2,1)S(1)}, u32[]{:S(2)}, u32[]{:S(2)}) %collective-permute-start.3) | collective-permute-done | bytes 524320 | tf_op jit(solution)/shard_map/cond/branch_1_fun/ppermute | solution.py:242
  407.4 40.0 %conditional.14 = (f32[128,2048]{1,0:T(8,128)S(1)}, bf16[2048,4096]{1,0:T(8,128)(2,1)}) conditional(s32[]{:T(128)} %bitcast.69, () %tuple.130, (f32[1024,2048]{1,0:T(8,128)S(1)}, bf16[1024,4096]{1,0:T(8,128)(2,1)}, bf16[1024,4096]{1,0:T(8,128)(2,1)}) %tuple.138), branch_computations={%region_19.20_spmd, %region_20.21_spmd} | conditional | flops 36438016 | bytes 99090648 | solution.py:354
  419.0 11.8 %collective-permute-done.35 = bf16[2,128,1024]{2,1,0:T(8,128)(2,1)S(1)} collective-permute-done((bf16[2,128,1024]{2,1,0:T(8,128)(2,1)S(1)}, bf16[2,128,1024]{2,1,0:T(8,128)(2,1)S(1)}, u32[]{:S(2)}, u32[]{:S(2)}) %collective-permute-start.35) | collective-permute-done | bytes 524320 | tf_op jit(solution)/shard_map/cond/branch_1_fun/ppermute | solution.py:242
  433.5 13.7 %pad_maximum_fusion.1 = bf16[2048,4096]{1,0:T(8,128)(2,1)} fusion(bf16[1024,4096]{1,0:T(8,128)(2,1)} %get-tuple-element.76, bf16[1024,4096]{1,0:T(8,128)(2,1)} %get-tuple-element.75), kind=kLoop, calls=%fused_computation.35 | loop fusion | flops 33554432 | bytes 33554432 | tf_op jit(solution)/shard_map/cond/branch_1_fun/concatenate | solution.py:489
  449.9 26.6 %conditional.15 = (bf16[1024,2048]{1,0:T(8,128)(2,1)}) conditional(s32[]{:T(128)} %bitcast.69, () %tuple.140, bf16[128,2048]{1,0:T(8,128)(2,1)S(1)} %get-tuple-element.264), branch_computations={%region_22.23_spmd, %region_23.24_spmd} | conditional | bytes 26214608 | solution.py:354
  495.0 11.1 %fusion.55 = bf16[1024,1024]{1,0:T(8,128)(2,1)S(1)} fusion(f32[1024,1024]{1,0:T(8,128)} %copy-done.82, bf16[1024,2048]{1,0:T(8,128)(2,1)} %constant_dynamic-update-slice_fusion.65, bf16[1024,2048]{1,0:T(8,128)(2,1)} %all-gather.14.cloned.1.call-done), kind=kOutput, calls=%fused_computation.191 | convolution fusion | flops 4320133120 | bytes 14680064 | tf_op jit(solution)/shard_map/dot_general | solution.py:48
  530.3 52.7 %conditional.16 = (f32[128,2048]{1,0:T(8,128)S(1)}, f32[128,2048]{1,0:T(8,128)S(1)}) conditional(s32[]{:T(128)} %bitcast.69, () %tuple.139, (f32[1024,2048]{1,0:T(8,128)S(1)}, f32[1024,2048]{1,0:T(8,128)}) %tuple.143), branch_computations={%region_24.25_spmd, %region_25.26_spmd} | conditional | flops 5767168 | bytes 131072416 | solution.py:354
  586.0 27.1 %conditional.17 = (bf16[1024,2048]{1,0:T(8,128)(2,1)}) conditional(s32[]{:T(128)} %bitcast.69, () %tuple.146, bf16[128,2048]{1,0:T(8,128)(2,1)} %get-tuple-element.179), branch_computations={%region_27.28_spmd, %region_28.29_spmd} | conditional | bytes 26214608 | solution.py:354
  613.1 29.8 %conditional.18 = (bf16[1024,256]{0,1:T(8,128)(2,1)}, bf16[2048,256]{0,1:T(8,128)(2,1)}, bf16[2048,256]{0,1:T(8,128)(2,1)}, bf16[2,256,2048]{2,1,0:T(8,128)(2,1)}) conditional(s32[]{:T(128)} %bitcast.69, () %tuple.145, (bf16[1024,2048]{1,0:T(8,128)(2,1)}, bf16[256,2048]{1,0:T(8,128)(2,1)}, bf16[8,256,2,128]{3,2,1,0:T(2,128)(2,1)}, ...), branch_computations={%region_30.31_spmd, %region_31.33_spmd} | conditional | flops 1616640000 | bytes 66601200 | solution.py:354
  680.6 36.4 %conditional.19 = (f32[128,2048]{1,0:T(8,128)}) conditional(s32[]{:T(128)} %bitcast.69, () %tuple.144, f32[1024,2048]{1,0:T(8,128)} %fusion.119), branch_computations={%region_33.34_spmd, %region_34.35_spmd} | conditional | flops 2883584 | bytes 65536208 | solution.py:354
  695.0 11.9 %collective-permute-done.50 = bf16[2,128,1024]{2,1,0:T(8,128)(2,1)S(1)} collective-permute-done((bf16[2,128,1024]{2,1,0:T(8,128)(2,1)S(1)}, bf16[2,128,1024]{2,1,0:T(8,128)(2,1)S(1)}, u32[]{:S(2)}, u32[]{:S(2)}) %collective-permute-start.50) | collective-permute-done | bytes 524320 | tf_op jit(solution)/shard_map/cond/branch_1_fun/ppermute | solution.py:242
  721.8 26.6 %conditional.20 = (bf16[1024,2048]{1,0:T(8,128)(2,1)}) conditional(s32[]{:T(128)} %bitcast.69, () %tuple.150, bf16[128,2048]{1,0:T(8,128)(2,1)} %get-tuple-element.184), branch_computations={%region_37.38_spmd, %region_38.39_spmd} | conditional | bytes 26214608 | solution.py:354
  798.3 105.7 %conditional.21 = (f32[128,2048]{1,0:T(8,128)}, f32[3,2048]{1,0:T(4,128)S(1)}, bf16[4,256,2048]{2,1,0:T(8,128)(2,1)}) conditional(s32[]{:T(128)} %bitcast.69, () %tuple.149, (f32[1024,2048]{1,0:T(8,128)S(1)}, f32[3,2048]{1,0:T(4,128)S(1)}, f32[128,2048]{1,0:T(8,128)S(1)}, f32[128,2048]{1,0:T(8,128)S(1)}, f32[128,2048]{1,0:T(8,128)S(1)}, ...), branch_computations={%region_45.46_spmd, %region_46.50_spmd} | conditional | flops 9767680 | bytes 91698648 | solution.py:354
  814.7 59.2 %collective-permute-done.55 = bf16[2,128,1024]{2,1,0:T(8,128)(2,1)S(1)} collective-permute-done((bf16[2,128,1024]{2,1,0:T(8,128)(2,1)S(1)}, bf16[2,128,1024]{2,1,0:T(8,128)(2,1)S(1)}, u32[]{:S(2)}, u32[]{:S(2)}) %collective-permute-start.55) | collective-permute-done | bytes 524320 | tf_op jit(solution)/shard_map/cond/branch_1_fun/ppermute | solution.py:242
  909.6 10.0 collective-permute-done.80
  932.9 23.8 %collective-permute-done.81 = bf16[256,2048]{1,0:T(8,128)(2,1)} collective-permute-done((bf16[256,2048]{1,0:T(8,128)(2,1)}, bf16[256,2048]{1,0:T(8,128)(2,1)}, u32[]{:S(2)}, u32[]{:S(2)}) %collective-permute-start.81) | collective-permute-done | bytes 1048608 | tf_op jit(solution)/shard_map/ppermute | solution.py:507
  963.4 24.3 %adam_tiles.3 = (f32[6,256,2048]{2,1,0:T(8,128)}, f32[6,256,2048]{2,1,0:T(8,128)}, f32[6,256,2048]{2,1,0:T(8,128)}, f32[8,128]{1,0:T(8,128)}) custom-call(s32[3]{0:T(128)S(1)} %call_exported.2.visit_ref, s32[3]{0:T(128)S(1)} %bitcast.367, s32[24]{0:T(128)S(1)} %reshape.491.cp_ref, s32[3]{0:T(128)S(1)} %get-tuple-element.375.rp_ref, ...), custom_call_target="tpu_custom_call" | custom-call | flops 47185920 | bytes 40894464 | tf_op jit(solution)/shard_map/adam_tiles/pallas_call | solution.py:212
  987.7 24.2 %adam_tiles.4 = (f32[6,256,2048]{2,1,0:T(8,128)}, f32[6,256,2048]{2,1,0:T(8,128)}, f32[6,256,2048]{2,1,0:T(8,128)}, f32[8,128]{1,0:T(8,128)}) custom-call(s32[3]{0:T(128)S(1)} %copy-done.7, s32[3]{0:T(128)S(1)} %slice.565.mode_ref, s32[24]{0:T(128)S(1)} %reshape.490.cp_ref, ...), custom_call_target="tpu_custom_call", output_to_operand_aliasing={{0}: (10, {}), {1}: (11, {}), {2}: (12, {})} | custom-call | flops 47185920 | bytes 40894464 | tf_op jit(solution)/shard_map/adam_tiles/pallas_call | solution.py:212
  1015.5 21.8 %adam_tiles.5 = (f32[6,256,2048]{2,1,0:T(8,128)}, f32[6,256,2048]{2,1,0:T(8,128)}, f32[6,256,2048]{2,1,0:T(8,128)}, f32[8,128]{1,0:T(8,128)}) custom-call(s32[5]{0:T(128)S(1)} %get-tuple-element.405.visit_ref, s32[5]{0:T(128)S(1)} %get-tuple-element.404.mode_ref, ...), custom_call_target="tpu_custom_call", output_to_operand_aliasing={{0}: (12, {}), {1}: (13, {}), {2}: (14, {})} | custom-call | flops 78643200 | bytes 68157440 | tf_op jit(solution)/shard_map/adam_tiles/pallas_call | solution.py:212
  (695 shorter events, 718.6 us)
Async XLA Ops:
  24.8 49.1 %all-to-all-start = ((bf16[8,3,256,256]{3,2,1,0:T(8,128)(2,1)}), bf16[8,3,256,256]{3,2,1,0:T(8,128)(2,1)S(1)}, u32[]{:S(2)}, u32[]{:S(2)}) async-start(bf16[8,3,256,256]{3,2,1,0:T(8,128)(2,1)} %copy-done), calls=%async_computation | async-start | bytes 6291456 | tf_op jit(solution)/shard_map/all_to_all | solution.py:361
  30.1 131.3 %all-gather.6.cloned.1.call-start = ((), (), s32[]{:S(2)}) async-start(), calls=%async_computation.9 | async-start | bytes 3932160 | tf_op jit(solution)/shard_map/all_gather | solution.py:382
  79.8 166.3 %all-gather.8.cloned.1.call-start = ((), (), s32[]{:S(2)}) async-start(), calls=%async_computation.10 | async-start | bytes 2621440 | tf_op jit(solution)/shard_map/all_gather | solution.py:417
  83.0 37.9 %collective-permute-start.73 = (bf16[2,256,2048]{2,1,0:T(8,128)(2,1)}, bf16[2,256,2048]{2,1,0:T(8,128)(2,1)}, u32[]{:S(2)}, u32[]{:S(2)}) collective-permute-start(bf16[2,256,2048]{2,1,0:T(8,128)(2,1)} %pad_maximum_fusion.12), channel_id=1, source_target_pairs={{0,1},{1,0},{2,3},{3,2},{4,5},{5,4},{6,7},{7,6},{8,9},{9,8},{10,11... | collective-permute-start | bytes 6291464 | tf_op jit(solution)/shard_map/ppermute | solution.py:242
  155.9 41.4 %all-to-all-start.1 = ((bf16[8,3,256,256]{3,2,1,0:T(8,128)(2,1)}), bf16[8,3,256,256]{3,2,1,0:T(8,128)(2,1)}, u32[]{:S(2)}, u32[]{:S(2)}) async-start(bf16[8,3,256,256]{3,2,1,0:T(8,128)(2,1)} %copy-done.1), calls=%async_computation.1 | async-start | bytes 6291456 | tf_op jit(solution)/shard_map/all_to_all | solution.py:389
  160.4 211.0 %all-gather.10.cloned.1.call-start = ((), (), s32[]{:S(2)}) async-start(), calls=%async_computation.11 | async-start | bytes 6553600 | tf_op jit(solution)/shard_map/all_gather | solution.py:382
  200.5 276.0 %all-gather.12.cloned.1.call-start = ((), (), s32[]{:S(2)}) async-start(), calls=%async_computation.12 | async-start | bytes 5242880 | tf_op jit(solution)/shard_map/all_gather | solution.py:382
  204.8 290.2 %all-gather.14.cloned.1.call-start = ((), (), s32[]{:S(2)}) async-start(), calls=%async_computation.13 | async-start | bytes 5242880 | tf_op jit(solution)/shard_map/all_gather | solution.py:382
  242.1 72.1 %collective-permute-start.78 = (bf16[256,4096]{1,0:T(8,128)(2,1)}, bf16[256,4096]{1,0:T(8,128)(2,1)}, u32[]{:S(2)}, u32[]{:S(2)}) collective-permute-start(bf16[256,4096]{1,0:T(8,128)(2,1)} %bitcast.101), channel_id=1, source_target_pairs={{0,2},{2,0},{1,3},{3,1},{4,6},{6,4},{5,7},{7,5},{8,10},{10,8},{9,1... | collective-permute-start | bytes 6291464 | tf_op jit(solution)/shard_map/ppermute | solution.py:242
  243.8 70.4 %collective-permute-start.79 = (bf16[256,4096]{1,0:T(8,128)(2,1)}, bf16[256,4096]{1,0:T(8,128)(2,1)}, u32[]{:S(2)}, u32[]{:S(2)}) collective-permute-start(bf16[256,4096]{1,0:T(8,128)(2,1)} %bitcast.101), channel_id=1, source_target_pairs={{0,4},{4,0},{1,5},{5,1},{2,6},{6,2},{3,7},{7,3},{8,12},{12,8},{9,1... | collective-permute-start | bytes 6291464 | tf_op jit(solution)/shard_map/ppermute | solution.py:242
  246.0 367.1 %reduce-scatter.6.cloned.1.call-start = ((), (), s32[]{:S(2)}) async-start(), calls=%async_computation.14 | async-start | bytes 5242880 | tf_op jit(solution)/shard_map/reduce_scatter | solution.py:503
  264.5 37.4 %collective-permute-start.30 = (bf16[2,128,1024]{2,1,0:T(8,128)(2,1)S(1)}, bf16[2,128,1024]{2,1,0:T(8,128)(2,1)S(1)}, u32[]{:S(2)}, u32[]{:S(2)}) collective-permute-start(bf16[2,128,1024]{2,1,0:T(8,128)(2,1)S(1)} %slice_bitcast_fusion.3), channel_id=1, source_target_pairs={{0,4},{4,0},{1,5},{5,1},{2,6},{6,2},{3,7},{7,3},{8,12},{12,8},{9,1... | collective-permute-start | bytes 1572872 | tf_op jit(solution)/shard_map/cond/branch_1_fun/ppermute | solution.py:242
  266.1 36.7 %collective-permute-start.28 = (bf16[2,128,1024]{2,1,0:T(8,128)(2,1)S(1)}, bf16[2,128,1024]{2,1,0:T(8,128)(2,1)S(1)}, u32[]{:S(2)}, u32[]{:S(2)}) collective-permute-start(bf16[2,128,1024]{2,1,0:T(8,128)(2,1)S(1)} %slice_bitcast_fusion.5), channel_id=1, source_target_pairs={{0,2},{2,0},{1,3},{3,1},{4,6},{6,4},{5,7},{7,5},{8,10},{10,8},{9,1... | collective-permute-start | bytes 1572872 | tf_op jit(solution)/shard_map/cond/branch_1_fun/ppermute | solution.py:242
  494.7 227.0 %reduce-scatter.8.cloned.1.call-start = ((), (), s32[]{:S(2)}) async-start(), calls=%async_computation.15 | async-start | bytes 5242880 | tf_op jit(solution)/shard_map/reduce_scatter | solution.py:503
  515.9 263.8 %reduce-scatter.10.cloned.1.call-start = ((), (), s32[]{:S(2)}) async-start(), calls=%async_computation.16 | async-start | bytes 6553600 | tf_op jit(solution)/shard_map/reduce_scatter | solution.py:503
  669.1 234.9 %reduce-scatter.12.cloned.1.call-start = ((), (), s32[]{:S(2)}) async-start(), calls=%async_computation.17 | async-start | bytes 3932160 | tf_op jit(solution)/shard_map/reduce_scatter | solution.py:503
  779.6 126.6 %reduce-scatter.14.cloned.1.call-start = ((), (), s32[]{:S(2)}) async-start(), calls=%async_computation.18 | async-start | bytes 2621440 | tf_op jit(solution)/shard_map/reduce_scatter | solution.py:503
  787.0 139.9 %all-to-all-start.2 = ((bf16[8,6,256,256]{3,2,1,0:T(8,128)(2,1)}), bf16[8,6,256,256]{3,2,1,0:T(8,128)(2,1)}, u32[]{:S(2)}, u32[]{:S(2)}) async-start(bf16[8,6,256,256]{3,2,1,0:T(8,128)(2,1)} %pack_gradients.1), calls=%async_computation.5 | async-start | bytes 12582912 | tf_op jit(solution)/shard_map/all_to_all | solution.py:580
  800.0 89.9 %collective-permute-start.62 = (bf16[2,256,2048]{2,1,0:T(8,128)(2,1)}, bf16[2,256,2048]{2,1,0:T(8,128)(2,1)S(1)}, u32[]{:S(2)}, u32[]{:S(2)}) collective-permute-start(bf16[2,256,2048]{2,1,0:T(8,128)(2,1)} %get-tuple-element.92), channel_id=1, source_target_pairs={{0,1},{1,0},{2,3},{3,2},{4,5},{5,4},{6,7},{7,6},{8,9},{9,8},{10,11... | collective-permute-start | bytes 6291464 | tf_op jit(solution)/shard_map/cond/branch_1_fun/ppermute | solution.py:242
  810.6 63.2 %collective-permute-start.55 = (bf16[2,128,1024]{2,1,0:T(8,128)(2,1)S(1)}, bf16[2,128,1024]{2,1,0:T(8,128)(2,1)S(1)}, u32[]{:S(2)}, u32[]{:S(2)}) collective-permute-start(bf16[2,128,1024]{2,1,0:T(8,128)(2,1)S(1)} %slice_bitcast_fusion.33), channel_id=1, source_target_pairs={{0,4},{4,0},{1,5},{5,1},{2,6},{6,2},{3,7},{7,3},{8,12},{12,8},{9,1... | collective-permute-start | bytes 1572872 | tf_op jit(solution)/shard_map/cond/branch_1_fun/ppermute | solution.py:242
  813.1 62.4 %collective-permute-start.53 = (bf16[2,128,1024]{2,1,0:T(8,128)(2,1)S(1)}, bf16[2,128,1024]{2,1,0:T(8,128)(2,1)S(1)}, u32[]{:S(2)}, u32[]{:S(2)}) collective-permute-start(bf16[2,128,1024]{2,1,0:T(8,128)(2,1)S(1)} %slice_bitcast_fusion.35), channel_id=1, source_target_pairs={{0,2},{2,0},{1,3},{3,1},{4,6},{6,4},{5,7},{7,5},{8,10},{10,8},{9,1... | collective-permute-start | bytes 1572872 | tf_op jit(solution)/shard_map/cond/branch_1_fun/ppermute | solution.py:242
  920.8 35.9 %collective-permute-start.81 = (bf16[256,2048]{1,0:T(8,128)(2,1)}, bf16[256,2048]{1,0:T(8,128)(2,1)}, u32[]{:S(2)}, u32[]{:S(2)}) collective-permute-start(bf16[256,2048]{1,0:T(8,128)(2,1)} %maximum_select_fusion.1), channel_id=1, source_target_pairs={{0,2},{2,0},{4,6},{6,4},{9,11},{11,9},{13,15},{15,13},{16,18},{18,... | collective-permute-start | bytes 3145736 | tf_op jit(solution)/shard_map/ppermute | solution.py:507
  926.9 88.6 %all-to-all-start.3 = ((bf16[8,3,256,256]{3,2,1,0:T(8,128)(2,1)}), bf16[8,3,256,256]{3,2,1,0:T(8,128)(2,1)S(1)}, u32[]{:S(2)}, u32[]{:S(2)}) async-start(bf16[8,3,256,256]{3,2,1,0:T(8,128)(2,1)} %bitcast.374), calls=%async_computation.7 | async-start | bytes 6291456 | tf_op jit(solution)/shard_map/all_to_all | solution.py:594
  959.5 52.5 %collective-permute-start.82 = (bf16[2,256,2048]{2,1,0:T(8,128)(2,1)}, bf16[2,256,2048]{2,1,0:T(8,128)(2,1)}, u32[]{:S(2)}, u32[]{:S(2)}) collective-permute-start(bf16[2,256,2048]{2,1,0:T(8,128)(2,1)} %pad_maximum_fusion.15), channel_id=1, source_target_pairs={{0,1},{1,0},{2,3},{3,2},{4,5},{5,4},{6,7},{7,6},{8,9},{9,8},{10,11... | collective-permute-start | bytes 6291464 | tf_op jit(solution)/shard_map/ppermute | solution.py:242
  (158 other events, 2327.3 us)
Sparse Core Ops, SparseCore 0:
  79.9 63.7 all-gather.5
  156.0 47.5 all-gather.7
  205.2 96.8 all-gather.9
  303.5 79.1 all-gather.11
  384.0 79.2 all-gather.13
  494.8 77.8 reduce-scatter.5
  575.1 77.2 reduce-scatter.7
  669.2 94.7 reduce-scatter.9
  779.7 61.5 reduce-scatter.11
  843.5 43.8 reduce-scatter.13

commit v14 on v13

--- a/solution.py
+++ b/solution.py
@@ -166,13 +166,12 @@
     width = columns // 8
     n_visit = visit.shape[0]
     n_col, n_row = len(columns_from), len(rows_from)
-    kept = () if previous is None else tuple(previous[:3])
+    kept = () if previous is None else tuple(previous)
 
     def kernel(visit_ref, mode_ref, cp_ref, rp_ref, hold_ref, *refs):
         w_ref, m_ref, v_ref = refs[:3]
         grads = refs[3 : 3 + n_col + n_row]
-        outs = refs[3 + n_col + n_row + len(kept) : -1]
-        refs[-1][...] = jnp.zeros_like(refs[-1])
+        outs = refs[3 + n_col + n_row + len(kept) :]
         how = mode_ref[pl.program_id(0)]
 
         @pl.when(how == 1)
@@ -211,7 +210,7 @@
     n_before = 5 + 3 + n_col + n_row
     return pl.pallas_call(
         kernel,
-        out_shape=(shape, shape, shape, jax.ShapeDtypeStruct((8, 128), f32)),
+        out_shape=(shape, shape, shape),
         grid_spec=pltpu.PrefetchScalarGridSpec(
             num_scalar_prefetch=5,
             grid=(n_visit, 8),
@@ -223,7 +222,7 @@
                 *(row_spec(n_col + number) for number in range(n_row)),
                 *(pl.BlockSpec(memory_space=pl.ANY) for _ in kept),
             ],
-            out_specs=(state, state, state, pl.BlockSpec((8, 128), lambda *_: (0, 0))),
+            out_specs=(state, state, state),
         ),
         input_output_aliases={n_before + n: n for n in range(len(kept))},
         compiler_params=pltpu.CompilerParams(vmem_limit_bytes=VMEM_LIMIT),
@@ -593,7 +592,6 @@
     sent = jnp.broadcast_to(by_tile[:, None], (2, 4, 3, rows, block)).reshape(8, 3, rows, block)
     late_grads = lax.all_to_all(sent, PLANE, 0, 0, tiled=True).reshape(8 * 3, rows, block)
     back_swap = [(target, source) for source, target in pair_swap]
-    other_half = lax.ppermute(after(g_outer, sent), ALL_AXES, back_swap)
     place = np.arange(8)
     source_x, source_f = (place % 2)[None, :], ((place // 2)[None, :] - my_shift[:, None]) % 4
     slot = np.arange(cap, dtype=np.int32)
@@ -604,30 +602,27 @@
     early_mode = jnp.where(my_used == 0, 1, jnp.where(late, 0, jnp.where(my_row == 1, 3, 2)))
     states = (master, moment_one, moment_two)
 
-    def adam_early(first, mode, previous):
-        chosen = slice(first, first + half_cap)
-        return adam_tiles(
-            *states,
-            [early_grads],
-            [out_grads],
-            slot[chosen],
-            mode[chosen],
-            column_place[chosen].reshape(-1),
-            row_source[chosen],
-            np.zeros(half_cap, np.int32),
-            previous,
-        )
-
-    early = adam_early(0, early_mode, None)
-    other_half = after(other_half, early[3])
-    outer_grad = jnp.where(
-        odd == 0,
-        jnp.concatenate([g_outer, other_half], axis=0),
-        jnp.concatenate([other_half, g_outer], axis=0),
-    )
-    outer_pair = from_y(outer_grad, lambda zz, place, _: place % 4 in (zz, (zz + 2) % 4))
-    early = adam_early(half_cap, after(early_mode, outer_grad), early)
-    outer_grads = with_core(outer_pair)
+    def early_step(early_grads, out_grads, half):
+        other_half = lax.ppermute(half, ALL_AXES, back_swap)
+        in_order = jnp.where(odd == 0, jnp.stack([half, other_half]), jnp.stack([other_half, half]))
+        outer_pair = from_y(in_order.reshape(rows, width), lambda zz, place, _: place % 4 in (zz, (zz + 2) % 4))
+        early = None
+        for first in (0, half_cap):
+            chosen = slice(first, first + half_cap)
+            early = adam_tiles(
+                *states,
+                [early_grads],
+                [out_grads],
+                slot[chosen],
+                early_mode[chosen],
+                column_place[chosen].reshape(-1),
+                row_source[chosen],
+                np.zeros(half_cap, np.int32),
+                early,
+            )
+        return *early, with_core(outer_pair)
+
+    *early, outer_grads = chain_step(early_step, early_grads, out_grads, g_outer)
 
     n_late = 5
     order = jnp.sum(jnp.where(slot[None, :] < slot[:, None], late.astype(jnp.int32)[None, :], 0), axis=1)
@@ -648,7 +643,7 @@
     mode = jnp.where(hold == 1, 0, jnp.where(some, late_mode, first_mode))
     late_place = ((place % 2)[None, :] * 4 + (place // 2)[None, :]) * 3 + tile[:, None]
     late_place = jnp.where(some, late_place, column_place[:1])
-    new_w, new_m, new_v, _ = adam_tiles(
+    new_w, new_m, new_v = adam_tiles(
         *states,
         [early_grads, late_grads],
         [out_grads, outer_grads],

time: 1060 us -> 1050 us (level)
    unnamed x170 -> x156, local copies, waits for them, and re-layouts: 30.8 us -> 30.7 us
    cond x35 -> x47, local copies, waits for them, and re-layouts: 33.6 us -> 33.6 us
  transfers between devices with their start and end apart: 97 -> 97, of which waited for: 54 -> 53; matrix products, arithmetic and copies ran while one was open for 38% -> 38% of each run, Pallas kernels for 6% -> 6%
where the time goes in v14:
time: 1050 us; the launch traced here: 1040 us
  waiting for transfers between devices  382 us (36%)
  matrix products  164 us (16%)
  local copies, waits for them, and re-layouts  158 us (15%)
  starting transfers between devices  102 us (10%)
  other arithmetic  101 us (10%)
  Pallas kernels  90 us (9%)
  between operations  43.3 us (4%)
    ppermute x75, waiting for transfers between devices, swap(): return lax.ppermute(value, axis, [(0, 1), (1, 0)])  305 us
    pallas_call x3, Pallas kernels, adam_tiles(): pl.pallas_call(kernel, out_shape=(shape, shape, shape), grid_spec=pltpu.P...  68.3 us
    ppermute x75, starting transfers between devices, swap(): return lax.ppermute(value, axis, [(0, 1), (1, 0)])  63 us
    dot_general x10, matrix products, matmul(): return jnp.dot(left, right, preferred_element_type=f32)  52 us
    dot_general x8, matrix products, matmul_left(): lax.dot_general(left, right, (((0,), (0,)), ((), ())), preferred_element_...  50.9 us
    dot_general x6, matrix products, matmul_right(): lax.dot_general(left, right, (((1,), (1,)), ((), ())), preferred_element_...  39.1 us
    cond x47, local copies, waits for them, and re-layouts  33.6 us
    unnamed x156, local copies, waits for them, and re-layouts  30.7 us
  transfers between devices with their start and end apart: 97, of which 53 were waited for; matrix products, arithmetic and copies ran while one was open for 38% of the time, Pallas kernels for 6%

profile of v14, /device:TPU:0, one launch (start us, length us, event | category | flops | bytes accessed | tf_op | source)
XLA Modules:
  0.0 1042.4 jit_solution(17044000753500936799)
XLA Ops:
  186.1 11.3 %all-to-all-done.1 = bf16[8,3,256,256]{3,2,1,0:T(8,128)(2,1)} async-done(((bf16[8,3,256,256]{3,2,1,0:T(8,128)(2,1)}), bf16[8,3,256,256]{3,2,1,0:T(8,128)(2,1)}, u32[]{:S(2)}, u32[]{:S(2)}) %all-to-all-start.1) | async-done | bytes 3145760 | tf_op jit(solution)/shard_map/all_to_all | solution.py:388
  220.1 21.5 %collective-permute-done.80 = bf16[256,2048]{1,0:T(8,128)(2,1)S(1)} collective-permute-done((bf16[256,2048]{1,0:T(8,128)(2,1)S(1)}, bf16[256,2048]{1,0:T(8,128)(2,1)S(1)}, u32[]{:S(2)}, u32[]{:S(2)}) %collective-permute-start.80) | collective-permute-done | bytes 1048608 | tf_op jit(solution)/shard_map/ppermute | solution.py:396
  254.0 57.2 %conditional.13 = (f32[128,2048]{1,0:T(8,128)S(1)}) conditional(s32[]{:T(128)} %bitcast.74, () %tuple.120, f32[1024,2048]{1,0:T(8,128)} %fusion.134), branch_computations={%region_12.13_spmd, %region_13.14_spmd} | conditional | flops 2883584 | bytes 65536208 | solution.py:353
  268.3 35.2 %collective-permute-done.33 = bf16[2,128,1024]{2,1,0:T(8,128)(2,1)S(1)} collective-permute-done((bf16[2,128,1024]{2,1,0:T(8,128)(2,1)S(1)}, bf16[2,128,1024]{2,1,0:T(8,128)(2,1)S(1)}, u32[]{:S(2)}, u32[]{:S(2)}) %collective-permute-start.33) | collective-permute-done | bytes 524320 | tf_op jit(solution)/shard_map/cond/branch_1_fun/ppermute | solution.py:241
  315.5 57.3 %conditional.14 = (bf16[1024,2048]{1,0:T(8,128)(2,1)}, bf16[1024,4096]{1,0:T(8,128)(2,1)}, bf16[1024,4096]{1,0:T(8,128)(2,1)}) conditional(s32[]{:T(128)} %bitcast.74, () %tuple.136, (bf16[128,2048]{1,0:T(8,128)(2,1)S(1)}, bf16[256,4096]{1,0:T(8,128)(2,1)}, bf16[256,4096]{1,0:T(8,128)(2,1)}, bf16[256,4096]{1,0:T(8,128)(2,1)}) %tuple.142), branch_computations={%region_15.16_spmd, %region_16.17_spmd} | conditional | bytes 89129304 | solution.py:353
  345.9 11.5 %collective-permute-done.3 = bf16[128,2048]{1,0:T(8,128)(2,1)S(1)} collective-permute-done((bf16[128,2048]{1,0:T(8,128)(2,1)S(1)}, bf16[128,2048]{1,0:T(8,128)(2,1)S(1)}, u32[]{:S(2)}, u32[]{:S(2)}) %collective-permute-start.3) | collective-permute-done | bytes 524320 | tf_op jit(solution)/shard_map/cond/branch_1_fun/ppermute | solution.py:241
  409.2 39.8 %conditional.15 = (f32[128,2048]{1,0:T(8,128)S(1)}, bf16[2048,4096]{1,0:T(8,128)(2,1)}) conditional(s32[]{:T(128)} %bitcast.74, () %tuple.135, (f32[1024,2048]{1,0:T(8,128)S(1)}, bf16[1024,4096]{1,0:T(8,128)(2,1)}, bf16[1024,4096]{1,0:T(8,128)(2,1)}) %tuple.143), branch_computations={%region_19.20_spmd, %region_20.21_spmd} | conditional | flops 36438016 | bytes 99090648 | solution.py:353
  420.6 12.3 %collective-permute-done.38 = bf16[2,128,1024]{2,1,0:T(8,128)(2,1)S(1)} collective-permute-done((bf16[2,128,1024]{2,1,0:T(8,128)(2,1)S(1)}, bf16[2,128,1024]{2,1,0:T(8,128)(2,1)S(1)}, u32[]{:S(2)}, u32[]{:S(2)}) %collective-permute-start.38) | collective-permute-done | bytes 524320 | tf_op jit(solution)/shard_map/cond/branch_1_fun/ppermute | solution.py:241
  435.1 13.7 %pad_maximum_fusion.1 = bf16[2048,4096]{1,0:T(8,128)(2,1)} fusion(bf16[1024,4096]{1,0:T(8,128)(2,1)} %get-tuple-element.104, bf16[1024,4096]{1,0:T(8,128)(2,1)} %get-tuple-element.103), kind=kLoop, calls=%fused_computation.35 | loop fusion | flops 33554432 | bytes 33554432 | tf_op jit(solution)/shard_map/cond/branch_1_fun/concatenate | solution.py:488
  451.5 26.8 %conditional.16 = (bf16[1024,2048]{1,0:T(8,128)(2,1)}) conditional(s32[]{:T(128)} %bitcast.74, () %tuple.145, bf16[128,2048]{1,0:T(8,128)(2,1)S(1)} %get-tuple-element.311), branch_computations={%region_22.23_spmd, %region_23.24_spmd} | conditional | bytes 26214608 | solution.py:353
  496.8 11.1 %fusion.55 = bf16[1024,1024]{1,0:T(8,128)(2,1)S(1)} fusion(f32[1024,1024]{1,0:T(8,128)} %copy-done.78, bf16[1024,2048]{1,0:T(8,128)(2,1)} %constant_dynamic-update-slice_fusion.65, bf16[1024,2048]{1,0:T(8,128)(2,1)} %all-gather.14.cloned.1.call-done), kind=kOutput, calls=%fused_computation.194 | convolution fusion | flops 4320133120 | bytes 14680064 | tf_op jit(solution)/shard_map/dot_general | solution.py:48
  532.1 52.7 %conditional.17 = (f32[128,2048]{1,0:T(8,128)S(1)}, f32[128,2048]{1,0:T(8,128)S(1)}) conditional(s32[]{:T(128)} %bitcast.74, () %tuple.144, (f32[1024,2048]{1,0:T(8,128)S(1)}, f32[1024,2048]{1,0:T(8,128)}) %tuple.148), branch_computations={%region_24.25_spmd, %region_25.26_spmd} | conditional | flops 5767168 | bytes 131072416 | solution.py:353
  587.8 27.1 %conditional.18 = (bf16[1024,2048]{1,0:T(8,128)(2,1)}) conditional(s32[]{:T(128)} %bitcast.74, () %tuple.151, bf16[128,2048]{1,0:T(8,128)(2,1)} %get-tuple-element.223), branch_computations={%region_27.28_spmd, %region_28.29_spmd} | conditional | bytes 26214608 | solution.py:353
  614.8 30.0 %conditional.19 = (bf16[1024,256]{0,1:T(8,128)(2,1)}, bf16[2048,256]{0,1:T(8,128)(2,1)}, bf16[2048,256]{0,1:T(8,128)(2,1)}, bf16[2,256,2048]{2,1,0:T(8,128)(2,1)}) conditional(s32[]{:T(128)} %bitcast.74, () %tuple.150, (bf16[1024,2048]{1,0:T(8,128)(2,1)}, bf16[256,2048]{1,0:T(8,128)(2,1)}, bf16[8,256,2,128]{3,2,1,0:T(2,128)(2,1)}, ...), branch_computations={%region_30.31_spmd, %region_31.33_spmd} | conditional | flops 1616640000 | bytes 66601200 | solution.py:353
  682.6 36.3 %conditional.20 = (f32[128,2048]{1,0:T(8,128)}) conditional(s32[]{:T(128)} %bitcast.74, () %tuple.149, f32[1024,2048]{1,0:T(8,128)} %fusion.119), branch_computations={%region_33.34_spmd, %region_34.35_spmd} | conditional | flops 2883584 | bytes 65536208 | solution.py:353
  697.1 11.7 %collective-permute-done.53 = bf16[2,128,1024]{2,1,0:T(8,128)(2,1)S(1)} collective-permute-done((bf16[2,128,1024]{2,1,0:T(8,128)(2,1)S(1)}, bf16[2,128,1024]{2,1,0:T(8,128)(2,1)S(1)}, u32[]{:S(2)}, u32[]{:S(2)}) %collective-permute-start.53) | collective-permute-done | bytes 524320 | tf_op jit(solution)/shard_map/cond/branch_1_fun/ppermute | solution.py:241
  723.6 26.6 %conditional.21 = (bf16[1024,2048]{1,0:T(8,128)(2,1)}) conditional(s32[]{:T(128)} %bitcast.74, () %tuple.155, bf16[128,2048]{1,0:T(8,128)(2,1)} %get-tuple-element.228), branch_computations={%region_37.38_spmd, %region_38.39_spmd} | conditional | bytes 26214608 | solution.py:353
  799.8 105.3 %conditional.22 = (f32[128,2048]{1,0:T(8,128)}, f32[3,2048]{1,0:T(4,128)S(1)}, bf16[4,256,2048]{2,1,0:T(8,128)(2,1)}) conditional(s32[]{:T(128)} %bitcast.74, () %tuple.154, (f32[1024,2048]{1,0:T(8,128)S(1)}, f32[3,2048]{1,0:T(4,128)S(1)}, f32[128,2048]{1,0:T(8,128)S(1)}, f32[128,2048]{1,0:T(8,128)S(1)}, f32[128,2048]{1,0:T(8,128)S(1)}, ...), branch_computations={%region_45.46_spmd, %region_46.50_spmd} | conditional | flops 9767680 | bytes 91698648 | solution.py:353
  816.1 58.7 %collective-permute-done.58 = bf16[2,128,1024]{2,1,0:T(8,128)(2,1)S(1)} collective-permute-done((bf16[2,128,1024]{2,1,0:T(8,128)(2,1)S(1)}, bf16[2,128,1024]{2,1,0:T(8,128)(2,1)S(1)}, u32[]{:S(2)}, u32[]{:S(2)}) %collective-permute-start.58) | collective-permute-done | bytes 524320 | tf_op jit(solution)/shard_map/cond/branch_1_fun/ppermute | solution.py:241
  919.6 93.9 %conditional.23 = (f32[6,256,2048]{2,1,0:T(8,128)}, f32[6,256,2048]{2,1,0:T(8,128)}, f32[6,256,2048]{2,1,0:T(8,128)}, bf16[4,256,2048]{2,1,0:T(8,128)(2,1)}) conditional(s32[]{:T(128)} %bitcast.74, () %tuple.162, (s32[6]{0:T(128)S(1)}, s32[6,8]{1,0:T(8,128)S(1)}, s32[6]{0:T(128)S(1)}, s32[3]{0:T(128)S(1)}, s32[]{:T(128)}, ...), branch_computations={%region_64.65_spmd, %region_65.66_spmd} | conditional | flops 101187584 | bytes 157287648 | solution.py:353
  936.9 24.3 %collective-permute-done.27 = bf16[256,2048]{1,0:T(8,128)(2,1)S(1)} collective-permute-done((bf16[256,2048]{1,0:T(8,128)(2,1)S(1)}, bf16[256,2048]{1,0:T(8,128)(2,1)S(1)}, u32[]{:S(2)}, u32[]{:S(2)}) %collective-permute-start.27) | collective-permute-done | bytes 1048608 | tf_op jit(solution)/shard_map/cond/branch_1_fun/ppermute | solution.py:506
  963.2 24.9 %adam_tiles.3 = (f32[6,256,2048]{2,1,0:T(8,128)}, f32[6,256,2048]{2,1,0:T(8,128)}, f32[6,256,2048]{2,1,0:T(8,128)}) custom-call(s32[3]{0:T(128)S(1)} %get-tuple-element.256.visit_ref, s32[3]{0:T(128)S(1)} %get-tuple-element.384.mode_ref, s32[24]{0:T(128)S(1)} %reshape.417.cp_ref, s32[3]{0:T(128)S(1)} %get-tuple-element.379.rp_ref, ...), custom_call_target="tpu_custom_call" | custom-call | flops 47185920 | bytes 40894464 | tf_op jit(solution)/shard_map/cond/branch_1_fun/adam_tiles/pallas_call | solution.py:211
  988.1 21.6 %adam_tiles.4 = (f32[6,256,2048]{2,1,0:T(8,128)}, f32[6,256,2048]{2,1,0:T(8,128)}, f32[6,256,2048]{2,1,0:T(8,128)}) custom-call(s32[3]{0:T(128)S(1)} %copy-done.7, s32[3]{0:T(128)S(1)} %get-tuple-element.383.mode_ref, s32[24]{0:T(128)S(1)} %reshape.416.cp_ref, ...), custom_call_target="tpu_custom_call", output_to_operand_aliasing={{0}: (10, {}), {1}: (11, {}), {2}: (12, {})} | custom-call | flops 47185920 | bytes 40894464 | tf_op jit(solution)/shard_map/cond/branch_1_fun/adam_tiles/pallas_call | solution.py:211
  1013.5 21.8 %adam_tiles.5 = (f32[6,256,2048]{2,1,0:T(8,128)}, f32[6,256,2048]{2,1,0:T(8,128)}, f32[6,256,2048]{2,1,0:T(8,128)}) custom-call(s32[5]{0:T(128)S(1)} %get-tuple-element.456.visit_ref, s32[5]{0:T(128)S(1)} %get-tuple-element.455.mode_ref, s32[40]{0:T(128)S(1)} %select_n.469.cp_ref, ...), custom_call_target="tpu_custom_call", output_to_operand_aliasing={{0}: (12, {}), {1}: (13, {}), {2}: (14, {})} | custom-call | flops 78643200 | bytes 68157440 | tf_op jit(solution)/shard_map/adam_tiles/pallas_call | solution.py:211
  (694 shorter events, 726.7 us)
Async XLA Ops:
  24.7 49.1 %all-to-all-start = ((bf16[8,3,256,256]{3,2,1,0:T(8,128)(2,1)}), bf16[8,3,256,256]{3,2,1,0:T(8,128)(2,1)S(1)}, u32[]{:S(2)}, u32[]{:S(2)}) async-start(bf16[8,3,256,256]{3,2,1,0:T(8,128)(2,1)} %copy-done), calls=%async_computation | async-start | bytes 6291456 | tf_op jit(solution)/shard_map/all_to_all | solution.py:360
  30.1 131.3 %all-gather.6.cloned.1.call-start = ((), (), s32[]{:S(2)}) async-start(), calls=%async_computation.9 | async-start | bytes 3932160 | tf_op jit(solution)/shard_map/all_gather | solution.py:381
  79.7 168.0 %all-gather.8.cloned.1.call-start = ((), (), s32[]{:S(2)}) async-start(), calls=%async_computation.10 | async-start | bytes 2621440 | tf_op jit(solution)/shard_map/all_gather | solution.py:416
  82.9 38.0 %collective-permute-start.76 = (bf16[2,256,2048]{2,1,0:T(8,128)(2,1)}, bf16[2,256,2048]{2,1,0:T(8,128)(2,1)}, u32[]{:S(2)}, u32[]{:S(2)}) collective-permute-start(bf16[2,256,2048]{2,1,0:T(8,128)(2,1)} %pad_maximum_fusion.13), channel_id=1, source_target_pairs={{0,1},{1,0},{2,3},{3,2},{4,5},{5,4},{6,7},{7,6},{8,9},{9,8},{10,11... | collective-permute-start | bytes 6291464 | tf_op jit(solution)/shard_map/ppermute | solution.py:241
  155.9 41.4 %all-to-all-start.1 = ((bf16[8,3,256,256]{3,2,1,0:T(8,128)(2,1)}), bf16[8,3,256,256]{3,2,1,0:T(8,128)(2,1)}, u32[]{:S(2)}, u32[]{:S(2)}) async-start(bf16[8,3,256,256]{3,2,1,0:T(8,128)(2,1)} %copy-done.1), calls=%async_computation.1 | async-start | bytes 6291456 | tf_op jit(solution)/shard_map/all_to_all | solution.py:388
  160.4 212.5 %all-gather.10.cloned.1.call-start = ((), (), s32[]{:S(2)}) async-start(), calls=%async_computation.11 | async-start | bytes 6553600 | tf_op jit(solution)/shard_map/all_gather | solution.py:381
  201.3 277.0 %all-gather.12.cloned.1.call-start = ((), (), s32[]{:S(2)}) async-start(), calls=%async_computation.12 | async-start | bytes 5242880 | tf_op jit(solution)/shard_map/all_gather | solution.py:381
  207.3 289.5 %all-gather.14.cloned.1.call-start = ((), (), s32[]{:S(2)}) async-start(), calls=%async_computation.13 | async-start | bytes 5242880 | tf_op jit(solution)/shard_map/all_gather | solution.py:381
  244.0 71.5 %collective-permute-start.81 = (bf16[256,4096]{1,0:T(8,128)(2,1)}, bf16[256,4096]{1,0:T(8,128)(2,1)}, u32[]{:S(2)}, u32[]{:S(2)}) collective-permute-start(bf16[256,4096]{1,0:T(8,128)(2,1)} %bitcast.106), channel_id=1, source_target_pairs={{0,2},{2,0},{1,3},{3,1},{4,6},{6,4},{5,7},{7,5},{8,10},{10,8},{9,1... | collective-permute-start | bytes 6291464 | tf_op jit(solution)/shard_map/ppermute | solution.py:241
  245.5 70.1 %collective-permute-start.82 = (bf16[256,4096]{1,0:T(8,128)(2,1)}, bf16[256,4096]{1,0:T(8,128)(2,1)}, u32[]{:S(2)}, u32[]{:S(2)}) collective-permute-start(bf16[256,4096]{1,0:T(8,128)(2,1)} %bitcast.106), channel_id=1, source_target_pairs={{0,4},{4,0},{1,5},{5,1},{2,6},{6,2},{3,7},{7,3},{8,12},{12,8},{9,1... | collective-permute-start | bytes 6291464 | tf_op jit(solution)/shard_map/ppermute | solution.py:241
  247.6 367.2 %reduce-scatter.6.cloned.1.call-start = ((), (), s32[]{:S(2)}) async-start(), calls=%async_computation.14 | async-start | bytes 5242880 | tf_op jit(solution)/shard_map/reduce_scatter | solution.py:502
  266.2 37.4 %collective-permute-start.33 = (bf16[2,128,1024]{2,1,0:T(8,128)(2,1)S(1)}, bf16[2,128,1024]{2,1,0:T(8,128)(2,1)S(1)}, u32[]{:S(2)}, u32[]{:S(2)}) collective-permute-start(bf16[2,128,1024]{2,1,0:T(8,128)(2,1)S(1)} %slice_bitcast_fusion.3), channel_id=1, source_target_pairs={{0,4},{4,0},{1,5},{5,1},{2,6},{6,2},{3,7},{7,3},{8,12},{12,8},{9,1... | collective-permute-start | bytes 1572872 | tf_op jit(solution)/shard_map/cond/branch_1_fun/ppermute | solution.py:241
  267.7 36.7 %collective-permute-start.31 = (bf16[2,128,1024]{2,1,0:T(8,128)(2,1)S(1)}, bf16[2,128,1024]{2,1,0:T(8,128)(2,1)S(1)}, u32[]{:S(2)}, u32[]{:S(2)}) collective-permute-start(bf16[2,128,1024]{2,1,0:T(8,128)(2,1)S(1)} %slice_bitcast_fusion.5), channel_id=1, source_target_pairs={{0,2},{2,0},{1,3},{3,1},{4,6},{6,4},{5,7},{7,5},{8,10},{10,8},{9,1... | collective-permute-start | bytes 1572872 | tf_op jit(solution)/shard_map/cond/branch_1_fun/ppermute | solution.py:241
  343.0 29.6 %collective-permute-start.10 = (bf16[1024,4096]{1,0:T(8,128)(2,1)}, bf16[1024,4096]{1,0:T(8,128)(2,1)}, u32[]{:S(2)}, u32[]{:S(2)}) collective-permute-start(bf16[1024,4096]{1,0:T(8,128)(2,1)} %constant_dynamic-update-slice_fusion.11), channel_id=1, source_target_pairs={{0,1},{1,0},{2,3},{3,2},{4,5},{5,4},{6,7},{7,6},{8,9},{9,8},{10,11... | collective-permute-start | bytes 25165832 | tf_op jit(solution)/shard_map/cond/branch_1_fun/ppermute | solution.py:241
  496.5 227.1 %reduce-scatter.8.cloned.1.call-start = ((), (), s32[]{:S(2)}) async-start(), calls=%async_computation.15 | async-start | bytes 5242880 | tf_op jit(solution)/shard_map/reduce_scatter | solution.py:502
  517.6 264.4 %reduce-scatter.10.cloned.1.call-start = ((), (), s32[]{:S(2)}) async-start(), calls=%async_computation.16 | async-start | bytes 6553600 | tf_op jit(solution)/shard_map/reduce_scatter | solution.py:502
  671.0 234.1 %reduce-scatter.12.cloned.1.call-start = ((), (), s32[]{:S(2)}) async-start(), calls=%async_computation.17 | async-start | bytes 3932160 | tf_op jit(solution)/shard_map/reduce_scatter | solution.py:502
  788.2 119.2 %all-to-all-start.2 = ((bf16[8,6,256,256]{3,2,1,0:T(8,128)(2,1)}), bf16[8,6,256,256]{3,2,1,0:T(8,128)(2,1)}, u32[]{:S(2)}, u32[]{:S(2)}) async-start(bf16[8,6,256,256]{3,2,1,0:T(8,128)(2,1)} %pack_gradients.1), calls=%async_computation.5 | async-start | bytes 12582912 | tf_op jit(solution)/shard_map/all_to_all | solution.py:579
  793.0 126.6 %reduce-scatter.14.cloned.1.call-start = ((), (), s32[]{:S(2)}) async-start(), calls=%async_computation.18 | async-start | bytes 2621440 | tf_op jit(solution)/shard_map/reduce_scatter | solution.py:502
  801.4 89.5 %collective-permute-start.65 = (bf16[2,256,2048]{2,1,0:T(8,128)(2,1)}, bf16[2,256,2048]{2,1,0:T(8,128)(2,1)S(1)}, u32[]{:S(2)}, u32[]{:S(2)}) collective-permute-start(bf16[2,256,2048]{2,1,0:T(8,128)(2,1)} %get-tuple-element.120), channel_id=1, source_target_pairs={{0,1},{1,0},{2,3},{3,2},{4,5},{5,4},{6,7},{7,6},{8,9},{9,8},{10,11... | collective-permute-start | bytes 6291464 | tf_op jit(solution)/shard_map/cond/branch_1_fun/ppermute | solution.py:241
  812.0 62.8 %collective-permute-start.58 = (bf16[2,128,1024]{2,1,0:T(8,128)(2,1)S(1)}, bf16[2,128,1024]{2,1,0:T(8,128)(2,1)S(1)}, u32[]{:S(2)}, u32[]{:S(2)}) collective-permute-start(bf16[2,128,1024]{2,1,0:T(8,128)(2,1)S(1)} %slice_bitcast_fusion.33), channel_id=1, source_target_pairs={{0,4},{4,0},{1,5},{5,1},{2,6},{6,2},{3,7},{7,3},{8,12},{12,8},{9,1... | collective-permute-start | bytes 1572872 | tf_op jit(solution)/shard_map/cond/branch_1_fun/ppermute | solution.py:241
  814.6 61.9 %collective-permute-start.56 = (bf16[2,128,1024]{2,1,0:T(8,128)(2,1)S(1)}, bf16[2,128,1024]{2,1,0:T(8,128)(2,1)S(1)}, u32[]{:S(2)}, u32[]{:S(2)}) collective-permute-start(bf16[2,128,1024]{2,1,0:T(8,128)(2,1)S(1)} %slice_bitcast_fusion.35), channel_id=1, source_target_pairs={{0,2},{2,0},{1,3},{3,1},{4,6},{6,4},{5,7},{7,5},{8,10},{10,8},{9,1... | collective-permute-start | bytes 1572872 | tf_op jit(solution)/shard_map/cond/branch_1_fun/ppermute | solution.py:241
  909.5 104.0 %all-to-all-start.3 = ((bf16[8,3,256,256]{3,2,1,0:T(8,128)(2,1)}), bf16[8,3,256,256]{3,2,1,0:T(8,128)(2,1)S(1)}, u32[]{:S(2)}, u32[]{:S(2)}) async-start(bf16[8,3,256,256]{3,2,1,0:T(8,128)(2,1)} %bitcast.374), calls=%async_computation.7 | async-start | bytes 6291456 | tf_op jit(solution)/shard_map/all_to_all | solution.py:593
  962.9 46.8 %collective-permute-start.28 = (bf16[2,256,2048]{2,1,0:T(8,128)(2,1)}, bf16[2,256,2048]{2,1,0:T(8,128)(2,1)}, u32[]{:S(2)}, u32[]{:S(2)}) collective-permute-start(bf16[2,256,2048]{2,1,0:T(8,128)(2,1)} %pad_maximum_fusion.11), channel_id=1, source_target_pairs={{0,1},{1,0},{2,3},{3,2},{4,5},{5,4},{6,7},{7,6},{8,9},{9,8},{10,11... | collective-permute-start | bytes 6291464 | tf_op jit(solution)/shard_map/cond/branch_1_fun/ppermute | solution.py:241
  (157 other events, 2204.7 us)
Sparse Core Ops, SparseCore 0:
  79.8 63.8 all-gather.5
  156.0 46.8 all-gather.7
  204.5 96.7 all-gather.9
  302.7 79.1 all-gather.11
  383.3 79.2 all-gather.13
  496.6 78.3 reduce-scatter.5
  577.4 77.2 reduce-scatter.7
  671.1 95.0 reduce-scatter.9
  781.5 61.9 reduce-scatter.11
  845.7 43.8 reduce-scatter.13

commit v15 on v14

--- a/solution.py
+++ b/solution.py
@@ -605,7 +605,8 @@
     def early_step(early_grads, out_grads, half):
         other_half = lax.ppermute(half, ALL_AXES, back_swap)
         in_order = jnp.where(odd == 0, jnp.stack([half, other_half]), jnp.stack([other_half, half]))
-        outer_pair = from_y(in_order.reshape(rows, width), lambda zz, place, _: place % 4 in (zz, (zz + 2) % 4))
+        in_order = in_order.reshape(rows, width)
+        counts = jnp.where(f % 2 == z % 2, in_order, swap(in_order, "c"))
         early = None
         for first in (0, half_cap):
             chosen = slice(first, first + half_cap)
@@ -620,7 +621,7 @@
                 np.zeros(half_cap, np.int32),
                 early,
             )
-        return *early, with_core(outer_pair)
+        return *early, from_y(counts)
 
     *early, outer_grads = chain_step(early_step, early_grads, out_grads, g_outer)
 
@@ -650,7 +651,7 @@
         visit,
         mode,
         late_place.reshape(-1),
-        jnp.where(some, at_step(row_source), row_source[0]),
+        jnp.where(some, at_step(other_row // 2), row_source[0]),
         hold,
         early,
     )

time: 1050 us -> 1030 us (0.981)
  waiting for transfers between devices: 382 us -> 362 us
    ppermute x2, waiting for transfers between devices: 24.3 us -> 0.01 us  [from_y(): lax.ppermute(value, ALL_AXES, flip_pairs(2, keep_pair))]
    cond x47 -> x43, local copies, waits for them, and re-layouts: 33.6 us -> 33.6 us
  transfers between devices with their start and end apart: 97 -> 97, of which waited for: 53 -> 53; matrix products, arithmetic and copies ran while one was open for 38% -> 39% of each run, Pallas kernels for 6% -> 6%
where the time goes in v15:
time: 1030 us; the launch traced here: 1020 us
  waiting for transfers between devices  362 us (35%)
  matrix products  164 us (16%)
  local copies, waits for them, and re-layouts  158 us (15%)
  other arithmetic  102 us (10%)
  starting transfers between devices  98.9 us (10%)
  Pallas kernels  89.2 us (9%)
  between operations  43.4 us (4%)
    ppermute x75, waiting for transfers between devices, swap(): return lax.ppermute(value, axis, [(0, 1), (1, 0)])  310 us
    pallas_call x3, Pallas kernels, adam_tiles(): pl.pallas_call(kernel, out_shape=(shape, shape, shape), grid_spec=pltpu.P...  68.3 us
    ppermute x75, starting transfers between devices, swap(): return lax.ppermute(value, axis, [(0, 1), (1, 0)])  61.7 us
    dot_general x10, matrix products, matmul(): return jnp.dot(left, right, preferred_element_type=f32)  51.8 us
    dot_general x8, matrix products, matmul_left(): lax.dot_general(left, right, (((0,), (0,)), ((), ())), preferred_element_...  51.3 us
    dot_general x6, matrix products, matmul_right(): lax.dot_general(left, right, (((1,), (1,)), ((), ())), preferred_element_...  39.1 us
    cond x43, local copies, waits for them, and re-layouts  33.6 us
    unnamed x156, local copies, waits for them, and re-layouts  30.6 us
  transfers between devices with their start and end apart: 97, of which 53 were waited for; matrix products, arithmetic and copies ran while one was open for 39% of the time, Pallas kernels for 6%

profile of v15, /device:TPU:0, one launch (start us, length us, event | category | flops | bytes accessed | tf_op | source)
XLA Modules:
  0.0 1019.4 jit_solution(15033866265133976090)
XLA Ops:
  186.3 11.3 %all-to-all-done.1 = bf16[8,3,256,256]{3,2,1,0:T(8,128)(2,1)} async-done(((bf16[8,3,256,256]{3,2,1,0:T(8,128)(2,1)}), bf16[8,3,256,256]{3,2,1,0:T(8,128)(2,1)}, u32[]{:S(2)}, u32[]{:S(2)}) %all-to-all-start.1) | async-done | bytes 3145760 | tf_op jit(solution)/shard_map/all_to_all | solution.py:388
  220.0 21.2 %collective-permute-done.80 = bf16[256,2048]{1,0:T(8,128)(2,1)S(1)} collective-permute-done((bf16[256,2048]{1,0:T(8,128)(2,1)S(1)}, bf16[256,2048]{1,0:T(8,128)(2,1)S(1)}, u32[]{:S(2)}, u32[]{:S(2)}) %collective-permute-start.80) | collective-permute-done | bytes 1048608 | tf_op jit(solution)/shard_map/ppermute | solution.py:396
  253.5 57.3 %conditional.13 = (f32[128,2048]{1,0:T(8,128)S(1)}) conditional(s32[]{:T(128)} %bitcast.74, () %tuple.120, f32[1024,2048]{1,0:T(8,128)} %fusion.134), branch_computations={%region_12.13_spmd, %region_13.14_spmd} | conditional | flops 2883584 | bytes 65536208 | solution.py:353
  267.9 35.3 %collective-permute-done.33 = bf16[2,128,1024]{2,1,0:T(8,128)(2,1)S(1)} collective-permute-done((bf16[2,128,1024]{2,1,0:T(8,128)(2,1)S(1)}, bf16[2,128,1024]{2,1,0:T(8,128)(2,1)S(1)}, u32[]{:S(2)}, u32[]{:S(2)}) %collective-permute-start.33) | collective-permute-done | bytes 524320 | tf_op jit(solution)/shard_map/cond/branch_1_fun/ppermute | solution.py:241
  315.2 57.2 %conditional.14 = (bf16[1024,2048]{1,0:T(8,128)(2,1)}, bf16[1024,4096]{1,0:T(8,128)(2,1)}, bf16[1024,4096]{1,0:T(8,128)(2,1)}) conditional(s32[]{:T(128)} %bitcast.74, () %tuple.136, (bf16[128,2048]{1,0:T(8,128)(2,1)S(1)}, bf16[256,4096]{1,0:T(8,128)(2,1)}, bf16[256,4096]{1,0:T(8,128)(2,1)}, bf16[256,4096]{1,0:T(8,128)(2,1)}) %tuple.142), branch_computations={%region_15.16_spmd, %region_16.17_spmd} | conditional | bytes 89129304 | solution.py:353
  345.5 11.4 %collective-permute-done.3 = bf16[128,2048]{1,0:T(8,128)(2,1)S(1)} collective-permute-done((bf16[128,2048]{1,0:T(8,128)(2,1)S(1)}, bf16[128,2048]{1,0:T(8,128)(2,1)S(1)}, u32[]{:S(2)}, u32[]{:S(2)}) %collective-permute-start.3) | collective-permute-done | bytes 524320 | tf_op jit(solution)/shard_map/cond/branch_1_fun/ppermute | solution.py:241
  408.6 40.0 %conditional.15 = (f32[128,2048]{1,0:T(8,128)S(1)}, bf16[2048,4096]{1,0:T(8,128)(2,1)}) conditional(s32[]{:T(128)} %bitcast.74, () %tuple.135, (f32[1024,2048]{1,0:T(8,128)S(1)}, bf16[1024,4096]{1,0:T(8,128)(2,1)}, bf16[1024,4096]{1,0:T(8,128)(2,1)}) %tuple.143), branch_computations={%region_19.20_spmd, %region_20.21_spmd} | conditional | flops 36438016 | bytes 99090648 | solution.py:353
  420.3 12.0 %collective-permute-done.38 = bf16[2,128,1024]{2,1,0:T(8,128)(2,1)S(1)} collective-permute-done((bf16[2,128,1024]{2,1,0:T(8,128)(2,1)S(1)}, bf16[2,128,1024]{2,1,0:T(8,128)(2,1)S(1)}, u32[]{:S(2)}, u32[]{:S(2)}) %collective-permute-start.38) | collective-permute-done | bytes 524320 | tf_op jit(solution)/shard_map/cond/branch_1_fun/ppermute | solution.py:241
  434.7 13.7 %pad_maximum_fusion.1 = bf16[2048,4096]{1,0:T(8,128)(2,1)} fusion(bf16[1024,4096]{1,0:T(8,128)(2,1)} %get-tuple-element.108, bf16[1024,4096]{1,0:T(8,128)(2,1)} %get-tuple-element.107), kind=kLoop, calls=%fused_computation.35 | loop fusion | flops 33554432 | bytes 33554432 | tf_op jit(solution)/shard_map/cond/branch_1_fun/concatenate | solution.py:488
  451.2 26.7 %conditional.16 = (bf16[1024,2048]{1,0:T(8,128)(2,1)}) conditional(s32[]{:T(128)} %bitcast.74, () %tuple.145, bf16[128,2048]{1,0:T(8,128)(2,1)S(1)} %get-tuple-element.319), branch_computations={%region_22.23_spmd, %region_23.24_spmd} | conditional | bytes 26214608 | solution.py:353
  496.2 11.1 %fusion.55 = bf16[1024,1024]{1,0:T(8,128)(2,1)S(1)} fusion(f32[1024,1024]{1,0:T(8,128)} %copy-done.76, bf16[1024,2048]{1,0:T(8,128)(2,1)} %constant_dynamic-update-slice_fusion.65, bf16[1024,2048]{1,0:T(8,128)(2,1)} %all-gather.14.cloned.1.call-done), kind=kOutput, calls=%fused_computation.194 | convolution fusion | flops 4320133120 | bytes 14680064 | tf_op jit(solution)/shard_map/dot_general | solution.py:48
  531.5 52.5 %conditional.17 = (f32[128,2048]{1,0:T(8,128)S(1)}, f32[128,2048]{1,0:T(8,128)S(1)}) conditional(s32[]{:T(128)} %bitcast.74, () %tuple.144, (f32[1024,2048]{1,0:T(8,128)S(1)}, f32[1024,2048]{1,0:T(8,128)}) %tuple.148), branch_computations={%region_24.25_spmd, %region_25.26_spmd} | conditional | flops 5767168 | bytes 131072416 | solution.py:353
  587.1 27.2 %conditional.18 = (bf16[1024,2048]{1,0:T(8,128)(2,1)}) conditional(s32[]{:T(128)} %bitcast.74, () %tuple.151, bf16[128,2048]{1,0:T(8,128)(2,1)} %get-tuple-element.229), branch_computations={%region_27.28_spmd, %region_28.29_spmd} | conditional | bytes 26214608 | solution.py:353
  614.3 30.0 %conditional.19 = (bf16[1024,256]{0,1:T(8,128)(2,1)}, bf16[2048,256]{0,1:T(8,128)(2,1)}, bf16[2048,256]{0,1:T(8,128)(2,1)}, bf16[2,256,2048]{2,1,0:T(8,128)(2,1)}) conditional(s32[]{:T(128)} %bitcast.74, () %tuple.150, (bf16[1024,2048]{1,0:T(8,128)(2,1)}, bf16[256,2048]{1,0:T(8,128)(2,1)}, bf16[8,256,2,128]{3,2,1,0:T(2,128)(2,1)}, ...), branch_computations={%region_30.31_spmd, %region_31.33_spmd} | conditional | flops 1616640000 | bytes 66601200 | solution.py:353
  682.4 36.2 %conditional.20 = (f32[128,2048]{1,0:T(8,128)}) conditional(s32[]{:T(128)} %bitcast.74, () %tuple.149, f32[1024,2048]{1,0:T(8,128)} %fusion.119), branch_computations={%region_33.34_spmd, %region_34.35_spmd} | conditional | flops 2883584 | bytes 65536208 | solution.py:353
  696.6 12.0 %collective-permute-done.53 = bf16[2,128,1024]{2,1,0:T(8,128)(2,1)S(1)} collective-permute-done((bf16[2,128,1024]{2,1,0:T(8,128)(2,1)S(1)}, bf16[2,128,1024]{2,1,0:T(8,128)(2,1)S(1)}, u32[]{:S(2)}, u32[]{:S(2)}) %collective-permute-start.53) | collective-permute-done | bytes 524320 | tf_op jit(solution)/shard_map/cond/branch_1_fun/ppermute | solution.py:241
  723.3 26.8 %conditional.21 = (bf16[1024,2048]{1,0:T(8,128)(2,1)}) conditional(s32[]{:T(128)} %bitcast.74, () %tuple.155, bf16[128,2048]{1,0:T(8,128)(2,1)} %get-tuple-element.234), branch_computations={%region_37.38_spmd, %region_38.39_spmd} | conditional | bytes 26214608 | solution.py:353
  799.8 104.8 %conditional.22 = (f32[128,2048]{1,0:T(8,128)}, f32[3,2048]{1,0:T(4,128)S(1)}, bf16[4,256,2048]{2,1,0:T(8,128)(2,1)}) conditional(s32[]{:T(128)} %bitcast.74, () %tuple.154, (f32[1024,2048]{1,0:T(8,128)S(1)}, f32[3,2048]{1,0:T(4,128)S(1)}, f32[128,2048]{1,0:T(8,128)S(1)}, f32[128,2048]{1,0:T(8,128)S(1)}, f32[128,2048]{1,0:T(8,128)S(1)}, ...), branch_computations={%region_45.46_spmd, %region_46.50_spmd} | conditional | flops 9767680 | bytes 91698648 | solution.py:353
  816.1 58.7 %collective-permute-done.58 = bf16[2,128,1024]{2,1,0:T(8,128)(2,1)S(1)} collective-permute-done((bf16[2,128,1024]{2,1,0:T(8,128)(2,1)S(1)}, bf16[2,128,1024]{2,1,0:T(8,128)(2,1)S(1)}, u32[]{:S(2)}, u32[]{:S(2)}) %collective-permute-start.58) | collective-permute-done | bytes 524320 | tf_op jit(solution)/shard_map/cond/branch_1_fun/ppermute | solution.py:241
  919.1 71.4 %conditional.23 = (f32[6,256,2048]{2,1,0:T(8,128)}, f32[6,256,2048]{2,1,0:T(8,128)}, f32[6,256,2048]{2,1,0:T(8,128)}, bf16[2,256,2048]{2,1,0:T(8,128)(2,1)}) conditional(s32[]{:T(128)} %bitcast.74, () %tuple.162, (s32[6]{0:T(128)S(1)}, s32[6,8]{1,0:T(8,128)S(1)}, s32[6]{0:T(128)S(1)}, s32[3]{0:T(128)S(1)}, s32[]{:T(128)}, ...), branch_computations={%region_64.65_spmd, %region_65.66_spmd} | conditional | flops 97517568 | bytes 139462016 | solution.py:353
  920.6 10.1 collective-permute-done.26
  940.9 24.9 %adam_tiles.3 = (f32[6,256,2048]{2,1,0:T(8,128)}, f32[6,256,2048]{2,1,0:T(8,128)}, f32[6,256,2048]{2,1,0:T(8,128)}) custom-call(s32[3]{0:T(128)S(1)} %get-tuple-element.262.visit_ref, s32[3]{0:T(128)S(1)} %get-tuple-element.392.mode_ref, s32[24]{0:T(128)S(1)} %reshape.384.cp_ref, s32[3]{0:T(128)S(1)} %get-tuple-element.387.rp_ref, ...), custom_call_target="tpu_custom_call" | custom-call | flops 47185920 | bytes 40894464 | tf_op jit(solution)/shard_map/cond/branch_1_fun/adam_tiles/pallas_call | solution.py:211
  965.8 21.5 %adam_tiles.4 = (f32[6,256,2048]{2,1,0:T(8,128)}, f32[6,256,2048]{2,1,0:T(8,128)}, f32[6,256,2048]{2,1,0:T(8,128)}) custom-call(s32[3]{0:T(128)S(1)} %copy-done.7, s32[3]{0:T(128)S(1)} %get-tuple-element.391.mode_ref, s32[24]{0:T(128)S(1)} %reshape.383.cp_ref, ...), custom_call_target="tpu_custom_call", output_to_operand_aliasing={{0}: (10, {}), {1}: (11, {}), {2}: (12, {})} | custom-call | flops 47185920 | bytes 40894464 | tf_op jit(solution)/shard_map/cond/branch_1_fun/adam_tiles/pallas_call | solution.py:211
  990.5 21.8 %adam_tiles.5 = (f32[6,256,2048]{2,1,0:T(8,128)}, f32[6,256,2048]{2,1,0:T(8,128)}, f32[6,256,2048]{2,1,0:T(8,128)}) custom-call(s32[5]{0:T(128)S(1)} %broadcast_select_fusion.7.visit_ref, s32[5]{0:T(128)S(1)} %compare_select_fusion.15.mode_ref, s32[40]{0:T(128)S(1)} %select_n.470.cp_ref, ...), custom_call_target="tpu_custom_call", output_to_operand_aliasing={{0}: (12, {}), {1}: (13, {}), {2}: (14, {})} | custom-call | flops 78643200 | bytes 68157440 | tf_op jit(solution)/shard_map/adam_tiles/pallas_call | solution.py:211
  (690 shorter events, 718.1 us)
Async XLA Ops:
  24.7 49.1 %all-to-all-start = ((bf16[8,3,256,256]{3,2,1,0:T(8,128)(2,1)}), bf16[8,3,256,256]{3,2,1,0:T(8,128)(2,1)S(1)}, u32[]{:S(2)}, u32[]{:S(2)}) async-start(bf16[8,3,256,256]{3,2,1,0:T(8,128)(2,1)} %copy-done), calls=%async_computation | async-start | bytes 6291456 | tf_op jit(solution)/shard_map/all_to_all | solution.py:360
  30.1 131.6 %all-gather.6.cloned.1.call-start = ((), (), s32[]{:S(2)}) async-start(), calls=%async_computation.9 | async-start | bytes 3932160 | tf_op jit(solution)/shard_map/all_gather | solution.py:381
  79.7 167.5 %all-gather.8.cloned.1.call-start = ((), (), s32[]{:S(2)}) async-start(), calls=%async_computation.10 | async-start | bytes 2621440 | tf_op jit(solution)/shard_map/all_gather | solution.py:416
  82.9 38.0 %collective-permute-start.76 = (bf16[2,256,2048]{2,1,0:T(8,128)(2,1)}, bf16[2,256,2048]{2,1,0:T(8,128)(2,1)}, u32[]{:S(2)}, u32[]{:S(2)}) collective-permute-start(bf16[2,256,2048]{2,1,0:T(8,128)(2,1)} %pad_maximum_fusion.12), channel_id=1, source_target_pairs={{0,1},{1,0},{2,3},{3,2},{4,5},{5,4},{6,7},{7,6},{8,9},{9,8},{10,11... | collective-permute-start | bytes 6291464 | tf_op jit(solution)/shard_map/ppermute | solution.py:241
  156.2 41.4 %all-to-all-start.1 = ((bf16[8,3,256,256]{3,2,1,0:T(8,128)(2,1)}), bf16[8,3,256,256]{3,2,1,0:T(8,128)(2,1)}, u32[]{:S(2)}, u32[]{:S(2)}) async-start(bf16[8,3,256,256]{3,2,1,0:T(8,128)(2,1)} %copy-done.1), calls=%async_computation.1 | async-start | bytes 6291456 | tf_op jit(solution)/shard_map/all_to_all | solution.py:388
  160.7 211.7 %all-gather.10.cloned.1.call-start = ((), (), s32[]{:S(2)}) async-start(), calls=%async_computation.11 | async-start | bytes 6553600 | tf_op jit(solution)/shard_map/all_gather | solution.py:381
  200.8 277.0 %all-gather.12.cloned.1.call-start = ((), (), s32[]{:S(2)}) async-start(), calls=%async_computation.12 | async-start | bytes 5242880 | tf_op jit(solution)/shard_map/all_gather | solution.py:381
  206.8 289.4 %all-gather.14.cloned.1.call-start = ((), (), s32[]{:S(2)}) async-start(), calls=%async_computation.13 | async-start | bytes 5242880 | tf_op jit(solution)/shard_map/all_gather | solution.py:381
  243.5 71.7 %collective-permute-start.81 = (bf16[256,4096]{1,0:T(8,128)(2,1)}, bf16[256,4096]{1,0:T(8,128)(2,1)}, u32[]{:S(2)}, u32[]{:S(2)}) collective-permute-start(bf16[256,4096]{1,0:T(8,128)(2,1)} %bitcast.106), channel_id=1, source_target_pairs={{0,2},{2,0},{1,3},{3,1},{4,6},{6,4},{5,7},{7,5},{8,10},{10,8},{9,1... | collective-permute-start | bytes 6291464 | tf_op jit(solution)/shard_map/ppermute | solution.py:241
  245.0 70.2 %collective-permute-start.82 = (bf16[256,4096]{1,0:T(8,128)(2,1)}, bf16[256,4096]{1,0:T(8,128)(2,1)}, u32[]{:S(2)}, u32[]{:S(2)}) collective-permute-start(bf16[256,4096]{1,0:T(8,128)(2,1)} %bitcast.106), channel_id=1, source_target_pairs={{0,4},{4,0},{1,5},{5,1},{2,6},{6,2},{3,7},{7,3},{8,12},{12,8},{9,1... | collective-permute-start | bytes 6291464 | tf_op jit(solution)/shard_map/ppermute | solution.py:241
  247.1 367.1 %reduce-scatter.6.cloned.1.call-start = ((), (), s32[]{:S(2)}) async-start(), calls=%async_computation.14 | async-start | bytes 5242880 | tf_op jit(solution)/shard_map/reduce_scatter | solution.py:502
  265.7 37.4 %collective-permute-start.33 = (bf16[2,128,1024]{2,1,0:T(8,128)(2,1)S(1)}, bf16[2,128,1024]{2,1,0:T(8,128)(2,1)S(1)}, u32[]{:S(2)}, u32[]{:S(2)}) collective-permute-start(bf16[2,128,1024]{2,1,0:T(8,128)(2,1)S(1)} %slice_bitcast_fusion.3), channel_id=1, source_target_pairs={{0,4},{4,0},{1,5},{5,1},{2,6},{6,2},{3,7},{7,3},{8,12},{12,8},{9,1... | collective-permute-start | bytes 1572872 | tf_op jit(solution)/shard_map/cond/branch_1_fun/ppermute | solution.py:241
  267.3 36.6 %collective-permute-start.31 = (bf16[2,128,1024]{2,1,0:T(8,128)(2,1)S(1)}, bf16[2,128,1024]{2,1,0:T(8,128)(2,1)S(1)}, u32[]{:S(2)}, u32[]{:S(2)}) collective-permute-start(bf16[2,128,1024]{2,1,0:T(8,128)(2,1)S(1)} %slice_bitcast_fusion.5), channel_id=1, source_target_pairs={{0,2},{2,0},{1,3},{3,1},{4,6},{6,4},{5,7},{7,5},{8,10},{10,8},{9,1... | collective-permute-start | bytes 1572872 | tf_op jit(solution)/shard_map/cond/branch_1_fun/ppermute | solution.py:241
  342.6 29.6 %collective-permute-start.10 = (bf16[1024,4096]{1,0:T(8,128)(2,1)}, bf16[1024,4096]{1,0:T(8,128)(2,1)}, u32[]{:S(2)}, u32[]{:S(2)}) collective-permute-start(bf16[1024,4096]{1,0:T(8,128)(2,1)} %constant_dynamic-update-slice_fusion.11), channel_id=1, source_target_pairs={{0,1},{1,0},{2,3},{3,2},{4,5},{5,4},{6,7},{7,6},{8,9},{9,8},{10,11... | collective-permute-start | bytes 25165832 | tf_op jit(solution)/shard_map/cond/branch_1_fun/ppermute | solution.py:241
  496.0 227.4 %reduce-scatter.8.cloned.1.call-start = ((), (), s32[]{:S(2)}) async-start(), calls=%async_computation.15 | async-start | bytes 5242880 | tf_op jit(solution)/shard_map/reduce_scatter | solution.py:502
  517.1 264.9 %reduce-scatter.10.cloned.1.call-start = ((), (), s32[]{:S(2)}) async-start(), calls=%async_computation.16 | async-start | bytes 6553600 | tf_op jit(solution)/shard_map/reduce_scatter | solution.py:502
  670.7 233.8 %reduce-scatter.12.cloned.1.call-start = ((), (), s32[]{:S(2)}) async-start(), calls=%async_computation.17 | async-start | bytes 3932160 | tf_op jit(solution)/shard_map/reduce_scatter | solution.py:502
  788.2 118.7 %all-to-all-start.2 = ((bf16[8,6,256,256]{3,2,1,0:T(8,128)(2,1)}), bf16[8,6,256,256]{3,2,1,0:T(8,128)(2,1)}, u32[]{:S(2)}, u32[]{:S(2)}) async-start(bf16[8,6,256,256]{3,2,1,0:T(8,128)(2,1)} %pack_gradients.1), calls=%async_computation.5 | async-start | bytes 12582912 | tf_op jit(solution)/shard_map/all_to_all | solution.py:579
  793.0 126.1 %reduce-scatter.14.cloned.1.call-start = ((), (), s32[]{:S(2)}) async-start(), calls=%async_computation.18 | async-start | bytes 2621440 | tf_op jit(solution)/shard_map/reduce_scatter | solution.py:502
  801.4 89.4 %collective-permute-start.65 = (bf16[2,256,2048]{2,1,0:T(8,128)(2,1)}, bf16[2,256,2048]{2,1,0:T(8,128)(2,1)S(1)}, u32[]{:S(2)}, u32[]{:S(2)}) collective-permute-start(bf16[2,256,2048]{2,1,0:T(8,128)(2,1)} %get-tuple-element.124), channel_id=1, source_target_pairs={{0,1},{1,0},{2,3},{3,2},{4,5},{5,4},{6,7},{7,6},{8,9},{9,8},{10,11... | collective-permute-start | bytes 6291464 | tf_op jit(solution)/shard_map/cond/branch_1_fun/ppermute | solution.py:241
  812.0 62.8 %collective-permute-start.58 = (bf16[2,128,1024]{2,1,0:T(8,128)(2,1)S(1)}, bf16[2,128,1024]{2,1,0:T(8,128)(2,1)S(1)}, u32[]{:S(2)}, u32[]{:S(2)}) collective-permute-start(bf16[2,128,1024]{2,1,0:T(8,128)(2,1)S(1)} %slice_bitcast_fusion.33), channel_id=1, source_target_pairs={{0,4},{4,0},{1,5},{5,1},{2,6},{6,2},{3,7},{7,3},{8,12},{12,8},{9,1... | collective-permute-start | bytes 1572872 | tf_op jit(solution)/shard_map/cond/branch_1_fun/ppermute | solution.py:241
  814.5 61.9 %collective-permute-start.56 = (bf16[2,128,1024]{2,1,0:T(8,128)(2,1)S(1)}, bf16[2,128,1024]{2,1,0:T(8,128)(2,1)S(1)}, u32[]{:S(2)}, u32[]{:S(2)}) collective-permute-start(bf16[2,128,1024]{2,1,0:T(8,128)(2,1)S(1)} %slice_bitcast_fusion.35), channel_id=1, source_target_pairs={{0,2},{2,0},{1,3},{3,1},{4,6},{6,4},{5,7},{7,5},{8,10},{10,8},{9,1... | collective-permute-start | bytes 1572872 | tf_op jit(solution)/shard_map/cond/branch_1_fun/ppermute | solution.py:241
  908.9 81.6 %all-to-all-start.3 = ((bf16[8,3,256,256]{3,2,1,0:T(8,128)(2,1)}), bf16[8,3,256,256]{3,2,1,0:T(8,128)(2,1)S(1)}, u32[]{:S(2)}, u32[]{:S(2)}) async-start(bf16[8,3,256,256]{3,2,1,0:T(8,128)(2,1)} %bitcast.375), calls=%async_computation.7 | async-start | bytes 6291456 | tf_op jit(solution)/shard_map/all_to_all | solution.py:593
  938.7 48.7 %collective-permute-start.28 = (bf16[256,2048]{1,0:T(8,128)(2,1)}, bf16[256,2048]{1,0:T(8,128)(2,1)}, u32[]{:S(2)}, u32[]{:S(2)}) collective-permute-start(bf16[256,2048]{1,0:T(8,128)(2,1)} %broadcast_select_fusion), channel_id=1, source_target_pairs={{0,2},{1,3},{2,0},{3,1},{4,6},{5,7},{6,4},{7,5},{8,10},{9,11},{10,... | collective-permute-start | bytes 3145736 | tf_op jit(solution)/shard_map/cond/branch_1_fun/ppermute | solution.py:506
  (155 other events, 2143.6 us)
Sparse Core Ops, SparseCore 0:
  79.8 63.8 all-gather.5
  156.3 46.7 all-gather.7
  204.7 96.7 all-gather.9
  303.0 79.1 all-gather.11
  383.6 79.2 all-gather.13
  496.1 78.1 reduce-scatter.5
  576.7 77.2 reduce-scatter.7
  670.9 94.6 reduce-scatter.9
  781.5 61.6 reduce-scatter.11
  845.4 43.8 reduce-scatter.13

commit v16 on v15

--- a/solution.py
+++ b/solution.py
@@ -384,23 +384,25 @@
     w_qkv = gather_z(local)
     a_all = gather_rows(after(a_in, local))
     d_ff = gather_rows(after(grad_out.astype(bf16), local))
-    sent = pack_second(after(master, a_all, d_ff))
-    received.append(lax.all_to_all(sent, PLANE, 0, 0, tiled=True).reshape(8 * half_cap, rows, block))
-
-    def take_rows(kind, blocks, keep_pair):
+    def meet_on_chip(kind, blocks):
         here, there = row_owners[2 * kind], row_owners[2 * kind + 1]
         core = f % 2
         from_core = swap(jnp.stack([blocks[1], blocks[3]]), "c")
         mine = jnp.where(here % 2 == core, blocks[0], from_core[0])
-        across = jnp.where(there % 2 == core, blocks[2], from_core[1])
-        from_y = lax.ppermute(across, ALL_AXES, flip_pairs(2, keep_pair))
-        return jnp.where(here // 2 == f // 2, mine, from_y)
+        return mine, jnp.where(there % 2 == core, blocks[2], from_core[1])
+
+    def mine_or_over_y(kind, mine, over_y):
+        return jnp.where(row_owners[2 * kind] // 2 == f // 2, mine, over_y)
+
+    out_mine, out_across = meet_on_chip(1, [after(value, local) for value in out_blocks])
+    sent = pack_second(after(master, a_all, d_ff, out_across))
+    received.append(lax.all_to_all(sent, PLANE, 0, 0, tiled=True).reshape(8 * half_cap, rows, block))
 
     def needs_outer(zz, place, target):
         return target % 4 in (zz, (zz + 2) % 4)
 
-    outer = take_rows(0, [after(value, local) for value in outer_blocks], needs_outer)
-    out_rows = take_rows(1, [after(value, local) for value in out_blocks], None)
+    outer_mine, across = meet_on_chip(0, [after(value, local) for value in outer_blocks])
+    outer = mine_or_over_y(0, outer_mine, lax.ppermute(across, ALL_AXES, flip_pairs(2, needs_outer)))
     half_rows = rows // 2
     odd = z % 2
     to_pair = lax.dynamic_slice_in_dim(after(outer, sent), (1 - odd) * half_rows, half_rows, 0)
@@ -450,11 +452,14 @@
     w_cross = gather_z(local_cross)
     w_in = gather_z(local_in)
 
-    w_out = gather_z(after(out_rows, local_cross, local_in))
     slots, ctx_len, ctx_width = context.shape
-    ctx = after(context.reshape(slots * ctx_len, ctx_width), local_cross, local_in, out_rows)
+    ctx = after(context.reshape(slots * ctx_len, ctx_width), local_cross, local_in)
     ctx_x, ctx_y = swap(ctx, "x"), swap(ctx, "y")
-    h1 = h0 + chain_step(scatter_rows, matmul(after(attended, local_in), w_self_out))
+    h1, over_y = chain_step(
+        lambda one, two: (scatter_rows(one), swap(two, "y")), matmul(after(attended, local_in), w_self_out), out_across
+    )
+    h1 = h0 + h1
+    w_out = gather_z(mine_or_over_y(1, out_mine, over_y))
 
     def second_step(one, own, over_x, over_y):
         half = over_x.shape[0] // 2

time: 1030 us -> 1030 us (level)
    ppermute x75 -> x76, waiting for transfers between devices: 310 us -> 335 us  [swap(): return lax.ppermute(value, axis, [(0, 1), (1, 0)])]
    ppermute x2 -> x1, waiting for transfers between devices: 21.2 us -> 0.01 us  [plane_body(): lax.ppermute(across, ALL_AXES, flip_pairs(2, needs_outer))]
    ppermute x75 -> x76, starting transfers between devices: 61.7 us -> 66.4 us  [swap(): return lax.ppermute(value, axis, [(0, 1), (1, 0)])]
    cond x43 -> x41, local copies, waits for them, and re-layouts: 33.6 us -> 30.8 us
    unnamed x156 -> x162, local copies, waits for them, and re-layouts: 30.6 us -> 31.1 us
  transfers between devices with their start and end apart: 97 -> 97, of which waited for: 53 -> 54; matrix products, arithmetic and copies ran while one was open for 39% -> 38% of each run, Pallas kernels for 6% -> 6%
where the time goes in v16:
time: 1030 us; the launch traced here: 1020 us
  waiting for transfers between devices  366 us (36%)
  matrix products  164 us (16%)
  local copies, waits for them, and re-layouts  151 us (15%)
  starting transfers between devices  100 us (10%)
  other arithmetic  99.8 us (10%)
  Pallas kernels  91.1 us (9%)
  between operations  43.3 us (4%)
    ppermute x76, waiting for transfers between devices, swap(): return lax.ppermute(value, axis, [(0, 1), (1, 0)])  335 us
    pallas_call x3, Pallas kernels, adam_tiles(): pl.pallas_call(kernel, out_shape=(shape, shape, shape), grid_spec=pltpu.P...  71.9 us
    ppermute x76, starting transfers between devices, swap(): return lax.ppermute(value, axis, [(0, 1), (1, 0)])  66.4 us
    dot_general x8, matrix products, matmul_left(): lax.dot_general(left, right, (((0,), (0,)), ((), ())), preferred_element_...  53.8 us
    dot_general x10, matrix products, matmul(): return jnp.dot(left, right, preferred_element_type=f32)  48.9 us
    dot_general x6, matrix products, matmul_right(): lax.dot_general(left, right, (((1,), (1,)), ((), ())), preferred_element_...  39.3 us
    unnamed x162, local copies, waits for them, and re-layouts  31.1 us
    cond x41, local copies, waits for them, and re-layouts  30.8 us
  transfers between devices with their start and end apart: 97, of which 54 were waited for; matrix products, arithmetic and copies ran while one was open for 38% of the time, Pallas kernels for 6%

profile of v16, /device:TPU:0, one launch (start us, length us, event | category | flops | bytes accessed | tf_op | source)
XLA Modules:
  0.0 1019.1 jit_solution(14595067715589719117)
XLA Ops:
  188.2 11.8 %all-to-all-done.1 = bf16[8,3,256,256]{3,2,1,0:T(8,128)(2,1)} async-done(((bf16[8,3,256,256]{3,2,1,0:T(8,128)(2,1)}), bf16[8,3,256,256]{3,2,1,0:T(8,128)(2,1)}, u32[]{:S(2)}, u32[]{:S(2)}) %all-to-all-start.1) | async-done | bytes 3145760 | tf_op jit(solution)/shard_map/all_to_all | solution.py:399
  218.3 82.0 %conditional.13 = (f32[128,2048]{1,0:T(8,128)S(1)}, bf16[256,2048]{1,0:T(8,128)(2,1)}) conditional(s32[]{:T(128)} %bitcast.74, () %tuple.121, (f32[1024,2048]{1,0:T(8,128)S(1)}, bf16[256,2048]{1,0:T(8,128)(2,1)S(1)}) %tuple.328), branch_computations={%region_12.13_spmd, %region_13.14_spmd} | conditional | flops 2883584 | bytes 69730560 | solution.py:353
  231.2 41.3 %collective-permute-done.31 = bf16[2,128,1024]{2,1,0:T(8,128)(2,1)S(1)} collective-permute-done((bf16[2,128,1024]{2,1,0:T(8,128)(2,1)S(1)}, bf16[2,128,1024]{2,1,0:T(8,128)(2,1)S(1)}, u32[]{:S(2)}, u32[]{:S(2)}) %collective-permute-start.31) | collective-permute-done | bytes 524320 | tf_op jit(solution)/shard_map/cond/branch_1_fun/ppermute | solution.py:241
  280.2 19.9 %collective-permute-done.34 = bf16[128,1024]{1,0:T(8,128)(2,1)S(1)} collective-permute-done((bf16[128,1024]{1,0:T(8,128)(2,1)S(1)}, bf16[128,1024]{1,0:T(8,128)(2,1)S(1)}, u32[]{:S(2)}, u32[]{:S(2)}) %collective-permute-start.34) | collective-permute-done | bytes 262176 | tf_op jit(solution)/shard_map/cond/branch_1_fun/ppermute | solution.py:241
  307.4 59.4 %conditional.14 = (bf16[1024,2048]{1,0:T(8,128)(2,1)}, bf16[1024,4096]{1,0:T(8,128)(2,1)}, bf16[1024,4096]{1,0:T(8,128)(2,1)}) conditional(s32[]{:T(128)} %bitcast.74, () %tuple.141, (bf16[128,2048]{1,0:T(8,128)(2,1)S(1)}, bf16[256,4096]{1,0:T(8,128)(2,1)}, bf16[256,4096]{1,0:T(8,128)(2,1)}, bf16[256,4096]{1,0:T(8,128)(2,1)S(1)}) %tuple.327), branch_computations={%region_15.16_spmd, %region_16.17_spmd} | conditional | bytes 89129304 | solution.py:353
  320.2 13.6 %collective-permute-done.8 = bf16[128,4096]{1,0:T(8,128)(2,1)S(1)} collective-permute-done((bf16[128,4096]{1,0:T(8,128)(2,1)S(1)}, bf16[128,4096]{1,0:T(8,128)(2,1)S(1)}, u32[]{:S(2)}, u32[]{:S(2)}) %collective-permute-start.8) | collective-permute-done | bytes 1048608 | tf_op jit(solution)/shard_map/cond/branch_1_fun/ppermute | solution.py:241
  339.2 11.4 %collective-permute-done.3 = bf16[128,2048]{1,0:T(8,128)(2,1)S(1)} collective-permute-done((bf16[128,2048]{1,0:T(8,128)(2,1)S(1)}, bf16[128,2048]{1,0:T(8,128)(2,1)S(1)}, u32[]{:S(2)}, u32[]{:S(2)}) %collective-permute-start.3) | collective-permute-done | bytes 524320 | tf_op jit(solution)/shard_map/cond/branch_1_fun/ppermute | solution.py:241
  403.7 39.8 %conditional.15 = (f32[128,2048]{1,0:T(8,128)S(1)}, bf16[2048,4096]{1,0:T(8,128)(2,1)}) conditional(s32[]{:T(128)} %bitcast.74, () %tuple.140, (f32[1024,2048]{1,0:T(8,128)S(1)}, bf16[1024,4096]{1,0:T(8,128)(2,1)}, bf16[1024,4096]{1,0:T(8,128)(2,1)}) %tuple.144), branch_computations={%region_19.20_spmd, %region_20.21_spmd} | conditional | flops 36438016 | bytes 99090648 | solution.py:353
  415.1 12.2 %collective-permute-done.37 = bf16[2,128,1024]{2,1,0:T(8,128)(2,1)S(1)} collective-permute-done((bf16[2,128,1024]{2,1,0:T(8,128)(2,1)S(1)}, bf16[2,128,1024]{2,1,0:T(8,128)(2,1)S(1)}, u32[]{:S(2)}, u32[]{:S(2)}) %collective-permute-start.37) | collective-permute-done | bytes 524320 | tf_op jit(solution)/shard_map/cond/branch_1_fun/ppermute | solution.py:241
  429.5 13.7 %pad_maximum_fusion.1 = bf16[2048,4096]{1,0:T(8,128)(2,1)} fusion(bf16[1024,4096]{1,0:T(8,128)(2,1)} %get-tuple-element.110, bf16[1024,4096]{1,0:T(8,128)(2,1)} %get-tuple-element.109), kind=kLoop, calls=%fused_computation.35 | loop fusion | flops 33554432 | bytes 33554432 | tf_op jit(solution)/shard_map/cond/branch_1_fun/concatenate | solution.py:493
  446.0 26.7 %conditional.16 = (bf16[1024,2048]{1,0:T(8,128)(2,1)}) conditional(s32[]{:T(128)} %bitcast.74, () %tuple.146, bf16[128,2048]{1,0:T(8,128)(2,1)S(1)} %get-tuple-element.323), branch_computations={%region_22.23_spmd, %region_23.24_spmd} | conditional | bytes 26214608 | solution.py:353
  491.1 11.1 %fusion.55 = bf16[1024,1024]{1,0:T(8,128)(2,1)S(1)} fusion(f32[1024,1024]{1,0:T(8,128)} %copy-done.76, bf16[1024,2048]{1,0:T(8,128)(2,1)} %constant_dynamic-update-slice_fusion.65, bf16[1024,2048]{1,0:T(8,128)(2,1)} %all-gather.14.cloned.1.call-done), kind=kOutput, calls=%fused_computation.194 | convolution fusion | flops 4320133120 | bytes 14680064 | tf_op jit(solution)/shard_map/dot_general | solution.py:48
  526.5 53.0 %conditional.17 = (f32[128,2048]{1,0:T(8,128)S(1)}, f32[128,2048]{1,0:T(8,128)S(1)}) conditional(s32[]{:T(128)} %bitcast.74, () %tuple.145, (f32[1024,2048]{1,0:T(8,128)S(1)}, f32[1024,2048]{1,0:T(8,128)}) %tuple.149), branch_computations={%region_24.25_spmd, %region_25.26_spmd} | conditional | flops 5767168 | bytes 131072416 | solution.py:353
  582.5 27.0 %conditional.18 = (bf16[1024,2048]{1,0:T(8,128)(2,1)}) conditional(s32[]{:T(128)} %bitcast.74, () %tuple.152, bf16[128,2048]{1,0:T(8,128)(2,1)} %get-tuple-element.233), branch_computations={%region_27.28_spmd, %region_28.29_spmd} | conditional | bytes 26214608 | solution.py:353
  609.5 30.5 %conditional.19 = (bf16[1024,256]{0,1:T(8,128)(2,1)}, bf16[2048,256]{0,1:T(8,128)(2,1)}, bf16[2048,256]{0,1:T(8,128)(2,1)}, bf16[2,256,2048]{2,1,0:T(8,128)(2,1)}) conditional(s32[]{:T(128)} %bitcast.74, () %tuple.151, (bf16[1024,2048]{1,0:T(8,128)(2,1)}, bf16[256,2048]{1,0:T(8,128)(2,1)}, bf16[8,256,2,128]{3,2,1,0:T(2,128)(2,1)}, ...), branch_computations={%region_30.31_spmd, %region_31.33_spmd} | conditional | flops 1616640000 | bytes 62406868 | solution.py:353
  678.0 35.8 %conditional.20 = (f32[128,2048]{1,0:T(8,128)}) conditional(s32[]{:T(128)} %bitcast.74, () %tuple.150, f32[1024,2048]{1,0:T(8,128)} %fusion.119), branch_computations={%region_33.34_spmd, %region_34.35_spmd} | conditional | flops 2883584 | bytes 65536208 | solution.py:353
  692.0 12.3 %collective-permute-done.52 = bf16[2,128,1024]{2,1,0:T(8,128)(2,1)S(1)} collective-permute-done((bf16[2,128,1024]{2,1,0:T(8,128)(2,1)S(1)}, bf16[2,128,1024]{2,1,0:T(8,128)(2,1)S(1)}, u32[]{:S(2)}, u32[]{:S(2)}) %collective-permute-start.52) | collective-permute-done | bytes 524320 | tf_op jit(solution)/shard_map/cond/branch_1_fun/ppermute | solution.py:241
  718.5 26.8 %conditional.21 = (bf16[1024,2048]{1,0:T(8,128)(2,1)}) conditional(s32[]{:T(128)} %bitcast.74, () %tuple.156, bf16[128,2048]{1,0:T(8,128)(2,1)} %get-tuple-element.238), branch_computations={%region_37.38_spmd, %region_38.39_spmd} | conditional | bytes 26214608 | solution.py:353
  796.6 103.9 %conditional.22 = (f32[128,2048]{1,0:T(8,128)}, f32[3,2048]{1,0:T(4,128)S(1)}, bf16[4,256,2048]{2,1,0:T(8,128)(2,1)}) conditional(s32[]{:T(128)} %bitcast.74, () %tuple.155, (f32[1024,2048]{1,0:T(8,128)S(1)}, f32[3,2048]{1,0:T(4,128)S(1)}, f32[128,2048]{1,0:T(8,128)S(1)}, f32[128,2048]{1,0:T(8,128)S(1)}, f32[128,2048]{1,0:T(8,128)S(1)}, ...), branch_computations={%region_45.46_spmd, %region_46.50_spmd} | conditional | flops 9767680 | bytes 91698648 | solution.py:353
  812.9 58.7 %collective-permute-done.57 = bf16[2,128,1024]{2,1,0:T(8,128)(2,1)S(1)} collective-permute-done((bf16[2,128,1024]{2,1,0:T(8,128)(2,1)S(1)}, bf16[2,128,1024]{2,1,0:T(8,128)(2,1)S(1)}, u32[]{:S(2)}, u32[]{:S(2)}) %collective-permute-start.57) | collective-permute-done | bytes 524320 | tf_op jit(solution)/shard_map/cond/branch_1_fun/ppermute | solution.py:241
  915.0 70.4 %conditional.23 = (f32[6,256,2048]{2,1,0:T(8,128)}, f32[6,256,2048]{2,1,0:T(8,128)}, f32[6,256,2048]{2,1,0:T(8,128)}, bf16[2,256,2048]{2,1,0:T(8,128)(2,1)}) conditional(s32[]{:T(128)} %bitcast.74, () %tuple.163, (s32[6]{0:T(128)S(1)}, s32[6,8]{1,0:T(8,128)S(1)}, s32[6]{0:T(128)S(1)}, s32[3]{0:T(128)S(1)}, s32[]{:T(128)}, ...), branch_computations={%region_64.65_spmd, %region_65.66_spmd} | conditional | flops 97517568 | bytes 139462016 | solution.py:353
  936.8 24.9 %adam_tiles.3 = (f32[6,256,2048]{2,1,0:T(8,128)}, f32[6,256,2048]{2,1,0:T(8,128)}, f32[6,256,2048]{2,1,0:T(8,128)}) custom-call(s32[3]{0:T(128)S(1)} %get-tuple-element.266.visit_ref, s32[3]{0:T(128)S(1)} %get-tuple-element.396.mode_ref, s32[24]{0:T(128)S(1)} %reshape.384.cp_ref, s32[3]{0:T(128)S(1)} %get-tuple-element.391.rp_ref, ...), custom_call_target="tpu_custom_call" | custom-call | flops 47185920 | bytes 40894464 | tf_op jit(solution)/shard_map/cond/branch_1_fun/adam_tiles/pallas_call | solution.py:211
  961.8 20.5 %adam_tiles.4 = (f32[6,256,2048]{2,1,0:T(8,128)}, f32[6,256,2048]{2,1,0:T(8,128)}, f32[6,256,2048]{2,1,0:T(8,128)}) custom-call(s32[3]{0:T(128)S(1)} %copy-done.7, s32[3]{0:T(128)S(1)} %get-tuple-element.395.mode_ref, s32[24]{0:T(128)S(1)} %reshape.383.cp_ref, ...), custom_call_target="tpu_custom_call", output_to_operand_aliasing={{0}: (10, {}), {1}: (11, {}), {2}: (12, {})} | custom-call | flops 47185920 | bytes 40894464 | tf_op jit(solution)/shard_map/cond/branch_1_fun/adam_tiles/pallas_call | solution.py:211
  985.5 26.5 %adam_tiles.5 = (f32[6,256,2048]{2,1,0:T(8,128)}, f32[6,256,2048]{2,1,0:T(8,128)}, f32[6,256,2048]{2,1,0:T(8,128)}) custom-call(s32[5]{0:T(128)S(1)} %broadcast_select_fusion.7.visit_ref, s32[5]{0:T(128)S(1)} %compare_select_fusion.15.mode_ref, s32[40]{0:T(128)S(1)} %select_n.470.cp_ref, ...), custom_call_target="tpu_custom_call", output_to_operand_aliasing={{0}: (12, {}), {1}: (13, {}), {2}: (14, {})} | custom-call | flops 78643200 | bytes 68157440 | tf_op jit(solution)/shard_map/adam_tiles/pallas_call | solution.py:211
  (695 shorter events, 705.4 us)
Async XLA Ops:
  24.7 49.1 %all-to-all-start = ((bf16[8,3,256,256]{3,2,1,0:T(8,128)(2,1)}), bf16[8,3,256,256]{3,2,1,0:T(8,128)(2,1)S(1)}, u32[]{:S(2)}, u32[]{:S(2)}) async-start(bf16[8,3,256,256]{3,2,1,0:T(8,128)(2,1)} %copy-done), calls=%async_computation | async-start | bytes 6291456 | tf_op jit(solution)/shard_map/all_to_all | solution.py:360
  30.0 133.7 %all-gather.6.cloned.1.call-start = ((), (), s32[]{:S(2)}) async-start(), calls=%async_computation.9 | async-start | bytes 3932160 | tf_op jit(solution)/shard_map/all_gather | solution.py:381
  79.7 135.5 %all-gather.8.cloned.1.call-start = ((), (), s32[]{:S(2)}) async-start(), calls=%async_computation.10 | async-start | bytes 2621440 | tf_op jit(solution)/shard_map/all_gather | solution.py:418
  84.9 44.7 %collective-permute-start.77 = (bf16[2,256,2048]{2,1,0:T(8,128)(2,1)}, bf16[2,256,2048]{2,1,0:T(8,128)(2,1)}, u32[]{:S(2)}, u32[]{:S(2)}) collective-permute-start(bf16[2,256,2048]{2,1,0:T(8,128)(2,1)} %pad_maximum_fusion.12), channel_id=1, source_target_pairs={{0,1},{1,0},{2,3},{3,2},{4,5},{5,4},{6,7},{7,6},{8,9},{9,8},{10,11... | collective-permute-start | bytes 6291464 | tf_op jit(solution)/shard_map/ppermute | solution.py:241
  158.2 41.7 %all-to-all-start.1 = ((bf16[8,3,256,256]{3,2,1,0:T(8,128)(2,1)}), bf16[8,3,256,256]{3,2,1,0:T(8,128)(2,1)}, u32[]{:S(2)}, u32[]{:S(2)}) async-start(bf16[8,3,256,256]{3,2,1,0:T(8,128)(2,1)} %copy-done.1), calls=%async_computation.1 | async-start | bytes 6291456 | tf_op jit(solution)/shard_map/all_to_all | solution.py:399
  162.7 204.1 %all-gather.10.cloned.1.call-start = ((), (), s32[]{:S(2)}) async-start(), calls=%async_computation.11 | async-start | bytes 6553600 | tf_op jit(solution)/shard_map/all_gather | solution.py:381
  203.2 269.5 %all-gather.12.cloned.1.call-start = ((), (), s32[]{:S(2)}) async-start(), calls=%async_computation.12 | async-start | bytes 5242880 | tf_op jit(solution)/shard_map/all_gather | solution.py:381
  207.4 283.8 %all-gather.14.cloned.1.call-start = ((), (), s32[]{:S(2)}) async-start(), calls=%async_computation.13 | async-start | bytes 5242880 | tf_op jit(solution)/shard_map/all_gather | solution.py:381
  212.6 94.9 %collective-permute-start.81 = (bf16[256,4096]{1,0:T(8,128)(2,1)}, bf16[256,4096]{1,0:T(8,128)(2,1)}, u32[]{:S(2)}, u32[]{:S(2)}) collective-permute-start(bf16[256,4096]{1,0:T(8,128)(2,1)} %bitcast.392), channel_id=1, source_target_pairs={{0,2},{2,0},{1,3},{3,1},{4,6},{6,4},{5,7},{7,5},{8,10},{10,8},{9,1... | collective-permute-start | bytes 6291464 | tf_op jit(solution)/shard_map/ppermute | solution.py:241
  214.6 92.8 %collective-permute-start.82 = (bf16[256,4096]{1,0:T(8,128)(2,1)}, bf16[256,4096]{1,0:T(8,128)(2,1)}, u32[]{:S(2)}, u32[]{:S(2)}) collective-permute-start(bf16[256,4096]{1,0:T(8,128)(2,1)} %bitcast.393), channel_id=1, source_target_pairs={{0,4},{4,0},{1,5},{5,1},{2,6},{6,2},{3,7},{7,3},{8,12},{12,8},{9,1... | collective-permute-start | bytes 6291464 | tf_op jit(solution)/shard_map/ppermute | solution.py:241
  227.5 45.1 %collective-permute-start.31 = (bf16[2,128,1024]{2,1,0:T(8,128)(2,1)S(1)}, bf16[2,128,1024]{2,1,0:T(8,128)(2,1)S(1)}, u32[]{:S(2)}, u32[]{:S(2)}) collective-permute-start(bf16[2,128,1024]{2,1,0:T(8,128)(2,1)S(1)} %slice_bitcast_fusion.5), channel_id=1, source_target_pairs={{0,2},{2,0},{1,3},{3,1},{4,6},{6,4},{5,7},{7,5},{8,10},{10,8},{9,1... | collective-permute-start | bytes 1572872 | tf_op jit(solution)/shard_map/cond/branch_1_fun/ppermute | solution.py:241
  228.3 71.9 %collective-permute-start.35 = (bf16[256,2048]{1,0:T(8,128)(2,1)S(1)}, bf16[256,2048]{1,0:T(8,128)(2,1)}, u32[]{:S(2)}, u32[]{:S(2)}) collective-permute-start(bf16[256,2048]{1,0:T(8,128)(2,1)S(1)} %get-tuple-element.103), channel_id=1, source_target_pairs={{0,2},{2,0},{1,3},{3,1},{4,6},{6,4},{5,7},{7,5},{8,10},{10,8},{9,1... | collective-permute-start | bytes 3145736 | tf_op jit(solution)/shard_map/cond/branch_1_fun/ppermute | solution.py:241
  229.6 44.5 %collective-permute-start.33 = (bf16[2,128,1024]{2,1,0:T(8,128)(2,1)S(1)}, bf16[2,128,1024]{2,1,0:T(8,128)(2,1)S(1)}, u32[]{:S(2)}, u32[]{:S(2)}) collective-permute-start(bf16[2,128,1024]{2,1,0:T(8,128)(2,1)S(1)} %slice_bitcast_fusion.3), channel_id=1, source_target_pairs={{0,4},{4,0},{1,5},{5,1},{2,6},{6,2},{3,7},{7,3},{8,12},{12,8},{9,1... | collective-permute-start | bytes 1572872 | tf_op jit(solution)/shard_map/cond/branch_1_fun/ppermute | solution.py:241
  303.0 306.4 %reduce-scatter.6.cloned.1.call-start = ((), (), s32[]{:S(2)}) async-start(), calls=%async_computation.14 | async-start | bytes 5242880 | tf_op jit(solution)/shard_map/reduce_scatter | solution.py:507
  490.9 227.7 %reduce-scatter.8.cloned.1.call-start = ((), (), s32[]{:S(2)}) async-start(), calls=%async_computation.15 | async-start | bytes 5242880 | tf_op jit(solution)/shard_map/reduce_scatter | solution.py:507
  512.0 266.8 %reduce-scatter.10.cloned.1.call-start = ((), (), s32[]{:S(2)}) async-start(), calls=%async_computation.16 | async-start | bytes 6553600 | tf_op jit(solution)/shard_map/reduce_scatter | solution.py:507
  666.2 234.4 %reduce-scatter.12.cloned.1.call-start = ((), (), s32[]{:S(2)}) async-start(), calls=%async_computation.17 | async-start | bytes 3932160 | tf_op jit(solution)/shard_map/reduce_scatter | solution.py:507
  785.0 117.8 %all-to-all-start.2 = ((bf16[8,6,256,256]{3,2,1,0:T(8,128)(2,1)}), bf16[8,6,256,256]{3,2,1,0:T(8,128)(2,1)}, u32[]{:S(2)}, u32[]{:S(2)}) async-start(bf16[8,6,256,256]{3,2,1,0:T(8,128)(2,1)} %pack_gradients.1), calls=%async_computation.5 | async-start | bytes 12582912 | tf_op jit(solution)/shard_map/all_to_all | solution.py:584
  789.8 125.2 %reduce-scatter.14.cloned.1.call-start = ((), (), s32[]{:S(2)}) async-start(), calls=%async_computation.18 | async-start | bytes 2621440 | tf_op jit(solution)/shard_map/reduce_scatter | solution.py:507
  798.2 89.4 %collective-permute-start.66 = (bf16[2,256,2048]{2,1,0:T(8,128)(2,1)}, bf16[2,256,2048]{2,1,0:T(8,128)(2,1)S(1)}, u32[]{:S(2)}, u32[]{:S(2)}) collective-permute-start(bf16[2,256,2048]{2,1,0:T(8,128)(2,1)} %get-tuple-element.126), channel_id=1, source_target_pairs={{0,1},{1,0},{2,3},{3,2},{4,5},{5,4},{6,7},{7,6},{8,9},{9,8},{10,11... | collective-permute-start | bytes 6291464 | tf_op jit(solution)/shard_map/cond/branch_1_fun/ppermute | solution.py:241
  808.8 62.8 %collective-permute-start.57 = (bf16[2,128,1024]{2,1,0:T(8,128)(2,1)S(1)}, bf16[2,128,1024]{2,1,0:T(8,128)(2,1)S(1)}, u32[]{:S(2)}, u32[]{:S(2)}) collective-permute-start(bf16[2,128,1024]{2,1,0:T(8,128)(2,1)S(1)} %slice_bitcast_fusion.35), channel_id=1, source_target_pairs={{0,2},{2,0},{1,3},{3,1},{4,6},{6,4},{5,7},{7,5},{8,10},{10,8},{9,1... | collective-permute-start | bytes 1572872 | tf_op jit(solution)/shard_map/cond/branch_1_fun/ppermute | solution.py:241
  811.3 62.0 %collective-permute-start.59 = (bf16[2,128,1024]{2,1,0:T(8,128)(2,1)S(1)}, bf16[2,128,1024]{2,1,0:T(8,128)(2,1)S(1)}, u32[]{:S(2)}, u32[]{:S(2)}) collective-permute-start(bf16[2,128,1024]{2,1,0:T(8,128)(2,1)S(1)} %slice_bitcast_fusion.33), channel_id=1, source_target_pairs={{0,4},{4,0},{1,5},{5,1},{2,6},{6,2},{3,7},{7,3},{8,12},{12,8},{9,1... | collective-permute-start | bytes 1572872 | tf_op jit(solution)/shard_map/cond/branch_1_fun/ppermute | solution.py:241
  904.9 80.6 %all-to-all-start.3 = ((bf16[8,3,256,256]{3,2,1,0:T(8,128)(2,1)}), bf16[8,3,256,256]{3,2,1,0:T(8,128)(2,1)S(1)}, u32[]{:S(2)}, u32[]{:S(2)}) async-start(bf16[8,3,256,256]{3,2,1,0:T(8,128)(2,1)} %bitcast.375), calls=%async_computation.7 | async-start | bytes 6291456 | tf_op jit(solution)/shard_map/all_to_all | solution.py:598
  934.7 47.7 %collective-permute-start.28 = (bf16[256,2048]{1,0:T(8,128)(2,1)}, bf16[256,2048]{1,0:T(8,128)(2,1)}, u32[]{:S(2)}, u32[]{:S(2)}) collective-permute-start(bf16[256,2048]{1,0:T(8,128)(2,1)} %broadcast_select_fusion), channel_id=1, source_target_pairs={{0,2},{1,3},{2,0},{3,1},{4,6},{5,7},{6,4},{7,5},{8,10},{9,11},{10,... | collective-permute-start | bytes 3145736 | tf_op jit(solution)/shard_map/cond/branch_1_fun/ppermute | solution.py:511
  (157 other events, 2205.0 us)
Sparse Core Ops, SparseCore 0:
  79.8 63.7 all-gather.5
  158.4 48.0 all-gather.7
  208.0 96.7 all-gather.9
  306.2 79.1 all-gather.11
  386.8 79.2 all-gather.13
  491.0 78.4 reduce-scatter.5
  571.9 77.2 reduce-scatter.7
  666.3 94.4 reduce-scatter.9
  778.4 61.5 reduce-scatter.11
  842.1 43.8 reduce-scatter.13

commit v17 on v16

--- a/solution.py
+++ b/solution.py
@@ -455,11 +455,7 @@
     slots, ctx_len, ctx_width = context.shape
     ctx = after(context.reshape(slots * ctx_len, ctx_width), local_cross, local_in)
     ctx_x, ctx_y = swap(ctx, "x"), swap(ctx, "y")
-    h1, over_y = chain_step(
-        lambda one, two: (scatter_rows(one), swap(two, "y")), matmul(after(attended, local_in), w_self_out), out_across
-    )
-    h1 = h0 + h1
-    w_out = gather_z(mine_or_over_y(1, out_mine, over_y))
+    h1 = h0 + chain_step(scatter_rows, matmul(after(attended, local_in), w_self_out))
 
     def second_step(one, own, over_x, over_y):
         half = over_x.shape[0] // 2
@@ -472,15 +468,16 @@
     )
 
     w_cross_q = w_cross[:, :block]
-    w_low = w_cross[:, block : 3 * block]
-    w_high = w_cross[:, 3 * block :]
-    ctx_kv = jnp.concatenate(
-        [
-            (matmul(part[:, :width], w_low) + matmul(part[:, width:], w_high)).astype(bf16)
-            for part in (ctx_here, ctx_there)
-        ],
-        axis=0,
-    )
+
+    def keys_step(here, there, weights, moved):
+        w_low, w_high = weights[:, block : 3 * block], weights[:, 3 * block :]
+        parts = [
+            (matmul(part[:, :width], w_low) + matmul(part[:, width:], w_high)).astype(bf16) for part in (here, there)
+        ]
+        return jnp.concatenate(parts, axis=0), swap(moved, "y")
+
+    ctx_kv, over_y = chain_step(keys_step, ctx_here, ctx_there, w_cross, out_across)
+    w_out = gather_z(mine_or_over_y(1, out_mine, over_y))
     cross_q = matmul(b_all, w_cross_q)
     cross_q = split(cross_q.astype(bf16))
     cross_k, cross_v = split(ctx_kv[:, :block]), split(ctx_kv[:, block:])

time: 1030 us -> 1020 us (level)
  waiting for transfers between devices: 366 us -> 337 us
  local copies, waits for them, and re-layouts: 151 us -> 163 us
    ppermute x76, waiting for transfers between devices: 335 us -> 306 us  [swap(): return lax.ppermute(value, axis, [(0, 1), (1, 0)])]
    cond x41 -> x49, local copies, waits for them, and re-layouts: 30.8 us -> 36.8 us
    unnamed x162 -> x154, local copies, waits for them, and re-layouts: 31.1 us -> 31.8 us
  transfers between devices with their start and end apart: 97 -> 97, of which waited for: 54 -> 53; matrix products, arithmetic and copies ran while one was open for 38% -> 40% of each run, Pallas kernels for 6% -> 6%
where the time goes in v17:
time: 1020 us; the launch traced here: 1000 us
  waiting for transfers between devices  337 us (33%)
  matrix products  170 us (17%)
  local copies, waits for them, and re-layouts  163 us (16%)
  other arithmetic  102 us (10%)
  starting transfers between devices  98.8 us (10%)
  Pallas kernels  84.3 us (8%)
  between operations  43.6 us (4%)
    ppermute x76, waiting for transfers between devices, swap(): return lax.ppermute(value, axis, [(0, 1), (1, 0)])  306 us
    ppermute x76, starting transfers between devices, swap(): return lax.ppermute(value, axis, [(0, 1), (1, 0)])  63.1 us
    pallas_call x3, Pallas kernels, adam_tiles(): pl.pallas_call(kernel, out_shape=(shape, shape, shape), grid_spec=pltpu.P...  61.8 us
    dot_general x8, matrix products, matmul_left(): lax.dot_general(left, right, (((0,), (0,)), ((), ())), preferred_element_...  53.7 us
    dot_general x10, matrix products, matmul(): return jnp.dot(left, right, preferred_element_type=f32)  53.1 us
    dot_general x6, matrix products, matmul_right(): lax.dot_general(left, right, (((1,), (1,)), ((), ())), preferred_element_...  39.6 us
    unnamed x154, local copies, waits for them, and re-layouts  31.8 us
    cond x47, local copies, waits for them, and re-layouts  30.7 us
  transfers between devices with their start and end apart: 97, of which 53 were waited for; matrix products, arithmetic and copies ran while one was open for 40% of the time, Pallas kernels for 6%

profile of v17, /device:TPU:0, one launch (start us, length us, event | category | flops | bytes accessed | tf_op | source)
XLA Modules:
  0.0 1000.4 jit_solution(13392950302829000588)
XLA Ops:
  188.5 11.7 %all-to-all-done.1 = bf16[8,3,256,256]{3,2,1,0:T(8,128)(2,1)} async-done(((bf16[8,3,256,256]{3,2,1,0:T(8,128)(2,1)}), bf16[8,3,256,256]{3,2,1,0:T(8,128)(2,1)}, u32[]{:S(2)}, u32[]{:S(2)}) %all-to-all-start.1) | async-done | bytes 3145760 | tf_op jit(solution)/shard_map/all_to_all | solution.py:399
  224.2 53.6 %conditional.14 = (f32[128,2048]{1,0:T(8,128)S(1)}) conditional(s32[]{:T(128)} %bitcast.74, () %tuple.129, f32[1024,2048]{1,0:T(8,128)} %fusion.133), branch_computations={%region_12.13_spmd, %region_13.14_spmd} | conditional | flops 2883584 | bytes 65536208 | solution.py:353
  238.9 31.0 %collective-permute-done.32 = bf16[2,128,1024]{2,1,0:T(8,128)(2,1)S(1)} collective-permute-done((bf16[2,128,1024]{2,1,0:T(8,128)(2,1)S(1)}, bf16[2,128,1024]{2,1,0:T(8,128)(2,1)S(1)}, u32[]{:S(2)}, u32[]{:S(2)}) %collective-permute-start.32) | collective-permute-done | bytes 524320 | tf_op jit(solution)/shard_map/cond/branch_1_fun/ppermute | solution.py:241
  280.2 58.1 %conditional.15 = (bf16[1024,2048]{1,0:T(8,128)(2,1)}, bf16[1024,4096]{1,0:T(8,128)(2,1)}, bf16[1024,4096]{1,0:T(8,128)(2,1)}) conditional(s32[]{:T(128)} %bitcast.74, () %tuple.149, (bf16[128,2048]{1,0:T(8,128)(2,1)S(1)}, bf16[256,4096]{1,0:T(8,128)(2,1)}, bf16[256,4096]{1,0:T(8,128)(2,1)}, bf16[256,4096]{1,0:T(8,128)(2,1)S(1)}) %tuple.342), branch_computations={%region_15.16_spmd, %region_16.17_spmd} | conditional | bytes 89129304 | solution.py:353
  293.5 11.5 %collective-permute-done.8 = bf16[128,4096]{1,0:T(8,128)(2,1)S(1)} collective-permute-done((bf16[128,4096]{1,0:T(8,128)(2,1)S(1)}, bf16[128,4096]{1,0:T(8,128)(2,1)S(1)}, u32[]{:S(2)}, u32[]{:S(2)}) %collective-permute-start.8) | collective-permute-done | bytes 1048608 | tf_op jit(solution)/shard_map/cond/branch_1_fun/ppermute | solution.py:241
  310.9 12.1 %collective-permute-done.3 = bf16[128,2048]{1,0:T(8,128)(2,1)S(1)} collective-permute-done((bf16[128,2048]{1,0:T(8,128)(2,1)S(1)}, bf16[128,2048]{1,0:T(8,128)(2,1)S(1)}, u32[]{:S(2)}, u32[]{:S(2)}) %collective-permute-start.3) | collective-permute-done | bytes 524320 | tf_op jit(solution)/shard_map/cond/branch_1_fun/ppermute | solution.py:241
  338.3 35.1 %conditional.16 = (bf16[2048,512]{1,0:T(8,128)(2,1)}, bf16[256,2048]{1,0:T(8,128)(2,1)}, bf16[2048,256]{1,0:T(8,128)(2,1)}, bf16[2048,256]{1,0:T(8,128)(2,1)}, b...) conditional(s32[]{:T(128)} %bitcast.74, () %tuple.148, ...), branch_computations={%region_17.18_spmd, %region_18.19_spmd} | conditional | flops 8600420352 | bytes 85983416 | solution.py:353
  395.3 39.9 %conditional.17 = (f32[128,2048]{1,0:T(8,128)S(1)}, bf16[2048,4096]{1,0:T(8,128)(2,1)}) conditional(s32[]{:T(128)} %bitcast.74, () %tuple.147, (f32[1024,2048]{1,0:T(8,128)S(1)}, bf16[1024,4096]{1,0:T(8,128)(2,1)}, bf16[1024,4096]{1,0:T(8,128)(2,1)}) %tuple.153), branch_computations={%region_21.22_spmd, %region_22.23_spmd} | conditional | flops 36438016 | bytes 99090648 | solution.py:353
  406.8 11.7 %collective-permute-done.37 = bf16[2,128,1024]{2,1,0:T(8,128)(2,1)S(1)} collective-permute-done((bf16[2,128,1024]{2,1,0:T(8,128)(2,1)S(1)}, bf16[2,128,1024]{2,1,0:T(8,128)(2,1)S(1)}, u32[]{:S(2)}, u32[]{:S(2)}) %collective-permute-start.37) | collective-permute-done | bytes 524320 | tf_op jit(solution)/shard_map/cond/branch_1_fun/ppermute | solution.py:241
  421.2 13.7 %pad_maximum_fusion.2 = bf16[2048,4096]{1,0:T(8,128)(2,1)} fusion(bf16[1024,4096]{1,0:T(8,128)(2,1)} %get-tuple-element.124, bf16[1024,4096]{1,0:T(8,128)(2,1)} %get-tuple-element.123), kind=kLoop, calls=%fused_computation.56 | loop fusion | flops 33554432 | bytes 33554432 | tf_op jit(solution)/shard_map/cond/branch_1_fun/concatenate | solution.py:490
  437.6 26.7 %conditional.18 = (bf16[1024,2048]{1,0:T(8,128)(2,1)}) conditional(s32[]{:T(128)} %bitcast.74, () %tuple.155, bf16[128,2048]{1,0:T(8,128)(2,1)S(1)} %get-tuple-element.341), branch_computations={%region_24.25_spmd, %region_25.26_spmd} | conditional | bytes 26214608 | solution.py:353
  482.6 11.1 %fusion.77 = bf16[1024,1024]{1,0:T(8,128)(2,1)S(1)} fusion(f32[1024,1024]{1,0:T(8,128)} %copy-done.77, bf16[1024,2048]{1,0:T(8,128)(2,1)} %constant_dynamic-update-slice_fusion.65, bf16[1024,2048]{1,0:T(8,128)(2,1)} %all-gather.14.cloned.1.call-done), kind=kOutput, calls=%fused_computation.215 | convolution fusion | flops 4320133120 | bytes 14680064 | tf_op jit(solution)/shard_map/dot_general | solution.py:48
  518.3 52.3 %conditional.19 = (f32[128,2048]{1,0:T(8,128)S(1)}, f32[128,2048]{1,0:T(8,128)S(1)}) conditional(s32[]{:T(128)} %bitcast.74, () %tuple.154, (f32[1024,2048]{1,0:T(8,128)S(1)}, f32[1024,2048]{1,0:T(8,128)}) %tuple.158), branch_computations={%region_26.27_spmd, %region_27.28_spmd} | conditional | flops 5767168 | bytes 131072416 | solution.py:353
  573.5 27.1 %conditional.20 = (bf16[1024,2048]{1,0:T(8,128)(2,1)}) conditional(s32[]{:T(128)} %bitcast.74, () %tuple.161, bf16[128,2048]{1,0:T(8,128)(2,1)} %get-tuple-element.249), branch_computations={%region_29.30_spmd, %region_30.31_spmd} | conditional | bytes 26214608 | solution.py:353
  600.7 30.2 %conditional.21 = (bf16[1024,256]{0,1:T(8,128)(2,1)}, bf16[2048,256]{0,1:T(8,128)(2,1)}, bf16[2048,256]{0,1:T(8,128)(2,1)}, bf16[2,256,2048]{2,1,0:T(8,128)(2,1)}) conditional(s32[]{:T(128)} %bitcast.74, () %tuple.160, (bf16[1024,2048]{1,0:T(8,128)(2,1)}, bf16[256,2048]{1,0:T(8,128)(2,1)}, bf16[8,256,2,128]{3,2,1,0:T(2,128)(2,1)}, ...), branch_computations={%region_32.33_spmd, %region_33.35_spmd} | conditional | flops 1616640000 | bytes 62406868 | solution.py:353
  669.1 35.9 %conditional.22 = (f32[128,2048]{1,0:T(8,128)}) conditional(s32[]{:T(128)} %bitcast.74, () %tuple.159, f32[1024,2048]{1,0:T(8,128)} %fusion.117), branch_computations={%region_35.36_spmd, %region_36.37_spmd} | conditional | flops 2883584 | bytes 65536208 | solution.py:353
  682.8 12.6 %collective-permute-done.52 = bf16[2,128,1024]{2,1,0:T(8,128)(2,1)S(1)} collective-permute-done((bf16[2,128,1024]{2,1,0:T(8,128)(2,1)S(1)}, bf16[2,128,1024]{2,1,0:T(8,128)(2,1)S(1)}, u32[]{:S(2)}, u32[]{:S(2)}) %collective-permute-start.52) | collective-permute-done | bytes 524320 | tf_op jit(solution)/shard_map/cond/branch_1_fun/ppermute | solution.py:241
  709.6 26.9 %conditional.23 = (bf16[1024,2048]{1,0:T(8,128)(2,1)}) conditional(s32[]{:T(128)} %bitcast.74, () %tuple.165, bf16[128,2048]{1,0:T(8,128)(2,1)} %get-tuple-element.254), branch_computations={%region_39.40_spmd, %region_40.41_spmd} | conditional | bytes 26214608 | solution.py:353
  787.8 104.5 %conditional.24 = (f32[128,2048]{1,0:T(8,128)}, f32[3,2048]{1,0:T(4,128)S(1)}, bf16[4,256,2048]{2,1,0:T(8,128)(2,1)}) conditional(s32[]{:T(128)} %bitcast.74, () %tuple.164, (f32[1024,2048]{1,0:T(8,128)S(1)}, f32[3,2048]{1,0:T(4,128)S(1)}, f32[128,2048]{1,0:T(8,128)S(1)}, f32[128,2048]{1,0:T(8,128)S(1)}, f32[128,2048]{1,0:T(8,128)S(1)}, ...), branch_computations={%region_47.48_spmd, %region_48.52_spmd} | conditional | flops 9767680 | bytes 91698648 | solution.py:353
  804.1 58.6 %collective-permute-done.57 = bf16[2,128,1024]{2,1,0:T(8,128)(2,1)S(1)} collective-permute-done((bf16[2,128,1024]{2,1,0:T(8,128)(2,1)S(1)}, bf16[2,128,1024]{2,1,0:T(8,128)(2,1)S(1)}, u32[]{:S(2)}, u32[]{:S(2)}) %collective-permute-start.57) | collective-permute-done | bytes 524320 | tf_op jit(solution)/shard_map/cond/branch_1_fun/ppermute | solution.py:241
  906.7 68.9 %conditional.25 = (f32[6,256,2048]{2,1,0:T(8,128)}, f32[6,256,2048]{2,1,0:T(8,128)}, f32[6,256,2048]{2,1,0:T(8,128)}, bf16[2,256,2048]{2,1,0:T(8,128)(2,1)}) conditional(s32[]{:T(128)} %bitcast.74, () %tuple.172, (s32[6]{0:T(128)S(1)}, s32[6,8]{1,0:T(8,128)S(1)}, s32[6]{0:T(128)S(1)}, s32[3]{0:T(128)S(1)}, s32[]{:T(128)}, ...), branch_computations={%region_66.67_spmd, %region_67.68_spmd} | conditional | flops 97517568 | bytes 139462016 | solution.py:353
  928.4 24.9 %adam_tiles.3 = (f32[6,256,2048]{2,1,0:T(8,128)}, f32[6,256,2048]{2,1,0:T(8,128)}, f32[6,256,2048]{2,1,0:T(8,128)}) custom-call(s32[3]{0:T(128)S(1)} %get-tuple-element.282.visit_ref, s32[3]{0:T(128)S(1)} %get-tuple-element.416.mode_ref, s32[24]{0:T(128)S(1)} %reshape.392.cp_ref, s32[3]{0:T(128)S(1)} %get-tuple-element.411.rp_ref, ...), custom_call_target="tpu_custom_call" | custom-call | flops 47185920 | bytes 40894464 | tf_op jit(solution)/shard_map/cond/branch_1_fun/adam_tiles/pallas_call | solution.py:211
  953.3 19.3 %adam_tiles.4 = (f32[6,256,2048]{2,1,0:T(8,128)}, f32[6,256,2048]{2,1,0:T(8,128)}, f32[6,256,2048]{2,1,0:T(8,128)}) custom-call(s32[3]{0:T(128)S(1)} %copy-done.7, s32[3]{0:T(128)S(1)} %get-tuple-element.415.mode_ref, s32[24]{0:T(128)S(1)} %reshape.391.cp_ref, ...), custom_call_target="tpu_custom_call", output_to_operand_aliasing={{0}: (10, {}), {1}: (11, {}), {2}: (12, {})} | custom-call | flops 47185920 | bytes 40894464 | tf_op jit(solution)/shard_map/cond/branch_1_fun/adam_tiles/pallas_call | solution.py:211
  975.6 17.7 %adam_tiles.5 = (f32[6,256,2048]{2,1,0:T(8,128)}, f32[6,256,2048]{2,1,0:T(8,128)}, f32[6,256,2048]{2,1,0:T(8,128)}) custom-call(s32[5]{0:T(128)S(1)} %broadcast_select_fusion.7.visit_ref, s32[5]{0:T(128)S(1)} %compare_select_fusion.15.mode_ref, s32[40]{0:T(128)S(1)} %select_n.470.cp_ref, ...), custom_call_target="tpu_custom_call", output_to_operand_aliasing={{0}: (12, {}), {1}: (13, {}), {2}: (14, {})} | custom-call | flops 78643200 | bytes 68157440 | tf_op jit(solution)/shard_map/adam_tiles/pallas_call | solution.py:211
  (696 shorter events, 729.0 us)
Async XLA Ops:
  24.7 49.1 %all-to-all-start = ((bf16[8,3,256,256]{3,2,1,0:T(8,128)(2,1)}), bf16[8,3,256,256]{3,2,1,0:T(8,128)(2,1)S(1)}, u32[]{:S(2)}, u32[]{:S(2)}) async-start(bf16[8,3,256,256]{3,2,1,0:T(8,128)(2,1)} %copy-done), calls=%async_computation | async-start | bytes 6291456 | tf_op jit(solution)/shard_map/all_to_all | solution.py:360
  30.0 134.0 %all-gather.6.cloned.1.call-start = ((), (), s32[]{:S(2)}) async-start(), calls=%async_computation.9 | async-start | bytes 3932160 | tf_op jit(solution)/shard_map/all_gather | solution.py:381
  79.7 138.2 %all-gather.8.cloned.1.call-start = ((), (), s32[]{:S(2)}) async-start(), calls=%async_computation.10 | async-start | bytes 2621440 | tf_op jit(solution)/shard_map/all_gather | solution.py:418
  84.9 45.0 %collective-permute-start.77 = (bf16[2,256,2048]{2,1,0:T(8,128)(2,1)}, bf16[2,256,2048]{2,1,0:T(8,128)(2,1)}, u32[]{:S(2)}, u32[]{:S(2)}) collective-permute-start(bf16[2,256,2048]{2,1,0:T(8,128)(2,1)} %pad_maximum_fusion.13), channel_id=1, source_target_pairs={{0,1},{1,0},{2,3},{3,2},{4,5},{5,4},{6,7},{7,6},{8,9},{9,8},{10,11... | collective-permute-start | bytes 6291464 | tf_op jit(solution)/shard_map/ppermute | solution.py:241
  158.6 41.6 %all-to-all-start.1 = ((bf16[8,3,256,256]{3,2,1,0:T(8,128)(2,1)}), bf16[8,3,256,256]{3,2,1,0:T(8,128)(2,1)}, u32[]{:S(2)}, u32[]{:S(2)}) async-start(bf16[8,3,256,256]{3,2,1,0:T(8,128)(2,1)} %copy-done.1), calls=%async_computation.1 | async-start | bytes 6291456 | tf_op jit(solution)/shard_map/all_to_all | solution.py:399
  163.1 175.3 %all-gather.10.cloned.1.call-start = ((), (), s32[]{:S(2)}) async-start(), calls=%async_computation.11 | async-start | bytes 6553600 | tf_op jit(solution)/shard_map/all_gather | solution.py:381
  205.0 259.3 %all-gather.12.cloned.1.call-start = ((), (), s32[]{:S(2)}) async-start(), calls=%async_computation.12 | async-start | bytes 5242880 | tf_op jit(solution)/shard_map/all_gather | solution.py:381
  210.9 271.7 %all-gather.14.cloned.1.call-start = ((), (), s32[]{:S(2)}) async-start(), calls=%async_computation.13 | async-start | bytes 5242880 | tf_op jit(solution)/shard_map/all_gather | solution.py:381
  210.9 68.4 %collective-permute-start.81 = (bf16[256,4096]{1,0:T(8,128)(2,1)}, bf16[256,4096]{1,0:T(8,128)(2,1)}, u32[]{:S(2)}, u32[]{:S(2)}) collective-permute-start(bf16[256,4096]{1,0:T(8,128)(2,1)} %bitcast.394), channel_id=1, source_target_pairs={{0,2},{2,0},{1,3},{3,1},{4,6},{6,4},{5,7},{7,5},{8,10},{10,8},{9,1... | collective-permute-start | bytes 6291464 | tf_op jit(solution)/shard_map/ppermute | solution.py:241
  212.3 67.1 %collective-permute-start.82 = (bf16[256,4096]{1,0:T(8,128)(2,1)}, bf16[256,4096]{1,0:T(8,128)(2,1)}, u32[]{:S(2)}, u32[]{:S(2)}) collective-permute-start(bf16[256,4096]{1,0:T(8,128)(2,1)} %bitcast.395), channel_id=1, source_target_pairs={{0,4},{4,0},{1,5},{5,1},{2,6},{6,2},{3,7},{7,3},{8,12},{12,8},{9,1... | collective-permute-start | bytes 6291464 | tf_op jit(solution)/shard_map/ppermute | solution.py:241
  236.4 33.5 %collective-permute-start.32 = (bf16[2,128,1024]{2,1,0:T(8,128)(2,1)S(1)}, bf16[2,128,1024]{2,1,0:T(8,128)(2,1)S(1)}, u32[]{:S(2)}, u32[]{:S(2)}) collective-permute-start(bf16[2,128,1024]{2,1,0:T(8,128)(2,1)S(1)} %slice_bitcast_fusion.5), channel_id=1, source_target_pairs={{0,2},{2,0},{1,3},{3,1},{4,6},{6,4},{5,7},{7,5},{8,10},{10,8},{9,1... | collective-permute-start | bytes 1572872 | tf_op jit(solution)/shard_map/cond/branch_1_fun/ppermute | solution.py:241
  237.9 32.9 %collective-permute-start.34 = (bf16[2,128,1024]{2,1,0:T(8,128)(2,1)S(1)}, bf16[2,128,1024]{2,1,0:T(8,128)(2,1)S(1)}, u32[]{:S(2)}, u32[]{:S(2)}) collective-permute-start(bf16[2,128,1024]{2,1,0:T(8,128)(2,1)S(1)} %slice_bitcast_fusion.3), channel_id=1, source_target_pairs={{0,4},{4,0},{1,5},{5,1},{2,6},{6,2},{3,7},{7,3},{8,12},{12,8},{9,1... | collective-permute-start | bytes 1572872 | tf_op jit(solution)/shard_map/cond/branch_1_fun/ppermute | solution.py:241
  338.3 35.1 %collective-permute-start.11 = (bf16[256,2048]{1,0:T(8,128)(2,1)}, bf16[256,2048]{1,0:T(8,128)(2,1)}, u32[]{:S(2)}, u32[]{:S(2)}) collective-permute-start(bf16[256,2048]{1,0:T(8,128)(2,1)} %get-tuple-element.121), channel_id=1, source_target_pairs={{0,2},{2,0},{1,3},{3,1},{4,6},{6,4},{5,7},{7,5},{8,10},{10,8},{9,1... | collective-permute-start | bytes 3145736 | tf_op jit(solution)/shard_map/cond/branch_1_fun/ppermute | solution.py:241
  376.1 224.5 %reduce-scatter.6.cloned.1.call-start = ((), (), s32[]{:S(2)}) async-start(), calls=%async_computation.14 | async-start | bytes 5242880 | tf_op jit(solution)/shard_map/reduce_scatter | solution.py:504
  482.5 227.1 %reduce-scatter.8.cloned.1.call-start = ((), (), s32[]{:S(2)}) async-start(), calls=%async_computation.15 | async-start | bytes 5242880 | tf_op jit(solution)/shard_map/reduce_scatter | solution.py:504
  503.5 266.5 %reduce-scatter.10.cloned.1.call-start = ((), (), s32[]{:S(2)}) async-start(), calls=%async_computation.16 | async-start | bytes 6553600 | tf_op jit(solution)/shard_map/reduce_scatter | solution.py:504
  657.1 235.2 %reduce-scatter.12.cloned.1.call-start = ((), (), s32[]{:S(2)}) async-start(), calls=%async_computation.17 | async-start | bytes 3932160 | tf_op jit(solution)/shard_map/reduce_scatter | solution.py:504
  776.2 118.3 %all-to-all-start.2 = ((bf16[8,6,256,256]{3,2,1,0:T(8,128)(2,1)}), bf16[8,6,256,256]{3,2,1,0:T(8,128)(2,1)}, u32[]{:S(2)}, u32[]{:S(2)}) async-start(bf16[8,6,256,256]{3,2,1,0:T(8,128)(2,1)} %pack_gradients.1), calls=%async_computation.5 | async-start | bytes 12582912 | tf_op jit(solution)/shard_map/all_to_all | solution.py:581
  781.0 125.7 %reduce-scatter.14.cloned.1.call-start = ((), (), s32[]{:S(2)}) async-start(), calls=%async_computation.18 | async-start | bytes 2621440 | tf_op jit(solution)/shard_map/reduce_scatter | solution.py:504
  789.4 89.4 %collective-permute-start.66 = (bf16[2,256,2048]{2,1,0:T(8,128)(2,1)}, bf16[2,256,2048]{2,1,0:T(8,128)(2,1)S(1)}, u32[]{:S(2)}, u32[]{:S(2)}) collective-permute-start(bf16[2,256,2048]{2,1,0:T(8,128)(2,1)} %get-tuple-element.140), channel_id=1, source_target_pairs={{0,1},{1,0},{2,3},{3,2},{4,5},{5,4},{6,7},{7,6},{8,9},{9,8},{10,11... | collective-permute-start | bytes 6291464 | tf_op jit(solution)/shard_map/cond/branch_1_fun/ppermute | solution.py:241
  800.0 62.7 %collective-permute-start.57 = (bf16[2,128,1024]{2,1,0:T(8,128)(2,1)S(1)}, bf16[2,128,1024]{2,1,0:T(8,128)(2,1)S(1)}, u32[]{:S(2)}, u32[]{:S(2)}) collective-permute-start(bf16[2,128,1024]{2,1,0:T(8,128)(2,1)S(1)} %slice_bitcast_fusion.35), channel_id=1, source_target_pairs={{0,2},{2,0},{1,3},{3,1},{4,6},{6,4},{5,7},{7,5},{8,10},{10,8},{9,1... | collective-permute-start | bytes 1572872 | tf_op jit(solution)/shard_map/cond/branch_1_fun/ppermute | solution.py:241
  802.6 61.9 %collective-permute-start.59 = (bf16[2,128,1024]{2,1,0:T(8,128)(2,1)S(1)}, bf16[2,128,1024]{2,1,0:T(8,128)(2,1)S(1)}, u32[]{:S(2)}, u32[]{:S(2)}) collective-permute-start(bf16[2,128,1024]{2,1,0:T(8,128)(2,1)S(1)} %slice_bitcast_fusion.33), channel_id=1, source_target_pairs={{0,4},{4,0},{1,5},{5,1},{2,6},{6,2},{3,7},{7,3},{8,12},{12,8},{9,1... | collective-permute-start | bytes 1572872 | tf_op jit(solution)/shard_map/cond/branch_1_fun/ppermute | solution.py:241
  896.5 79.1 %all-to-all-start.3 = ((bf16[8,3,256,256]{3,2,1,0:T(8,128)(2,1)}), bf16[8,3,256,256]{3,2,1,0:T(8,128)(2,1)S(1)}, u32[]{:S(2)}, u32[]{:S(2)}) async-start(bf16[8,3,256,256]{3,2,1,0:T(8,128)(2,1)} %bitcast.377), calls=%async_computation.7 | async-start | bytes 6291456 | tf_op jit(solution)/shard_map/all_to_all | solution.py:595
  926.2 46.3 %collective-permute-start.29 = (bf16[256,2048]{1,0:T(8,128)(2,1)}, bf16[256,2048]{1,0:T(8,128)(2,1)}, u32[]{:S(2)}, u32[]{:S(2)}) collective-permute-start(bf16[256,2048]{1,0:T(8,128)(2,1)} %broadcast_select_fusion), channel_id=1, source_target_pairs={{0,2},{1,3},{2,0},{3,1},{4,6},{5,7},{6,4},{7,5},{8,10},{9,11},{10,... | collective-permute-start | bytes 3145736 | tf_op jit(solution)/shard_map/cond/branch_1_fun/ppermute | solution.py:508
  (156 other events, 2151.7 us)
Sparse Core Ops, SparseCore 0:
  79.9 63.7 all-gather.5
  158.7 47.2 all-gather.7
  207.6 96.7 all-gather.9
  305.8 79.1 all-gather.11
  386.4 79.2 all-gather.13
  482.6 77.2 reduce-scatter.5
  562.4 77.2 reduce-scatter.7
  657.2 94.0 reduce-scatter.9
  769.6 61.2 reduce-scatter.11
  833.0 43.8 reduce-scatter.13

commit v18 on v17

--- a/solution.py
+++ b/solution.py
@@ -583,9 +583,9 @@
     def last_step(part, out_pair, gain_grad_one, gain_grad_two):
         part_zero, gain_grad_zero = jax.vjp(normalize, h0, gains[0])[1](scatter_rows(part))
         gain_grads = jnp.stack([gain_grad_zero, gain_grad_one, gain_grad_two])
-        return part_zero, sum_everywhere(gain_grads), with_core(out_pair)
-
-    part_zero, gain_total, out_grads = chain_step(
+        return part_zero, gain_grads, with_core(out_pair)
+
+    part_zero, gain_grads, out_grads = chain_step(
         last_step, matmul_right(after(d_qkv, sent), w_qkv), out_grads, gain_grad_one, gain_grad_two
     )
     grad_tokens = (dh1 + part_zero).astype(bf16)
@@ -604,7 +604,7 @@
     early_mode = jnp.where(my_used == 0, 1, jnp.where(late, 0, jnp.where(my_row == 1, 3, 2)))
     states = (master, moment_one, moment_two)
 
-    def early_step(early_grads, out_grads, half):
+    def early_step(early_grads, out_grads, half, gain_grads):
         other_half = lax.ppermute(half, ALL_AXES, back_swap)
         in_order = jnp.where(odd == 0, jnp.stack([half, other_half]), jnp.stack([other_half, half]))
         in_order = in_order.reshape(rows, width)
@@ -623,9 +623,9 @@
                 np.zeros(half_cap, np.int32),
                 early,
             )
-        return *early, from_y(counts)
-
-    *early, outer_grads = chain_step(early_step, early_grads, out_grads, g_outer)
+        return *early, from_y(counts), sum_everywhere(gain_grads)
+
+    *early, outer_grads, gain_total = chain_step(early_step, early_grads, out_grads, g_outer, gain_grads)
 
     n_late = 5
     order = jnp.sum(jnp.where(slot[None, :] < slot[:, None], late.astype(jnp.int32)[None, :], 0), axis=1)

time: 1020 us -> 1030 us (level); the launches traced: 1000 us -> 1020 us
  waiting for transfers between devices: 337 us -> 363 us
    ppermute x76, waiting for transfers between devices: 306 us -> 331 us  [swap(): return lax.ppermute(value, axis, [(0, 1), (1, 0)])]
    unnamed x154 -> x158, local copies, waits for them, and re-layouts: 31.8 us -> 30.8 us
  transfers between devices with their start and end apart: 97 -> 97, of which waited for: 53 -> 55; matrix products, arithmetic and copies ran while one was open for 40% -> 39% of each run, Pallas kernels for 6% -> 6%
where the time goes in v18:
time: 1030 us; the launch traced here: 1020 us
  waiting for transfers between devices  363 us (35%)
  matrix products  167 us (16%)
  local copies, waits for them, and re-layouts  160 us (16%)
  starting transfers between devices  99.5 us (10%)
  other arithmetic  97.8 us (9%)
  Pallas kernels  89.2 us (9%)
  between operations  43.2 us (4%)
    ppermute x76, waiting for transfers between devices, swap(): return lax.ppermute(value, axis, [(0, 1), (1, 0)])  331 us
    pallas_call x3, Pallas kernels, adam_tiles(): pl.pallas_call(kernel, out_shape=(shape, shape, shape), grid_spec=pltpu.P...  68.3 us
    ppermute x76, starting transfers between devices, swap(): return lax.ppermute(value, axis, [(0, 1), (1, 0)])  64 us
    dot_general x8, matrix products, matmul_left(): lax.dot_general(left, right, (((0,), (0,)), ((), ())), preferred_element_...  53.4 us
    dot_general x10, matrix products, matmul(): return jnp.dot(left, right, preferred_element_type=f32)  53.3 us
    dot_general x6, matrix products, matmul_right(): lax.dot_general(left, right, (((1,), (1,)), ((), ())), preferred_element_...  39.4 us
    unnamed x158, local copies, waits for them, and re-layouts  30.8 us
    cond x47, local copies, waits for them, and re-layouts  29.6 us
  transfers between devices with their start and end apart: 97, of which 55 were waited for; matrix products, arithmetic and copies ran while one was open for 39% of the time, Pallas kernels for 6%

profile of v18, /device:TPU:0, one launch (start us, length us, event | category | flops | bytes accessed | tf_op | source)
XLA Modules:
  0.0 1021.0 jit_solution(10786141807562013063)
XLA Ops:
  188.5 11.7 %all-to-all-done.1 = bf16[8,3,256,256]{3,2,1,0:T(8,128)(2,1)} async-done(((bf16[8,3,256,256]{3,2,1,0:T(8,128)(2,1)}), bf16[8,3,256,256]{3,2,1,0:T(8,128)(2,1)}, u32[]{:S(2)}, u32[]{:S(2)}) %all-to-all-start.1) | async-done | bytes 3145760 | tf_op jit(solution)/shard_map/all_to_all | solution.py:399
  222.6 53.6 %conditional.14 = (f32[128,2048]{1,0:T(8,128)S(1)}) conditional(s32[]{:T(128)} %bitcast.74, () %tuple.129, f32[1024,2048]{1,0:T(8,128)} %fusion.132), branch_computations={%region_12.13_spmd, %region_13.14_spmd} | conditional | flops 2883584 | bytes 65536208 | solution.py:353
  237.2 31.0 %collective-permute-done.37 = bf16[2,128,1024]{2,1,0:T(8,128)(2,1)S(1)} collective-permute-done((bf16[2,128,1024]{2,1,0:T(8,128)(2,1)S(1)}, bf16[2,128,1024]{2,1,0:T(8,128)(2,1)S(1)}, u32[]{:S(2)}, u32[]{:S(2)}) %collective-permute-start.37) | collective-permute-done | bytes 524320 | tf_op jit(solution)/shard_map/cond/branch_1_fun/ppermute | solution.py:241
  278.6 57.9 %conditional.15 = (bf16[1024,2048]{1,0:T(8,128)(2,1)}, bf16[1024,4096]{1,0:T(8,128)(2,1)}, bf16[1024,4096]{1,0:T(8,128)(2,1)}) conditional(s32[]{:T(128)} %bitcast.74, () %tuple.149, (bf16[128,2048]{1,0:T(8,128)(2,1)S(1)}, bf16[256,4096]{1,0:T(8,128)(2,1)}, bf16[256,4096]{1,0:T(8,128)(2,1)}, bf16[256,4096]{1,0:T(8,128)(2,1)S(1)}) %tuple.342), branch_computations={%region_15.16_spmd, %region_16.17_spmd} | conditional | bytes 89129304 | solution.py:353
  291.8 11.3 %collective-permute-done.8 = bf16[128,4096]{1,0:T(8,128)(2,1)S(1)} collective-permute-done((bf16[128,4096]{1,0:T(8,128)(2,1)S(1)}, bf16[128,4096]{1,0:T(8,128)(2,1)S(1)}, u32[]{:S(2)}, u32[]{:S(2)}) %collective-permute-start.8) | collective-permute-done | bytes 1048608 | tf_op jit(solution)/shard_map/cond/branch_1_fun/ppermute | solution.py:241
  309.1 12.1 %collective-permute-done.3 = bf16[128,2048]{1,0:T(8,128)(2,1)S(1)} collective-permute-done((bf16[128,2048]{1,0:T(8,128)(2,1)S(1)}, bf16[128,2048]{1,0:T(8,128)(2,1)S(1)}, u32[]{:S(2)}, u32[]{:S(2)}) %collective-permute-start.3) | collective-permute-done | bytes 524320 | tf_op jit(solution)/shard_map/cond/branch_1_fun/ppermute | solution.py:241
  336.5 35.3 %conditional.16 = (bf16[2048,512]{1,0:T(8,128)(2,1)}, bf16[256,2048]{1,0:T(8,128)(2,1)}, bf16[2048,256]{1,0:T(8,128)(2,1)}, bf16[2048,256]{1,0:T(8,128)(2,1)}, b...) conditional(s32[]{:T(128)} %bitcast.74, () %tuple.148, ...), branch_computations={%region_17.18_spmd, %region_18.19_spmd} | conditional | flops 8600420352 | bytes 85983416 | solution.py:353
  393.5 39.8 %conditional.17 = (f32[128,2048]{1,0:T(8,128)S(1)}, bf16[2048,4096]{1,0:T(8,128)(2,1)}) conditional(s32[]{:T(128)} %bitcast.74, () %tuple.147, (f32[1024,2048]{1,0:T(8,128)S(1)}, bf16[1024,4096]{1,0:T(8,128)(2,1)}, bf16[1024,4096]{1,0:T(8,128)(2,1)}) %tuple.153), branch_computations={%region_21.22_spmd, %region_22.23_spmd} | conditional | flops 36438016 | bytes 99090648 | solution.py:353
  404.9 11.8 %collective-permute-done.42 = bf16[2,128,1024]{2,1,0:T(8,128)(2,1)S(1)} collective-permute-done((bf16[2,128,1024]{2,1,0:T(8,128)(2,1)S(1)}, bf16[2,128,1024]{2,1,0:T(8,128)(2,1)S(1)}, u32[]{:S(2)}, u32[]{:S(2)}) %collective-permute-start.42) | collective-permute-done | bytes 524320 | tf_op jit(solution)/shard_map/cond/branch_1_fun/ppermute | solution.py:241
  419.4 13.7 %pad_maximum_fusion.2 = bf16[2048,4096]{1,0:T(8,128)(2,1)} fusion(bf16[1024,4096]{1,0:T(8,128)(2,1)} %get-tuple-element.126, bf16[1024,4096]{1,0:T(8,128)(2,1)} %get-tuple-element.125), kind=kLoop, calls=%fused_computation.56 | loop fusion | flops 33554432 | bytes 33554432 | tf_op jit(solution)/shard_map/cond/branch_1_fun/concatenate | solution.py:490
  434.9 26.7 %conditional.18 = (bf16[1024,2048]{1,0:T(8,128)(2,1)}) conditional(s32[]{:T(128)} %bitcast.74, () %tuple.155, bf16[128,2048]{1,0:T(8,128)(2,1)S(1)} %get-tuple-element.346), branch_computations={%region_24.25_spmd, %region_25.26_spmd} | conditional | bytes 26214608 | solution.py:353
  515.5 52.4 %conditional.19 = (f32[128,2048]{1,0:T(8,128)S(1)}, f32[128,2048]{1,0:T(8,128)S(1)}) conditional(s32[]{:T(128)} %bitcast.74, () %tuple.154, (f32[1024,2048]{1,0:T(8,128)S(1)}, f32[1024,2048]{1,0:T(8,128)}) %tuple.158), branch_computations={%region_26.27_spmd, %region_27.28_spmd} | conditional | flops 5767168 | bytes 131072416 | solution.py:353
  569.9 27.1 %conditional.20 = (bf16[1024,2048]{1,0:T(8,128)(2,1)}) conditional(s32[]{:T(128)} %bitcast.74, () %tuple.161, bf16[128,2048]{1,0:T(8,128)(2,1)} %get-tuple-element.253), branch_computations={%region_29.30_spmd, %region_30.31_spmd} | conditional | bytes 26214608 | solution.py:353
  597.0 28.6 %conditional.21 = (bf16[1024,256]{0,1:T(8,128)(2,1)}, bf16[2048,256]{0,1:T(8,128)(2,1)}, bf16[2048,256]{0,1:T(8,128)(2,1)}, bf16[2,256,2048]{2,1,0:T(8,128)(2,1)}) conditional(s32[]{:T(128)} %bitcast.74, () %tuple.160, (bf16[1024,2048]{1,0:T(8,128)(2,1)}, bf16[256,2048]{1,0:T(8,128)(2,1)}, bf16[8,256,2,128]{3,2,1,0:T(2,128)(2,1)}, ...), branch_computations={%region_32.33_spmd, %region_33.35_spmd} | conditional | flops 1616640000 | bytes 62406868 | solution.py:353
  663.6 35.2 %conditional.22 = (f32[128,2048]{1,0:T(8,128)S(1)}) conditional(s32[]{:T(128)} %bitcast.74, () %tuple.159, f32[1024,2048]{1,0:T(8,128)} %fusion.116), branch_computations={%region_35.36_spmd, %region_36.37_spmd} | conditional | flops 2883584 | bytes 65536208 | solution.py:353
  677.5 12.4 %collective-permute-done.57 = bf16[2,128,1024]{2,1,0:T(8,128)(2,1)S(1)} collective-permute-done((bf16[2,128,1024]{2,1,0:T(8,128)(2,1)S(1)}, bf16[2,128,1024]{2,1,0:T(8,128)(2,1)S(1)}, u32[]{:S(2)}, u32[]{:S(2)}) %collective-permute-start.57) | collective-permute-done | bytes 524320 | tf_op jit(solution)/shard_map/cond/branch_1_fun/ppermute | solution.py:241
  701.8 26.5 %conditional.23 = (bf16[1024,2048]{1,0:T(8,128)(2,1)}) conditional(s32[]{:T(128)} %bitcast.74, () %tuple.165, bf16[128,2048]{1,0:T(8,128)(2,1)S(1)} %get-tuple-element.258), branch_computations={%region_39.40_spmd, %region_40.41_spmd} | conditional | bytes 26214608 | solution.py:353
  775.6 86.5 %conditional.24 = (f32[128,2048]{1,0:T(8,128)}, f32[3,2048]{1,0:T(4,128)S(1)}, bf16[4,256,2048]{2,1,0:T(8,128)(2,1)}) conditional(s32[]{:T(128)} %bitcast.74, () %tuple.164, (f32[1024,2048]{1,0:T(8,128)S(1)}, f32[3,2048]{1,0:T(4,128)S(1)}, f32[128,2048]{1,0:T(8,128)S(1)}, f32[128,2048]{1,0:T(8,128)S(1)}, f32[128,2048]{1,0:T(8,128)S(1)}, ...), branch_computations={%region_47.48_spmd, %region_48.52_spmd} | conditional | flops 9706240 | bytes 90813712 | solution.py:353
  790.4 60.1 %collective-permute-done.62 = bf16[2,128,1024]{2,1,0:T(8,128)(2,1)S(1)} collective-permute-done((bf16[2,128,1024]{2,1,0:T(8,128)(2,1)S(1)}, bf16[2,128,1024]{2,1,0:T(8,128)(2,1)S(1)}, u32[]{:S(2)}, u32[]{:S(2)}) %collective-permute-start.62) | collective-permute-done | bytes 524320 | tf_op jit(solution)/shard_map/cond/branch_1_fun/ppermute | solution.py:241
  875.8 115.7 %conditional.25 = (f32[6,256,2048]{2,1,0:T(8,128)}, f32[6,256,2048]{2,1,0:T(8,128)}, f32[6,256,2048]{2,1,0:T(8,128)}, bf16[2,256,2048]{2,1,0:T(8,128)(2,1)}, f32[3,2048]{1,0:T(4,128)S(1)}) conditional(s32[]{:T(128)} %bitcast.74, () %tuple.172, (s32[6]{0:T(128)S(1)}, s32[6,8]{1,0:T(8,128)S(1)}, s32[6]{0:T(128)S(1)}, s32[3]{0:T(128)S(1)}, ...), branch_computations={%region_66.67_spmd, %region_67.68_spmd} | conditional | flops 97548288 | bytes 140322336 | solution.py:353
  898.6 31.4 %collective-permute-done.31 = f32[3,2048]{1,0:T(4,128)S(1)} collective-permute-done((f32[3,2048]{1,0:T(4,128)S(1)}, f32[3,2048]{1,0:T(4,128)S(1)}, u32[]{:S(2)}, u32[]{:S(2)}) %collective-permute-start.31) | collective-permute-done | bytes 24608 | tf_op jit(solution)/shard_map/cond/branch_1_fun/ppermute | solution.py:241
  941.9 24.9 %adam_tiles.3 = (f32[6,256,2048]{2,1,0:T(8,128)}, f32[6,256,2048]{2,1,0:T(8,128)}, f32[6,256,2048]{2,1,0:T(8,128)}) custom-call(s32[3]{0:T(128)S(1)} %get-tuple-element.287.visit_ref, s32[3]{0:T(128)S(1)} %get-tuple-element.421.mode_ref, s32[24]{0:T(128)S(1)} %reshape.392.cp_ref, s32[3]{0:T(128)S(1)} %get-tuple-element.416.rp_ref, ...), custom_call_target="tpu_custom_call" | custom-call | flops 47185920 | bytes 40894464 | tf_op jit(solution)/shard_map/cond/branch_1_fun/adam_tiles/pallas_call | solution.py:211
  966.9 21.5 %adam_tiles.4 = (f32[6,256,2048]{2,1,0:T(8,128)}, f32[6,256,2048]{2,1,0:T(8,128)}, f32[6,256,2048]{2,1,0:T(8,128)}) custom-call(s32[3]{0:T(128)S(1)} %copy-done.7, s32[3]{0:T(128)S(1)} %get-tuple-element.420.mode_ref, s32[24]{0:T(128)S(1)} %reshape.391.cp_ref, ...), custom_call_target="tpu_custom_call", output_to_operand_aliasing={{0}: (10, {}), {1}: (11, {}), {2}: (12, {})} | custom-call | flops 47185920 | bytes 40894464 | tf_op jit(solution)/shard_map/cond/branch_1_fun/adam_tiles/pallas_call | solution.py:211
  992.2 21.8 %adam_tiles.5 = (f32[6,256,2048]{2,1,0:T(8,128)}, f32[6,256,2048]{2,1,0:T(8,128)}, f32[6,256,2048]{2,1,0:T(8,128)}) custom-call(s32[5]{0:T(128)S(1)} %broadcast_select_fusion.7.visit_ref, s32[5]{0:T(128)S(1)} %compare_select_fusion.15.mode_ref, s32[40]{0:T(128)S(1)} %select_n.470.cp_ref, ...), custom_call_target="tpu_custom_call", output_to_operand_aliasing={{0}: (12, {}), {1}: (13, {}), {2}: (14, {})} | custom-call | flops 78643200 | bytes 68157440 | tf_op jit(solution)/shard_map/adam_tiles/pallas_call | solution.py:211
  (700 shorter events, 722.2 us)
Async XLA Ops:
  24.7 49.1 %all-to-all-start = ((bf16[8,3,256,256]{3,2,1,0:T(8,128)(2,1)}), bf16[8,3,256,256]{3,2,1,0:T(8,128)(2,1)S(1)}, u32[]{:S(2)}, u32[]{:S(2)}) async-start(bf16[8,3,256,256]{3,2,1,0:T(8,128)(2,1)} %copy-done), calls=%async_computation | async-start | bytes 6291456 | tf_op jit(solution)/shard_map/all_to_all | solution.py:360
  30.0 134.0 %all-gather.6.cloned.1.call-start = ((), (), s32[]{:S(2)}) async-start(), calls=%async_computation.9 | async-start | bytes 3932160 | tf_op jit(solution)/shard_map/all_gather | solution.py:381
  79.7 136.4 %all-gather.8.cloned.1.call-start = ((), (), s32[]{:S(2)}) async-start(), calls=%async_computation.10 | async-start | bytes 2621440 | tf_op jit(solution)/shard_map/all_gather | solution.py:418
  84.9 45.0 %collective-permute-start.77 = (bf16[2,256,2048]{2,1,0:T(8,128)(2,1)}, bf16[2,256,2048]{2,1,0:T(8,128)(2,1)}, u32[]{:S(2)}, u32[]{:S(2)}) collective-permute-start(bf16[2,256,2048]{2,1,0:T(8,128)(2,1)} %pad_maximum_fusion.13), channel_id=1, source_target_pairs={{0,1},{1,0},{2,3},{3,2},{4,5},{5,4},{6,7},{7,6},{8,9},{9,8},{10,11... | collective-permute-start | bytes 6291464 | tf_op jit(solution)/shard_map/ppermute | solution.py:241
  158.6 41.7 %all-to-all-start.1 = ((bf16[8,3,256,256]{3,2,1,0:T(8,128)(2,1)}), bf16[8,3,256,256]{3,2,1,0:T(8,128)(2,1)}, u32[]{:S(2)}, u32[]{:S(2)}) async-start(bf16[8,3,256,256]{3,2,1,0:T(8,128)(2,1)} %copy-done.1), calls=%async_computation.1 | async-start | bytes 6291456 | tf_op jit(solution)/shard_map/all_to_all | solution.py:399
  163.0 173.4 %all-gather.10.cloned.1.call-start = ((), (), s32[]{:S(2)}) async-start(), calls=%async_computation.11 | async-start | bytes 6553600 | tf_op jit(solution)/shard_map/all_gather | solution.py:381
  203.4 258.1 %all-gather.12.cloned.1.call-start = ((), (), s32[]{:S(2)}) async-start(), calls=%async_computation.12 | async-start | bytes 5242880 | tf_op jit(solution)/shard_map/all_gather | solution.py:381
  209.3 270.5 %all-gather.14.cloned.1.call-start = ((), (), s32[]{:S(2)}) async-start(), calls=%async_computation.13 | async-start | bytes 5242880 | tf_op jit(solution)/shard_map/all_gather | solution.py:381
  209.3 68.3 %collective-permute-start.81 = (bf16[256,4096]{1,0:T(8,128)(2,1)}, bf16[256,4096]{1,0:T(8,128)(2,1)}, u32[]{:S(2)}, u32[]{:S(2)}) collective-permute-start(bf16[256,4096]{1,0:T(8,128)(2,1)} %bitcast.394), channel_id=1, source_target_pairs={{0,2},{2,0},{1,3},{3,1},{4,6},{6,4},{5,7},{7,5},{8,10},{10,8},{9,1... | collective-permute-start | bytes 6291464 | tf_op jit(solution)/shard_map/ppermute | solution.py:241
  210.6 67.1 %collective-permute-start.82 = (bf16[256,4096]{1,0:T(8,128)(2,1)}, bf16[256,4096]{1,0:T(8,128)(2,1)}, u32[]{:S(2)}, u32[]{:S(2)}) collective-permute-start(bf16[256,4096]{1,0:T(8,128)(2,1)} %bitcast.395), channel_id=1, source_target_pairs={{0,4},{4,0},{1,5},{5,1},{2,6},{6,2},{3,7},{7,3},{8,12},{12,8},{9,1... | collective-permute-start | bytes 6291464 | tf_op jit(solution)/shard_map/ppermute | solution.py:241
  234.8 33.4 %collective-permute-start.37 = (bf16[2,128,1024]{2,1,0:T(8,128)(2,1)S(1)}, bf16[2,128,1024]{2,1,0:T(8,128)(2,1)S(1)}, u32[]{:S(2)}, u32[]{:S(2)}) collective-permute-start(bf16[2,128,1024]{2,1,0:T(8,128)(2,1)S(1)} %slice_bitcast_fusion.5), channel_id=1, source_target_pairs={{0,2},{2,0},{1,3},{3,1},{4,6},{6,4},{5,7},{7,5},{8,10},{10,8},{9,1... | collective-permute-start | bytes 1572872 | tf_op jit(solution)/shard_map/cond/branch_1_fun/ppermute | solution.py:241
  336.5 35.3 %collective-permute-start.11 = (bf16[256,2048]{1,0:T(8,128)(2,1)}, bf16[256,2048]{1,0:T(8,128)(2,1)}, u32[]{:S(2)}, u32[]{:S(2)}) collective-permute-start(bf16[256,2048]{1,0:T(8,128)(2,1)} %get-tuple-element.123), channel_id=1, source_target_pairs={{0,2},{2,0},{1,3},{3,1},{4,6},{6,4},{5,7},{7,5},{8,10},{10,8},{9,1... | collective-permute-start | bytes 3145736 | tf_op jit(solution)/shard_map/cond/branch_1_fun/ppermute | solution.py:241
  374.5 222.5 %reduce-scatter.6.cloned.1.call-start = ((), (), s32[]{:S(2)}) async-start(), calls=%async_computation.14 | async-start | bytes 5242880 | tf_op jit(solution)/shard_map/reduce_scatter | solution.py:504
  479.7 222.1 %reduce-scatter.8.cloned.1.call-start = ((), (), s32[]{:S(2)}) async-start(), calls=%async_computation.15 | async-start | bytes 5242880 | tf_op jit(solution)/shard_map/reduce_scatter | solution.py:504
  500.7 257.1 %reduce-scatter.10.cloned.1.call-start = ((), (), s32[]{:S(2)}) async-start(), calls=%async_computation.16 | async-start | bytes 6553600 | tf_op jit(solution)/shard_map/reduce_scatter | solution.py:504
  651.6 210.4 %reduce-scatter.12.cloned.1.call-start = ((), (), s32[]{:S(2)}) async-start(), calls=%async_computation.17 | async-start | bytes 3932160 | tf_op jit(solution)/shard_map/reduce_scatter | solution.py:504
  764.1 100.3 %all-to-all-start.2 = ((bf16[8,6,256,256]{3,2,1,0:T(8,128)(2,1)}), bf16[8,6,256,256]{3,2,1,0:T(8,128)(2,1)}, u32[]{:S(2)}, u32[]{:S(2)}) async-start(bf16[8,6,256,256]{3,2,1,0:T(8,128)(2,1)} %pack_gradients.1), calls=%async_computation.5 | async-start | bytes 12582912 | tf_op jit(solution)/shard_map/all_to_all | solution.py:581
  768.8 107.0 %reduce-scatter.14.cloned.1.call-start = ((), (), s32[]{:S(2)}) async-start(), calls=%async_computation.18 | async-start | bytes 2621440 | tf_op jit(solution)/shard_map/reduce_scatter | solution.py:504
  778.9 74.3 %collective-permute-start.66 = (bf16[2,256,2048]{2,1,0:T(8,128)(2,1)}, bf16[2,256,2048]{2,1,0:T(8,128)(2,1)S(1)}, u32[]{:S(2)}, u32[]{:S(2)}) collective-permute-start(bf16[2,256,2048]{2,1,0:T(8,128)(2,1)} %get-tuple-element.142), channel_id=1, source_target_pairs={{0,1},{1,0},{2,3},{3,2},{4,5},{5,4},{6,7},{7,6},{8,9},{9,8},{10,11... | collective-permute-start | bytes 6291464 | tf_op jit(solution)/shard_map/cond/branch_1_fun/ppermute | solution.py:241
  786.7 63.8 %collective-permute-start.62 = (bf16[2,128,1024]{2,1,0:T(8,128)(2,1)S(1)}, bf16[2,128,1024]{2,1,0:T(8,128)(2,1)S(1)}, u32[]{:S(2)}, u32[]{:S(2)}) collective-permute-start(bf16[2,128,1024]{2,1,0:T(8,128)(2,1)S(1)} %slice_bitcast_fusion.35), channel_id=1, source_target_pairs={{0,2},{2,0},{1,3},{3,1},{4,6},{6,4},{5,7},{7,5},{8,10},{10,8},{9,1... | collective-permute-start | bytes 1572872 | tf_op jit(solution)/shard_map/cond/branch_1_fun/ppermute | solution.py:241
  788.9 63.4 %collective-permute-start.64 = (bf16[2,128,1024]{2,1,0:T(8,128)(2,1)S(1)}, bf16[2,128,1024]{2,1,0:T(8,128)(2,1)S(1)}, u32[]{:S(2)}, u32[]{:S(2)}) collective-permute-start(bf16[2,128,1024]{2,1,0:T(8,128)(2,1)S(1)} %slice_bitcast_fusion.33), channel_id=1, source_target_pairs={{0,4},{4,0},{1,5},{5,1},{2,6},{6,2},{3,7},{7,3},{8,12},{12,8},{9,1... | collective-permute-start | bytes 1572872 | tf_op jit(solution)/shard_map/cond/branch_1_fun/ppermute | solution.py:241
  866.3 125.8 %all-to-all-start.3 = ((bf16[8,3,256,256]{3,2,1,0:T(8,128)(2,1)}), bf16[8,3,256,256]{3,2,1,0:T(8,128)(2,1)S(1)}, u32[]{:S(2)}, u32[]{:S(2)}) async-start(bf16[8,3,256,256]{3,2,1,0:T(8,128)(2,1)} %bitcast.377), calls=%async_computation.7 | async-start | bytes 6291456 | tf_op jit(solution)/shard_map/all_to_all | solution.py:595
  895.2 93.2 %collective-permute-start.29 = (bf16[256,2048]{1,0:T(8,128)(2,1)}, bf16[256,2048]{1,0:T(8,128)(2,1)}, u32[]{:S(2)}, u32[]{:S(2)}) collective-permute-start(bf16[256,2048]{1,0:T(8,128)(2,1)} %broadcast_select_fusion), channel_id=1, source_target_pairs={{0,2},{1,3},{2,0},{3,1},{4,6},{5,7},{6,4},{7,5},{8,10},{9,11},{10,... | collective-permute-start | bytes 3145736 | tf_op jit(solution)/shard_map/cond/branch_1_fun/ppermute | solution.py:508
  938.0 50.4 %collective-permute-start.34 = (f32[3,2048]{1,0:T(4,128)S(1)}, f32[3,2048]{1,0:T(4,128)S(1)}, u32[]{:S(2)}, u32[]{:S(2)}) collective-permute-start(f32[3,2048]{1,0:T(4,128)S(1)} %add.386), channel_id=1, source_target_pairs={{0,16},{8,24},{16,0},{24,8},{1,17},{9,25},{17,1},{25,9},{2,18},{10... | collective-permute-start | bytes 73736 | tf_op jit(solution)/shard_map/cond/branch_1_fun/ppermute | solution.py:271
  (158 other events, 2429.0 us)
Sparse Core Ops, SparseCore 0:
  79.8 63.7 all-gather.5
  158.7 47.4 all-gather.7
  207.7 96.7 all-gather.9
  305.9 79.1 all-gather.11
  386.5 79.2 all-gather.13
  479.8 77.3 reduce-scatter.5
  559.7 77.2 reduce-scatter.7
  651.8 94.1 reduce-scatter.9
  757.4 61.3 reduce-scatter.11
  820.9 43.8 reduce-scatter.13
